TPU v7x, 128 devices: a whole 4x4x4 slice. The times are simulated.
128 devices in a mesh: fsdp: 64 (over x, y, z_lo, core), tp: 2 (over z_hi).
Axes of the slice: x: 4, y: 4, z: 4 (z_hi: 2, z_lo: 2; z = z_hi * 2 + z_lo), core: 2. Of those that a mesh axis runs over, the one named last changes fastest.
Arguments:
- inputs: float32 [25600, 768], P(('fsdp', 'tp')), may hold values from -6 to 6
- routes: int32 [25600, 2], P('fsdp'), may hold values from 0 to 15, all different within a row; in each aligned block of 400 rows (0 to 399, 400 to 799, ...) at most 63 rows name the same one
- attention_norm_gain: bfloat16 [768], P('fsdp'), may hold values from 0.099609375 to 1.8984375
- attention_norm_shift: bfloat16 [768], P('fsdp'), may hold values from -3 to 3
- qkv_weight: bfloat16 [3, 768, 768], P(None, 'fsdp', 'tp'), may hold values from -0.21875 to 0.21875
- proj_weight: bfloat16 [768, 768], P('tp', 'fsdp'), may hold values from -0.875 to 0.875
- expert_norm_gain: bfloat16 [768], P('fsdp'), may hold values from 0.099609375 to 1.8984375
- expert_norm_shift: bfloat16 [768], P('fsdp'), may hold values from -3 to 3
- router_weight: bfloat16 [768, 16], P('fsdp'), may hold values from -0.109375 to 0.109375
- expert_in: bfloat16 [768, 16, 3072], P('fsdp', None, 'tp'), may hold values from -0.21875 to 0.21875
- expert_out: bfloat16 [768, 16, 3072], P('fsdp', None, 'tp'), may hold values from -0.4375 to 0.4375
- cotangent: float32 [25600, 768], P(('fsdp', 'tp')), may hold values from -6 to 6
Outputs:
- outputs: float32 [25600, 768], P(('fsdp', 'tp'))
- input_grad: float32 [25600, 768], P(('fsdp', 'tp'))
- attn_gain_grad: float32 [768], P('fsdp')
- attn_shift_grad: float32 [768], P('fsdp')
- qkv_grad: float32 [3, 768, 768], P(None, 'fsdp', 'tp')
- proj_grad: float32 [768, 768], P('tp', 'fsdp')
- moe_gain_grad: float32 [768], P('fsdp')
- moe_shift_grad: float32 [768], P('fsdp')
- router_grad: float32 [768, 16], P('fsdp')
- expert_in_grad: float32 [768, 16, 3072], P('fsdp', None, 'tp')
- expert_out_grad: float32 [768, 16, 3072], P('fsdp', None, 'tp')
Inputs may be any that keep to these rules, and one draw needn't show every extreme that they name: `routes`: in each aligned block of 400 rows (one routing group) the two experts of a row differ and no expert is named by more than 63 rows; some expert is named by exactly 63 rows of some block.
All inputs are finite; a program needn't handle non-finite values.
Results may differ from a plain program's by a relative error of at most 0.01.
Values may be sent and summed in bfloat16 or wider, within the bound.
A program may use at most 192 MiB of HBM per device.

v0:
```python
import jax
import jax.numpy as jnp
from jax import lax
from jax.sharding import PartitionSpec as P

HEAD_DIM = 64
SEQ = 200
REAL_TOK = 197
CAP = 63


EPS = 1e-06
TOP = lax.Precision.HIGHEST


def gelu_exact(value):
    return jax.nn.gelu(value, approximate=False)


def normalize_rows(value, norm_gain, norm_shift):
    row_mean = jnp.mean(value, axis=-1, keepdims=True)
    centered_rows = value - row_mean
    inverse_deviation = lax.rsqrt(
        jnp.mean(centered_rows * centered_rows, axis=-1, keepdims=True) + EPS
    )
    standardized_rows = centered_rows * inverse_deviation
    normed_rows = (
        standardized_rows * norm_gain.astype(jnp.float32) + norm_shift.astype(jnp.float32)
    ).astype(jnp.bfloat16)
    return (normed_rows, standardized_rows, inverse_deviation)


def norm_backward(incoming_gradient, standardized_rows, inverse_deviation, norm_gain):
    scaled_gradient = incoming_gradient * norm_gain.astype(jnp.float32)
    inner_product = (
        scaled_gradient
        - jnp.mean(scaled_gradient, axis=-1, keepdims=True)
        - standardized_rows * jnp.mean(scaled_gradient * standardized_rows, axis=-1, keepdims=True)
    )
    return (
        inverse_deviation * inner_product,
        jnp.sum(incoming_gradient * standardized_rows, axis=0),
        jnp.sum(incoming_gradient, axis=0),
    )


def slot_table(routes, experts, capacity):
    picked = (routes[:, :, None] == jnp.arange(experts, dtype=jnp.int32)[None, None, :]).astype(
        jnp.int32
    )
    flat = picked.reshape(-1, experts)
    before = jnp.cumsum(flat, axis=0) - flat
    number = jnp.sum(before * flat, axis=-1)
    slot = routes.reshape(-1) * capacity + number
    owner = jnp.arange(flat.shape[0], dtype=jnp.int32) // 2
    token_of_slot = jnp.zeros((experts * capacity,), jnp.int32).at[slot].set(owner)
    filled = jnp.zeros((experts * capacity,), jnp.int32).at[slot].set(1)
    return (picked, slot, token_of_slot, filled)


def split_heads(value, images):
    input_rows, width = value.shape
    return value.reshape(images, input_rows // images, width // HEAD_DIM, HEAD_DIM)


def live_keys(length):
    return (jnp.arange(length) < REAL_TOK)[None, None, None, :]


def attend(query, key, value, images):
    query_h = split_heads(query, images)
    key_h = split_heads(key, images)
    value_h = split_heads(value, images)
    scores = jnp.einsum(
        "ishd,ithd->ihst", query_h, key_h, preferred_element_type=jnp.float32
    ) * HEAD_DIM ** (-0.5)
    live = live_keys(scores.shape[-1])
    lse = jnp.log(jnp.sum(jnp.where(live, jnp.exp(scores), 0.0), axis=-1, keepdims=True))
    probs = jnp.where(live, jnp.exp(scores - lse), 0.0).astype(jnp.bfloat16)
    context = jnp.einsum(
        "ihst,ithd->ishd", probs, value_h, preferred_element_type=jnp.float32
    ).astype(jnp.bfloat16)
    return (context.reshape(query.shape), lse)


def attend_back(query, key, value, lse, context_grad, images):
    query_h = split_heads(query, images)
    key_h = split_heads(key, images)
    value_h = split_heads(value, images)
    grad_h = split_heads(context_grad, images)
    scores = jnp.einsum(
        "ishd,ithd->ihst", query_h, key_h, preferred_element_type=jnp.float32
    ) * HEAD_DIM ** (-0.5)
    live = live_keys(scores.shape[-1])
    probs = jnp.where(live, jnp.exp(scores - lse), 0.0)
    value_grad = jnp.einsum(
        "ihst,ishd->ithd", probs.astype(jnp.bfloat16), grad_h, preferred_element_type=jnp.float32
    ).astype(jnp.bfloat16)
    inner_product = jnp.einsum(
        "ishd,ithd->ihst", grad_h, value_h, preferred_element_type=jnp.float32
    )
    score_grad = (
        probs
        * (inner_product - jnp.sum(probs * inner_product, axis=-1, keepdims=True))
        * HEAD_DIM ** (-0.5)
    ).astype(jnp.bfloat16)
    query_grad = jnp.einsum(
        "ihst,ithd->ishd", score_grad, key_h, preferred_element_type=jnp.float32
    ).astype(jnp.bfloat16)
    key_grad = jnp.einsum(
        "ihst,ishd->ithd", score_grad, query_h, preferred_element_type=jnp.float32
    ).astype(jnp.bfloat16)
    shape = query.shape
    return (query_grad.reshape(shape), key_grad.reshape(shape), value_grad.reshape(shape))


def gather_dense(
    qkv_weight,
    proj_weight,
    router_weight,
    attention_norm_gain,
    attention_norm_shift,
    expert_norm_gain,
    expert_norm_shift,
):
    return (
        lax.all_gather(qkv_weight, "fsdp", axis=1, tiled=True),
        lax.all_gather(proj_weight, "fsdp", axis=1, tiled=True),
        lax.all_gather(router_weight, "fsdp", axis=0, tiled=True),
        lax.all_gather(attention_norm_gain, "fsdp", axis=0, tiled=True),
        lax.all_gather(attention_norm_shift, "fsdp", axis=0, tiled=True),
        lax.all_gather(expert_norm_gain, "fsdp", axis=0, tiled=True),
        lax.all_gather(expert_norm_shift, "fsdp", axis=0, tiled=True),
    )


def group_rows(value):
    return lax.all_gather(value, "tp", axis=0, tiled=True)


def owned_rows(value):
    return lax.psum_scatter(value, "tp", scatter_dimension=0, tiled=True)


def to_owners(slots, holders):
    experts, capacity, width = slots.shape
    spread = jnp.broadcast_to(slots[:, None], (experts, holders, capacity, width)).reshape(
        experts * holders, capacity, width
    )
    moved = lax.all_to_all(spread, "fsdp", split_axis=0, concat_axis=0, tiled=True)
    return moved.reshape(-1, width)


def to_groups(partial_value, experts, holders, capacity):
    width = partial_value.shape[1]
    pieces = partial_value.reshape(experts * holders, capacity, width)
    moved = lax.all_to_all(pieces, "fsdp", split_axis=0, concat_axis=0, tiled=True)
    return jnp.sum(moved.reshape(experts, holders, capacity, width), axis=1)


def per_device(
    inputs,
    routes,
    attention_norm_gain,
    attention_norm_shift,
    qkv_weight,
    proj_weight,
    expert_norm_gain,
    expert_norm_shift,
    router_weight,
    expert_in,
    expert_out,
    cotangent,
):
    f32 = jnp.float32
    bf16 = jnp.bfloat16
    dense = gather_dense(
        qkv_weight,
        proj_weight,
        router_weight,
        attention_norm_gain,
        attention_norm_shift,
        expert_norm_gain,
        expert_norm_shift,
    )
    qkv_full, proj_full, router_full, attention_gain, attention_shift, expert_gain, expert_shift = (
        dense
    )
    group = routes.shape[0]
    images = group // SEQ
    experts = router_full.shape[1]
    width = qkv_full.shape[1]
    units = expert_in.shape[2]
    local_rows = expert_in.shape[0]
    holders = lax.axis_size("fsdp") // experts
    block_units = units // holders
    attention_normed, attention_standardized, attention_inverse_deviation = normalize_rows(
        inputs, attention_gain, attention_shift
    )
    tokens_a = group_rows(attention_normed)
    proj = jnp.einsum("td,idh->ith", tokens_a, qkv_full, preferred_element_type=f32).astype(bf16)
    context, lse = attend(proj[0], proj[1], proj[2], images)
    residual_middle = inputs + owned_rows(jnp.dot(context, proj_full, preferred_element_type=f32))
    expert_normed, expert_standardized, expert_inverse_deviation = normalize_rows(
        residual_middle, expert_gain, expert_shift
    )
    tokens_m = group_rows(expert_normed)
    logits = jnp.dot(tokens_m, router_full, preferred_element_type=f32)
    raised = jnp.exp(logits)
    probs = raised / jnp.sum(raised, axis=-1, keepdims=True)
    picked, slot, token_of_slot, filled = slot_table(routes, experts, CAP)
    gates = jnp.sum(picked.astype(f32) * probs[:, None, :], axis=-1)
    slotted = jnp.where(filled[:, None] > 0, tokens_m[token_of_slot], jnp.zeros((), bf16)).reshape(
        experts, CAP, width
    )
    regroup_in = expert_in.reshape(local_rows, experts * holders, block_units)
    regroup_out = expert_out.reshape(local_rows, experts * holders, block_units)
    own_in, own_out = (
        lax.all_to_all(regroup_in, "fsdp", split_axis=1, concat_axis=0, tiled=True),
        lax.all_to_all(regroup_out, "fsdp", split_axis=1, concat_axis=0, tiled=True),
    )
    own_in = own_in.reshape(width, block_units)
    own_out = own_out.reshape(width, block_units)
    owner_x = to_owners(slotted, holders)
    owner_pre = jnp.dot(owner_x, own_in, preferred_element_type=f32)
    owner_hidden = gelu_exact(owner_pre).astype(bf16)
    owner_res = jnp.einsum("cf,df->cd", owner_hidden, own_out, preferred_element_type=f32)
    expert_res = to_groups(owner_res, experts, holders, CAP)
    routed = expert_res.reshape(experts * CAP, width)[slot].reshape(group, 2, width)
    outputs = residual_middle + owned_rows(jnp.sum(gates[:, :, None] * routed, axis=1))
    (
        qkv_back,
        proj_back,
        router_back,
        attention_gain_gradient,
        shift_unused,
        expert_gain_gradient,
        shift_spare,
    ) = gather_dense(
        qkv_weight,
        proj_weight,
        router_weight,
        attention_norm_gain,
        attention_norm_shift,
        expert_norm_gain,
        expert_norm_shift,
    )
    dout = group_rows(cotangent.astype(bf16))
    dout_f = dout.astype(f32)
    gate_of_slot = jnp.zeros((experts * CAP,), f32).at[slot].set(gates.reshape(-1))
    slot_grad = (
        jnp.where(filled[:, None] > 0, gate_of_slot[:, None] * dout_f[token_of_slot], 0.0)
        .astype(bf16)
        .reshape(experts, CAP, width)
    )
    gate_grad = jnp.sum(dout_f[:, None, :] * routed, axis=-1)
    owner_g = to_owners(slot_grad, holders)
    owner_hgrad = jnp.dot(owner_g, own_out, preferred_element_type=f32)
    owner_pgrad = jax.vjp(gelu_exact, owner_pre)[1](owner_hgrad)[0].astype(bf16)
    owner_back = jnp.einsum("cf,df->cd", owner_pgrad, own_in, preferred_element_type=f32)
    slot_in_grad = to_groups(owner_back, experts, holders, CAP)
    in_local = jnp.einsum("cd,cf->df", owner_x, owner_pgrad, preferred_element_type=f32)
    out_local = jnp.einsum("cd,cf->df", owner_g, owner_hidden, preferred_element_type=f32)
    in_home, out_home = (
        lax.all_to_all(
            in_local.reshape(width, 1, block_units).astype(jnp.bfloat16),
            "fsdp",
            split_axis=0,
            concat_axis=1,
            tiled=True,
        ).astype(jnp.float32),
        lax.all_to_all(
            out_local.reshape(width, 1, block_units).astype(jnp.bfloat16),
            "fsdp",
            split_axis=0,
            concat_axis=1,
            tiled=True,
        ).astype(jnp.float32),
    )
    in_grad = in_home.reshape(local_rows, experts, units)
    out_grad = out_home.reshape(local_rows, experts, units)
    choice_grad = jnp.sum(picked.astype(f32) * gate_grad[:, :, None], axis=1)
    logit_grad = probs * (choice_grad - jnp.sum(probs * choice_grad, axis=-1, keepdims=True))
    router_part = jnp.einsum("td,te->de", tokens_m.astype(f32), logit_grad, precision=TOP)
    routed_in = slot_in_grad.reshape(experts * CAP, width)[slot].reshape(group, 2, width)
    token_gradient = jnp.sum(routed_in, axis=1) + jnp.einsum(
        "te,de->td", logit_grad, router_back.astype(f32), precision=TOP
    )
    expert_norm_backward, expert_gain_partial, expert_shift_partial = norm_backward(
        owned_rows(token_gradient),
        expert_standardized,
        expert_inverse_deviation,
        expert_gain_gradient,
    )
    middle_grad = cotangent + expert_norm_backward
    mid_rows = group_rows(middle_grad.astype(bf16))
    proj_part = jnp.einsum("th,td->hd", context, mid_rows, preferred_element_type=f32)
    context_grad = jnp.einsum("td,hd->th", mid_rows, proj_back, preferred_element_type=f32).astype(
        bf16
    )
    query_grad, key_grad, value_grad = attend_back(
        proj[0], proj[1], proj[2], lse, context_grad, images
    )
    stacked = jnp.stack([query_grad, key_grad, value_grad])
    qkv_part = jnp.einsum("td,ith->idh", tokens_a, stacked, preferred_element_type=f32)
    attention_input_gradient = owned_rows(
        jnp.einsum("ith,idh->td", stacked, qkv_back, preferred_element_type=f32)
    )
    attention_norm_backward, attention_gain_partial, attention_shift_partial = norm_backward(
        attention_input_gradient,
        attention_standardized,
        attention_inverse_deviation,
        attention_gain_gradient,
    )
    input_grad = middle_grad + attention_norm_backward
    sums = (
        lax.psum_scatter(qkv_part, "fsdp", scatter_dimension=1, tiled=True),
        lax.psum_scatter(proj_part, "fsdp", scatter_dimension=1, tiled=True),
        lax.psum_scatter(router_part, "fsdp", scatter_dimension=0, tiled=True),
        lax.psum_scatter(attention_gain_partial, "fsdp", scatter_dimension=0, tiled=True),
        lax.psum_scatter(attention_shift_partial, "fsdp", scatter_dimension=0, tiled=True),
        lax.psum_scatter(expert_gain_partial, "fsdp", scatter_dimension=0, tiled=True),
        lax.psum_scatter(expert_shift_partial, "fsdp", scatter_dimension=0, tiled=True),
    )
    shared = lax.psum((sums[2], sums[3], sums[4], sums[5], sums[6]), "tp")
    return (
        outputs,
        input_grad,
        shared[1],
        shared[2],
        sums[0],
        sums[1],
        shared[3],
        shared[4],
        shared[0],
        in_grad,
        out_grad,
    )


def solution(mesh):
    return jax.shard_map(
        per_device,
        mesh=mesh,
        in_specs=(
            P(("fsdp", "tp"), None),
            P("fsdp", None),
            P("fsdp"),
            P("fsdp"),
            P(None, "fsdp", "tp"),
            P("tp", "fsdp"),
            P("fsdp"),
            P("fsdp"),
            P("fsdp", None),
            P("fsdp", None, "tp"),
            P("fsdp", None, "tp"),
            P(("fsdp", "tp"), None),
        ),
        out_specs=(
            P(("fsdp", "tp"), None),
            P(("fsdp", "tp"), None),
            P("fsdp"),
            P("fsdp"),
            P(None, "fsdp", "tp"),
            P("tp", "fsdp"),
            P("fsdp"),
            P("fsdp"),
            P("fsdp", None),
            P("fsdp", None, "tp"),
            P("fsdp", None, "tp"),
        ),
        check_vma=False,
    )
```

profile of v0, /device:TPU:1, one launch (start us, length us, event | category | flops | bytes accessed | tf_op | source)
XLA Modules:
  0.0 1772.1 jit_solution(14402707574367524282)
XLA Ops:
  14.2 142.1 %all-reduce.16 = (bf16[768]{0:T(1024)(128)(2,1)S(1)}, bf16[768]{0:T(1024)(128)(2,1)S(1)}, bf16[768]{0:T(1024)(128)(2,1)S(1)}, bf16[768]{0:T(1024)(128)(2,1)S(1)}) all-reduce(bf16[768]{0:T(1024)(128)(2,1)S(1)} %dynamic-update-slice.1, bf16[768]{0:T(1024)(128)(2,1)S(1)} %dynamic-update-slice, ...), channel_id=1, replica_groups=mesh['fsdp'=64,'tp'=2] {'fsdp'}, use_global_device_ids=true, to_apply=%add.2 | all-reduce | flops 3072 | bytes 12288
  156.3 84.4 %all-gather = bf16[64,12,384]{2,1,0:T(8,128)(2,1)S(1)} all-gather(bf16[1,12,384]{2,1,0:T(8,128)(2,1)} %bitcast.133), channel_id=1, replica_groups=mesh['fsdp'=64,'tp'=2] {'fsdp'}, dimensions={0}, use_global_device_ids=true | all-gather | bytes 599040 | tf_op jit(solution)/shard_map/all_gather | solution.py:128
  244.1 11.5 all_gather.40
  273.6 5.4 all-to-all-start.1
  282.1 5.3 scatter_custom_fusion.1
  287.4 5.3 scatter_custom_fusion
  294.4 9.6 reduce-scatter.9.cloned.1.call-done
  305.5 8.0 all-to-all-start.2
  313.7 19.0 %all_gather.45 = bf16[400,768]{1,0:T(8,128)(2,1)S(1)} all-gather(bf16[200,768]{1,0:T(8,128)(2,1)S(1)} %add_convert_fusion.1), channel_id=1, replica_groups=mesh['fsdp'=64,'tp'=2] {'tp'}, dimensions={0}, use_global_device_ids=true | all-gather | bytes 921600 | tf_op jit(solution)/shard_map/all_gather | solution.py:138
  332.8 5.2 gather_fusion
  343.3 4.8 broadcast_in_dim.63
  348.1 7.0 all-to-all-start
  355.1 145.6 %all-gather.1 = bf16[64,12,16]{2,1,0:T(8,128)(2,1)S(1)} all-gather(bf16[1,12,16]{2,1,0:T(8,128)(2,1)S(1)} %bitcast.134), channel_id=1, replica_groups=mesh['fsdp'=64,'tp'=2] {'fsdp'}, dimensions={0}, use_global_device_ids=true | all-gather | bytes 24960 | tf_op jit(solution)/shard_map/all_gather | solution.py:129
  501.5 10.9 all_gather.47
  512.5 5.3 gather_fusion.2
  522.7 5.3 scatter_custom_fusion.2
  536.2 6.2 all-to-all-start.4
  543.7 8.5 reshape.247
  552.2 8.9 fusion.100
  561.1 59.0 %all-to-all-done.4 = bf16[64,63,768]{2,1,0:T(8,128)(2,1)} async-done(((bf16[64,63,768]{2,1,0:T(8,128)(2,1)}), bf16[64,63,768]{2,1,0:T(8,128)(2,1)}, u32[]{:S(2)}, u32[]{:S(2)}) %all-to-all-start.4) | async-done | bytes 6193184 | tf_op jit(solution)/shard_map/all_to_all | solution.py:150
  620.1 8.5 reshape.257
  628.5 20.1 %add_convert_fusion = (bf16[4032,384]{1,0:T(8,128)(2,1)}, f32[4032,384]{1,0:T(8,128)}) fusion(f32[4032,384]{1,0:T(8,128)} %fusion.100, bf16[4032,768]{1,0:T(8,128)(2,1)} %reshape.257, bf16[768,384]{1,0:T(8,128)(2,1)S(1)} %reshape.251), kind=kOutput, calls=%fused_computation.13 | convolution fusion | flops 2489647104 | bytes 22265856 | tf_op jit(solution)/shard_map/dot_general | solution.py:258
  653.3 9.9 fusion.102
  663.1 11.6 all-to-all-start.5
  674.9 6.9 multiply_convert_fusion
  686.3 9.9 fusion.101
  696.2 143.0 %all-to-all-done.5 = f32[64,63,768]{2,1,0:T(8,128)} async-done(((f32[64,63,768]{2,1,0:T(8,128)}), f32[64,63,768]{2,1,0:T(8,128)}, u32[]{:S(2)}, u32[]{:S(2)}) %all-to-all-start.5) | async-done | bytes 12386336 | tf_op jit(solution)/shard_map/all_to_all | solution.py:157
  839.2 19.4 %all-to-all-start.3 = ((f32[64,63,768]{2,1,0:T(8,128)}), f32[64,63,768]{2,1,0:T(8,128)}, u32[]{:S(2)}, u32[]{:S(2)}) async-start(f32[64,63,768]{2,1,0:T(8,128)} %fusion.101), calls=%async_computation.4 | async-start | bytes 25165824 | tf_op jit(solution)/shard_map/all_to_all | solution.py:157
  858.6 7.6 bitcast_reduce_fusion
  869.9 6.6 gather_fusion.3
  885.2 137.7 %all-to-all-done.3 = f32[64,63,768]{2,1,0:T(8,128)} async-done(((f32[64,63,768]{2,1,0:T(8,128)}), f32[64,63,768]{2,1,0:T(8,128)}, u32[]{:S(2)}, u32[]{:S(2)}) %all-to-all-start.3) | async-done | bytes 12386336 | tf_op jit(solution)/shard_map/all_to_all | solution.py:157
  1023.0 7.7 bitcast_reduce_fusion.1
  1033.8 6.6 gather_fusion.1
  1044.6 8.1 multiply_reduce_fusion.1
  1059.5 33.0 %reduce-scatter.13.cloned.1.call-done = f32[200,768]{1,0:T(8,128)} async-done(((f32[400,768]{1,0:T(8,128)}), f32[200,768]{1,0:T(8,128)}) %reduce-scatter.13.cloned.1.call-update) | async-done | bytes 614416 | tf_op jit(solution)/shard_map/reduce_scatter | solution.py:142
  1094.6 25.9 %reduce-scatter.11.cloned.1.call-done = f32[200,768]{1,0:T(8,128)} async-done(((f32[400,768]{1,0:T(8,128)}), f32[200,768]{1,0:T(8,128)}) %reduce-scatter.11.cloned.1.call-update) | async-done | bytes 614416 | tf_op jit(solution)/shard_map/reduce_scatter | solution.py:142
  1123.0 10.3 all_gather.48
  1167.6 6.6 fusion.29
  1177.9 8.9 all-to-all-start.6
  1186.9 8.0 fusion.30
  1200.1 8.5 all-to-all-start.7
  1209.3 153.9 %fusion.91 = (f32[16,16]{1,0:T(8,128)S(1)}, f32[384,16]{0,1:T(8,128)}) fusion(f32[768,16]{1,0:T(8,128)} %fusion.66, f32[384,768]{0,1:T(8,128)S(1)} %fusion.104), kind=kCustom, calls=%all-reduce-scatter.2 | all-reduce-scatter fusion | flops 409601 | bytes 1254912
  1376.3 12.4 collective-permute-start.25
  1398.2 5.8 collective-permute-start.20
  1444.7 12.3 concatenate.1
  1470.3 10.3 concatenate
  1482.2 269.2 %all-reduce.14 = (f32[768]{0:T(1024)S(1)}, f32[768]{0:T(1024)S(1)}, f32[768]{0:T(1024)S(1)}, f32[768]{0:T(1024)S(1)}) all-reduce(f32[768]{0:T(1024)S(1)} %get-tuple-element.81, f32[768]{0:T(1024)S(1)} %get-tuple-element.86, f32[768]{0:T(1024)S(1)} %copy-done.52, f32[768]{0:T(1024)S(1)} %copy-done.53), channel_id=6, replica_groups=mesh['fsdp'=64,'tp'=2] {'fsdp'}, use_global_device_ids=true, to_apply=%region_30.31.clone | all-reduce | flops 3072 | bytes 24576
  1752.2 8.9 all-reduce.15
  (372 shorter events, 218.9 us)
Async XLA Ops:
  7.2 248.4 %all-gather.4.cloned.1.call-start = ((), (), s32[]{:S(2)}) async-start(), calls=%async_computation.12 | async-start | bytes 2396160 | tf_op jit(solution)/shard_map/all_gather | solution.py:127
  8.7 295.3 %reduce-scatter.9.cloned.1.call-start = ((), (), s32[]{:S(2)}) async-start(), calls=%async_computation.13 | async-start | bytes 1843200 | tf_op jit(solution)/shard_map/reduce_scatter | solution.py:142
  273.6 31.9 %all-to-all-start.1 = ((bf16[12,64,384]{2,0,1:T(8,128)(2,1)}), bf16[12,64,384]{2,0,1:T(8,128)(2,1)S(1)}, u32[]{:S(2)}, u32[]{:S(2)}) async-start(bf16[12,64,384]{2,0,1:T(8,128)(2,1)} %copy.230), calls=%async_computation.2 | async-start | bytes 1572864 | tf_op jit(solution)/shard_map/all_to_all | solution.py:219
  305.5 37.8 %all-to-all-start.2 = ((bf16[12,64,384]{2,0,1:T(8,128)(2,1)}), bf16[12,64,384]{2,0,1:T(8,128)(2,1)S(1)}, u32[]{:S(2)}, u32[]{:S(2)}) async-start(bf16[12,64,384]{2,0,1:T(8,128)(2,1)} %copy.231), calls=%async_computation.3 | async-start | bytes 1572864 | tf_op jit(solution)/shard_map/all_to_all | solution.py:220
  348.1 183.3 %all-to-all-start = ((bf16[64,63,768]{2,1,0:T(8,128)(2,1)}), bf16[64,63,768]{2,1,0:T(8,128)(2,1)}, u32[]{:S(2)}, u32[]{:S(2)}) async-start(bf16[64,63,768]{2,1,0:T(8,128)(2,1)} %bitcast.124), calls=%async_computation.1 | async-start | bytes 12582912 | tf_op jit(solution)/shard_map/all_to_all | solution.py:150
  522.3 530.5 %copy-start.27 = (f32[400,16]{0,1:T(8,128)}, f32[400,16]{0,1:T(8,128)S(1)}, u32[]{:S(2)}) copy-start(f32[400,16]{0,1:T(8,128)S(1)} %broadcast_divide_fusion) | copy-start | bytes 76804
  536.2 83.8 %all-to-all-start.4 = ((bf16[64,63,768]{2,1,0:T(8,128)(2,1)}), bf16[64,63,768]{2,1,0:T(8,128)(2,1)}, u32[]{:S(2)}, u32[]{:S(2)}) async-start(bf16[64,63,768]{2,1,0:T(8,128)(2,1)} %bitcast.125), calls=%async_computation.6 | async-start | bytes 12582912 | tf_op jit(solution)/shard_map/all_to_all | solution.py:150
  663.1 176.0 %all-to-all-start.5 = ((f32[64,63,768]{2,1,0:T(8,128)}), f32[64,63,768]{2,1,0:T(8,128)}, u32[]{:S(2)}, u32[]{:S(2)}) async-start(f32[64,63,768]{2,1,0:T(8,128)} %fusion.102), calls=%async_computation.7 | async-start | bytes 25165824 | tf_op jit(solution)/shard_map/all_to_all | solution.py:157
  839.2 183.8 %all-to-all-start.3 = ((f32[64,63,768]{2,1,0:T(8,128)}), f32[64,63,768]{2,1,0:T(8,128)}, u32[]{:S(2)}, u32[]{:S(2)}) async-start(f32[64,63,768]{2,1,0:T(8,128)} %fusion.101), calls=%async_computation.4 | async-start | bytes 25165824 | tf_op jit(solution)/shard_map/all_to_all | solution.py:157
  858.5 234.0 %reduce-scatter.13.cloned.1.call-start = ((), (), s32[]{:S(2)}) async-start(), calls=%async_computation.15 | async-start | bytes 1843200 | tf_op jit(solution)/shard_map/reduce_scatter | solution.py:142
  1054.6 65.9 %reduce-scatter.11.cloned.1.call-start = ((), (), s32[]{:S(2)}) async-start(), calls=%async_computation.14 | async-start | bytes 1843200 | tf_op jit(solution)/shard_map/reduce_scatter | solution.py:142
  1055.3 425.4 %reduce-scatter.15.cloned.1.call-start = ((), (), s32[]{:S(2)}) async-start(), calls=%async_computation.16 | async-start | bytes 1843200 | tf_op jit(solution)/shard_map/reduce_scatter | solution.py:142
  1158.9 604.3 %all-reduce.20.cloned.1.call-start = ((), (), s32[]{:S(2)}) async-start(), calls=%async_computation.17 | async-start | bytes 9437184
  1177.9 22.2 %all-to-all-start.6 = ((bf16[64,2,2304]{2,1,0:T(2,128)(2,1)}), bf16[64,2,2304]{2,1,0:T(2,128)(2,1)S(1)}, u32[]{:S(2)}, u32[]{:S(2)}) async-start(bf16[64,2,2304]{2,1,0:T(2,128)(2,1)} %reshape.378), calls=%async_computation.10 | async-start | bytes 1179648 | tf_op jit(solution)/shard_map/all_to_all | solution.py:265
  1200.1 226.2 %all-to-all-start.7 = ((bf16[64,2,2304]{2,1,0:T(2,128)(2,1)}), bf16[64,2,2304]{2,1,0:T(2,128)(2,1)S(1)}, u32[]{:S(2)}, u32[]{:S(2)}) async-start(bf16[64,2,2304]{2,1,0:T(2,128)(2,1)} %reshape.380), calls=%async_computation.11 | async-start | bytes 1179648 | tf_op jit(solution)/shard_map/all_to_all | solution.py:272
  1364.0 59.4 %collective-permute-start.15 = (f32[384,12]{0,1:T(8,128)S(1)}, f32[384,12]{0,1:T(8,128)S(1)}, u32[]{:S(2)}, u32[]{:S(2)}) collective-permute-start(f32[384,12]{0,1:T(8,128)S(1)} %slice.40), channel_id=1, source_target_pairs={{0,32},{2,34},{4,36},{6,38},{8,40},{10,42},{12,44},{14,46},{16,48}... | collective-permute-start | bytes 55304
  1365.3 9.7 collective-permute-start.30
  1366.6 9.7 collective-permute-start.29
  1367.9 5.7 collective-permute-start.31
  1372.3 16.4 collective-permute-start.28
  1373.6 17.3 collective-permute-start.27
  1375.0 17.6 collective-permute-start.26
  1376.3 20.6 %collective-permute-start.25 = (f32[16,16]{1,0:T(8,128)S(1)}, f32[16,16]{1,0:T(8,128)S(1)}, u32[]{:S(2)}, u32[]{:S(2)}) collective-permute-start(f32[16,16]{1,0:T(8,128)S(1)} %get-tuple-element.102), channel_id=1, source_target_pairs={{0,20},{2,22},{4,24},{6,26},{8,28},{10,30},{12,32},{14,34},{16,36}... | collective-permute-start | bytes 3080
  1388.7 9.5 collective-permute-start.24
  1390.9 13.1 collective-permute-start.23
  1392.6 12.7 collective-permute-start.22
  1396.9 11.0 collective-permute-start.21
  1398.2 12.3 collective-permute-start.20
  1404.0 11.9 collective-permute-start.19
  1405.3 11.9 collective-permute-start.18
  1407.9 12.2 collective-permute-start.17
  1410.5 11.3 collective-permute-start.16
  1416.0 10.9 collective-permute-start.14
  1417.3 13.1 collective-permute-start.13
  1420.2 13.2 collective-permute-start.12
  1421.8 14.4 collective-permute-start.11
  1423.4 15.6 collective-permute-start.10
  1426.9 30.2 %collective-permute-start.9 = (f32[384,16]{0,1:T(8,128)}, f32[384,16]{0,1:T(8,128)}, u32[]{:S(2)}, u32[]{:S(2)}) collective-permute-start(f32[384,16]{0,1:T(8,128)} %get-tuple-element.103), channel_id=1, source_target_pairs={{0,20},{2,22},{4,24},{6,26},{8,28},{10,30},{12,32},{14,34},{16,36}... | collective-permute-start | bytes 73736
  1430.4 28.7 %collective-permute-start.8 = (f32[384,16]{0,1:T(8,128)}, f32[384,16]{0,1:T(8,128)}, u32[]{:S(2)}, u32[]{:S(2)}) collective-permute-start(f32[384,16]{0,1:T(8,128)} %get-tuple-element.103), channel_id=1, source_target_pairs={{0,18},{2,20},{4,22},{6,24},{8,26},{10,28},{12,30},{14,32},{16,34}... | collective-permute-start | bytes 73736
  1433.4 27.0 %collective-permute-start.7 = (f32[384,16]{0,1:T(8,128)}, f32[384,16]{0,1:T(8,128)}, u32[]{:S(2)}, u32[]{:S(2)}) collective-permute-start(f32[384,16]{0,1:T(8,128)} %get-tuple-element.103), channel_id=1, source_target_pairs={{0,16},{2,18},{4,20},{6,22},{8,24},{10,26},{12,28},{14,30},{16,32}... | collective-permute-start | bytes 73736
  1436.2 26.8 %collective-permute-start.6 = (f32[384,16]{0,1:T(8,128)}, f32[384,16]{0,1:T(8,128)}, u32[]{:S(2)}, u32[]{:S(2)}) collective-permute-start(f32[384,16]{0,1:T(8,128)} %get-tuple-element.103), channel_id=1, source_target_pairs={{0,14},{2,16},{4,18},{6,20},{8,22},{10,24},{12,26},{14,28},{16,30}... | collective-permute-start | bytes 73736
  1439.0 26.6 %collective-permute-start.5 = (f32[384,16]{0,1:T(8,128)}, f32[384,16]{0,1:T(8,128)}, u32[]{:S(2)}, u32[]{:S(2)}) collective-permute-start(f32[384,16]{0,1:T(8,128)} %get-tuple-element.103), channel_id=1, source_target_pairs={{0,12},{2,14},{4,16},{6,18},{8,20},{10,22},{12,24},{14,26},{16,28}... | collective-permute-start | bytes 73736
  1443.5 317.6 %copy-start.14 = (f32[200,768]{1,0:T(8,128)S(1)}, f32[200,768]{1,0:T(8,128)}, u32[]{:S(2)}) copy-start(f32[200,768]{1,0:T(8,128)} %get-tuple-element.105) | copy-start | bytes 1843204
  1457.1 12.2 collective-permute-start.4
  1459.1 10.1 collective-permute-start.3
  1460.5 8.8 collective-permute-start.2
  1463.0 6.2 collective-permute-start.1
  1465.5 4.8 collective-permute-start
  (71 other events, 1965.8 us)
Sparse Core Ops, SparseCore 0:
  10.3 107.7 all-gather.3
  272.1 31.9 reduce-scatter.8
  1054.7 37.7 reduce-scatter.12
  1094.8 25.6 reduce-scatter.10
  1159.1 26.5 reduce-scatter.14
  1188.0 561.8 all-reduce.19
where the time goes:
time: 1790 us; the launch traced here: 1770 us
  blocking collectives  856 us (48%)
  waiting for transfers between devices  410 us (23%)
  local copies, waits for them, and re-layouts  162 us (9%)
  starting transfers between devices  160 us (9%)
  matrix products  104 us (6%)
  other arithmetic  61.5 us (3%)
  between operations  18.4 us (1%)
    unnamed x3, blocking collectives  565 us
    all_to_all x2, waiting for transfers between devices, to_groups(): lax.all_to_all(pieces, 'fsdp', split_axis=0, concat_axis=0, tiled=True)  281 us
    all_gather x1, blocking collectives, gather_dense(): lax.all_gather(router_weight, 'fsdp', axis=0, tiled=True)  146 us
    unnamed x33, starting transfers between devices  84.9 us
    all_gather x1, blocking collectives, gather_dense(): lax.all_gather(proj_weight, 'fsdp', axis=1, tiled=True)  84.4 us
    reduce_scatter x4, waiting for transfers between devices, owned_rows(): return lax.psum_scatter(value, 'tp', scatter_dimension=0, tiled=True)  68.6 us
    all_to_all x2, waiting for transfers between devices, to_owners(): lax.all_to_all(spread, 'fsdp', split_axis=0, concat_axis=0, tiled=True)  59 us
    all_gather x4, blocking collectives, group_rows(): return lax.all_gather(value, 'tp', axis=0, tiled=True)  51.7 us
  transfers between devices with their start and end apart: 46, of which 8 were waited for; matrix products, arithmetic and copies ran while one was open for 20% of the time, Pallas kernels for 0%

commit v1 on v0

--- a/solution.py
+++ b/solution.py
@@ -123,15 +123,56 @@
     expert_norm_gain,
     expert_norm_shift,
 ):
-    return (
-        lax.all_gather(qkv_weight, "fsdp", axis=1, tiled=True),
-        lax.all_gather(proj_weight, "fsdp", axis=1, tiled=True),
-        lax.all_gather(router_weight, "fsdp", axis=0, tiled=True),
-        lax.all_gather(attention_norm_gain, "fsdp", axis=0, tiled=True),
-        lax.all_gather(attention_norm_shift, "fsdp", axis=0, tiled=True),
-        lax.all_gather(expert_norm_gain, "fsdp", axis=0, tiled=True),
-        lax.all_gather(expert_norm_shift, "fsdp", axis=0, tiled=True),
-    )
+    rows = qkv_weight.shape[1]
+    heads_width = qkv_weight.shape[2]
+    experts = router_weight.shape[1]
+    packed = jnp.concatenate(
+        [
+            jnp.transpose(qkv_weight, (1, 0, 2)).reshape(rows, -1),
+            proj_weight.T,
+            router_weight,
+            jnp.stack(
+                [attention_norm_gain, attention_norm_shift, expert_norm_gain, expert_norm_shift],
+                axis=1,
+            ),
+        ],
+        axis=1,
+    )
+    full = lax.all_gather(packed, "fsdp", axis=0, tiled=True)
+    width = full.shape[0]
+    at = 3 * heads_width
+    qkv_full = jnp.transpose(full[:, :at].reshape(width, 3, heads_width), (1, 0, 2))
+    proj_full = full[:, at : at + heads_width].T
+    at += heads_width
+    router_full = full[:, at : at + experts]
+    at += experts
+    norms = full[:, at : at + 4]
+    return (qkv_full, proj_full, router_full, norms[:, 0], norms[:, 1], norms[:, 2], norms[:, 3])
+
+
+def reduce_dense(qkv_part, proj_part, router_part, norm_parts):
+    width = qkv_part.shape[1]
+    heads_width = qkv_part.shape[2]
+    experts = router_part.shape[1]
+    packed = jnp.concatenate(
+        [
+            jnp.transpose(qkv_part, (1, 0, 2)).reshape(width, -1),
+            proj_part.T,
+            router_part,
+            jnp.stack(norm_parts, axis=1),
+        ],
+        axis=1,
+    )
+    part = lax.psum_scatter(packed, "fsdp", scatter_dimension=0, tiled=True)
+    rows = part.shape[0]
+    at = 3 * heads_width
+    qkv_grad = jnp.transpose(part[:, :at].reshape(rows, 3, heads_width), (1, 0, 2))
+    proj_grad = part[:, at : at + heads_width].T
+    at += heads_width
+    shared = lax.psum(part[:, at:], "tp")
+    router_grad = shared[:, :experts]
+    norm_grads = [shared[:, experts + i] for i in range(len(norm_parts))]
+    return qkv_grad, proj_grad, router_grad, norm_grads
 
 
 def group_rows(value):
@@ -228,23 +269,8 @@
     expert_res = to_groups(owner_res, experts, holders, CAP)
     routed = expert_res.reshape(experts * CAP, width)[slot].reshape(group, 2, width)
     outputs = residual_middle + owned_rows(jnp.sum(gates[:, :, None] * routed, axis=1))
-    (
-        qkv_back,
-        proj_back,
-        router_back,
-        attention_gain_gradient,
-        shift_unused,
-        expert_gain_gradient,
-        shift_spare,
-    ) = gather_dense(
-        qkv_weight,
-        proj_weight,
-        router_weight,
-        attention_norm_gain,
-        attention_norm_shift,
-        expert_norm_gain,
-        expert_norm_shift,
-    )
+    qkv_back, proj_back, router_back = qkv_full, proj_full, router_full
+    attention_gain_gradient, expert_gain_gradient = attention_gain, expert_gain
     dout = group_rows(cotangent.astype(bf16))
     dout_f = dout.astype(f32)
     gate_of_slot = jnp.zeros((experts * CAP,), f32).at[slot].set(gates.reshape(-1))
@@ -313,26 +339,22 @@
         attention_gain_gradient,
     )
     input_grad = middle_grad + attention_norm_backward
-    sums = (
-        lax.psum_scatter(qkv_part, "fsdp", scatter_dimension=1, tiled=True),
-        lax.psum_scatter(proj_part, "fsdp", scatter_dimension=1, tiled=True),
-        lax.psum_scatter(router_part, "fsdp", scatter_dimension=0, tiled=True),
-        lax.psum_scatter(attention_gain_partial, "fsdp", scatter_dimension=0, tiled=True),
-        lax.psum_scatter(attention_shift_partial, "fsdp", scatter_dimension=0, tiled=True),
-        lax.psum_scatter(expert_gain_partial, "fsdp", scatter_dimension=0, tiled=True),
-        lax.psum_scatter(expert_shift_partial, "fsdp", scatter_dimension=0, tiled=True),
-    )
-    shared = lax.psum((sums[2], sums[3], sums[4], sums[5], sums[6]), "tp")
+    qkv_grad, proj_grad, router_grad, norm_grads = reduce_dense(
+        qkv_part,
+        proj_part,
+        router_part,
+        [attention_gain_partial, attention_shift_partial, expert_gain_partial, expert_shift_partial],
+    )
     return (
         outputs,
         input_grad,
-        shared[1],
-        shared[2],
-        sums[0],
-        sums[1],
-        shared[3],
-        shared[4],
-        shared[0],
+        norm_grads[0],
+        norm_grads[1],
+        qkv_grad,
+        proj_grad,
+        norm_grads[2],
+        norm_grads[3],
+        router_grad,
         in_grad,
         out_grad,
     )

time: 1790 us -> 1620 us (0.905)
  blocking collectives: 856 us -> 102 us
  waiting for transfers between devices: 410 us -> 1060 us
  starting transfers between devices: 160 us -> 93.2 us
    unnamed x3 -> x0, blocking collectives: 565 us -> none
    unnamed x39 -> x7, waiting for transfers between devices: 1.76 us -> 510 us
    all_gather x2 -> x0, blocking collectives: 230 us -> none  [the longest x1 146 us: gather_dense(): lax.all_gather(router_weight, 'fsdp', axis=0, tiled=True)]
    all_gather x1, waiting for transfers between devices: 0.01 us -> 106 us  [gather_dense(): full = lax.all_gather(packed, 'fsdp', axis=0, tiled=True)]
    unnamed x33 -> x1, starting transfers between devices: 84.9 us -> 0.25 us
    all_gather x4, blocking collectives: 51.7 us -> 97.1 us  [group_rows(): return lax.all_gather(value, 'tp', axis=0, tiled=True)]
    unnamed x177 -> x87, local copies, waits for them, and re-layouts: 42.5 us -> 8.98 us
    all_to_all x2, starting transfers between devices: 13.2 us -> 34.1 us  [to_owners(): lax.all_to_all(spread, 'fsdp', split_axis=0, concat_axis=0, tiled=True)]
  transfers between devices with their start and end apart: 46 -> 14, of which waited for: 8 -> 12; matrix products, arithmetic and copies ran while one was open for 20% -> 10% of each run, Pallas kernels for 0% -> 0%
where the time goes in v1:
time: 1620 us; the launch traced here: 1600 us
  waiting for transfers between devices  1060 us (65%)
  local copies, waits for them, and re-layouts  171 us (11%)
  matrix products  106 us (7%)
  blocking collectives  102 us (6%)
  starting transfers between devices  93.2 us (6%)
  other arithmetic  60.1 us (4%)
    unnamed x7, waiting for transfers between devices  510 us
    all_to_all x2, waiting for transfers between devices, to_groups(): lax.all_to_all(pieces, 'fsdp', split_axis=0, concat_axis=0, tiled=True)  281 us
    all_gather x1, waiting for transfers between devices, gather_dense(): full = lax.all_gather(packed, 'fsdp', axis=0, tiled=True)  106 us
    all_gather x4, blocking collectives, group_rows(): return lax.all_gather(value, 'tp', axis=0, tiled=True)  97.1 us
    reduce_scatter x4, waiting for transfers between devices, owned_rows(): return lax.psum_scatter(value, 'tp', scatter_dimension=0, tiled=True)  83.6 us
    all_to_all x2, waiting for transfers between devices, to_owners(): lax.all_to_all(spread, 'fsdp', split_axis=0, concat_axis=0, tiled=True)  61.2 us
    all_to_all x2, starting transfers between devices, to_owners(): lax.all_to_all(spread, 'fsdp', split_axis=0, concat_axis=0, tiled=True)  34.1 us
  transfers between devices with their start and end apart: 14, of which 12 were waited for; matrix products, arithmetic and copies ran while one was open for 10% of the time, Pallas kernels for 0%

profile of v1, /device:TPU:1, one launch (start us, length us, event | category | flops | bytes accessed | tf_op | source)
XLA Modules:
  0.0 1604.5 jit_solution(12377187689971864063)
XLA Ops:
  15.1 106.3 %all-gather.3.cloned.1.call-done = bf16[64,12,1556]{2,1,0:T(8,128)(2,1)} async-done(((bf16[1,12,1556]{2,1,0:T(8,128)(2,1)}), bf16[64,12,1556]{2,1,0:T(8,128)(2,1)}) %all-gather.3.cloned.1.call-update) | async-done | bytes 2390032 | tf_op jit(solution)/shard_map/all_gather | solution.py:141
  127.8 10.9 all_gather.16
  179.7 7.3 all-to-all-start.1
  190.2 5.3 scatter_custom_fusion.1
  195.5 5.3 scatter_custom_fusion
  202.5 9.0 reduce-scatter.5.cloned.1.call-done
  213.0 8.0 all-to-all-start.2
  221.2 19.1 %all_gather.17 = bf16[400,768]{1,0:T(8,128)(2,1)S(1)} all-gather(bf16[200,768]{1,0:T(8,128)(2,1)S(1)} %add_convert_fusion.1), channel_id=1, replica_groups=mesh['fsdp'=64,'tp'=2] {'tp'}, dimensions={0}, use_global_device_ids=true | all-gather | bytes 921600 | tf_op jit(solution)/shard_map/all_gather | solution.py:179
  240.3 5.2 gather_fusion
  250.8 4.8 broadcast_in_dim.63
  255.7 7.0 all-to-all-start
  262.7 56.9 %all_gather.18 = bf16[400,768]{1,0:T(8,128)(2,1)S(1)} all-gather(bf16[200,768]{1,0:T(8,128)(2,1)S(1)} %convert_element_type.180), channel_id=1, replica_groups=mesh['fsdp'=64,'tp'=2] {'tp'}, dimensions={0}, use_global_device_ids=true | all-gather | bytes 921600 | tf_op jit(solution)/shard_map/all_gather | solution.py:179
  319.7 5.3 gather_fusion.2
  329.8 5.3 scatter_custom_fusion.2
  340.5 4.8 broadcast_in_dim.66
  345.3 27.1 %all-to-all-start.4 = ((bf16[64,63,768]{2,1,0:T(8,128)(2,1)}), bf16[64,63,768]{2,1,0:T(8,128)(2,1)}, u32[]{:S(2)}, u32[]{:S(2)}) async-start(bf16[64,63,768]{2,1,0:T(8,128)(2,1)} %bitcast.138), calls=%async_computation.6 | async-start | bytes 12582912 | tf_op jit(solution)/shard_map/all_to_all | solution.py:191
  373.7 8.5 reshape.285
  382.2 8.8 fusion.111
  391.0 59.3 %all-to-all-done.4 = bf16[64,63,768]{2,1,0:T(8,128)(2,1)} async-done(((bf16[64,63,768]{2,1,0:T(8,128)(2,1)}), bf16[64,63,768]{2,1,0:T(8,128)(2,1)}, u32[]{:S(2)}, u32[]{:S(2)}) %all-to-all-start.4) | async-done | bytes 6193184 | tf_op jit(solution)/shard_map/all_to_all | solution.py:191
  450.3 8.5 reshape.295
  458.9 20.1 %add_convert_fusion = (bf16[4032,384]{1,0:T(8,128)(2,1)}, f32[4032,384]{1,0:T(8,128)}) fusion(f32[4032,384]{1,0:T(8,128)} %fusion.111, bf16[4032,768]{1,0:T(8,128)(2,1)} %reshape.295, bf16[768,384]{1,0:T(8,128)(2,1)S(1)} %reshape.289), kind=kOutput, calls=%fused_computation.13 | convolution fusion | flops 2489647104 | bytes 22265856 | tf_op jit(solution)/shard_map/dot_general | solution.py:284
  478.9 4.6 dot_general.77
  483.6 9.8 fusion.113
  493.4 11.0 all-to-all-start.5
  504.6 6.9 multiply_convert_fusion
  516.0 9.9 fusion.112
  526.0 142.9 %all-to-all-done.5 = f32[64,63,768]{2,1,0:T(8,128)} async-done(((f32[64,63,768]{2,1,0:T(8,128)}), f32[64,63,768]{2,1,0:T(8,128)}, u32[]{:S(2)}, u32[]{:S(2)}) %all-to-all-start.5) | async-done | bytes 12386336 | tf_op jit(solution)/shard_map/all_to_all | solution.py:198
  668.8 19.4 %all-to-all-start.3 = ((f32[64,63,768]{2,1,0:T(8,128)}), f32[64,63,768]{2,1,0:T(8,128)}, u32[]{:S(2)}, u32[]{:S(2)}) async-start(f32[64,63,768]{2,1,0:T(8,128)} %fusion.112), calls=%async_computation.4 | async-start | bytes 25165824 | tf_op jit(solution)/shard_map/all_to_all | solution.py:198
  688.3 7.6 bitcast_reduce_fusion
  699.7 6.6 gather_fusion.3
  710.4 4.6 reduce_sum.230
  715.0 137.7 %all-to-all-done.3 = f32[64,63,768]{2,1,0:T(8,128)} async-done(((f32[64,63,768]{2,1,0:T(8,128)}), f32[64,63,768]{2,1,0:T(8,128)}, u32[]{:S(2)}, u32[]{:S(2)}) %all-to-all-start.3) | async-done | bytes 12386336 | tf_op jit(solution)/shard_map/all_to_all | solution.py:198
  852.7 7.7 bitcast_reduce_fusion.1
  863.6 6.6 gather_fusion.1
  874.3 8.1 multiply_reduce_fusion.1
  889.8 33.2 %reduce-scatter.9.cloned.1.call-done = f32[200,768]{1,0:T(8,128)} async-done(((f32[400,768]{1,0:T(8,128)}), f32[200,768]{1,0:T(8,128)}) %reduce-scatter.9.cloned.1.call-update) | async-done | bytes 614416 | tf_op jit(solution)/shard_map/reduce_scatter | solution.py:183
  924.5 26.5 %reduce-scatter.7.cloned.1.call-done = f32[200,768]{1,0:T(8,128)} async-done(((f32[400,768]{1,0:T(8,128)}), f32[200,768]{1,0:T(8,128)}) %reduce-scatter.7.cloned.1.call-update) | async-done | bytes 614416 | tf_op jit(solution)/shard_map/reduce_scatter | solution.py:183
  953.5 10.3 all_gather.19
  995.6 5.3 copy.312
  1001.6 14.8 reduce-scatter.11.cloned.1.call-done
  1018.1 6.1 concatenate.7
  1024.3 7.1 fusion.37
  1034.0 8.0 all-to-all-start.6
  1042.0 7.1 fusion.38
  1055.8 4.7 all-to-all-start.7
  1064.8 9.3 all-to-all-done.7
  1078.2 509.2 %all-reduce.4.cloned.1.call-done = f32[768,1556]{1,0:T(8,128)} async-done(((f32[768,1556]{1,0:T(8,128)}), f32[768,1556]{1,0:T(8,128)}) %all-reduce.4.cloned.1.call-update) | async-done | bytes 4780048
  1588.2 5.3 psum.7
  (230 shorter events, 165.1 us)
Async XLA Ops:
  7.2 114.2 %all-gather.3.cloned.1.call-start = ((), (), s32[]{:S(2)}) async-start(), calls=%async_computation.16 | async-start | bytes 3461120 | tf_op jit(solution)/shard_map/all_gather | solution.py:141
  12.5 199.0 %reduce-scatter.5.cloned.1.call-start = ((), (), s32[]{:S(2)}) async-start(), calls=%async_computation.12 | async-start | bytes 1843200 | tf_op jit(solution)/shard_map/reduce_scatter | solution.py:183
  13.8 152.0 %copy-start.36 = (pred[200]{0:T(512)(128)(4,1)}, pred[200]{0:T(512)(128)(4,1)S(1)}, u32[]{:S(2)}) copy-start(pred[200]{0:T(512)(128)(4,1)S(1)} %iota_compare_fusion.3) | copy-start | bytes 604
  13.8 113.9 %copy-start.27 = (f32[200]{0:T(256)}, f32[200]{0:T(256)S(1)}, u32[]{:S(2)}) copy-start(f32[200]{0:T(256)S(1)} %broadcast_multiply_fusion.6) | copy-start | bytes 2404
  15.1 112.6 %copy-start.31 = (f32[200]{0:T(256)}, f32[200]{0:T(256)S(1)}, u32[]{:S(2)}) copy-start(f32[200]{0:T(256)S(1)} %add_rsqrt_fusion.1) | copy-start | bytes 2404
  125.6 48.8 %copy-start.6 = (bf16[768,1556]{1,0:T(8,128)(2,1)}, bf16[768,1556]{1,0:T(8,128)(2,1)S(1)}, u32[]{:S(2)}) copy-start(bf16[768,1556]{1,0:T(8,128)(2,1)S(1)} %reshape.370) | copy-start | bytes 7170052
  126.1 94.9 %copy-start.24 = (f32[768]{0:T(1024)}, f32[768]{0:T(1024)S(1)}, u32[]{:S(2)}) copy-start(f32[768]{0:T(1024)S(1)} %get-tuple-element.11) | copy-start | bytes 9220
  176.9 10.1 copy-start.26
  176.9 23.9 %copy-start.18 = (bf16[12,16,1536]{2,1,0:T(8,128)(2,1)S(1)}, bf16[12,16,1536]{2,1,0:T(8,128)(2,1)}, u32[]{:S(2)}) copy-start(bf16[12,16,1536]{2,1,0:T(8,128)(2,1)} %param.22) | copy-start | bytes 1769476
  179.7 33.3 %all-to-all-start.1 = ((bf16[12,64,384]{2,0,1:T(8,128)(2,1)}), bf16[12,64,384]{2,0,1:T(8,128)(2,1)S(1)}, u32[]{:S(2)}, u32[]{:S(2)}) async-start(bf16[12,64,384]{2,0,1:T(8,128)(2,1)} %copy.285), calls=%async_computation.2 | async-start | bytes 1572864 | tf_op jit(solution)/shard_map/all_to_all | solution.py:260
  212.7 32.8 %copy-start.4 = (f32[200,768]{1,0:T(8,128)}, f32[200,768]{1,0:T(8,128)S(1)}, u32[]{:S(2)}) copy-start(f32[200,768]{1,0:T(8,128)S(1)} %get-tuple-element.34) | copy-start | bytes 1843204
  212.7 32.8 %copy-start.29 = (f32[200]{0:T(256)}, f32[200]{0:T(256)S(1)}, u32[]{:S(2)}) copy-start(f32[200]{0:T(256)S(1)} %broadcast_multiply_fusion.5) | copy-start | bytes 2404
  213.0 32.5 %copy-start.33 = (f32[200]{0:T(256)}, f32[200]{0:T(256)S(1)}, u32[]{:S(2)}) copy-start(f32[200]{0:T(256)S(1)} %add_rsqrt_fusion) | copy-start | bytes 2404
  213.0 37.8 %all-to-all-start.2 = ((bf16[12,64,384]{2,0,1:T(8,128)(2,1)}), bf16[12,64,384]{2,0,1:T(8,128)(2,1)S(1)}, u32[]{:S(2)}, u32[]{:S(2)}) async-start(bf16[12,64,384]{2,0,1:T(8,128)(2,1)} %copy.286), calls=%async_computation.3 | async-start | bytes 1572864 | tf_op jit(solution)/shard_map/all_to_all | solution.py:261
  240.3 87.9 %copy-start = (bf16[400,768]{1,0:T(8,128)(2,1)}, bf16[400,768]{1,0:T(8,128)(2,1)S(1)}, u32[]{:S(2)}) copy-start(bf16[400,768]{1,0:T(8,128)(2,1)S(1)} %all_gather.17) | copy-start | bytes 1843204
  255.6 7.0 copy-start.8
  255.7 84.8 %all-to-all-start = ((bf16[64,63,768]{2,1,0:T(8,128)(2,1)}), bf16[64,63,768]{2,1,0:T(8,128)(2,1)}, u32[]{:S(2)}, u32[]{:S(2)}) async-start(bf16[64,63,768]{2,1,0:T(8,128)(2,1)} %bitcast.137), calls=%async_computation.1 | async-start | bytes 12582912 | tf_op jit(solution)/shard_map/all_to_all | solution.py:191
  329.5 15.8 copy-start.20
  329.7 15.6 copy-start.13
  345.3 105.0 %all-to-all-start.4 = ((bf16[64,63,768]{2,1,0:T(8,128)(2,1)}), bf16[64,63,768]{2,1,0:T(8,128)(2,1)}, u32[]{:S(2)}, u32[]{:S(2)}) async-start(bf16[64,63,768]{2,1,0:T(8,128)(2,1)} %bitcast.138), calls=%async_computation.6 | async-start | bytes 12582912 | tf_op jit(solution)/shard_map/all_to_all | solution.py:191
  493.4 175.5 %all-to-all-start.5 = ((f32[64,63,768]{2,1,0:T(8,128)}), f32[64,63,768]{2,1,0:T(8,128)}, u32[]{:S(2)}, u32[]{:S(2)}) async-start(f32[64,63,768]{2,1,0:T(8,128)} %fusion.113), calls=%async_computation.7 | async-start | bytes 25165824 | tf_op jit(solution)/shard_map/all_to_all | solution.py:198
  668.8 183.8 %all-to-all-start.3 = ((f32[64,63,768]{2,1,0:T(8,128)}), f32[64,63,768]{2,1,0:T(8,128)}, u32[]{:S(2)}, u32[]{:S(2)}) async-start(f32[64,63,768]{2,1,0:T(8,128)} %fusion.112), calls=%async_computation.4 | async-start | bytes 25165824 | tf_op jit(solution)/shard_map/all_to_all | solution.py:198
  688.2 234.9 %reduce-scatter.9.cloned.1.call-start = ((), (), s32[]{:S(2)}) async-start(), calls=%async_computation.14 | async-start | bytes 1843200 | tf_op jit(solution)/shard_map/reduce_scatter | solution.py:183
  870.2 4.1 copy-start.14
  882.4 4.6 copy-start.15
  882.4 4.6 copy-start.16
  882.4 4.6 copy-start.37
  886.1 65.0 %reduce-scatter.7.cloned.1.call-start = ((), (), s32[]{:S(2)}) async-start(), calls=%async_computation.13 | async-start | bytes 1843200 | tf_op jit(solution)/shard_map/reduce_scatter | solution.py:183
  886.7 36.4 %copy-start.5 = (f32[200,768]{1,0:T(8,128)S(1)}, f32[200,768]{1,0:T(8,128)}, u32[]{:S(2)}) copy-start(f32[200,768]{1,0:T(8,128)} %copy-done.4) | copy-start | bytes 1843204
  886.7 36.4 %copy-start.25 = (f32[768]{0:T(1024)S(1)}, f32[768]{0:T(1024)}, u32[]{:S(2)}) copy-start(f32[768]{0:T(1024)} %copy-done.24) | copy-start | bytes 9220
  886.7 36.4 %copy-start.30 = (f32[200]{0:T(256)S(1)}, f32[200]{0:T(256)}, u32[]{:S(2)}) copy-start(f32[200]{0:T(256)} %copy-done.29) | copy-start | bytes 2404
  886.7 36.4 %copy-start.34 = (f32[200]{0:T(256)S(1)}, f32[200]{0:T(256)}, u32[]{:S(2)}) copy-start(f32[200]{0:T(256)} %copy-done.33) | copy-start | bytes 2404
  886.7 64.3 %copy-start.9 = (f32[200,768]{1,0:T(8,128)S(1)}, f32[200,768]{1,0:T(8,128)}, u32[]{:S(2)}) copy-start(f32[200,768]{1,0:T(8,128)} %param.23) | copy-start | bytes 1843204
  886.7 129.7 %reduce-scatter.11.cloned.1.call-start = ((), (), s32[]{:S(2)}) async-start(), calls=%async_computation.15 | async-start | bytes 1843200 | tf_op jit(solution)/shard_map/reduce_scatter | solution.py:183
  981.0 3.9 copy-start.19
  986.0 3.9 copy-start.1
  989.6 3.1 copy-start.12
  989.6 597.8 %all-reduce.4.cloned.1.call-start = ((), (), s32[]{:S(2)}) async-start(), calls=%async_computation.17 | async-start | bytes 10223616
  995.6 5.4 copy-start.7
  995.6 20.8 %copy-start.3 = (f32[200,768]{1,0:T(8,128)S(1)}, f32[200,768]{1,0:T(8,128)}, u32[]{:S(2)}) copy-start(f32[200,768]{1,0:T(8,128)} %param.12) | copy-start | bytes 1843204
  995.6 20.8 %copy-start.23 = (f32[768]{0:T(1024)S(1)}, f32[768]{0:T(1024)}, u32[]{:S(2)}) copy-start(f32[768]{0:T(1024)} %copy-done.22) | copy-start | bytes 9220
  995.6 20.8 %copy-start.28 = (f32[200]{0:T(256)S(1)}, f32[200]{0:T(256)}, u32[]{:S(2)}) copy-start(f32[200]{0:T(256)} %copy-done.27) | copy-start | bytes 2404
  995.6 20.8 %copy-start.32 = (f32[200]{0:T(256)S(1)}, f32[200]{0:T(256)}, u32[]{:S(2)}) copy-start(f32[200]{0:T(256)} %copy-done.31) | copy-start | bytes 2404
  1034.0 21.8 %all-to-all-start.6 = ((bf16[64,2,2304]{2,1,0:T(2,128)(2,1)}), bf16[64,2,2304]{2,1,0:T(2,128)(2,1)S(1)}, u32[]{:S(2)}, u32[]{:S(2)}) async-start(bf16[64,2,2304]{2,1,0:T(2,128)(2,1)} %reshape.401), calls=%async_computation.10 | async-start | bytes 1179648 | tf_op jit(solution)/shard_map/all_to_all | solution.py:291
  1049.2 11.3 copy-start.35
  1055.8 18.3 %all-to-all-start.7 = ((bf16[64,2,2304]{2,1,0:T(2,128)(2,1)}), bf16[64,2,2304]{2,1,0:T(2,128)(2,1)S(1)}, u32[]{:S(2)}, u32[]{:S(2)}) async-start(bf16[64,2,2304]{2,1,0:T(2,128)(2,1)} %reshape.403), calls=%async_computation.11 | async-start | bytes 1179648 | tf_op jit(solution)/shard_map/all_to_all | solution.py:298
  1074.6 2.6 copy-start.10
  1593.5 3.8 copy-start.21
  (4 other events, 6.9 us)
Sparse Core Ops, SparseCore 0:
  12.6 108.7 all-gather.2
  177.1 34.3 reduce-scatter.4
  886.2 36.8 reduce-scatter.8
  925.3 25.6 reduce-scatter.6
  989.8 26.5 reduce-scatter.10
  1024.4 562.9 all-reduce.3

commit v2 on v1

--- a/solution.py
+++ b/solution.py
@@ -163,8 +163,11 @@
         ],
         axis=1,
     )
-    part = lax.psum_scatter(packed, "fsdp", scatter_dimension=0, tiled=True)
-    rows = part.shape[0]
+    holders = lax.axis_size("fsdp")
+    rows = width // holders
+    part = lax.psum_scatter(
+        packed.reshape(holders, rows, packed.shape[1]), "fsdp", scatter_dimension=0, tiled=True
+    ).reshape(rows, packed.shape[1])
     at = 3 * heads_width
     qkv_grad = jnp.transpose(part[:, :at].reshape(rows, 3, heads_width), (1, 0, 2))
     proj_grad = part[:, at : at + heads_width].T
@@ -194,9 +197,9 @@
 
 def to_groups(partial_value, experts, holders, capacity):
     width = partial_value.shape[1]
-    pieces = partial_value.reshape(experts * holders, capacity, width)
+    pieces = partial_value.astype(jnp.bfloat16).reshape(experts * holders, capacity, width)
     moved = lax.all_to_all(pieces, "fsdp", split_axis=0, concat_axis=0, tiled=True)
-    return jnp.sum(moved.reshape(experts, holders, capacity, width), axis=1)
+    return jnp.sum(moved.reshape(experts, holders, capacity, width).astype(jnp.float32), axis=1)
 
 
 def per_device(

time: 1620 us -> 1170 us (0.72)
  waiting for transfers between devices: 1060 us -> 611 us
  local copies, waits for them, and re-layouts: 171 us -> 193 us
    unnamed x7 -> x6, waiting for transfers between devices: 510 us -> 0.6 us
    reduce_scatter x0 -> x1, waiting for transfers between devices: none -> 238 us  [reduce_dense(): lax.psum_scatter(packed.reshape(holders, rows, packed.shape[1]), 'fsdp',...]
    all_to_all x2, waiting for transfers between devices: 281 us -> 111 us  [to_groups(): lax.all_to_all(pieces, 'fsdp', split_axis=0, concat_axis=0, tiled=True)]
  transfers between devices with their start and end apart: 14 -> 14, of which waited for: 12 -> 12; matrix products, arithmetic and copies ran while one was open for 10% -> 14% of each run, Pallas kernels for 0% -> 0%
where the time goes in v2:
time: 1170 us; the launch traced here: 1150 us
  waiting for transfers between devices  611 us (52%)
  local copies, waits for them, and re-layouts  193 us (16%)
  blocking collectives  104 us (9%)
  matrix products  97 us (8%)
  starting transfers between devices  84.3 us (7%)
  other arithmetic  47.1 us (4%)
  between operations  15.6 us (1%)
    reduce_scatter x1, waiting for transfers between devices, reduce_dense(): lax.psum_scatter(packed.reshape(holders, rows, packed.shape[1]), 'fsdp',...  238 us
    all_to_all x2, waiting for transfers between devices, to_groups(): lax.all_to_all(pieces, 'fsdp', split_axis=0, concat_axis=0, tiled=True)  111 us
    all_gather x1, waiting for transfers between devices, gather_dense(): full = lax.all_gather(packed, 'fsdp', axis=0, tiled=True)  106 us
    all_gather x4, blocking collectives, group_rows(): return lax.all_gather(value, 'tp', axis=0, tiled=True)  97 us
    reduce_scatter x4, waiting for transfers between devices, owned_rows(): return lax.psum_scatter(value, 'tp', scatter_dimension=0, tiled=True)  71.2 us
    all_to_all x2, waiting for transfers between devices, to_owners(): lax.all_to_all(spread, 'fsdp', split_axis=0, concat_axis=0, tiled=True)  68.8 us
    all_to_all x2, starting transfers between devices, to_owners(): lax.all_to_all(spread, 'fsdp', split_axis=0, concat_axis=0, tiled=True)  33.1 us
  transfers between devices with their start and end apart: 14, of which 12 were waited for; matrix products, arithmetic and copies ran while one was open for 14% of the time, Pallas kernels for 0%

profile of v2, /device:TPU:1, one launch (start us, length us, event | category | flops | bytes accessed | tf_op | source)
XLA Modules:
  0.0 1151.8 jit_solution(7666149518233055014)
XLA Ops:
  15.1 106.3 %all-gather.3.cloned.1.call-done = bf16[64,12,1556]{2,1,0:T(8,128)(2,1)} async-done(((bf16[1,12,1556]{2,1,0:T(8,128)(2,1)}), bf16[64,12,1556]{2,1,0:T(8,128)(2,1)}) %all-gather.3.cloned.1.call-update) | async-done | bytes 2390032 | tf_op jit(solution)/shard_map/all_gather | solution.py:141
  127.8 10.9 all_gather.16
  179.6 7.1 all-to-all-start.1
  189.8 5.3 scatter_custom_fusion.1
  195.1 5.3 scatter_custom_fusion
  202.1 9.3 reduce-scatter.6.cloned.1.call-done
  212.9 8.2 all-to-all-start.2
  221.3 19.0 %all_gather.17 = bf16[400,768]{1,0:T(8,128)(2,1)S(1)} all-gather(bf16[200,768]{1,0:T(8,128)(2,1)S(1)} %add_convert_fusion.1), channel_id=1, replica_groups=mesh['fsdp'=64,'tp'=2] {'tp'}, dimensions={0}, use_global_device_ids=true | all-gather | bytes 921600 | tf_op jit(solution)/shard_map/all_gather | solution.py:182
  240.3 5.2 gather_fusion
  248.5 4.8 broadcast_in_dim.63
  253.3 6.9 all-to-all-start
  260.3 56.9 %all_gather.18 = bf16[400,768]{1,0:T(8,128)(2,1)S(1)} all-gather(bf16[200,768]{1,0:T(8,128)(2,1)S(1)} %convert_element_type.201), channel_id=1, replica_groups=mesh['fsdp'=64,'tp'=2] {'tp'}, dimensions={0}, use_global_device_ids=true | all-gather | bytes 921600 | tf_op jit(solution)/shard_map/all_gather | solution.py:182
  317.3 5.3 gather_fusion.2
  327.4 5.3 scatter_custom_fusion.2
  341.5 26.1 %all-to-all-start.4 = ((bf16[64,63,768]{2,1,0:T(8,128)(2,1)}), bf16[64,63,768]{2,1,0:T(8,128)(2,1)}, u32[]{:S(2)}, u32[]{:S(2)}) async-start(bf16[64,63,768]{2,1,0:T(8,128)(2,1)} %bitcast.139), calls=%async_computation.6 | async-start | bytes 12582912 | tf_op jit(solution)/shard_map/all_to_all | solution.py:194
  369.0 8.5 reshape.302
  377.5 8.7 fusion.114
  386.2 65.8 %all-to-all-done.4 = bf16[64,63,768]{2,1,0:T(8,128)(2,1)} async-done(((bf16[64,63,768]{2,1,0:T(8,128)(2,1)}), bf16[64,63,768]{2,1,0:T(8,128)(2,1)}, u32[]{:S(2)}, u32[]{:S(2)}) %all-to-all-start.4) | async-done | bytes 6193184 | tf_op jit(solution)/shard_map/all_to_all | solution.py:194
  452.0 8.3 reshape.312
  460.4 19.9 %add_convert_fusion = (bf16[4032,384]{1,0:T(8,128)(2,1)}, f32[4032,384]{1,0:T(8,128)S(1)}) fusion(f32[4032,384]{1,0:T(8,128)} %fusion.114, bf16[4032,768]{1,0:T(8,128)(2,1)} %reshape.312, bf16[768,384]{1,0:T(8,128)(2,1)S(1)} %reshape.306), kind=kOutput, calls=%fused_computation.15 | convolution fusion | flops 2489647104 | bytes 22265856 | tf_op jit(solution)/shard_map/dot_general | solution.py:287
  482.7 5.3 convolution_convert_fusion.1
  488.0 8.4 reshape.307
  496.4 11.5 all-to-all-start.3
  507.9 7.9 convolution_convert_fusion
  515.9 8.5 reshape.313
  524.3 61.4 %all-to-all-done.3 = bf16[64,63,768]{2,1,0:T(8,128)(2,1)} async-done(((bf16[64,63,768]{2,1,0:T(8,128)(2,1)}), bf16[64,63,768]{2,1,0:T(8,128)(2,1)}, u32[]{:S(2)}, u32[]{:S(2)}) %all-to-all-start.3) | async-done | bytes 6193184 | tf_op jit(solution)/shard_map/all_to_all | solution.py:201
  585.8 11.0 all-to-all-start.5
  596.9 5.9 convert_reduce_fusion.1
  606.4 6.6 gather_fusion.1
  617.2 8.1 multiply_reduce_fusion.1
  625.4 49.2 %all-to-all-done.5 = bf16[64,63,768]{2,1,0:T(8,128)(2,1)} async-done(((bf16[64,63,768]{2,1,0:T(8,128)(2,1)}), bf16[64,63,768]{2,1,0:T(8,128)(2,1)}, u32[]{:S(2)}, u32[]{:S(2)}) %all-to-all-start.5) | async-done | bytes 6193184 | tf_op jit(solution)/shard_map/all_to_all | solution.py:201
  674.7 5.9 convert_reduce_fusion
  683.9 6.3 gather_fusion.3
  692.7 4.6 reduce_sum.230
  703.9 28.0 %reduce-scatter.10.cloned.1.call-done = f32[200,768]{1,0:T(8,128)} async-done(((f32[400,768]{1,0:T(8,128)}), f32[200,768]{1,0:T(8,128)}) %reduce-scatter.10.cloned.1.call-update) | async-done | bytes 614416 | tf_op jit(solution)/shard_map/reduce_scatter | solution.py:186
  733.4 26.5 %reduce-scatter.8.cloned.1.call-done = f32[200,768]{1,0:T(8,128)} async-done(((f32[400,768]{1,0:T(8,128)}), f32[200,768]{1,0:T(8,128)}) %reduce-scatter.8.cloned.1.call-update) | async-done | bytes 614416 | tf_op jit(solution)/shard_map/reduce_scatter | solution.py:186
  762.3 10.3 all_gather.19
  809.8 4.6 copy.292
  814.3 7.5 concatenate.20
  821.8 7.4 reduce-scatter.12.cloned.1.call-done
  832.7 8.1 concatenate.26
  840.8 7.1 fusion.37
  850.5 8.4 all-to-all-start.6
  858.9 7.1 fusion.38
  872.6 4.4 all-to-all-start.7
  880.0 10.6 all-to-all-done.7
  894.8 238.4 %reduce-scatter.14.cloned.1.call-done = f32[1,12,1556]{2,1,0:T(8,128)} async-done(((f32[64,12,1556]{2,1,0:T(8,128)}), f32[1,12,1556]{2,1,0:T(8,128)}) %reduce-scatter.14.cloned.1.call-update) | async-done | bytes 74704 | tf_op jit(solution)/shard_map/reduce_scatter | solution.py:168
  1136.1 7.0 psum.7
  (245 shorter events, 167.0 us)
Async XLA Ops:
  7.2 114.2 %all-gather.3.cloned.1.call-start = ((), (), s32[]{:S(2)}) async-start(), calls=%async_computation.18 | async-start | bytes 3461120 | tf_op jit(solution)/shard_map/all_gather | solution.py:141
  12.5 198.9 %reduce-scatter.6.cloned.1.call-start = ((), (), s32[]{:S(2)}) async-start(), calls=%async_computation.13 | async-start | bytes 1843200 | tf_op jit(solution)/shard_map/reduce_scatter | solution.py:186
  13.8 151.9 %copy-start.42 = (pred[200]{0:T(512)(128)(4,1)}, pred[200]{0:T(512)(128)(4,1)S(1)}, u32[]{:S(2)}) copy-start(pred[200]{0:T(512)(128)(4,1)S(1)} %iota_compare_fusion.3) | copy-start | bytes 604
  13.8 113.9 %copy-start.34 = (f32[200]{0:T(256)}, f32[200]{0:T(256)S(1)}, u32[]{:S(2)}) copy-start(f32[200]{0:T(256)S(1)} %broadcast_multiply_fusion.6) | copy-start | bytes 2404
  15.1 112.6 %copy-start.38 = (f32[200]{0:T(256)}, f32[200]{0:T(256)S(1)}, u32[]{:S(2)}) copy-start(f32[200]{0:T(256)S(1)} %add_rsqrt_fusion.1) | copy-start | bytes 2404
  125.6 48.6 %copy-start.4 = (bf16[768,1556]{1,0:T(8,128)(2,1)}, bf16[768,1556]{1,0:T(8,128)(2,1)S(1)}, u32[]{:S(2)}) copy-start(bf16[768,1556]{1,0:T(8,128)(2,1)S(1)} %reshape.389) | copy-start | bytes 7170052
  126.1 95.0 %copy-start.31 = (f32[768]{0:T(1024)}, f32[768]{0:T(1024)S(1)}, u32[]{:S(2)}) copy-start(f32[768]{0:T(1024)S(1)} %get-tuple-element.11) | copy-start | bytes 9220
  176.8 9.9 copy-start.33
  176.8 23.7 %copy-start.24 = (bf16[12,16,1536]{2,1,0:T(8,128)(2,1)S(1)}, bf16[12,16,1536]{2,1,0:T(8,128)(2,1)}, u32[]{:S(2)}) copy-start(bf16[12,16,1536]{2,1,0:T(8,128)(2,1)} %param.22) | copy-start | bytes 1769476
  179.6 33.3 %all-to-all-start.1 = ((bf16[12,64,384]{2,0,1:T(8,128)(2,1)}), bf16[12,64,384]{2,0,1:T(8,128)(2,1)S(1)}, u32[]{:S(2)}, u32[]{:S(2)}) async-start(bf16[12,64,384]{2,0,1:T(8,128)(2,1)} %copy.273), calls=%async_computation.2 | async-start | bytes 1572864 | tf_op jit(solution)/shard_map/all_to_all | solution.py:263
  212.6 32.8 %copy-start.2 = (f32[200,768]{1,0:T(8,128)}, f32[200,768]{1,0:T(8,128)S(1)}, u32[]{:S(2)}) copy-start(f32[200,768]{1,0:T(8,128)S(1)} %get-tuple-element.34) | copy-start | bytes 1843204
  212.6 32.8 %copy-start.36 = (f32[200]{0:T(256)}, f32[200]{0:T(256)S(1)}, u32[]{:S(2)}) copy-start(f32[200]{0:T(256)S(1)} %broadcast_multiply_fusion.5) | copy-start | bytes 2404
  212.9 32.6 %copy-start.40 = (f32[200]{0:T(256)}, f32[200]{0:T(256)S(1)}, u32[]{:S(2)}) copy-start(f32[200]{0:T(256)S(1)} %add_rsqrt_fusion) | copy-start | bytes 2404
  212.9 27.4 %copy-start.7 = (bf16[12,64,384]{2,0,1:T(8,128)(2,1)}, bf16[12,64,384]{2,0,1:T(8,128)(2,1)S(1)}, u32[]{:S(2)}) copy-start(bf16[12,64,384]{2,0,1:T(8,128)(2,1)S(1)} %all-to-all-done.1) | copy-start | bytes 1769476
  212.9 35.6 %all-to-all-start.2 = ((bf16[12,64,384]{2,0,1:T(8,128)(2,1)}), bf16[12,64,384]{2,0,1:T(8,128)(2,1)}, u32[]{:S(2)}, u32[]{:S(2)}) async-start(bf16[12,64,384]{2,0,1:T(8,128)(2,1)} %copy.274), calls=%async_computation.3 | async-start | bytes 1572864 | tf_op jit(solution)/shard_map/all_to_all | solution.py:264
  253.3 7.0 copy-start.10
  253.3 84.8 %all-to-all-start = ((bf16[64,63,768]{2,1,0:T(8,128)(2,1)}), bf16[64,63,768]{2,1,0:T(8,128)(2,1)}, u32[]{:S(2)}, u32[]{:S(2)}) async-start(bf16[64,63,768]{2,1,0:T(8,128)(2,1)} %bitcast.138), calls=%async_computation.1 | async-start | bytes 12582912 | tf_op jit(solution)/shard_map/all_to_all | solution.py:194
  327.3 5.4 copy-start.17
  341.5 26.1 %copy-start.8 = (bf16[12,64,384]{2,0,1:T(8,128)(2,1)S(1)}, bf16[12,64,384]{2,0,1:T(8,128)(2,1)}, u32[]{:S(2)}) copy-start(bf16[12,64,384]{2,0,1:T(8,128)(2,1)} %copy-done.7) | copy-start | bytes 1769476
  341.5 110.6 %all-to-all-start.4 = ((bf16[64,63,768]{2,1,0:T(8,128)(2,1)}), bf16[64,63,768]{2,1,0:T(8,128)(2,1)}, u32[]{:S(2)}, u32[]{:S(2)}) async-start(bf16[64,63,768]{2,1,0:T(8,128)(2,1)} %bitcast.139), calls=%async_computation.6 | async-start | bytes 12582912 | tf_op jit(solution)/shard_map/all_to_all | solution.py:194
  460.3 19.9 %copy-start.5 = (f32[4032,384]{1,0:T(8,128)S(1)}, f32[4032,384]{1,0:T(8,128)}, u32[]{:S(2)}) copy-start(f32[4032,384]{1,0:T(8,128)} %fusion.114) | copy-start | bytes 18579460
  496.4 89.4 %all-to-all-start.3 = ((bf16[64,63,768]{2,1,0:T(8,128)(2,1)}), bf16[64,63,768]{2,1,0:T(8,128)(2,1)}, u32[]{:S(2)}, u32[]{:S(2)}) async-start(bf16[64,63,768]{2,1,0:T(8,128)(2,1)} %reshape.307), calls=%async_computation.4 | async-start | bytes 12582912 | tf_op jit(solution)/shard_map/all_to_all | solution.py:201
  585.8 88.9 %all-to-all-start.5 = ((bf16[64,63,768]{2,1,0:T(8,128)(2,1)}), bf16[64,63,768]{2,1,0:T(8,128)(2,1)}, u32[]{:S(2)}, u32[]{:S(2)}) async-start(bf16[64,63,768]{2,1,0:T(8,128)(2,1)} %reshape.313), calls=%async_computation.7 | async-start | bytes 12582912 | tf_op jit(solution)/shard_map/all_to_all | solution.py:201
  596.8 135.1 %reduce-scatter.10.cloned.1.call-start = ((), (), s32[]{:S(2)}) async-start(), calls=%async_computation.15 | async-start | bytes 1843200 | tf_op jit(solution)/shard_map/reduce_scatter | solution.py:186
  613.0 4.1 copy-start.18
  625.4 71.9 %copy-start.25 = (f32[400,16]{0,1:T(8,128)}, f32[400,16]{0,1:T(8,128)S(1)}, u32[]{:S(2)}) copy-start(f32[400,16]{0,1:T(8,128)S(1)} %multiply_reduce_fusion.11) | copy-start | bytes 76804
  697.3 3.7 copy-start.21
  697.4 3.7 copy-start.22
  697.4 3.7 copy-start.43
  700.2 59.7 %reduce-scatter.8.cloned.1.call-start = ((), (), s32[]{:S(2)}) async-start(), calls=%async_computation.14 | async-start | bytes 1843200 | tf_op jit(solution)/shard_map/reduce_scatter | solution.py:186
  700.7 31.2 %copy-start.3 = (f32[200,768]{1,0:T(8,128)S(1)}, f32[200,768]{1,0:T(8,128)}, u32[]{:S(2)}) copy-start(f32[200,768]{1,0:T(8,128)} %copy-done.2) | copy-start | bytes 1843204
  700.8 31.1 %copy-start.32 = (f32[768]{0:T(1024)S(1)}, f32[768]{0:T(1024)}, u32[]{:S(2)}) copy-start(f32[768]{0:T(1024)} %copy-done.31) | copy-start | bytes 9220
  700.8 31.1 %copy-start.37 = (f32[200]{0:T(256)S(1)}, f32[200]{0:T(256)}, u32[]{:S(2)}) copy-start(f32[200]{0:T(256)} %copy-done.36) | copy-start | bytes 2404
  700.8 31.1 %copy-start.41 = (f32[200]{0:T(256)S(1)}, f32[200]{0:T(256)}, u32[]{:S(2)}) copy-start(f32[200]{0:T(256)} %copy-done.40) | copy-start | bytes 2404
  700.8 59.0 %copy-start.11 = (f32[200,768]{1,0:T(8,128)S(1)}, f32[200,768]{1,0:T(8,128)}, u32[]{:S(2)}) copy-start(f32[200,768]{1,0:T(8,128)} %param.23) | copy-start | bytes 1843204
  700.8 128.5 %reduce-scatter.12.cloned.1.call-start = ((), (), s32[]{:S(2)}) async-start(), calls=%async_computation.16 | async-start | bytes 1843200 | tf_op jit(solution)/shard_map/reduce_scatter | solution.py:186
  786.7 4.3 copy-start.27
  792.0 8.5 copy-start.19
  802.6 330.6 %reduce-scatter.14.cloned.1.call-start = ((), (), s32[]{:S(2)}) async-start(), calls=%async_computation.17 | async-start | bytes 6922240 | tf_op jit(solution)/shard_map/reduce_scatter | solution.py:168
  804.8 2.5 copy-start.16
  814.3 14.9 %copy-start.1 = (f32[200,768]{1,0:T(8,128)S(1)}, f32[200,768]{1,0:T(8,128)}, u32[]{:S(2)}) copy-start(f32[200,768]{1,0:T(8,128)} %param.12) | copy-start | bytes 1843204
  814.3 14.9 %copy-start.30 = (f32[768]{0:T(1024)S(1)}, f32[768]{0:T(1024)}, u32[]{:S(2)}) copy-start(f32[768]{0:T(1024)} %copy-done.29) | copy-start | bytes 9220
  814.3 14.9 %copy-start.35 = (f32[200]{0:T(256)S(1)}, f32[200]{0:T(256)}, u32[]{:S(2)}) copy-start(f32[200]{0:T(256)} %copy-done.34) | copy-start | bytes 2404
  814.3 14.9 %copy-start.39 = (f32[200]{0:T(256)S(1)}, f32[200]{0:T(256)}, u32[]{:S(2)}) copy-start(f32[200]{0:T(256)} %copy-done.38) | copy-start | bytes 2404
  850.5 22.0 %all-to-all-start.6 = ((bf16[64,2,2304]{2,1,0:T(2,128)(2,1)}), bf16[64,2,2304]{2,1,0:T(2,128)(2,1)S(1)}, u32[]{:S(2)}, u32[]{:S(2)}) async-start(bf16[64,2,2304]{2,1,0:T(2,128)(2,1)} %reshape.416), calls=%async_computation.11 | async-start | bytes 1179648 | tf_op jit(solution)/shard_map/all_to_all | solution.py:294
  872.6 18.1 %all-to-all-start.7 = ((bf16[64,2,2304]{2,1,0:T(2,128)(2,1)}), bf16[64,2,2304]{2,1,0:T(2,128)(2,1)S(1)}, u32[]{:S(2)}, u32[]{:S(2)}) async-start(bf16[64,2,2304]{2,1,0:T(2,128)(2,1)} %reshape.418), calls=%async_computation.12 | async-start | bytes 1179648 | tf_op jit(solution)/shard_map/all_to_all | solution.py:301
  891.2 2.6 copy-start.14
  891.2 2.5 copy-start.15
  (10 other events, 15.5 us)
Sparse Core Ops, SparseCore 0:
  12.6 108.7 all-gather.2
  176.9 34.4 reduce-scatter.5
  700.3 31.5 reduce-scatter.9
  734.1 25.6 reduce-scatter.7
  802.7 26.5 reduce-scatter.11
  840.9 292.1 reduce-scatter.13

commit v3 on v2

--- a/solution.py
+++ b/solution.py
@@ -114,6 +114,16 @@
     return (query_grad.reshape(shape), key_grad.reshape(shape), value_grad.reshape(shape))
 
 
+def gather_rows(pieces):
+    rows = pieces[0].shape[0]
+    packed = jnp.concatenate(pieces, axis=1)
+    spare = -packed.shape[1] % 128
+    if spare:
+        packed = jnp.pad(packed, ((0, 0), (0, spare)))
+    full = lax.all_gather(packed[None], "fsdp", axis=0, tiled=True)
+    return full.reshape(lax.axis_size("fsdp") * rows, packed.shape[1])
+
+
 def gather_dense(
     qkv_weight,
     proj_weight,
@@ -126,7 +136,7 @@
     rows = qkv_weight.shape[1]
     heads_width = qkv_weight.shape[2]
     experts = router_weight.shape[1]
-    packed = jnp.concatenate(
+    full = gather_rows(
         [
             jnp.transpose(qkv_weight, (1, 0, 2)).reshape(rows, -1),
             proj_weight.T,
@@ -135,10 +145,8 @@
                 [attention_norm_gain, attention_norm_shift, expert_norm_gain, expert_norm_shift],
                 axis=1,
             ),
-        ],
-        axis=1,
-    )
-    full = lax.all_gather(packed, "fsdp", axis=0, tiled=True)
+        ]
+    )
     width = full.shape[0]
     at = 3 * heads_width
     qkv_full = jnp.transpose(full[:, :at].reshape(width, 3, heads_width), (1, 0, 2))
@@ -146,36 +154,19 @@
     at += heads_width
     router_full = full[:, at : at + experts]
     at += experts
-    norms = full[:, at : at + 4]
-    return (qkv_full, proj_full, router_full, norms[:, 0], norms[:, 1], norms[:, 2], norms[:, 3])
-
-
-def reduce_dense(qkv_part, proj_part, router_part, norm_parts):
-    width = qkv_part.shape[1]
-    heads_width = qkv_part.shape[2]
-    experts = router_part.shape[1]
-    packed = jnp.concatenate(
-        [
-            jnp.transpose(qkv_part, (1, 0, 2)).reshape(width, -1),
-            proj_part.T,
-            router_part,
-            jnp.stack(norm_parts, axis=1),
-        ],
-        axis=1,
-    )
+    return (qkv_full, proj_full, router_full) + tuple(full[:, at + i] for i in range(4))
+
+
+def reduce_rows(pieces):
+    packed = jnp.concatenate(pieces, axis=1)
+    spare = -packed.shape[1] % 128
+    if spare:
+        packed = jnp.pad(packed, ((0, 0), (0, spare)))
     holders = lax.axis_size("fsdp")
-    rows = width // holders
-    part = lax.psum_scatter(
+    rows = packed.shape[0] // holders
+    return lax.psum_scatter(
         packed.reshape(holders, rows, packed.shape[1]), "fsdp", scatter_dimension=0, tiled=True
     ).reshape(rows, packed.shape[1])
-    at = 3 * heads_width
-    qkv_grad = jnp.transpose(part[:, :at].reshape(rows, 3, heads_width), (1, 0, 2))
-    proj_grad = part[:, at : at + heads_width].T
-    at += heads_width
-    shared = lax.psum(part[:, at:], "tp")
-    router_grad = shared[:, :experts]
-    norm_grads = [shared[:, experts + i] for i in range(len(norm_parts))]
-    return qkv_grad, proj_grad, router_grad, norm_grads
 
 
 def group_rows(value):
@@ -324,6 +315,11 @@
     middle_grad = cotangent + expert_norm_backward
     mid_rows = group_rows(middle_grad.astype(bf16))
     proj_part = jnp.einsum("th,td->hd", context, mid_rows, preferred_element_type=f32)
+    experts_w = router_part.shape[1]
+    heads_w = proj_part.shape[0]
+    early = reduce_rows(
+        [proj_part.T, router_part, jnp.stack([expert_gain_partial, expert_shift_partial], axis=1)]
+    )
     context_grad = jnp.einsum("td,hd->th", mid_rows, proj_back, preferred_element_type=f32).astype(
         bf16
     )
@@ -331,6 +327,7 @@
         proj[0], proj[1], proj[2], lse, context_grad, images
     )
     stacked = jnp.stack([query_grad, key_grad, value_grad])
+    early, stacked = lax.optimization_barrier((early, stacked))
     qkv_part = jnp.einsum("td,ith->idh", tokens_a, stacked, preferred_element_type=f32)
     attention_input_gradient = owned_rows(
         jnp.einsum("ith,idh->td", stacked, qkv_back, preferred_element_type=f32)
@@ -342,21 +339,30 @@
         attention_gain_gradient,
     )
     input_grad = middle_grad + attention_norm_backward
-    qkv_grad, proj_grad, router_grad, norm_grads = reduce_dense(
-        qkv_part,
-        proj_part,
-        router_part,
-        [attention_gain_partial, attention_shift_partial, expert_gain_partial, expert_shift_partial],
-    )
+    late = reduce_rows(
+        [
+            jnp.transpose(qkv_part, (1, 0, 2)).reshape(qkv_part.shape[1], -1),
+            jnp.stack([attention_gain_partial, attention_shift_partial], axis=1),
+        ]
+    )
+    rows = late.shape[0]
+    at = 3 * heads_w
+    qkv_grad = jnp.transpose(late[:, :at].reshape(rows, 3, heads_w), (1, 0, 2))
+    proj_grad = early[:, :heads_w].T
+    shared = lax.psum(
+        jnp.concatenate([early[:, heads_w : heads_w + experts_w + 2], late[:, at : at + 2]], axis=1),
+        "tp",
+    )
+    router_grad = shared[:, :experts_w]
     return (
         outputs,
         input_grad,
-        norm_grads[0],
-        norm_grads[1],
+        shared[:, experts_w + 2],
+        shared[:, experts_w + 3],
         qkv_grad,
         proj_grad,
-        norm_grads[2],
-        norm_grads[3],
+        shared[:, experts_w],
+        shared[:, experts_w + 1],
         router_grad,
         in_grad,
         out_grad,

time: 1170 us -> 1420 us (1.21)
  waiting for transfers between devices: 611 us -> 878 us
    reduce_scatter x1 -> x2, waiting for transfers between devices: 238 us -> 490 us  [reduce_rows(): lax.psum_scatter(packed.reshape(holders, rows, packed.shape[1]), 'fsdp',...]
    concatenate x9 -> x2, local copies, waits for them, and re-layouts: 21.2 us -> 5.33 us  [the longest x1 4.52 us: reduce_rows(): packed = jnp.concatenate(pieces, axis=1)]
    reduce_scatter x4, waiting for transfers between devices: 71.2 us -> 86.6 us  [owned_rows(): return lax.psum_scatter(value, 'tp', scatter_dimension=0, tiled=True)]
  transfers between devices with their start and end apart: 14 -> 15, of which waited for: 12 -> 13; matrix products, arithmetic and copies ran while one was open for 14% -> 12% of each run, Pallas kernels for 0% -> 0%
where the time goes in v3:
time: 1420 us; the launch traced here: 1410 us
  waiting for transfers between devices  878 us (62%)
  local copies, waits for them, and re-layouts  183 us (13%)
  blocking collectives  104 us (7%)
  matrix products  97.9 us (7%)
  starting transfers between devices  84.1 us (6%)
  other arithmetic  48.5 us (3%)
  between operations  15.4 us (1%)
    reduce_scatter x2, waiting for transfers between devices, reduce_rows(): lax.psum_scatter(packed.reshape(holders, rows, packed.shape[1]), 'fsdp',...  490 us
    all_to_all x2, waiting for transfers between devices, to_groups(): lax.all_to_all(pieces, 'fsdp', split_axis=0, concat_axis=0, tiled=True)  110 us
    all_gather x1, waiting for transfers between devices, gather_rows(): full = lax.all_gather(packed[None], 'fsdp', axis=0, tiled=True)  106 us
    all_gather x4, blocking collectives, group_rows(): return lax.all_gather(value, 'tp', axis=0, tiled=True)  97.1 us
    reduce_scatter x4, waiting for transfers between devices, owned_rows(): return lax.psum_scatter(value, 'tp', scatter_dimension=0, tiled=True)  86.6 us
    all_to_all x2, waiting for transfers between devices, to_owners(): lax.all_to_all(spread, 'fsdp', split_axis=0, concat_axis=0, tiled=True)  68.8 us
    all_to_all x2, starting transfers between devices, to_owners(): lax.all_to_all(spread, 'fsdp', split_axis=0, concat_axis=0, tiled=True)  33 us
  transfers between devices with their start and end apart: 15, of which 13 were waited for; matrix products, arithmetic and copies ran while one was open for 12% of the time, Pallas kernels for 0%

profile of v3, /device:TPU:1, one launch (start us, length us, event | category | flops | bytes accessed | tf_op | source)
XLA Modules:
  0.0 1410.3 jit_solution(17668735921415066721)
XLA Ops:
  15.1 106.3 %all-gather.4.cloned.1.call-done = bf16[64,12,1664]{2,1,0:T(8,128)(2,1)} async-done(((bf16[1,12,1664]{2,1,0:T(8,128)(2,1)}), bf16[64,12,1664]{2,1,0:T(8,128)(2,1)}) %all-gather.4.cloned.1.call-update) | async-done | bytes 2555920 | tf_op jit(solution)/shard_map/all_gather | solution.py:123
  127.4 10.9 all_gather.16
  179.2 7.2 all-to-all-start.1
  189.6 5.3 scatter_custom_fusion.1
  194.9 5.3 scatter_custom_fusion
  201.9 9.1 reduce-scatter.7.cloned.1.call-done
  212.5 8.2 all-to-all-start.2
  221.0 19.0 %all_gather.17 = bf16[400,768]{1,0:T(8,128)(2,1)S(1)} all-gather(bf16[200,768]{1,0:T(8,128)(2,1)S(1)} %add_convert_fusion.1), channel_id=1, replica_groups=mesh['fsdp'=64,'tp'=2] {'tp'}, dimensions={0}, use_global_device_ids=true | all-gather | bytes 921600 | tf_op jit(solution)/shard_map/all_gather | solution.py:173
  239.9 5.2 gather_fusion
  248.1 4.8 broadcast_in_dim.66
  253.0 6.9 all-to-all-start
  259.9 56.9 %all_gather.18 = bf16[400,768]{1,0:T(8,128)(2,1)S(1)} all-gather(bf16[200,768]{1,0:T(8,128)(2,1)S(1)} %convert_element_type.207), channel_id=1, replica_groups=mesh['fsdp'=64,'tp'=2] {'tp'}, dimensions={0}, use_global_device_ids=true | all-gather | bytes 921600 | tf_op jit(solution)/shard_map/all_gather | solution.py:173
  316.9 5.3 gather_fusion.2
  327.0 5.3 scatter_custom_fusion.2
  341.1 26.2 %all-to-all-start.4 = ((bf16[64,63,768]{2,1,0:T(8,128)(2,1)}), bf16[64,63,768]{2,1,0:T(8,128)(2,1)}, u32[]{:S(2)}, u32[]{:S(2)}) async-start(bf16[64,63,768]{2,1,0:T(8,128)(2,1)} %bitcast.144), calls=%async_computation.6 | async-start | bytes 12582912 | tf_op jit(solution)/shard_map/all_to_all | solution.py:185
  368.6 8.5 reshape.303
  377.1 8.7 fusion.111
  385.9 65.8 %all-to-all-done.4 = bf16[64,63,768]{2,1,0:T(8,128)(2,1)} async-done(((bf16[64,63,768]{2,1,0:T(8,128)(2,1)}), bf16[64,63,768]{2,1,0:T(8,128)(2,1)}, u32[]{:S(2)}, u32[]{:S(2)}) %all-to-all-start.4) | async-done | bytes 6193184 | tf_op jit(solution)/shard_map/all_to_all | solution.py:185
  451.6 8.3 reshape.313
  459.9 19.9 %add_convert_fusion = (bf16[4032,384]{1,0:T(8,128)(2,1)}, f32[4032,384]{1,0:T(8,128)S(1)}) fusion(f32[4032,384]{1,0:T(8,128)} %fusion.111, bf16[4032,768]{1,0:T(8,128)(2,1)} %reshape.313, bf16[768,384]{1,0:T(8,128)(2,1)S(1)} %reshape.307), kind=kOutput, calls=%fused_computation.15 | convolution fusion | flops 2489647104 | bytes 22265856 | tf_op jit(solution)/shard_map/dot_general | solution.py:278
  482.2 5.3 convolution_convert_fusion.1
  487.5 8.4 reshape.308
  496.0 11.6 all-to-all-start.3
  507.6 7.9 convolution_convert_fusion
  515.6 8.5 reshape.314
  524.1 61.2 %all-to-all-done.3 = bf16[64,63,768]{2,1,0:T(8,128)(2,1)} async-done(((bf16[64,63,768]{2,1,0:T(8,128)(2,1)}), bf16[64,63,768]{2,1,0:T(8,128)(2,1)}, u32[]{:S(2)}, u32[]{:S(2)}) %all-to-all-start.3) | async-done | bytes 6193184 | tf_op jit(solution)/shard_map/all_to_all | solution.py:192
  585.3 10.7 all-to-all-start.5
  596.0 5.9 convert_reduce_fusion.1
  605.5 6.6 gather_fusion.1
  616.3 8.1 multiply_reduce_fusion.1
  624.6 49.3 %all-to-all-done.5 = bf16[64,63,768]{2,1,0:T(8,128)(2,1)} async-done(((bf16[64,63,768]{2,1,0:T(8,128)(2,1)}), bf16[64,63,768]{2,1,0:T(8,128)(2,1)}, u32[]{:S(2)}, u32[]{:S(2)}) %all-to-all-start.5) | async-done | bytes 6193184 | tf_op jit(solution)/shard_map/all_to_all | solution.py:192
  673.8 5.9 convert_reduce_fusion
  683.0 6.3 gather_fusion.3
  691.8 4.6 reduce_sum.230
  700.4 30.9 %reduce-scatter.11.cloned.1.call-done = f32[200,768]{1,0:T(8,128)} async-done(((f32[400,768]{1,0:T(8,128)}), f32[200,768]{1,0:T(8,128)}) %reduce-scatter.11.cloned.1.call-update) | async-done | bytes 614416 | tf_op jit(solution)/shard_map/reduce_scatter | solution.py:177
  732.8 26.4 %reduce-scatter.9.cloned.1.call-done = f32[200,768]{1,0:T(8,128)} async-done(((f32[400,768]{1,0:T(8,128)}), f32[200,768]{1,0:T(8,128)}) %reduce-scatter.9.cloned.1.call-update) | async-done | bytes 614416 | tf_op jit(solution)/shard_map/reduce_scatter | solution.py:177
  761.7 10.3 all_gather.19
  800.9 255.8 %reduce-scatter.13.cloned.1.call-done = f32[1,12,512]{2,1,0:T(8,128)} async-done(((f32[64,12,512]{2,1,0:T(8,128)}), f32[1,12,512]{2,1,0:T(8,128)}) %reduce-scatter.13.cloned.1.call-update) | async-done | bytes 24592 | tf_op jit(solution)/shard_map/reduce_scatter | solution.py:167
  1063.6 5.2 copy.261
  1068.8 20.2 %reduce-scatter.15.cloned.1.call-done = f32[200,768]{1,0:T(8,128)} async-done(((f32[400,768]{1,0:T(8,128)}), f32[200,768]{1,0:T(8,128)}) %reduce-scatter.15.cloned.1.call-update) | async-done | bytes 614416 | tf_op jit(solution)/shard_map/reduce_scatter | solution.py:177
  1099.6 5.0 reshape.321
  1104.7 7.1 fusion.37
  1114.4 8.0 all-to-all-start.6
  1122.4 7.1 fusion.38
  1136.1 4.7 all-to-all-start.7
  1143.9 10.6 all-to-all-done.7
  1159.2 234.5 %reduce-scatter.17.cloned.1.call-done = f32[1,12,1280]{2,1,0:T(8,128)} async-done(((f32[64,12,1280]{2,1,0:T(8,128)}), f32[1,12,1280]{2,1,0:T(8,128)}) %reduce-scatter.17.cloned.1.call-update) | async-done | bytes 61456 | tf_op jit(solution)/shard_map/reduce_scatter | solution.py:167
  1395.3 6.5 psum.7
  (243 shorter events, 169.3 us)
Async XLA Ops:
  7.2 114.3 %all-gather.4.cloned.1.call-start = ((), (), s32[]{:S(2)}) async-start(), calls=%async_computation.20 | async-start | bytes 3461120 | tf_op jit(solution)/shard_map/all_gather | solution.py:123
  12.5 198.5 %reduce-scatter.7.cloned.1.call-start = ((), (), s32[]{:S(2)}) async-start(), calls=%async_computation.14 | async-start | bytes 1843200 | tf_op jit(solution)/shard_map/reduce_scatter | solution.py:177
  13.8 151.5 %copy-start.39 = (pred[200]{0:T(512)(128)(4,1)}, pred[200]{0:T(512)(128)(4,1)S(1)}, u32[]{:S(2)}) copy-start(pred[200]{0:T(512)(128)(4,1)S(1)} %iota_compare_fusion.3) | copy-start | bytes 604
  13.8 113.4 %copy-start.31 = (f32[200]{0:T(256)}, f32[200]{0:T(256)S(1)}, u32[]{:S(2)}) copy-start(f32[200]{0:T(256)S(1)} %broadcast_multiply_fusion.6) | copy-start | bytes 2404
  15.1 112.1 %copy-start.35 = (f32[200]{0:T(256)}, f32[200]{0:T(256)S(1)}, u32[]{:S(2)}) copy-start(f32[200]{0:T(256)S(1)} %add_rsqrt_fusion.1) | copy-start | bytes 2404
  125.2 48.7 %copy-start.4 = (bf16[768,1664]{1,0:T(8,128)(2,1)}, bf16[768,1664]{1,0:T(8,128)(2,1)S(1)}, u32[]{:S(2)}) copy-start(bf16[768,1664]{1,0:T(8,128)(2,1)S(1)} %reshape.396) | copy-start | bytes 7667716
  125.2 2.1 copy-start
  125.7 95.0 %copy-start.27 = (f32[768]{0:T(1024)}, f32[768]{0:T(1024)S(1)}, u32[]{:S(2)}) copy-start(f32[768]{0:T(1024)S(1)} %get-tuple-element.15) | copy-start | bytes 9220
  176.4 10.1 copy-start.29
  176.4 23.8 %copy-start.23 = (bf16[12,16,1536]{2,1,0:T(8,128)(2,1)S(1)}, bf16[12,16,1536]{2,1,0:T(8,128)(2,1)}, u32[]{:S(2)}) copy-start(bf16[12,16,1536]{2,1,0:T(8,128)(2,1)} %param.22) | copy-start | bytes 1769476
  179.2 33.3 %all-to-all-start.1 = ((bf16[12,64,384]{2,0,1:T(8,128)(2,1)}), bf16[12,64,384]{2,0,1:T(8,128)(2,1)S(1)}, u32[]{:S(2)}, u32[]{:S(2)}) async-start(bf16[12,64,384]{2,0,1:T(8,128)(2,1)} %copy.242), calls=%async_computation.2 | async-start | bytes 1572864 | tf_op jit(solution)/shard_map/all_to_all | solution.py:254
  212.2 32.9 %copy-start.2 = (f32[200,768]{1,0:T(8,128)}, f32[200,768]{1,0:T(8,128)S(1)}, u32[]{:S(2)}) copy-start(f32[200,768]{1,0:T(8,128)S(1)} %get-tuple-element.38) | copy-start | bytes 1843204
  212.2 8.5 copy-start.33
  212.5 32.6 %copy-start.37 = (f32[200]{0:T(256)}, f32[200]{0:T(256)S(1)}, u32[]{:S(2)}) copy-start(f32[200]{0:T(256)S(1)} %add_rsqrt_fusion) | copy-start | bytes 2404
  212.5 27.4 %copy-start.7 = (bf16[12,64,384]{2,0,1:T(8,128)(2,1)}, bf16[12,64,384]{2,0,1:T(8,128)(2,1)S(1)}, u32[]{:S(2)}) copy-start(bf16[12,64,384]{2,0,1:T(8,128)(2,1)S(1)} %all-to-all-done.1) | copy-start | bytes 1769476
  212.5 35.6 %all-to-all-start.2 = ((bf16[12,64,384]{2,0,1:T(8,128)(2,1)}), bf16[12,64,384]{2,0,1:T(8,128)(2,1)}, u32[]{:S(2)}, u32[]{:S(2)}) async-start(bf16[12,64,384]{2,0,1:T(8,128)(2,1)} %copy.243), calls=%async_computation.3 | async-start | bytes 1572864 | tf_op jit(solution)/shard_map/all_to_all | solution.py:255
  253.0 6.9 copy-start.10
  253.0 84.7 %all-to-all-start = ((bf16[64,63,768]{2,1,0:T(8,128)(2,1)}), bf16[64,63,768]{2,1,0:T(8,128)(2,1)}, u32[]{:S(2)}, u32[]{:S(2)}) async-start(bf16[64,63,768]{2,1,0:T(8,128)(2,1)} %bitcast.143), calls=%async_computation.1 | async-start | bytes 12582912 | tf_op jit(solution)/shard_map/all_to_all | solution.py:185
  326.9 5.4 copy-start.17
  341.1 26.2 %copy-start.8 = (bf16[12,64,384]{2,0,1:T(8,128)(2,1)S(1)}, bf16[12,64,384]{2,0,1:T(8,128)(2,1)}, u32[]{:S(2)}) copy-start(bf16[12,64,384]{2,0,1:T(8,128)(2,1)} %copy-done.7) | copy-start | bytes 1769476
  341.1 110.5 %all-to-all-start.4 = ((bf16[64,63,768]{2,1,0:T(8,128)(2,1)}), bf16[64,63,768]{2,1,0:T(8,128)(2,1)}, u32[]{:S(2)}, u32[]{:S(2)}) async-start(bf16[64,63,768]{2,1,0:T(8,128)(2,1)} %bitcast.144), calls=%async_computation.6 | async-start | bytes 12582912 | tf_op jit(solution)/shard_map/all_to_all | solution.py:185
  459.9 19.9 %copy-start.5 = (f32[4032,384]{1,0:T(8,128)S(1)}, f32[4032,384]{1,0:T(8,128)}, u32[]{:S(2)}) copy-start(f32[4032,384]{1,0:T(8,128)} %fusion.111) | copy-start | bytes 18579460
  496.0 89.3 %all-to-all-start.3 = ((bf16[64,63,768]{2,1,0:T(8,128)(2,1)}), bf16[64,63,768]{2,1,0:T(8,128)(2,1)}, u32[]{:S(2)}, u32[]{:S(2)}) async-start(bf16[64,63,768]{2,1,0:T(8,128)(2,1)} %reshape.308), calls=%async_computation.4 | async-start | bytes 12582912 | tf_op jit(solution)/shard_map/all_to_all | solution.py:192
  585.3 88.5 %all-to-all-start.5 = ((bf16[64,63,768]{2,1,0:T(8,128)(2,1)}), bf16[64,63,768]{2,1,0:T(8,128)(2,1)}, u32[]{:S(2)}, u32[]{:S(2)}) async-start(bf16[64,63,768]{2,1,0:T(8,128)(2,1)} %reshape.314), calls=%async_computation.7 | async-start | bytes 12582912 | tf_op jit(solution)/shard_map/all_to_all | solution.py:192
  595.9 135.3 %reduce-scatter.11.cloned.1.call-start = ((), (), s32[]{:S(2)}) async-start(), calls=%async_computation.16 | async-start | bytes 1843200 | tf_op jit(solution)/shard_map/reduce_scatter | solution.py:177
  612.1 4.1 copy-start.18
  696.4 34.8 %copy-start.3 = (f32[200,768]{1,0:T(8,128)S(1)}, f32[200,768]{1,0:T(8,128)}, u32[]{:S(2)}) copy-start(f32[200,768]{1,0:T(8,128)} %copy-done.2) | copy-start | bytes 1843204
  696.5 34.8 %copy-start.28 = (f32[768]{0:T(1024)S(1)}, f32[768]{0:T(1024)}, u32[]{:S(2)}) copy-start(f32[768]{0:T(1024)} %copy-done.27) | copy-start | bytes 9220
  696.5 34.8 %copy-start.34 = (f32[200]{0:T(256)S(1)}, f32[200]{0:T(256)}, u32[]{:S(2)}) copy-start(f32[200]{0:T(256)} %copy-done.33) | copy-start | bytes 2404
  696.5 34.8 %copy-start.38 = (f32[200]{0:T(256)S(1)}, f32[200]{0:T(256)}, u32[]{:S(2)}) copy-start(f32[200]{0:T(256)} %copy-done.37) | copy-start | bytes 2404
  699.2 60.0 %copy-start.11 = (f32[200,768]{1,0:T(8,128)S(1)}, f32[200,768]{1,0:T(8,128)}, u32[]{:S(2)}) copy-start(f32[200,768]{1,0:T(8,128)} %param.23) | copy-start | bytes 1843204
  699.2 60.0 %reduce-scatter.9.cloned.1.call-start = ((), (), s32[]{:S(2)}) async-start(), calls=%async_computation.15 | async-start | bytes 1843200 | tf_op jit(solution)/shard_map/reduce_scatter | solution.py:177
  699.8 356.8 %reduce-scatter.13.cloned.1.call-start = ((), (), s32[]{:S(2)}) async-start(), calls=%async_computation.17 | async-start | bytes 2129920 | tf_op jit(solution)/shard_map/reduce_scatter | solution.py:167
  732.7 40.1 %copy-start.6 = (bf16[400,384]{0,1:T(8,128)(2,1)S(1)}, bf16[400,384]{0,1:T(8,128)(2,1)}, u32[]{:S(2)}) copy-start(bf16[400,384]{0,1:T(8,128)(2,1)} %reshape.299) | copy-start | bytes 921604
  775.6 2.9 copy-start.13
  775.6 313.4 %reduce-scatter.15.cloned.1.call-start = ((), (), s32[]{:S(2)}) async-start(), calls=%async_computation.18 | async-start | bytes 1843200 | tf_op jit(solution)/shard_map/reduce_scatter | solution.py:177
  780.9 4.1 copy-start.22
  794.0 5.7 copy-start.21
  1056.6 4.1 copy-start.16
  1060.4 333.2 %reduce-scatter.17.cloned.1.call-start = ((), (), s32[]{:S(2)}) async-start(), calls=%async_computation.19 | async-start | bytes 5324800 | tf_op jit(solution)/shard_map/reduce_scatter | solution.py:167
  1063.6 25.5 %copy-start.1 = (f32[200,768]{1,0:T(8,128)S(1)}, f32[200,768]{1,0:T(8,128)}, u32[]{:S(2)}) copy-start(f32[200,768]{1,0:T(8,128)} %param.12) | copy-start | bytes 1843204
  1063.6 25.5 %copy-start.26 = (f32[768]{0:T(1024)S(1)}, f32[768]{0:T(1024)}, u32[]{:S(2)}) copy-start(f32[768]{0:T(1024)} %copy-done.25) | copy-start | bytes 9220
  1063.6 25.5 %copy-start.32 = (f32[200]{0:T(256)S(1)}, f32[200]{0:T(256)}, u32[]{:S(2)}) copy-start(f32[200]{0:T(256)} %copy-done.31) | copy-start | bytes 2404
  1063.6 25.5 %copy-start.36 = (f32[200]{0:T(256)S(1)}, f32[200]{0:T(256)}, u32[]{:S(2)}) copy-start(f32[200]{0:T(256)} %copy-done.35) | copy-start | bytes 2404
  1114.4 21.8 %all-to-all-start.6 = ((bf16[64,2,2304]{2,1,0:T(2,128)(2,1)}), bf16[64,2,2304]{2,1,0:T(2,128)(2,1)S(1)}, u32[]{:S(2)}, u32[]{:S(2)}) async-start(bf16[64,2,2304]{2,1,0:T(2,128)(2,1)} %reshape.419), calls=%async_computation.12 | async-start | bytes 1179648 | tf_op jit(solution)/shard_map/all_to_all | solution.py:285
  1136.1 18.3 %all-to-all-start.7 = ((bf16[64,2,2304]{2,1,0:T(2,128)(2,1)}), bf16[64,2,2304]{2,1,0:T(2,128)(2,1)S(1)}, u32[]{:S(2)}, u32[]{:S(2)}) async-start(bf16[64,2,2304]{2,1,0:T(2,128)(2,1)} %reshape.421), calls=%async_computation.13 | async-start | bytes 1179648 | tf_op jit(solution)/shard_map/all_to_all | solution.py:292
  1156.2 2.0 copy-start.14
  1156.2 1.9 copy-start.15
  (8 other events, 11.6 us)
Sparse Core Ops, SparseCore 0:
  12.7 108.7 all-gather.3
  176.5 34.4 reduce-scatter.6
  699.4 31.8 reduce-scatter.10
  733.5 25.6 reduce-scatter.8
  775.7 280.8 reduce-scatter.12
  1060.6 28.4 reduce-scatter.14
  1104.8 288.8 reduce-scatter.16

commit v4 on v2

--- a/solution.py
+++ b/solution.py
@@ -138,7 +138,10 @@
         ],
         axis=1,
     )
-    full = lax.all_gather(packed, "fsdp", axis=0, tiled=True)
+    holders = lax.axis_size("fsdp")
+    spread = jnp.broadcast_to(packed[None], (holders,) + packed.shape)
+    full = lax.all_to_all(spread, "fsdp", split_axis=0, concat_axis=0, tiled=True)
+    full = full.reshape(holders * rows, packed.shape[1])
     width = full.shape[0]
     at = 3 * heads_width
     qkv_full = jnp.transpose(full[:, :at].reshape(width, 3, heads_width), (1, 0, 2))
@@ -165,9 +168,10 @@
     )
     holders = lax.axis_size("fsdp")
     rows = width // holders
-    part = lax.psum_scatter(
-        packed.reshape(holders, rows, packed.shape[1]), "fsdp", scatter_dimension=0, tiled=True
-    ).reshape(rows, packed.shape[1])
+    moved = lax.all_to_all(
+        packed.reshape(holders, rows, packed.shape[1]), "fsdp", split_axis=0, concat_axis=0, tiled=True
+    )
+    part = jnp.sum(moved, axis=0)
     at = 3 * heads_width
     qkv_grad = jnp.transpose(part[:, :at].reshape(rows, 3, heads_width), (1, 0, 2))
     proj_grad = part[:, at : at + heads_width].T

time: 1170 us -> 944 us (0.81)
  waiting for transfers between devices: 611 us -> 364 us
  starting transfers between devices: 84.3 us -> 108 us
    reduce_scatter x1 -> x0, waiting for transfers between devices: 238 us -> none  [reduce_dense(): lax.psum_scatter(packed.reshape(holders, rows, packed.shape[1]), 'fsdp',...]
    all_to_all x0 -> x2, waiting for transfers between devices: none -> 118 us  [the longest x1 75.3 us: reduce_dense(): lax.all_to_all(packed.reshape(holders, rows, packed.shape[1]), 'fsdp', sp...]
    all_gather x1 -> x0, waiting for transfers between devices: 106 us -> none  [gather_dense(): full = lax.all_gather(packed, 'fsdp', axis=0, tiled=True)]
    all_to_all x0 -> x2, starting transfers between devices: none -> 20.1 us  [the longest x1 10.6 us: gather_dense(): lax.all_to_all(spread, 'fsdp', split_axis=0, concat_axis=0, tiled=True)]
  transfers between devices with their start and end apart: 14 -> 14, of which waited for: 12 -> 10; matrix products, arithmetic and copies ran while one was open for 14% -> 19% of each run, Pallas kernels for 0% -> 0%
where the time goes in v4:
time: 944 us; the launch traced here: 927 us
  waiting for transfers between devices  364 us (39%)
  local copies, waits for them, and re-layouts  189 us (20%)
  starting transfers between devices  108 us (11%)
  blocking collectives  103 us (11%)
  matrix products  97.9 us (10%)
  other arithmetic  49 us (5%)
  between operations  15.2 us (2%)
    all_to_all x2, waiting for transfers between devices, to_groups(): lax.all_to_all(pieces, 'fsdp', split_axis=0, concat_axis=0, tiled=True)  111 us
    all_gather x4, blocking collectives, group_rows(): return lax.all_gather(value, 'tp', axis=0, tiled=True)  97.9 us
    all_to_all x1, waiting for transfers between devices, reduce_dense(): lax.all_to_all(packed.reshape(holders, rows, packed.shape[1]), 'fsdp', sp...  75.3 us
    all_to_all x2, waiting for transfers between devices, to_owners(): lax.all_to_all(spread, 'fsdp', split_axis=0, concat_axis=0, tiled=True)  68.9 us
    reduce_scatter x4, waiting for transfers between devices, owned_rows(): return lax.psum_scatter(value, 'tp', scatter_dimension=0, tiled=True)  64.5 us
    all_to_all x1, waiting for transfers between devices, gather_dense(): lax.all_to_all(spread, 'fsdp', split_axis=0, concat_axis=0, tiled=True)  42.6 us
    all_to_all x2, starting transfers between devices, to_owners(): lax.all_to_all(spread, 'fsdp', split_axis=0, concat_axis=0, tiled=True)  33 us
    all_to_all x2, starting transfers between devices, to_groups(): lax.all_to_all(pieces, 'fsdp', split_axis=0, concat_axis=0, tiled=True)  22.5 us
  transfers between devices with their start and end apart: 14, of which 10 were waited for; matrix products, arithmetic and copies ran while one was open for 19% of the time, Pallas kernels for 0%

profile of v4, /device:TPU:1, one launch (start us, length us, event | category | flops | bytes accessed | tf_op | source)
XLA Modules:
  0.0 926.6 jit_solution(648911887123592722)
XLA Ops:
  13.8 10.6 %all-to-all-start = ((bf16[64,12,1556]{2,1,0:T(8,128)(2,1)}), bf16[64,12,1556]{2,1,0:T(8,128)(2,1)}, u32[]{:S(2)}, u32[]{:S(2)}) async-start(bf16[64,12,1556]{2,1,0:T(8,128)(2,1)} %broadcast_in_dim.58), calls=%async_computation | async-start | bytes 6815744 | tf_op jit(solution)/shard_map/all_to_all | solution.py:143
  25.0 42.6 %all-to-all-done = bf16[64,12,1556]{2,1,0:T(8,128)(2,1)} async-done(((bf16[64,12,1556]{2,1,0:T(8,128)(2,1)}), bf16[64,12,1556]{2,1,0:T(8,128)(2,1)}, u32[]{:S(2)}, u32[]{:S(2)}) %all-to-all-start) | async-done | bytes 2390048 | tf_op jit(solution)/shard_map/all_to_all | solution.py:143
  74.0 11.8 %all_gather.12 = bf16[400,768]{1,0:T(8,128)(2,1)} all-gather(bf16[200,768]{1,0:T(8,128)(2,1)S(1)} %add_convert_fusion.2), channel_id=1, replica_groups=mesh['fsdp'=64,'tp'=2] {'tp'}, dimensions={0}, use_global_device_ids=true | all-gather | bytes 921600 | tf_op jit(solution)/shard_map/all_gather | solution.py:186
  112.7 4.4 fusion.50
  126.6 7.2 all-to-all-start.2
  137.0 5.3 scatter_custom_fusion.1
  142.2 5.3 scatter_custom_fusion
  149.3 10.0 %reduce-scatter.5.cloned.1.call-done = f32[200,768]{1,0:T(8,128)} async-done(((f32[400,768]{1,0:T(8,128)}), f32[200,768]{1,0:T(8,128)}) %reduce-scatter.5.cloned.1.call-update) | async-done | bytes 614416 | tf_op jit(solution)/shard_map/reduce_scatter | solution.py:190
  160.7 8.2 all-to-all-start.3
  169.1 19.0 %all_gather.13 = bf16[400,768]{1,0:T(8,128)(2,1)S(1)} all-gather(bf16[200,768]{1,0:T(8,128)(2,1)S(1)} %add_convert_fusion.1), channel_id=1, replica_groups=mesh['fsdp'=64,'tp'=2] {'tp'}, dimensions={0}, use_global_device_ids=true | all-gather | bytes 921600 | tf_op jit(solution)/shard_map/all_gather | solution.py:186
  188.1 5.2 gather_fusion
  196.3 4.8 broadcast_in_dim.66
  201.1 6.9 all-to-all-start.1
  208.1 56.9 %all_gather.14 = bf16[400,768]{1,0:T(8,128)(2,1)S(1)} all-gather(bf16[200,768]{1,0:T(8,128)(2,1)S(1)} %convert_element_type.201), channel_id=1, replica_groups=mesh['fsdp'=64,'tp'=2] {'tp'}, dimensions={0}, use_global_device_ids=true | all-gather | bytes 921600 | tf_op jit(solution)/shard_map/all_gather | solution.py:186
  265.1 5.3 gather_fusion.2
  275.2 5.3 scatter_custom_fusion.2
  289.3 26.1 %all-to-all-start.5 = ((bf16[64,63,768]{2,1,0:T(8,128)(2,1)}), bf16[64,63,768]{2,1,0:T(8,128)(2,1)}, u32[]{:S(2)}, u32[]{:S(2)}) async-start(bf16[64,63,768]{2,1,0:T(8,128)(2,1)} %bitcast.137), calls=%async_computation.7 | async-start | bytes 12582912 | tf_op jit(solution)/shard_map/all_to_all | solution.py:198
  316.8 8.5 reshape.304
  325.3 8.7 fusion.114
  334.0 65.8 %all-to-all-done.5 = bf16[64,63,768]{2,1,0:T(8,128)(2,1)} async-done(((bf16[64,63,768]{2,1,0:T(8,128)(2,1)}), bf16[64,63,768]{2,1,0:T(8,128)(2,1)}, u32[]{:S(2)}, u32[]{:S(2)}) %all-to-all-start.5) | async-done | bytes 6193184 | tf_op jit(solution)/shard_map/all_to_all | solution.py:198
  399.8 8.3 reshape.314
  408.1 19.9 %add_convert_fusion = (bf16[4032,384]{1,0:T(8,128)(2,1)}, f32[4032,384]{1,0:T(8,128)S(1)}) fusion(f32[4032,384]{1,0:T(8,128)} %fusion.114, bf16[4032,768]{1,0:T(8,128)(2,1)} %reshape.314, bf16[768,384]{1,0:T(8,128)(2,1)S(1)} %reshape.308), kind=kOutput, calls=%fused_computation.15 | convolution fusion | flops 2489647104 | bytes 22265856 | tf_op jit(solution)/shard_map/dot_general | solution.py:291
  430.5 5.3 convolution_convert_fusion.1
  435.8 8.4 reshape.309
  444.2 11.5 %all-to-all-start.4 = ((bf16[64,63,768]{2,1,0:T(8,128)(2,1)}), bf16[64,63,768]{2,1,0:T(8,128)(2,1)}, u32[]{:S(2)}, u32[]{:S(2)}) async-start(bf16[64,63,768]{2,1,0:T(8,128)(2,1)} %reshape.309), calls=%async_computation.5 | async-start | bytes 12582912 | tf_op jit(solution)/shard_map/all_to_all | solution.py:205
  455.7 7.9 convolution_convert_fusion
  463.6 8.5 reshape.315
  472.1 61.4 %all-to-all-done.4 = bf16[64,63,768]{2,1,0:T(8,128)(2,1)} async-done(((bf16[64,63,768]{2,1,0:T(8,128)(2,1)}), bf16[64,63,768]{2,1,0:T(8,128)(2,1)}, u32[]{:S(2)}, u32[]{:S(2)}) %all-to-all-start.4) | async-done | bytes 6193184 | tf_op jit(solution)/shard_map/all_to_all | solution.py:205
  533.6 11.0 %all-to-all-start.6 = ((bf16[64,63,768]{2,1,0:T(8,128)(2,1)}), bf16[64,63,768]{2,1,0:T(8,128)(2,1)}, u32[]{:S(2)}, u32[]{:S(2)}) async-start(bf16[64,63,768]{2,1,0:T(8,128)(2,1)} %reshape.315), calls=%async_computation.8 | async-start | bytes 12582912 | tf_op jit(solution)/shard_map/all_to_all | solution.py:205
  544.7 5.9 convert_reduce_fusion.1
  554.2 6.6 gather_fusion.1
  564.9 8.1 multiply_reduce_fusion.1
  573.2 49.3 %all-to-all-done.6 = bf16[64,63,768]{2,1,0:T(8,128)(2,1)} async-done(((bf16[64,63,768]{2,1,0:T(8,128)(2,1)}), bf16[64,63,768]{2,1,0:T(8,128)(2,1)}, u32[]{:S(2)}, u32[]{:S(2)}) %all-to-all-start.6) | async-done | bytes 6193184 | tf_op jit(solution)/shard_map/all_to_all | solution.py:205
  622.5 5.9 convert_reduce_fusion
  648.7 27.9 %reduce-scatter.9.cloned.1.call-done = f32[200,768]{1,0:T(8,128)} async-done(((f32[400,768]{1,0:T(8,128)}), f32[200,768]{1,0:T(8,128)}) %reduce-scatter.9.cloned.1.call-update) | async-done | bytes 614416 | tf_op jit(solution)/shard_map/reduce_scatter | solution.py:190
  678.0 26.6 %reduce-scatter.7.cloned.1.call-done = f32[200,768]{1,0:T(8,128)} async-done(((f32[400,768]{1,0:T(8,128)}), f32[200,768]{1,0:T(8,128)}) %reduce-scatter.7.cloned.1.call-update) | async-done | bytes 614416 | tf_op jit(solution)/shard_map/reduce_scatter | solution.py:190
  707.2 10.3 %all_gather.15 = bf16[400,768]{1,0:T(8,128)(2,1)S(1)} all-gather(bf16[200,768]{1,0:T(8,128)(2,1)S(1)} %get-tuple-element.29), channel_id=1, replica_groups=mesh['fsdp'=64,'tp'=2] {'tp'}, dimensions={0}, use_global_device_ids=true | all-gather | bytes 921600 | tf_op jit(solution)/shard_map/all_gather | solution.py:186
  721.5 4.3 fusion.51
  744.0 6.4 fusion.38
  754.1 8.9 all-to-all-start.9
  763.0 7.2 fusion.37
  776.3 7.8 all-to-all-start.8
  789.9 4.6 copy.292
  794.5 7.5 concatenate.20
  805.4 8.3 concatenate.26
  813.7 9.4 %all-to-all-start.7 = ((f32[64,12,1556]{2,1,0:T(8,128)}), f32[64,12,1556]{2,1,0:T(8,128)}, u32[]{:S(2)}, u32[]{:S(2)}) async-start(f32[64,12,1556]{2,1,0:T(8,128)} %concatenate.26), calls=%async_computation.11 | async-start | bytes 13631488 | tf_op jit(solution)/shard_map/all_to_all | solution.py:171
  833.6 75.3 %all-to-all-done.7 = f32[64,12,1556]{2,1,0:T(8,128)} async-done(((f32[64,12,1556]{2,1,0:T(8,128)}), f32[64,12,1556]{2,1,0:T(8,128)}, u32[]{:S(2)}, u32[]{:S(2)}) %all-to-all-start.7) | async-done | bytes 4780064 | tf_op jit(solution)/shard_map/all_to_all | solution.py:171
  912.9 5.3 psum.7
  (245 shorter events, 165.6 us)
Async XLA Ops:
  13.8 10.7 %copy-start.2 = (f32[200,768]{1,0:T(8,128)S(1)}, f32[200,768]{1,0:T(8,128)}, u32[]{:S(2)}) copy-start(f32[200,768]{1,0:T(8,128)} %param.12) | copy-start | bytes 1843204
  13.8 53.7 %all-to-all-start = ((bf16[64,12,1556]{2,1,0:T(8,128)(2,1)}), bf16[64,12,1556]{2,1,0:T(8,128)(2,1)}, u32[]{:S(2)}, u32[]{:S(2)}) async-start(bf16[64,12,1556]{2,1,0:T(8,128)(2,1)} %broadcast_in_dim.58), calls=%async_computation | async-start | bytes 6815744 | tf_op jit(solution)/shard_map/all_to_all | solution.py:143
  24.5 134.7 %reduce-scatter.5.cloned.1.call-start = ((), (), s32[]{:S(2)}) async-start(), calls=%async_computation.14 | async-start | bytes 1843200 | tf_op jit(solution)/shard_map/reduce_scatter | solution.py:190
  24.7 88.0 %copy-start.42 = (pred[200]{0:T(512)(128)(4,1)}, pred[200]{0:T(512)(128)(4,1)S(1)}, u32[]{:S(2)}) copy-start(pred[200]{0:T(512)(128)(4,1)S(1)} %iota_compare_fusion.3) | copy-start | bytes 604
  24.7 49.1 %copy-start.34 = (f32[200]{0:T(256)}, f32[200]{0:T(256)S(1)}, u32[]{:S(2)}) copy-start(f32[200]{0:T(256)S(1)} %broadcast_multiply_fusion.6) | copy-start | bytes 2404
  24.9 48.8 %copy-start.38 = (f32[200]{0:T(256)}, f32[200]{0:T(256)S(1)}, u32[]{:S(2)}) copy-start(f32[200]{0:T(256)S(1)} %add_rsqrt_fusion.1) | copy-start | bytes 2404
  71.7 49.6 %copy-start.6 = (bf16[768,1556]{1,0:T(8,128)(2,1)}, bf16[768,1556]{1,0:T(8,128)(2,1)S(1)}, u32[]{:S(2)}) copy-start(bf16[768,1556]{1,0:T(8,128)(2,1)S(1)} %reshape.298) | copy-start | bytes 7170052
  72.2 96.7 %copy-start.31 = (f32[768]{0:T(1024)}, f32[768]{0:T(1024)S(1)}, u32[]{:S(2)}) copy-start(f32[768]{0:T(1024)S(1)} %get-tuple-element.11) | copy-start | bytes 9220
  123.8 10.0 %copy-start.33 = (s32[400,2]{0,1:T(2,128)S(1)}, s32[400,2]{0,1:T(2,128)}, u32[]{:S(2)}) copy-start(s32[400,2]{0,1:T(2,128)} %param.13) | copy-start | bytes 9604
  123.8 23.8 %copy-start.25 = (bf16[12,16,1536]{2,1,0:T(8,128)(2,1)S(1)}, bf16[12,16,1536]{2,1,0:T(8,128)(2,1)}, u32[]{:S(2)}) copy-start(bf16[12,16,1536]{2,1,0:T(8,128)(2,1)} %param.22) | copy-start | bytes 1769476
  126.6 34.1 %all-to-all-start.2 = ((bf16[12,64,384]{2,0,1:T(8,128)(2,1)}), bf16[12,64,384]{2,0,1:T(8,128)(2,1)S(1)}, u32[]{:S(2)}, u32[]{:S(2)}) async-start(bf16[12,64,384]{2,0,1:T(8,128)(2,1)} %copy.273), calls=%async_computation.3 | async-start | bytes 1572864 | tf_op jit(solution)/shard_map/all_to_all | solution.py:267
  160.4 32.9 %copy-start.4 = (f32[200,768]{1,0:T(8,128)}, f32[200,768]{1,0:T(8,128)S(1)}, u32[]{:S(2)}) copy-start(f32[200,768]{1,0:T(8,128)S(1)} %get-tuple-element.34) | copy-start | bytes 1843204
  160.5 32.8 %copy-start.36 = (f32[200]{0:T(256)}, f32[200]{0:T(256)S(1)}, u32[]{:S(2)}) copy-start(f32[200]{0:T(256)S(1)} %broadcast_multiply_fusion.5) | copy-start | bytes 2404
  160.7 32.6 %copy-start.40 = (f32[200]{0:T(256)}, f32[200]{0:T(256)S(1)}, u32[]{:S(2)}) copy-start(f32[200]{0:T(256)S(1)} %add_rsqrt_fusion) | copy-start | bytes 2404
  160.7 8.2 copy-start.9
  160.7 35.6 %all-to-all-start.3 = ((bf16[12,64,384]{2,0,1:T(8,128)(2,1)}), bf16[12,64,384]{2,0,1:T(8,128)(2,1)}, u32[]{:S(2)}, u32[]{:S(2)}) async-start(bf16[12,64,384]{2,0,1:T(8,128)(2,1)} %copy.274), calls=%async_computation.4 | async-start | bytes 1572864 | tf_op jit(solution)/shard_map/all_to_all | solution.py:268
  188.1 85.5 %copy-start = (bf16[400,768]{1,0:T(8,128)(2,1)}, bf16[400,768]{1,0:T(8,128)(2,1)S(1)}, u32[]{:S(2)}) copy-start(bf16[400,768]{1,0:T(8,128)(2,1)S(1)} %all_gather.13) | copy-start | bytes 1843204
  201.1 6.9 copy-start.13
  201.1 84.8 %all-to-all-start.1 = ((bf16[64,63,768]{2,1,0:T(8,128)(2,1)}), bf16[64,63,768]{2,1,0:T(8,128)(2,1)}, u32[]{:S(2)}, u32[]{:S(2)}) async-start(bf16[64,63,768]{2,1,0:T(8,128)(2,1)} %bitcast.136), calls=%async_computation.2 | async-start | bytes 12582912 | tf_op jit(solution)/shard_map/all_to_all | solution.py:198
  289.3 26.1 %copy-start.10 = (bf16[12,64,384]{2,0,1:T(8,128)(2,1)S(1)}, bf16[12,64,384]{2,0,1:T(8,128)(2,1)}, u32[]{:S(2)}) copy-start(bf16[12,64,384]{2,0,1:T(8,128)(2,1)} %copy-done.9) | copy-start | bytes 1769476
  289.3 110.5 %all-to-all-start.5 = ((bf16[64,63,768]{2,1,0:T(8,128)(2,1)}), bf16[64,63,768]{2,1,0:T(8,128)(2,1)}, u32[]{:S(2)}, u32[]{:S(2)}) async-start(bf16[64,63,768]{2,1,0:T(8,128)(2,1)} %bitcast.137), calls=%async_computation.7 | async-start | bytes 12582912 | tf_op jit(solution)/shard_map/all_to_all | solution.py:198
  408.1 19.9 %copy-start.7 = (f32[4032,384]{1,0:T(8,128)S(1)}, f32[4032,384]{1,0:T(8,128)}, u32[]{:S(2)}) copy-start(f32[4032,384]{1,0:T(8,128)} %fusion.114) | copy-start | bytes 18579460
  444.2 89.3 %all-to-all-start.4 = ((bf16[64,63,768]{2,1,0:T(8,128)(2,1)}), bf16[64,63,768]{2,1,0:T(8,128)(2,1)}, u32[]{:S(2)}, u32[]{:S(2)}) async-start(bf16[64,63,768]{2,1,0:T(8,128)(2,1)} %reshape.309), calls=%async_computation.5 | async-start | bytes 12582912 | tf_op jit(solution)/shard_map/all_to_all | solution.py:205
  533.6 88.9 %all-to-all-start.6 = ((bf16[64,63,768]{2,1,0:T(8,128)(2,1)}), bf16[64,63,768]{2,1,0:T(8,128)(2,1)}, u32[]{:S(2)}, u32[]{:S(2)}) async-start(bf16[64,63,768]{2,1,0:T(8,128)(2,1)} %reshape.315), calls=%async_computation.8 | async-start | bytes 12582912 | tf_op jit(solution)/shard_map/all_to_all | solution.py:205
  544.6 132.0 %reduce-scatter.9.cloned.1.call-start = ((), (), s32[]{:S(2)}) async-start(), calls=%async_computation.16 | async-start | bytes 1843200 | tf_op jit(solution)/shard_map/reduce_scatter | solution.py:190
  641.6 4.2 copy-start.22
  641.6 4.2 copy-start.23
  641.6 4.3 copy-start.43
  644.9 59.8 %reduce-scatter.7.cloned.1.call-start = ((), (), s32[]{:S(2)}) async-start(), calls=%async_computation.15 | async-start | bytes 1843200 | tf_op jit(solution)/shard_map/reduce_scatter | solution.py:190
  645.6 31.0 %copy-start.5 = (f32[200,768]{1,0:T(8,128)S(1)}, f32[200,768]{1,0:T(8,128)}, u32[]{:S(2)}) copy-start(f32[200,768]{1,0:T(8,128)} %copy-done.4) | copy-start | bytes 1843204
  645.6 31.0 %copy-start.32 = (f32[768]{0:T(1024)S(1)}, f32[768]{0:T(1024)}, u32[]{:S(2)}) copy-start(f32[768]{0:T(1024)} %copy-done.31) | copy-start | bytes 9220
  645.6 31.0 %copy-start.37 = (f32[200]{0:T(256)S(1)}, f32[200]{0:T(256)}, u32[]{:S(2)}) copy-start(f32[200]{0:T(256)} %copy-done.36) | copy-start | bytes 2404
  645.6 31.0 %copy-start.41 = (f32[200]{0:T(256)S(1)}, f32[200]{0:T(256)}, u32[]{:S(2)}) copy-start(f32[200]{0:T(256)} %copy-done.40) | copy-start | bytes 2404
  645.6 59.0 %copy-start.14 = (f32[200,768]{1,0:T(8,128)S(1)}, f32[200,768]{1,0:T(8,128)}, u32[]{:S(2)}) copy-start(f32[200,768]{1,0:T(8,128)} %param.23) | copy-start | bytes 1843204
  645.6 156.3 %reduce-scatter.11.cloned.1.call-start = ((), (), s32[]{:S(2)}) async-start(), calls=%async_computation.17 | async-start | bytes 1843200 | tf_op jit(solution)/shard_map/reduce_scatter | solution.py:190
  731.4 4.0 copy-start.27
  740.3 3.7 copy-start.12
  754.1 22.2 %all-to-all-start.9 = ((bf16[64,2,2304]{2,1,0:T(2,128)(2,1)}), bf16[64,2,2304]{2,1,0:T(2,128)(2,1)S(1)}, u32[]{:S(2)}, u32[]{:S(2)}) async-start(bf16[64,2,2304]{2,1,0:T(2,128)(2,1)} %reshape.417), calls=%async_computation.13 | async-start | bytes 1179648 | tf_op jit(solution)/shard_map/all_to_all | solution.py:305
  763.0 9.4 %copy-start.1 = (bf16[400,768]{1,0:T(8,128)(2,1)S(1)}, bf16[400,768]{1,0:T(8,128)(2,1)}, u32[]{:S(2)}) copy-start(bf16[400,768]{1,0:T(8,128)(2,1)} %copy-done) | copy-start | bytes 1843204
  770.2 4.4 copy-start.16
  772.7 11.4 %copy-start.8 = (bf16[400,384]{0,1:T(8,128)(2,1)S(1)}, bf16[400,384]{0,1:T(8,128)(2,1)}, u32[]{:S(2)}) copy-start(bf16[400,384]{0,1:T(8,128)(2,1)} %reshape.300) | copy-start | bytes 921604
  776.3 37.4 %all-to-all-start.8 = ((bf16[64,2,2304]{2,1,0:T(2,128)(2,1)}), bf16[64,2,2304]{2,1,0:T(2,128)(2,1)}, u32[]{:S(2)}, u32[]{:S(2)}) async-start(bf16[64,2,2304]{2,1,0:T(2,128)(2,1)} %reshape.415), calls=%async_computation.12 | async-start | bytes 1179648 | tf_op jit(solution)/shard_map/all_to_all | solution.py:298
  794.4 7.5 copy-start.3
  794.5 7.5 copy-start.30
  794.5 7.5 copy-start.35
  794.5 7.5 copy-start.39
  794.5 11.0 %copy-start.20 = (f32[64,12,16]{2,1,0:T(8,128)S(1)}, f32[64,12,16]{2,1,0:T(8,128)}, u32[]{:S(2)}) copy-start(f32[64,12,16]{2,1,0:T(8,128)} %copy.297) | copy-start | bytes 147460
  813.7 95.2 %all-to-all-start.7 = ((f32[64,12,1556]{2,1,0:T(8,128)}), f32[64,12,1556]{2,1,0:T(8,128)}, u32[]{:S(2)}, u32[]{:S(2)}) async-start(f32[64,12,1556]{2,1,0:T(8,128)} %concatenate.26), calls=%async_computation.11 | async-start | bytes 13631488 | tf_op jit(solution)/shard_map/all_to_all | solution.py:171
  (10 other events, 18.4 us)
Sparse Core Ops, SparseCore 0:
  124.0 35.1 reduce-scatter.4
  645.0 31.5 reduce-scatter.8
  679.0 25.6 reduce-scatter.6
  744.1 32.7 reduce-scatter.10

commit v5 on v4

--- a/solution.py
+++ b/solution.py
@@ -2,6 +2,48 @@
 import jax.numpy as jnp
 from jax import lax
 from jax.sharding import PartitionSpec as P
+from jax.experimental import pallas as pl
+from jax.experimental.pallas import tpu as pltpu
+
+MESH_IDS = pl.DeviceIdType.MESH
+
+
+def _swap_kernel(x_ref, out_ref, held, send_sem, recv_sem):
+    me = lax.axis_index("tp")
+    other = 1 - me
+    peer = (lax.axis_index("fsdp"), other)
+    barrier = pltpu.get_barrier_semaphore()
+    pl.semaphore_signal(barrier, inc=1, device_id=peer, device_id_type=MESH_IDS)
+    pl.semaphore_wait(barrier, 1)
+    copy = pltpu.make_async_remote_copy(
+        src_ref=x_ref,
+        dst_ref=held,
+        send_sem=send_sem,
+        recv_sem=recv_sem,
+        device_id=peer,
+        device_id_type=MESH_IDS,
+    )
+    copy.start()
+    out_ref[me] = x_ref[...]
+    copy.wait()
+    out_ref[other] = held[...]
+
+
+def tp_swap(x, call_id):
+    rows, width = x.shape
+    out = pl.pallas_call(
+        _swap_kernel,
+        out_shape=jax.ShapeDtypeStruct((2, rows, width), x.dtype),
+        in_specs=[pl.BlockSpec(memory_space=pltpu.VMEM)],
+        out_specs=pl.BlockSpec(memory_space=pltpu.VMEM),
+        scratch_shapes=[
+            pltpu.VMEM((rows, width), x.dtype),
+            pltpu.SemaphoreType.DMA(()),
+            pltpu.SemaphoreType.DMA(()),
+        ],
+        compiler_params=pltpu.CompilerParams(collective_id=call_id, has_side_effects=True),
+    )(x)
+    return out.reshape(2 * rows, width)
 
 HEAD_DIM = 64
 SEQ = 200
@@ -182,8 +224,8 @@
     return qkv_grad, proj_grad, router_grad, norm_grads
 
 
-def group_rows(value):
-    return lax.all_gather(value, "tp", axis=0, tiled=True)
+def group_rows(value, call_id):
+    return tp_swap(value, call_id)
 
 
 def owned_rows(value):
@@ -245,14 +287,14 @@
     attention_normed, attention_standardized, attention_inverse_deviation = normalize_rows(
         inputs, attention_gain, attention_shift
     )
-    tokens_a = group_rows(attention_normed)
+    tokens_a = group_rows(attention_normed, 0)
     proj = jnp.einsum("td,idh->ith", tokens_a, qkv_full, preferred_element_type=f32).astype(bf16)
     context, lse = attend(proj[0], proj[1], proj[2], images)
     residual_middle = inputs + owned_rows(jnp.dot(context, proj_full, preferred_element_type=f32))
     expert_normed, expert_standardized, expert_inverse_deviation = normalize_rows(
         residual_middle, expert_gain, expert_shift
     )
-    tokens_m = group_rows(expert_normed)
+    tokens_m = group_rows(expert_normed, 1)
     logits = jnp.dot(tokens_m, router_full, preferred_element_type=f32)
     raised = jnp.exp(logits)
     probs = raised / jnp.sum(raised, axis=-1, keepdims=True)
@@ -278,7 +320,7 @@
     outputs = residual_middle + owned_rows(jnp.sum(gates[:, :, None] * routed, axis=1))
     qkv_back, proj_back, router_back = qkv_full, proj_full, router_full
     attention_gain_gradient, expert_gain_gradient = attention_gain, expert_gain
-    dout = group_rows(cotangent.astype(bf16))
+    dout = group_rows(cotangent.astype(bf16), 2)
     dout_f = dout.astype(f32)
     gate_of_slot = jnp.zeros((experts * CAP,), f32).at[slot].set(gates.reshape(-1))
     slot_grad = (
@@ -326,7 +368,7 @@
         expert_gain_gradient,
     )
     middle_grad = cotangent + expert_norm_backward
-    mid_rows = group_rows(middle_grad.astype(bf16))
+    mid_rows = group_rows(middle_grad.astype(bf16), 3)
     proj_part = jnp.einsum("th,td->hd", context, mid_rows, preferred_element_type=f32)
     context_grad = jnp.einsum("td,hd->th", mid_rows, proj_back, preferred_element_type=f32).astype(
         bf16

time: 944 us -> 955 us (1.012)
  Pallas kernels: 0 us -> 101 us
  blocking collectives: 103 us -> 5.32 us
    pallas_call x0 -> x4, Pallas kernels: none -> 101 us  [tp_swap(): pl.pallas_call(_swap_kernel, out_shape=jax.ShapeDtypeStruct((2, rows, wid...]
    all_gather x4 -> x0, blocking collectives: 97.9 us -> none  [group_rows(): return lax.all_gather(value, 'tp', axis=0, tiled=True)]
    concatenate x8 -> x10, local copies, waits for them, and re-layouts: 21.6 us -> 18.7 us  [reduce_dense(): jnp.concatenate([jnp.transpose(qkv_part, (1, 0, 2)).reshape(width, -1), p...]
  transfers between devices with their start and end apart: 14 -> 14, of which waited for: 10 -> 10; matrix products, arithmetic and copies ran while one was open for 19% -> 20% of each run, Pallas kernels for 0% -> 8%
where the time goes in v5:
time: 955 us; the launch traced here: 937 us
  waiting for transfers between devices  357 us (37%)
  local copies, waits for them, and re-layouts  192 us (20%)
  starting transfers between devices  110 us (12%)
  matrix products  105 us (11%)
  Pallas kernels  101 us (11%)
  other arithmetic  51.9 us (5%)
  between operations  15.3 us (2%)
    all_to_all x2, waiting for transfers between devices, to_groups(): lax.all_to_all(pieces, 'fsdp', split_axis=0, concat_axis=0, tiled=True)  111 us
    pallas_call x4, Pallas kernels, tp_swap(): pl.pallas_call(_swap_kernel, out_shape=jax.ShapeDtypeStruct((2, rows, wid...  101 us
    all_to_all x1, waiting for transfers between devices, reduce_dense(): lax.all_to_all(packed.reshape(holders, rows, packed.shape[1]), 'fsdp', sp...  72 us
    all_to_all x2, waiting for transfers between devices, to_owners(): lax.all_to_all(spread, 'fsdp', split_axis=0, concat_axis=0, tiled=True)  66.7 us
    reduce_scatter x4, waiting for transfers between devices, owned_rows(): return lax.psum_scatter(value, 'tp', scatter_dimension=0, tiled=True)  63 us
    all_to_all x1, waiting for transfers between devices, gather_dense(): lax.all_to_all(spread, 'fsdp', split_axis=0, concat_axis=0, tiled=True)  42.6 us
    all_to_all x2, starting transfers between devices, to_owners(): lax.all_to_all(spread, 'fsdp', split_axis=0, concat_axis=0, tiled=True)  34.9 us
    all_to_all x2, starting transfers between devices, to_groups(): lax.all_to_all(pieces, 'fsdp', split_axis=0, concat_axis=0, tiled=True)  22.2 us
  transfers between devices with their start and end apart: 14, of which 10 were waited for; matrix products, arithmetic and copies ran while one was open for 20% of the time, Pallas kernels for 8%

profile of v5, /device:TPU:1, one launch (start us, length us, event | category | flops | bytes accessed | tf_op | source)
XLA Modules:
  0.0 937.3 jit_solution(7276186463530998134)
XLA Ops:
  13.8 10.6 %all-to-all-start = ((bf16[64,12,1556]{2,1,0:T(8,128)(2,1)}), bf16[64,12,1556]{2,1,0:T(8,128)(2,1)}, u32[]{:S(2)}, u32[]{:S(2)}) async-start(bf16[64,12,1556]{2,1,0:T(8,128)(2,1)} %broadcast_in_dim.58), calls=%async_computation | async-start | bytes 6815744 | tf_op jit(solution)/shard_map/all_to_all | solution.py:185
  25.0 42.6 %all-to-all-done = bf16[64,12,1556]{2,1,0:T(8,128)(2,1)} async-done(((bf16[64,12,1556]{2,1,0:T(8,128)(2,1)}), bf16[64,12,1556]{2,1,0:T(8,128)(2,1)}, u32[]{:S(2)}, u32[]{:S(2)}) %all-to-all-start) | async-done | bytes 2390048 | tf_op jit(solution)/shard_map/all_to_all | solution.py:185
  74.7 12.9 %shard_map.203 = bf16[2,200,768]{2,1,0:T(8,128)(2,1)} custom-call(bf16[200,768]{1,0:T(8,128)(2,1)} %add_convert_fusion.2.x_ref), custom_call_target="tpu_custom_call" | custom-call | tf_op jit(solution)/shard_map/pallas_call | solution.py:34
  128.4 7.2 all-to-all-start.2
  138.7 5.3 scatter_custom_fusion.1
  144.0 5.3 scatter_custom_fusion
  151.0 9.9 %reduce-scatter.5.cloned.1.call-done = f32[200,768]{1,0:T(8,128)} async-done(((f32[400,768]{1,0:T(8,128)}), f32[200,768]{1,0:T(8,128)}) %reduce-scatter.5.cloned.1.call-update) | async-done | bytes 614416 | tf_op jit(solution)/shard_map/reduce_scatter | solution.py:232
  162.5 8.2 all-to-all-start.3
  171.6 19.3 %shard_map.204 = bf16[2,200,768]{2,1,0:T(8,128)(2,1)} custom-call(bf16[200,768]{1,0:T(8,128)(2,1)} %add_convert_fusion.1.x_ref), custom_call_target="tpu_custom_call" | custom-call | tf_op jit(solution)/shard_map/pallas_call | solution.py:34
  190.9 6.7 gather_fusion
  200.6 4.8 broadcast_in_dim.66
  205.5 6.7 all-to-all-start.1
  212.9 57.0 %shard_map.205 = bf16[2,200,768]{2,1,0:T(8,128)(2,1)} custom-call(bf16[200,768]{1,0:T(8,128)(2,1)} %convert_element_type.208.x_ref), custom_call_target="tpu_custom_call" | custom-call | tf_op jit(solution)/shard_map/pallas_call | solution.py:34
  271.1 5.3 gather_fusion.2
  281.4 5.3 scatter_custom_fusion.2
  293.4 28.1 %all-to-all-start.5 = ((bf16[64,63,768]{2,1,0:T(8,128)(2,1)}), bf16[64,63,768]{2,1,0:T(8,128)(2,1)}, u32[]{:S(2)}, u32[]{:S(2)}) async-start(bf16[64,63,768]{2,1,0:T(8,128)(2,1)} %bitcast.146), calls=%async_computation.7 | async-start | bytes 12582912 | tf_op jit(solution)/shard_map/all_to_all | solution.py:240
  323.0 8.5 reshape.324
  331.4 8.7 fusion.115
  340.2 65.7 %all-to-all-done.5 = bf16[64,63,768]{2,1,0:T(8,128)(2,1)} async-done(((bf16[64,63,768]{2,1,0:T(8,128)(2,1)}), bf16[64,63,768]{2,1,0:T(8,128)(2,1)}, u32[]{:S(2)}, u32[]{:S(2)}) %all-to-all-start.5) | async-done | bytes 6193184 | tf_op jit(solution)/shard_map/all_to_all | solution.py:240
  405.8 8.3 reshape.334
  414.1 19.9 %add_convert_fusion = (bf16[4032,384]{1,0:T(8,128)(2,1)}, f32[4032,384]{1,0:T(8,128)S(1)}) fusion(f32[4032,384]{1,0:T(8,128)} %fusion.115, bf16[4032,768]{1,0:T(8,128)(2,1)} %reshape.334, bf16[768,384]{1,0:T(8,128)(2,1)S(1)} %reshape.328), kind=kOutput, calls=%fused_computation.15 | convolution fusion | flops 2489647104 | bytes 22265856 | tf_op jit(solution)/shard_map/dot_general | solution.py:333
  436.5 5.3 convolution_convert_fusion.1
  441.8 8.4 reshape.329
  450.2 11.1 %all-to-all-start.4 = ((bf16[64,63,768]{2,1,0:T(8,128)(2,1)}), bf16[64,63,768]{2,1,0:T(8,128)(2,1)}, u32[]{:S(2)}, u32[]{:S(2)}) async-start(bf16[64,63,768]{2,1,0:T(8,128)(2,1)} %reshape.329), calls=%async_computation.5 | async-start | bytes 12582912 | tf_op jit(solution)/shard_map/all_to_all | solution.py:247
  461.4 8.0 convolution_convert_fusion
  469.3 8.5 reshape.335
  477.8 61.4 %all-to-all-done.4 = bf16[64,63,768]{2,1,0:T(8,128)(2,1)} async-done(((bf16[64,63,768]{2,1,0:T(8,128)(2,1)}), bf16[64,63,768]{2,1,0:T(8,128)(2,1)}, u32[]{:S(2)}, u32[]{:S(2)}) %all-to-all-start.4) | async-done | bytes 6193184 | tf_op jit(solution)/shard_map/all_to_all | solution.py:247
  539.2 11.0 %all-to-all-start.6 = ((bf16[64,63,768]{2,1,0:T(8,128)(2,1)}), bf16[64,63,768]{2,1,0:T(8,128)(2,1)}, u32[]{:S(2)}, u32[]{:S(2)}) async-start(bf16[64,63,768]{2,1,0:T(8,128)(2,1)} %reshape.335), calls=%async_computation.8 | async-start | bytes 12582912 | tf_op jit(solution)/shard_map/all_to_all | solution.py:247
  550.3 5.9 convert_reduce_fusion.1
  559.9 6.6 gather_fusion.1
  570.6 8.1 multiply_reduce_fusion.1
  578.9 49.3 %all-to-all-done.6 = bf16[64,63,768]{2,1,0:T(8,128)(2,1)} async-done(((bf16[64,63,768]{2,1,0:T(8,128)(2,1)}), bf16[64,63,768]{2,1,0:T(8,128)(2,1)}, u32[]{:S(2)}, u32[]{:S(2)}) %all-to-all-start.6) | async-done | bytes 6193184 | tf_op jit(solution)/shard_map/all_to_all | solution.py:247
  628.1 5.9 convert_reduce_fusion
  637.3 6.3 gather_fusion.3
  659.4 26.4 %reduce-scatter.9.cloned.1.call-done = f32[200,768]{1,0:T(8,128)} async-done(((f32[400,768]{1,0:T(8,128)}), f32[200,768]{1,0:T(8,128)}) %reduce-scatter.9.cloned.1.call-update) | async-done | bytes 614416 | tf_op jit(solution)/shard_map/reduce_scatter | solution.py:232
  687.3 26.6 %reduce-scatter.7.cloned.1.call-done = f32[200,768]{1,0:T(8,128)} async-done(((f32[400,768]{1,0:T(8,128)}), f32[200,768]{1,0:T(8,128)}) %reduce-scatter.7.cloned.1.call-update) | async-done | bytes 614416 | tf_op jit(solution)/shard_map/reduce_scatter | solution.py:232
  716.8 11.5 %shard_map.206 = bf16[2,200,768]{2,1,0:T(8,128)(2,1)} custom-call(bf16[200,768]{1,0:T(8,128)(2,1)} %get-tuple-element.29.x_ref), custom_call_target="tpu_custom_call" | custom-call | tf_op jit(solution)/shard_map/pallas_call | solution.py:34
  737.1 5.4 fusion.52
  755.6 7.3 fusion.38
  765.5 9.1 all-to-all-start.9
  774.6 7.2 fusion.37
  787.8 8.3 all-to-all-start.8
  802.1 4.8 fusion.62
  809.8 6.2 concatenate.20
  816.0 8.3 copy.318
  824.3 9.5 %all-to-all-start.7 = ((f32[64,12,1556]{2,1,0:T(8,128)}), f32[64,12,1556]{2,1,0:T(8,128)}, u32[]{:S(2)}, u32[]{:S(2)}) async-start(f32[64,12,1556]{2,1,0:T(8,128)} %copy.318), calls=%async_computation.11 | async-start | bytes 13631488 | tf_op jit(solution)/shard_map/all_to_all | solution.py:213
  847.6 72.0 %all-to-all-done.7 = f32[64,12,1556]{2,1,0:T(8,128)} async-done(((f32[64,12,1556]{2,1,0:T(8,128)}), f32[64,12,1556]{2,1,0:T(8,128)}, u32[]{:S(2)}, u32[]{:S(2)}) %all-to-all-start.7) | async-done | bytes 4780064 | tf_op jit(solution)/shard_map/all_to_all | solution.py:213
  924.2 5.3 psum.7
  (247 shorter events, 172.0 us)
Async XLA Ops:
  13.8 10.7 %copy-start.1 = (f32[200,768]{1,0:T(8,128)S(1)}, f32[200,768]{1,0:T(8,128)}, u32[]{:S(2)}) copy-start(f32[200,768]{1,0:T(8,128)} %param.12) | copy-start | bytes 1843204
  13.8 53.7 %all-to-all-start = ((bf16[64,12,1556]{2,1,0:T(8,128)(2,1)}), bf16[64,12,1556]{2,1,0:T(8,128)(2,1)}, u32[]{:S(2)}, u32[]{:S(2)}) async-start(bf16[64,12,1556]{2,1,0:T(8,128)(2,1)} %broadcast_in_dim.58), calls=%async_computation | async-start | bytes 6815744 | tf_op jit(solution)/shard_map/all_to_all | solution.py:185
  24.5 136.5 %reduce-scatter.5.cloned.1.call-start = ((), (), s32[]{:S(2)}) async-start(), calls=%async_computation.14 | async-start | bytes 1843200 | tf_op jit(solution)/shard_map/reduce_scatter | solution.py:232
  24.7 89.8 %copy-start.40 = (pred[200]{0:T(512)(128)(4,1)}, pred[200]{0:T(512)(128)(4,1)S(1)}, u32[]{:S(2)}) copy-start(pred[200]{0:T(512)(128)(4,1)S(1)} %iota_compare_fusion.3) | copy-start | bytes 604
  24.7 49.1 %copy-start.32 = (f32[200]{0:T(256)}, f32[200]{0:T(256)S(1)}, u32[]{:S(2)}) copy-start(f32[200]{0:T(256)S(1)} %broadcast_multiply_fusion.6) | copy-start | bytes 2404
  24.9 48.8 %copy-start.36 = (f32[200]{0:T(256)}, f32[200]{0:T(256)S(1)}, u32[]{:S(2)}) copy-start(f32[200]{0:T(256)S(1)} %add_rsqrt_fusion.1) | copy-start | bytes 2404
  71.7 51.4 %copy-start.5 = (bf16[768,1556]{1,0:T(8,128)(2,1)}, bf16[768,1556]{1,0:T(8,128)(2,1)S(1)}, u32[]{:S(2)}) copy-start(bf16[768,1556]{1,0:T(8,128)(2,1)S(1)} %reshape.316) | copy-start | bytes 7170052
  72.2 98.4 %copy-start.29 = (f32[768]{0:T(1024)}, f32[768]{0:T(1024)S(1)}, u32[]{:S(2)}) copy-start(f32[768]{0:T(1024)S(1)} %get-tuple-element.11) | copy-start | bytes 9220
  125.6 10.0 %copy-start.31 = (s32[400,2]{0,1:T(2,128)S(1)}, s32[400,2]{0,1:T(2,128)}, u32[]{:S(2)}) copy-start(s32[400,2]{0,1:T(2,128)} %param.13) | copy-start | bytes 9604
  125.6 23.8 %copy-start.24 = (bf16[12,16,1536]{2,1,0:T(8,128)(2,1)S(1)}, bf16[12,16,1536]{2,1,0:T(8,128)(2,1)}, u32[]{:S(2)}) copy-start(bf16[12,16,1536]{2,1,0:T(8,128)(2,1)} %param.22) | copy-start | bytes 1769476
  128.4 34.0 %all-to-all-start.2 = ((bf16[12,64,384]{2,0,1:T(8,128)(2,1)}), bf16[12,64,384]{2,0,1:T(8,128)(2,1)S(1)}, u32[]{:S(2)}, u32[]{:S(2)}) async-start(bf16[12,64,384]{2,0,1:T(8,128)(2,1)} %copy.286), calls=%async_computation.3 | async-start | bytes 1572864 | tf_op jit(solution)/shard_map/all_to_all | solution.py:309
  162.2 35.4 %copy-start.3 = (f32[200,768]{1,0:T(8,128)}, f32[200,768]{1,0:T(8,128)S(1)}, u32[]{:S(2)}) copy-start(f32[200,768]{1,0:T(8,128)S(1)} %get-tuple-element.34) | copy-start | bytes 1843204
  162.2 35.4 %copy-start.34 = (f32[200]{0:T(256)}, f32[200]{0:T(256)S(1)}, u32[]{:S(2)}) copy-start(f32[200]{0:T(256)S(1)} %broadcast_multiply_fusion.5) | copy-start | bytes 2404
  162.4 28.5 %copy-start.8 = (bf16[12,64,384]{2,0,1:T(8,128)(2,1)}, bf16[12,64,384]{2,0,1:T(8,128)(2,1)S(1)}, u32[]{:S(2)}) copy-start(bf16[12,64,384]{2,0,1:T(8,128)(2,1)S(1)} %all-to-all-done.2) | copy-start | bytes 1769476
  162.5 38.2 %all-to-all-start.3 = ((bf16[12,64,384]{2,0,1:T(8,128)(2,1)}), bf16[12,64,384]{2,0,1:T(8,128)(2,1)}, u32[]{:S(2)}, u32[]{:S(2)}) async-start(bf16[12,64,384]{2,0,1:T(8,128)(2,1)} %copy.287), calls=%async_computation.4 | async-start | bytes 1572864 | tf_op jit(solution)/shard_map/all_to_all | solution.py:310
  170.7 27.0 %copy-start.38 = (f32[200]{0:T(256)}, f32[200]{0:T(256)S(1)}, u32[]{:S(2)}) copy-start(f32[200]{0:T(256)S(1)} %add_rsqrt_fusion) | copy-start | bytes 2404
  205.4 6.7 copy-start.11
  205.5 84.6 %all-to-all-start.1 = ((bf16[64,63,768]{2,1,0:T(8,128)(2,1)}), bf16[64,63,768]{2,1,0:T(8,128)(2,1)}, u32[]{:S(2)}, u32[]{:S(2)}) async-start(bf16[64,63,768]{2,1,0:T(8,128)(2,1)} %bitcast.145), calls=%async_computation.2 | async-start | bytes 12582912 | tf_op jit(solution)/shard_map/all_to_all | solution.py:240
  276.4 3.3 copy-start
  281.2 5.4 copy-start.16
  293.4 28.1 %copy-start.9 = (bf16[12,64,384]{2,0,1:T(8,128)(2,1)S(1)}, bf16[12,64,384]{2,0,1:T(8,128)(2,1)}, u32[]{:S(2)}) copy-start(bf16[12,64,384]{2,0,1:T(8,128)(2,1)} %copy-done.8) | copy-start | bytes 1769476
  293.4 112.4 %all-to-all-start.5 = ((bf16[64,63,768]{2,1,0:T(8,128)(2,1)}), bf16[64,63,768]{2,1,0:T(8,128)(2,1)}, u32[]{:S(2)}, u32[]{:S(2)}) async-start(bf16[64,63,768]{2,1,0:T(8,128)(2,1)} %bitcast.146), calls=%async_computation.7 | async-start | bytes 12582912 | tf_op jit(solution)/shard_map/all_to_all | solution.py:240
  414.1 19.9 %copy-start.6 = (f32[4032,384]{1,0:T(8,128)S(1)}, f32[4032,384]{1,0:T(8,128)}, u32[]{:S(2)}) copy-start(f32[4032,384]{1,0:T(8,128)} %fusion.115) | copy-start | bytes 18579460
  450.2 89.0 %all-to-all-start.4 = ((bf16[64,63,768]{2,1,0:T(8,128)(2,1)}), bf16[64,63,768]{2,1,0:T(8,128)(2,1)}, u32[]{:S(2)}, u32[]{:S(2)}) async-start(bf16[64,63,768]{2,1,0:T(8,128)(2,1)} %reshape.329), calls=%async_computation.5 | async-start | bytes 12582912 | tf_op jit(solution)/shard_map/all_to_all | solution.py:247
  539.2 88.9 %all-to-all-start.6 = ((bf16[64,63,768]{2,1,0:T(8,128)(2,1)}), bf16[64,63,768]{2,1,0:T(8,128)(2,1)}, u32[]{:S(2)}, u32[]{:S(2)}) async-start(bf16[64,63,768]{2,1,0:T(8,128)(2,1)} %reshape.335), calls=%async_computation.8 | async-start | bytes 12582912 | tf_op jit(solution)/shard_map/all_to_all | solution.py:247
  550.3 135.6 %reduce-scatter.9.cloned.1.call-start = ((), (), s32[]{:S(2)}) async-start(), calls=%async_computation.16 | async-start | bytes 1843200 | tf_op jit(solution)/shard_map/reduce_scatter | solution.py:232
  566.5 4.1 copy-start.17
  650.8 3.8 copy-start.12
  653.6 60.3 %reduce-scatter.7.cloned.1.call-start = ((), (), s32[]{:S(2)}) async-start(), calls=%async_computation.15 | async-start | bytes 1843200 | tf_op jit(solution)/shard_map/reduce_scatter | solution.py:232
  654.3 152.7 %reduce-scatter.11.cloned.1.call-start = ((), (), s32[]{:S(2)}) async-start(), calls=%async_computation.17 | async-start | bytes 1843200 | tf_op jit(solution)/shard_map/reduce_scatter | solution.py:232
  658.9 27.0 %copy-start.4 = (f32[200,768]{1,0:T(8,128)S(1)}, f32[200,768]{1,0:T(8,128)}, u32[]{:S(2)}) copy-start(f32[200,768]{1,0:T(8,128)} %copy-done.3) | copy-start | bytes 1843204
  658.9 27.0 %copy-start.30 = (f32[768]{0:T(1024)S(1)}, f32[768]{0:T(1024)}, u32[]{:S(2)}) copy-start(f32[768]{0:T(1024)} %copy-done.29) | copy-start | bytes 9220
  658.9 27.0 %copy-start.35 = (f32[200]{0:T(256)S(1)}, f32[200]{0:T(256)}, u32[]{:S(2)}) copy-start(f32[200]{0:T(256)} %copy-done.34) | copy-start | bytes 2404
  658.9 27.0 %copy-start.39 = (f32[200]{0:T(256)S(1)}, f32[200]{0:T(256)}, u32[]{:S(2)}) copy-start(f32[200]{0:T(256)} %copy-done.38) | copy-start | bytes 2404
  730.4 4.7 copy-start.23
  735.2 7.4 copy-start.22
  737.1 10.0 %copy-start.25 = (bf16[2,200,6,64]{1,3,2,0:T(8,128)(2,1)S(1)}, bf16[2,200,6,64]{1,3,2,0:T(8,128)(2,1)}, u32[]{:S(2)}) copy-start(bf16[2,200,6,64]{1,3,2,0:T(8,128)(2,1)} %fusion.51) | copy-start | bytes 921604
  765.5 22.3 %all-to-all-start.9 = ((bf16[64,2,2304]{2,1,0:T(2,128)(2,1)}), bf16[64,2,2304]{2,1,0:T(2,128)(2,1)}, u32[]{:S(2)}, u32[]{:S(2)}) async-start(bf16[64,2,2304]{2,1,0:T(2,128)(2,1)} %reshape.442), calls=%async_computation.13 | async-start | bytes 1179648 | tf_op jit(solution)/shard_map/all_to_all | solution.py:347
  781.8 4.4 copy-start.13
  783.9 12.2 %copy-start.7 = (bf16[400,384]{0,1:T(8,128)(2,1)S(1)}, bf16[400,384]{0,1:T(8,128)(2,1)}, u32[]{:S(2)}) copy-start(bf16[400,384]{0,1:T(8,128)(2,1)} %reshape.319) | copy-start | bytes 921604
  787.8 36.5 %all-to-all-start.8 = ((bf16[64,2,2304]{2,1,0:T(2,128)(2,1)}), bf16[64,2,2304]{2,1,0:T(2,128)(2,1)}, u32[]{:S(2)}, u32[]{:S(2)}) async-start(bf16[64,2,2304]{2,1,0:T(2,128)(2,1)} %reshape.440), calls=%async_computation.12 | async-start | bytes 1179648 | tf_op jit(solution)/shard_map/all_to_all | solution.py:340
  799.2 7.7 copy-start.2
  799.3 7.7 copy-start.28
  799.3 7.7 copy-start.33
  799.3 7.7 copy-start.37
  802.1 7.7 copy-start.19
  824.3 95.3 %all-to-all-start.7 = ((f32[64,12,1556]{2,1,0:T(8,128)}), f32[64,12,1556]{2,1,0:T(8,128)}, u32[]{:S(2)}, u32[]{:S(2)}) async-start(f32[64,12,1556]{2,1,0:T(8,128)} %copy.318), calls=%async_computation.11 | async-start | bytes 13631488 | tf_op jit(solution)/shard_map/all_to_all | solution.py:213
  844.0 2.6 copy-start.14
  (8 other events, 14.9 us)
Sparse Core Ops, SparseCore 0:
  125.8 35.1 reduce-scatter.4
  653.7 32.0 reduce-scatter.8
  688.2 25.6 reduce-scatter.6
  755.7 32.7 reduce-scatter.10

commit v6 on v4

--- a/solution.py
+++ b/solution.py
@@ -1,16 +1,22 @@
 import jax
 import jax.numpy as jnp
 from jax import lax
-from jax.sharding import PartitionSpec as P
+from jax.sharding import Mesh, PartitionSpec as P
 
 HEAD_DIM = 64
 SEQ = 200
 REAL_TOK = 197
 CAP = 63
+EXPERTS = 16
+FSDP = ("fa", "fb")
 
 
 EPS = 1e-06
 TOP = lax.Precision.HIGHEST
+
+
+def fsdp_size():
+    return lax.axis_size("fa") * lax.axis_size("fb")
 
 
 def gelu_exact(value):
@@ -138,9 +144,9 @@
         ],
         axis=1,
     )
-    holders = lax.axis_size("fsdp")
+    holders = fsdp_size()
     spread = jnp.broadcast_to(packed[None], (holders,) + packed.shape)
-    full = lax.all_to_all(spread, "fsdp", split_axis=0, concat_axis=0, tiled=True)
+    full = lax.all_to_all(spread, FSDP, split_axis=0, concat_axis=0, tiled=True)
     full = full.reshape(holders * rows, packed.shape[1])
     width = full.shape[0]
     at = 3 * heads_width
@@ -166,10 +172,10 @@
         ],
         axis=1,
     )
-    holders = lax.axis_size("fsdp")
+    holders = fsdp_size()
     rows = width // holders
     moved = lax.all_to_all(
-        packed.reshape(holders, rows, packed.shape[1]), "fsdp", split_axis=0, concat_axis=0, tiled=True
+        packed.reshape(holders, rows, packed.shape[1]), FSDP, split_axis=0, concat_axis=0, tiled=True
     )
     part = jnp.sum(moved, axis=0)
     at = 3 * heads_width
@@ -190,20 +196,36 @@
     return lax.psum_scatter(value, "tp", scatter_dimension=0, tiled=True)
 
 
-def to_owners(slots, holders):
-    experts, capacity, width = slots.shape
-    spread = jnp.broadcast_to(slots[:, None], (experts, holders, capacity, width)).reshape(
-        experts * holders, capacity, width
-    )
-    moved = lax.all_to_all(spread, "fsdp", split_axis=0, concat_axis=0, tiled=True)
-    return moved.reshape(-1, width)
-
-
-def to_groups(partial_value, experts, holders, capacity):
-    width = partial_value.shape[1]
-    pieces = partial_value.astype(jnp.bfloat16).reshape(experts * holders, capacity, width)
-    moved = lax.all_to_all(pieces, "fsdp", split_axis=0, concat_axis=0, tiled=True)
-    return jnp.sum(moved.reshape(experts, holders, capacity, width).astype(jnp.float32), axis=1)
+def to_owners(slots):
+    moved = lax.all_to_all(slots, "fa", split_axis=0, concat_axis=0, tiled=True)
+    return moved.reshape(-1, slots.shape[2])
+
+
+def to_groups(result, experts, capacity):
+    width = result.shape[1]
+    pieces = result.astype(jnp.bfloat16).reshape(experts, capacity, width)
+    moved = lax.all_to_all(pieces, "fa", split_axis=0, concat_axis=0, tiled=True)
+    return moved.astype(jnp.float32)
+
+
+def expert_weights(weight, holders):
+    rows, experts, units = weight.shape
+    spread = jnp.broadcast_to(weight[:, :, None, :], (rows, experts, holders, units))
+    moved = lax.all_to_all(
+        spread.reshape(rows, experts * holders, units), FSDP, split_axis=1, concat_axis=0, tiled=True
+    )
+    return moved.reshape(-1, units)
+
+
+def weight_home(partial, experts, holders):
+    width, units = partial.shape
+    devices = experts * holders
+    rows = width // devices
+    moved = lax.all_to_all(
+        partial.astype(jnp.bfloat16).reshape(devices, rows, units), FSDP, split_axis=0, concat_axis=0, tiled=True
+    )
+    summed = jnp.sum(moved.reshape(experts, holders, rows, units).astype(jnp.float32), axis=1)
+    return jnp.transpose(summed, (1, 0, 2))
 
 
 def per_device(
@@ -240,7 +262,7 @@
     width = qkv_full.shape[1]
     units = expert_in.shape[2]
     local_rows = expert_in.shape[0]
-    holders = lax.axis_size("fsdp") // experts
+    holders = fsdp_size() // experts
     block_units = units // holders
     attention_normed, attention_standardized, attention_inverse_deviation = normalize_rows(
         inputs, attention_gain, attention_shift
@@ -261,19 +283,14 @@
     slotted = jnp.where(filled[:, None] > 0, tokens_m[token_of_slot], jnp.zeros((), bf16)).reshape(
         experts, CAP, width
     )
-    regroup_in = expert_in.reshape(local_rows, experts * holders, block_units)
-    regroup_out = expert_out.reshape(local_rows, experts * holders, block_units)
-    own_in, own_out = (
-        lax.all_to_all(regroup_in, "fsdp", split_axis=1, concat_axis=0, tiled=True),
-        lax.all_to_all(regroup_out, "fsdp", split_axis=1, concat_axis=0, tiled=True),
-    )
-    own_in = own_in.reshape(width, block_units)
-    own_out = own_out.reshape(width, block_units)
-    owner_x = to_owners(slotted, holders)
+    holders = lax.axis_size("fb")
+    own_in = expert_weights(expert_in, holders)
+    own_out = expert_weights(expert_out, holders)
+    owner_x = to_owners(slotted)
     owner_pre = jnp.dot(owner_x, own_in, preferred_element_type=f32)
     owner_hidden = gelu_exact(owner_pre).astype(bf16)
     owner_res = jnp.einsum("cf,df->cd", owner_hidden, own_out, preferred_element_type=f32)
-    expert_res = to_groups(owner_res, experts, holders, CAP)
+    expert_res = to_groups(owner_res, experts, CAP)
     routed = expert_res.reshape(experts * CAP, width)[slot].reshape(group, 2, width)
     outputs = residual_middle + owned_rows(jnp.sum(gates[:, :, None] * routed, axis=1))
     qkv_back, proj_back, router_back = qkv_full, proj_full, router_full
@@ -287,31 +304,15 @@
         .reshape(experts, CAP, width)
     )
     gate_grad = jnp.sum(dout_f[:, None, :] * routed, axis=-1)
-    owner_g = to_owners(slot_grad, holders)
+    owner_g = to_owners(slot_grad)
     owner_hgrad = jnp.dot(owner_g, own_out, preferred_element_type=f32)
     owner_pgrad = jax.vjp(gelu_exact, owner_pre)[1](owner_hgrad)[0].astype(bf16)
     owner_back = jnp.einsum("cf,df->cd", owner_pgrad, own_in, preferred_element_type=f32)
-    slot_in_grad = to_groups(owner_back, experts, holders, CAP)
+    slot_in_grad = to_groups(owner_back, experts, CAP)
     in_local = jnp.einsum("cd,cf->df", owner_x, owner_pgrad, preferred_element_type=f32)
     out_local = jnp.einsum("cd,cf->df", owner_g, owner_hidden, preferred_element_type=f32)
-    in_home, out_home = (
-        lax.all_to_all(
-            in_local.reshape(width, 1, block_units).astype(jnp.bfloat16),
-            "fsdp",
-            split_axis=0,
-            concat_axis=1,
-            tiled=True,
-        ).astype(jnp.float32),
-        lax.all_to_all(
-            out_local.reshape(width, 1, block_units).astype(jnp.bfloat16),
-            "fsdp",
-            split_axis=0,
-            concat_axis=1,
-            tiled=True,
-        ).astype(jnp.float32),
-    )
-    in_grad = in_home.reshape(local_rows, experts, units)
-    out_grad = out_home.reshape(local_rows, experts, units)
+    in_grad = weight_home(in_local, experts, holders)
+    out_grad = weight_home(out_local, experts, holders)
     choice_grad = jnp.sum(picked.astype(f32) * gate_grad[:, :, None], axis=1)
     logit_grad = probs * (choice_grad - jnp.sum(probs * choice_grad, axis=-1, keepdims=True))
     router_part = jnp.einsum("td,te->de", tokens_m.astype(f32), logit_grad, precision=TOP)
@@ -368,35 +369,39 @@
 
 
 def solution(mesh):
+    fsdp = mesh.shape["fsdp"]
+    sub = Mesh(
+        mesh.devices.reshape(EXPERTS, fsdp // EXPERTS, mesh.shape["tp"]), ("fa", "fb", "tp")
+    )
     return jax.shard_map(
         per_device,
-        mesh=mesh,
+        mesh=sub,
         in_specs=(
-            P(("fsdp", "tp"), None),
-            P("fsdp", None),
-            P("fsdp"),
-            P("fsdp"),
-            P(None, "fsdp", "tp"),
-            P("tp", "fsdp"),
-            P("fsdp"),
-            P("fsdp"),
-            P("fsdp", None),
-            P("fsdp", None, "tp"),
-            P("fsdp", None, "tp"),
-            P(("fsdp", "tp"), None),
+            P(("fa", "fb", "tp"), None),
+            P(("fa", "fb"), None),
+            P(("fa", "fb")),
+            P(("fa", "fb")),
+            P(None, ("fa", "fb"), "tp"),
+            P("tp", ("fa", "fb")),
+            P(("fa", "fb")),
+            P(("fa", "fb")),
+            P(("fa", "fb"), None),
+            P(("fa", "fb"), None, "tp"),
+            P(("fa", "fb"), None, "tp"),
+            P(("fa", "fb", "tp"), None),
         ),
         out_specs=(
-            P(("fsdp", "tp"), None),
-            P(("fsdp", "tp"), None),
-            P("fsdp"),
-            P("fsdp"),
-            P(None, "fsdp", "tp"),
-            P("tp", "fsdp"),
-            P("fsdp"),
-            P("fsdp"),
-            P("fsdp", None),
-            P("fsdp", None, "tp"),
-            P("fsdp", None, "tp"),
+            P(("fa", "fb", "tp"), None),
+            P(("fa", "fb", "tp"), None),
+            P(("fa", "fb")),
+            P(("fa", "fb")),
+            P(None, ("fa", "fb"), "tp"),
+            P("tp", ("fa", "fb")),
+            P(("fa", "fb")),
+            P(("fa", "fb")),
+            P(("fa", "fb"), None),
+            P(("fa", "fb"), None, "tp"),
+            P(("fa", "fb"), None, "tp"),
         ),
         check_vma=False,
     )

time: 944 us -> 741 us (0.78)
  the two profiles are of different devices: /device:TPU:1 before, /device:TPU:18 now
where the time goes in v6:
time: 741 us; the launch traced here: 728 us
  waiting for transfers between devices  237 us (32%)
  local copies, waits for them, and re-layouts  179 us (24%)
  matrix products  96.5 us (13%)
  starting transfers between devices  81.5 us (11%)
  blocking collectives  77.8 us (10%)
  other arithmetic  41.6 us (6%)
  between operations  14.8 us (2%)
    reduce_scatter x4, waiting for transfers between devices, owned_rows(): return lax.psum_scatter(value, 'tp', scatter_dimension=0, tiled=True)  105 us
    all_to_all x1, waiting for transfers between devices, reduce_dense(): lax.all_to_all(packed.reshape(holders, rows, packed.shape[1]), FSDP, spli...  81.7 us
    all_gather x4, blocking collectives, group_rows(): return lax.all_gather(value, 'tp', axis=0, tiled=True)  71.4 us
    all_to_all x1, waiting for transfers between devices, gather_dense(): full = lax.all_to_all(spread, FSDP, split_axis=0, concat_axis=0, tiled=True)  41 us
    concatenate x8, local copies, waits for them, and re-layouts, reduce_dense(): jnp.concatenate([jnp.transpose(qkv_part, (1, 0, 2)).reshape(width, -1), p...  20.7 us
    dot_general x1, matrix products, per_device(): owner_hgrad = jnp.dot(owner_g, own_out, preferred_element_type=f32)  20 us
    all_to_all x2, starting transfers between devices, weight_home(): lax.all_to_all(partial.astype(jnp.bfloat16).reshape(devices, rows, units)...  17.5 us
    all_to_all x2, starting transfers between devices, expert_weights(): lax.all_to_all(spread.reshape(rows, experts * holders, units), FSDP, spli...  16.8 us
  transfers between devices with their start and end apart: 14, of which 7 were waited for; matrix products, arithmetic and copies ran while one was open for 34% of the time, Pallas kernels for 0%

profile of v6, /device:TPU:18, one launch (start us, length us, event | category | flops | bytes accessed | tf_op | source)
XLA Modules:
  0.0 728.2 jit_solution(7627684323233690648)
XLA Ops:
  13.8 9.5 %all-to-all-start = ((bf16[64,12,1556]{2,1,0:T(8,128)(2,1)}), bf16[64,12,1556]{2,1,0:T(8,128)(2,1)}, u32[]{:S(2)}, u32[]{:S(2)}) async-start(bf16[64,12,1556]{2,1,0:T(8,128)(2,1)} %broadcast_in_dim.54), calls=%async_computation | async-start | bytes 6815744 | tf_op jit(solution)/shard_map/all_to_all | solution.py:149
  24.1 41.0 %all-to-all-done = bf16[64,12,1556]{2,1,0:T(8,128)(2,1)} async-done(((bf16[64,12,1556]{2,1,0:T(8,128)(2,1)}), bf16[64,12,1556]{2,1,0:T(8,128)(2,1)}, u32[]{:S(2)}, u32[]{:S(2)}) %all-to-all-start) | async-done | bytes 2390048 | tf_op jit(solution)/shard_map/all_to_all | solution.py:149
  67.2 8.6 %all-to-all-start.2 = ((bf16[12,64,1536]{2,0,1:T(8,128)(2,1)}), bf16[12,64,1536]{2,0,1:T(8,128)(2,1)}, u32[]{:S(2)}, u32[]{:S(2)}) async-start(bf16[12,64,1536]{2,0,1:T(8,128)(2,1)} %bitcast.115), calls=%async_computation.3 | async-start | bytes 6291456 | tf_op jit(solution)/shard_map/all_to_all | solution.py:214
  75.9 4.2 reshape.276
  82.3 38.4 %all_gather.12 = bf16[400,768]{1,0:T(8,128)(2,1)} all-gather(bf16[200,768]{1,0:T(8,128)(2,1)S(1)} %add_convert_fusion.2), channel_id=1, replica_groups=mesh['fa'=16,'fb'=4,'tp'=2] {'tp'}, dimensions={0}, use_global_device_ids=true | all-gather | bytes 921600 | tf_op jit(solution)/shard_map/all_gather | solution.py:192
  147.7 4.4 fusion.48
  164.4 8.2 %all-to-all-start.3 = ((bf16[12,64,1536]{2,0,1:T(8,128)(2,1)}), bf16[12,64,1536]{2,0,1:T(8,128)(2,1)}, u32[]{:S(2)}, u32[]{:S(2)}) async-start(bf16[12,64,1536]{2,0,1:T(8,128)(2,1)} %bitcast.116), calls=%async_computation.4 | async-start | bytes 6291456 | tf_op jit(solution)/shard_map/all_to_all | solution.py:214
  172.7 5.3 scatter_custom_fusion.1
  178.0 5.3 scatter_custom_fusion
  183.4 34.7 %reduce-scatter.5.cloned.1.call-done = f32[200,768]{1,0:T(8,128)} async-done(((f32[400,768]{1,0:T(8,128)}), f32[200,768]{1,0:T(8,128)}) %reduce-scatter.5.cloned.1.call-update) | async-done | bytes 614416 | tf_op jit(solution)/shard_map/reduce_scatter | solution.py:196
  219.8 11.6 %all_gather.13 = bf16[400,768]{1,0:T(8,128)(2,1)S(1)} all-gather(bf16[200,768]{1,0:T(8,128)(2,1)S(1)} %add_convert_fusion.1), channel_id=1, replica_groups=mesh['fa'=16,'fb'=4,'tp'=2] {'tp'}, dimensions={0}, use_global_device_ids=true | all-gather | bytes 921600 | tf_op jit(solution)/shard_map/all_gather | solution.py:192
  231.4 5.2 gather_fusion
  242.1 7.2 all-to-all-start.1
  249.4 9.8 %all_gather.14 = bf16[400,768]{1,0:T(8,128)(2,1)S(1)} all-gather(bf16[200,768]{1,0:T(8,128)(2,1)S(1)} %convert_element_type.166), channel_id=1, replica_groups=mesh['fa'=16,'fb'=4,'tp'=2] {'tp'}, dimensions={0}, use_global_device_ids=true | all-gather | bytes 921600 | tf_op jit(solution)/shard_map/all_gather | solution.py:192
  259.2 5.3 gather_fusion.2
  270.0 5.3 scatter_custom_fusion.2
  278.8 7.2 all-to-all-start.5
  286.0 4.9 reshape.283
  290.9 4.9 reshape.285
  298.4 7.3 %fusion.112 = f32[1008,1536]{1,0:T(8,128)} fusion(bf16[1008,768]{1,0:T(8,128)(2,1)} %reshape.281, bf16[768,1536]{1,0:T(8,128)(2,1)} %reshape.283), kind=kOutput, calls=%fused_computation.173 | convolution fusion | flops 2378170368 | bytes 10100736 | tf_op jit(solution)/shard_map/dot_general | solution.py:290
  308.3 20.0 %add_convert_fusion = (bf16[1008,1536]{1,0:T(8,128)(2,1)}, f32[1008,1536]{1,0:T(8,128)S(1)}) fusion(f32[1008,1536]{1,0:T(8,128)} %fusion.112, bf16[1008,768]{1,0:T(8,128)(2,1)} %reshape.291, bf16[768,1536]{1,0:T(8,128)(2,1)} %reshape.285), kind=kOutput, calls=%fused_computation.13 | convolution fusion | flops 2489647104 | bytes 19390464 | tf_op jit(solution)/shard_map/dot_general | solution.py:308
  331.5 5.4 convolution_convert_fusion.3
  339.5 7.2 all-to-all-start.4
  346.7 6.3 convolution_convert_fusion.2
  355.6 8.6 %all-to-all-done.4 = bf16[16,63,768]{2,1,0:T(8,128)(2,1)} async-done(((bf16[16,63,768]{2,1,0:T(8,128)(2,1)}), bf16[16,63,768]{2,1,0:T(8,128)(2,1)}, u32[]{:S(2)}, u32[]{:S(2)}) %all-to-all-start.4) | async-done | bytes 1548320 | tf_op jit(solution)/shard_map/all_to_all | solution.py:207
  364.2 7.4 %all-to-all-start.6 = ((bf16[16,63,768]{2,1,0:T(8,128)(2,1)}), bf16[16,63,768]{2,1,0:T(8,128)(2,1)}, u32[]{:S(2)}, u32[]{:S(2)}) async-start(bf16[16,63,768]{2,1,0:T(8,128)(2,1)} %reshape.292), calls=%async_computation.8 | async-start | bytes 3145728 | tf_op jit(solution)/shard_map/all_to_all | solution.py:207
  374.8 6.6 gather_fusion.1
  385.5 8.1 %multiply_reduce_fusion.1 = (f32[400,2]{1,0:T(8,128)S(1)}, f32[400,768]{1,0:T(8,128)}) fusion(f32[400,2,768]{2,1,0:T(2,128)} %reshape.289, f32[400,768]{1,0:T(8,128)S(1)} %convert_element_type.167, f32[400,2]{1,0:T(8,128)S(1)} %copy.211), kind=kLoop, calls=%fused_computation.37 | loop fusion | flops 2149600 | bytes 4921600 | tf_op jit(solution)/shard_map/reduce_sum | solution.py:306
  397.6 6.6 gather_fusion.3
  408.3 4.6 reduce_sum.237
  419.5 6.4 convolution_convert_fusion
  425.9 4.8 reshape.299
  430.7 8.2 %all-to-all-start.9 = ((bf16[64,12,1536]{2,1,0:T(8,128)(2,1)}), bf16[64,12,1536]{2,1,0:T(8,128)(2,1)}, u32[]{:S(2)}, u32[]{:S(2)}) async-start(bf16[64,12,1536]{2,1,0:T(8,128)(2,1)} %reshape.299), calls=%async_computation.13 | async-start | bytes 6291456 | tf_op jit(solution)/shard_map/all_to_all | solution.py:224
  442.9 46.8 %reduce-scatter.7.cloned.1.call-done = f32[200,768]{1,0:T(8,128)} async-done(((f32[400,768]{1,0:T(8,128)}), f32[200,768]{1,0:T(8,128)}) %reduce-scatter.7.cloned.1.call-update) | async-done | bytes 614416 | tf_op jit(solution)/shard_map/reduce_scatter | solution.py:196
  492.2 11.6 %all_gather.15 = bf16[400,768]{1,0:T(8,128)(2,1)S(1)} all-gather(bf16[200,768]{1,0:T(8,128)(2,1)S(1)} %get-tuple-element.62), channel_id=1, replica_groups=mesh['fa'=16,'fb'=4,'tp'=2] {'tp'}, dimensions={0}, use_global_device_ids=true | all-gather | bytes 921600 | tf_op jit(solution)/shard_map/all_gather | solution.py:192
  506.3 4.5 fusion.49
  516.3 5.6 fusion.50
  524.6 4.8 fusion.53
  537.6 6.4 convolution_convert_fusion.1
  544.0 4.8 reshape.298
  548.8 9.3 %all-to-all-start.8 = ((bf16[64,12,1536]{2,1,0:T(8,128)(2,1)}), bf16[64,12,1536]{2,1,0:T(8,128)(2,1)}, u32[]{:S(2)}, u32[]{:S(2)}) async-start(bf16[64,12,1536]{2,1,0:T(8,128)(2,1)} %reshape.298), calls=%async_computation.12 | async-start | bytes 6291456 | tf_op jit(solution)/shard_map/all_to_all | solution.py:224
  561.5 4.6 copy.235
  566.1 7.4 %concatenate.20 = f32[64,12,1152]{2,1,0:T(8,128)} reshape(f32[768,3,384]{2,1,0:T(4,128)} %copy.235) | data formatting | bytes 7077888 | tf_op jit(solution)/shard_map/concatenate | solution.py:166
  577.1 20.9 %reduce-scatter.11.cloned.1.call-done = f32[200,768]{1,0:T(8,128)} async-done(((f32[400,768]{1,0:T(8,128)}), f32[200,768]{1,0:T(8,128)}) %reduce-scatter.11.cloned.1.call-update) | async-done | bytes 614416 | tf_op jit(solution)/shard_map/reduce_scatter | solution.py:196
  601.5 8.1 %concatenate.26 = f32[64,12,1556]{2,1,0:T(8,128)} concatenate(f32[64,12,1152]{2,1,0:T(8,128)} %concatenate.20, f32[64,12,384]{2,1,0:T(8,128)S(1)} %copy.239, f32[64,12,16]{2,1,0:T(8,128)S(1)} %copy-done.10, f32[64,12,1]{2,1,0:T(8,128)} %concatenate.27, f32[64,12,1]{2,1,0:T(8,128)} %concatenate.28, f32[64,12,1]{2,1,0:T(8,128)S(1)} %concatenate.29, f32[64,12,1]{2,1,0:T(8,128)} %concatenate.30), dimensions={2} | concatenate | bytes 9560064 | tf_op jit(solution)/shard_map/concatenate | solution.py:166
  609.6 8.3 %all-to-all-start.7 = ((f32[64,12,1556]{2,1,0:T(8,128)}), f32[64,12,1556]{2,1,0:T(8,128)}, u32[]{:S(2)}, u32[]{:S(2)}) async-start(f32[64,12,1556]{2,1,0:T(8,128)} %concatenate.26), calls=%async_computation.11 | async-start | bytes 13631488 | tf_op jit(solution)/shard_map/all_to_all | solution.py:177
  628.0 81.7 %all-to-all-done.7 = f32[64,12,1556]{2,1,0:T(8,128)} async-done(((f32[64,12,1556]{2,1,0:T(8,128)}), f32[64,12,1556]{2,1,0:T(8,128)}, u32[]{:S(2)}, u32[]{:S(2)}) %all-to-all-start.7) | async-done | bytes 4780064 | tf_op jit(solution)/shard_map/all_to_all | solution.py:177
  714.2 6.5 psum.7
  (220 shorter events, 153.8 us)
Async XLA Ops:
  13.8 9.5 %copy-start.17 = (bf16[12,16,1536]{2,1,0:T(8,128)(2,1)S(1)}, bf16[12,16,1536]{2,1,0:T(8,128)(2,1)}, u32[]{:S(2)}) copy-start(bf16[12,16,1536]{2,1,0:T(8,128)(2,1)} %param.21) | copy-start | bytes 1769476
  13.8 9.9 %copy-start = (f32[200,768]{1,0:T(8,128)S(1)}, f32[200,768]{1,0:T(8,128)}, u32[]{:S(2)}) copy-start(f32[200,768]{1,0:T(8,128)} %param.12) | copy-start | bytes 1843204
  13.8 51.3 %all-to-all-start = ((bf16[64,12,1556]{2,1,0:T(8,128)(2,1)}), bf16[64,12,1556]{2,1,0:T(8,128)(2,1)}, u32[]{:S(2)}, u32[]{:S(2)}) async-start(bf16[64,12,1556]{2,1,0:T(8,128)(2,1)} %broadcast_in_dim.54), calls=%async_computation | async-start | bytes 6815744 | tf_op jit(solution)/shard_map/all_to_all | solution.py:149
  23.8 123.8 %copy-start.35 = (pred[200]{0:T(512)(128)(4,1)}, pred[200]{0:T(512)(128)(4,1)S(1)}, u32[]{:S(2)}) copy-start(pred[200]{0:T(512)(128)(4,1)S(1)} %iota_compare_fusion.3) | copy-start | bytes 604
  23.9 58.3 %copy-start.26 = (f32[200]{0:T(256)}, f32[200]{0:T(256)S(1)}, u32[]{:S(2)}) copy-start(f32[200]{0:T(256)S(1)} %broadcast_multiply_fusion.6) | copy-start | bytes 2404
  24.1 58.0 %copy-start.31 = (f32[200]{0:T(256)}, f32[200]{0:T(256)S(1)}, u32[]{:S(2)}) copy-start(f32[200]{0:T(256)S(1)} %add_rsqrt_fusion.1) | copy-start | bytes 2404
  67.2 95.1 %all-to-all-start.2 = ((bf16[12,64,1536]{2,0,1:T(8,128)(2,1)}), bf16[12,64,1536]{2,0,1:T(8,128)(2,1)}, u32[]{:S(2)}, u32[]{:S(2)}) async-start(bf16[12,64,1536]{2,0,1:T(8,128)(2,1)} %bitcast.115), calls=%async_computation.3 | async-start | bytes 6291456 | tf_op jit(solution)/shard_map/all_to_all | solution.py:214
  75.8 142.3 %reduce-scatter.5.cloned.1.call-start = ((), (), s32[]{:S(2)}) async-start(), calls=%async_computation.14 | async-start | bytes 1843200 | tf_op jit(solution)/shard_map/reduce_scatter | solution.py:196
  80.1 76.2 %copy-start.1 = (bf16[768,1556]{1,0:T(8,128)(2,1)}, bf16[768,1556]{1,0:T(8,128)(2,1)S(1)}, u32[]{:S(2)}) copy-start(bf16[768,1556]{1,0:T(8,128)(2,1)S(1)} %reshape.276) | copy-start | bytes 7170052
  80.6 1.5 copy-start.21
  152.1 6.8 copy-start.23
  158.8 3.0 copy-start.18
  164.4 77.7 %all-to-all-start.3 = ((bf16[12,64,1536]{2,0,1:T(8,128)(2,1)}), bf16[12,64,1536]{2,0,1:T(8,128)(2,1)}, u32[]{:S(2)}, u32[]{:S(2)}) async-start(bf16[12,64,1536]{2,0,1:T(8,128)(2,1)} %bitcast.116), calls=%async_computation.4 | async-start | bytes 6291456 | tf_op jit(solution)/shard_map/all_to_all | solution.py:214
  219.3 17.2 %copy-start.28 = (f32[200]{0:T(256)}, f32[200]{0:T(256)S(1)}, u32[]{:S(2)}) copy-start(f32[200]{0:T(256)S(1)} %broadcast_multiply_fusion.5) | copy-start | bytes 2404
  219.6 17.0 %copy-start.33 = (f32[200]{0:T(256)}, f32[200]{0:T(256)S(1)}, u32[]{:S(2)}) copy-start(f32[200]{0:T(256)S(1)} %add_rsqrt_fusion) | copy-start | bytes 2404
  239.2 10.2 %copy-start.5 = (f32[200,768]{1,0:T(8,128)S(1)}, f32[200,768]{1,0:T(8,128)}, u32[]{:S(2)}) copy-start(f32[200,768]{1,0:T(8,128)} %param.23) | copy-start | bytes 1843204
  242.1 36.7 %all-to-all-start.1 = ((bf16[16,63,768]{2,1,0:T(8,128)(2,1)}), bf16[16,63,768]{2,1,0:T(8,128)(2,1)}, u32[]{:S(2)}, u32[]{:S(2)}) async-start(bf16[16,63,768]{2,1,0:T(8,128)(2,1)} %broadcast_select_fusion), calls=%async_computation.2 | async-start | bytes 3145728 | tf_op jit(solution)/shard_map/all_to_all | solution.py:200
  278.8 26.9 %all-to-all-start.5 = ((bf16[16,63,768]{2,1,0:T(8,128)(2,1)}), bf16[16,63,768]{2,1,0:T(8,128)(2,1)}, u32[]{:S(2)}, u32[]{:S(2)}) async-start(bf16[16,63,768]{2,1,0:T(8,128)(2,1)} %select_convert_fusion), calls=%async_computation.7 | async-start | bytes 3145728 | tf_op jit(solution)/shard_map/all_to_all | solution.py:200
  308.2 20.1 %copy-start.2 = (f32[1008,1536]{1,0:T(8,128)S(1)}, f32[1008,1536]{1,0:T(8,128)}, u32[]{:S(2)}) copy-start(f32[1008,1536]{1,0:T(8,128)} %fusion.112) | copy-start | bytes 18579460
  329.9 1.6 copy-start.4
  339.5 24.7 %all-to-all-start.4 = ((bf16[16,63,768]{2,1,0:T(8,128)(2,1)}), bf16[16,63,768]{2,1,0:T(8,128)(2,1)}, u32[]{:S(2)}, u32[]{:S(2)}) async-start(bf16[16,63,768]{2,1,0:T(8,128)(2,1)} %reshape.286), calls=%async_computation.5 | async-start | bytes 3145728 | tf_op jit(solution)/shard_map/all_to_all | solution.py:207
  364.2 30.4 %all-to-all-start.6 = ((bf16[16,63,768]{2,1,0:T(8,128)(2,1)}), bf16[16,63,768]{2,1,0:T(8,128)(2,1)}, u32[]{:S(2)}, u32[]{:S(2)}) async-start(bf16[16,63,768]{2,1,0:T(8,128)(2,1)} %reshape.292), calls=%async_computation.8 | async-start | bytes 3145728 | tf_op jit(solution)/shard_map/all_to_all | solution.py:207
  371.5 69.9 %reduce-scatter.9.cloned.1.call-start = ((), (), s32[]{:S(2)}) async-start(), calls=%async_computation.16 | async-start | bytes 1843200 | tf_op jit(solution)/shard_map/reduce_scatter | solution.py:196
  371.8 9.7 %copy-start.24 = (s32[1024]{0:T(1024)}, s32[1024]{0:T(1024)S(1)}, u32[]{:S(2)}) copy-start(s32[1024]{0:T(1024)S(1)} %pad_clamp_fusion) | copy-start | bytes 12292
  393.6 4.0 copy-start.25
  412.9 3.5 copy-start.11
  412.9 3.5 copy-start.36
  415.6 1.0 copy-start.13
  415.7 74.0 %reduce-scatter.7.cloned.1.call-start = ((), (), s32[]{:S(2)}) async-start(), calls=%async_computation.15 | async-start | bytes 1843200 | tf_op jit(solution)/shard_map/reduce_scatter | solution.py:196
  430.7 10.8 %copy-start.29 = (f32[200]{0:T(256)S(1)}, f32[200]{0:T(256)}, u32[]{:S(2)}) copy-start(f32[200]{0:T(256)} %copy-done.28) | copy-start | bytes 2404
  430.7 10.8 %copy-start.34 = (f32[200]{0:T(256)S(1)}, f32[200]{0:T(256)}, u32[]{:S(2)}) copy-start(f32[200]{0:T(256)} %copy-done.33) | copy-start | bytes 2404
  430.7 59.0 %copy-start.6 = (f32[200,768]{1,0:T(8,128)S(1)}, f32[200,768]{1,0:T(8,128)}, u32[]{:S(2)}) copy-start(f32[200,768]{1,0:T(8,128)} %param.23) | copy-start | bytes 1843204
  430.7 118.1 %all-to-all-start.9 = ((bf16[64,12,1536]{2,1,0:T(8,128)(2,1)}), bf16[64,12,1536]{2,1,0:T(8,128)(2,1)}, u32[]{:S(2)}, u32[]{:S(2)}) async-start(bf16[64,12,1536]{2,1,0:T(8,128)(2,1)} %reshape.299), calls=%async_computation.13 | async-start | bytes 6291456 | tf_op jit(solution)/shard_map/all_to_all | solution.py:224
  438.9 159.2 %reduce-scatter.11.cloned.1.call-start = ((), (), s32[]{:S(2)}) async-start(), calls=%async_computation.17 | async-start | bytes 1843200 | tf_op jit(solution)/shard_map/reduce_scatter | solution.py:196
  506.2 4.5 copy-start.16
  506.3 7.1 copy-start.15
  512.2 4.2 copy-start.14
  516.3 8.2 %copy-start.12 = (bf16[2,200,6,64]{1,3,2,0:T(8,128)(2,1)S(1)}, bf16[2,200,6,64]{1,3,2,0:T(8,128)(2,1)}, u32[]{:S(2)}) copy-start(bf16[2,200,6,64]{1,3,2,0:T(8,128)(2,1)} %copy.207) | copy-start | bytes 921604
  548.8 11.5 %copy-start.9 = (bf16[400,768]{1,0:T(8,128)(2,1)S(1)}, bf16[400,768]{1,0:T(8,128)(2,1)}, u32[]{:S(2)}) copy-start(bf16[400,768]{1,0:T(8,128)(2,1)} %all_gather.12) | copy-start | bytes 1843204
  548.8 60.8 %all-to-all-start.8 = ((bf16[64,12,1536]{2,1,0:T(8,128)(2,1)}), bf16[64,12,1536]{2,1,0:T(8,128)(2,1)}, u32[]{:S(2)}, u32[]{:S(2)}) async-start(bf16[64,12,1536]{2,1,0:T(8,128)(2,1)} %reshape.298), calls=%async_computation.12 | async-start | bytes 6291456 | tf_op jit(solution)/shard_map/all_to_all | solution.py:224
  573.5 1.0 copy-start.3
  575.1 22.9 %copy-start.22 = (f32[768]{0:T(1024)S(1)}, f32[768]{0:T(1024)}, u32[]{:S(2)}) copy-start(f32[768]{0:T(1024)} %copy-done.21) | copy-start | bytes 9220
  575.1 22.9 %copy-start.27 = (f32[200]{0:T(256)S(1)}, f32[200]{0:T(256)}, u32[]{:S(2)}) copy-start(f32[200]{0:T(256)} %copy-done.26) | copy-start | bytes 2404
  575.1 22.9 %copy-start.32 = (f32[200]{0:T(256)S(1)}, f32[200]{0:T(256)}, u32[]{:S(2)}) copy-start(f32[200]{0:T(256)} %copy-done.31) | copy-start | bytes 2404
  575.1 26.4 %copy-start.10 = (f32[64,12,16]{2,1,0:T(8,128)S(1)}, f32[64,12,16]{2,1,0:T(8,128)}, u32[]{:S(2)}) copy-start(f32[64,12,16]{2,1,0:T(8,128)} %copy.240) | copy-start | bytes 147460
  609.6 100.0 %all-to-all-start.7 = ((f32[64,12,1556]{2,1,0:T(8,128)}), f32[64,12,1556]{2,1,0:T(8,128)}, u32[]{:S(2)}, u32[]{:S(2)}) async-start(f32[64,12,1556]{2,1,0:T(8,128)} %concatenate.26), calls=%async_computation.11 | async-start | bytes 13631488 | tf_op jit(solution)/shard_map/all_to_all | solution.py:177
  625.1 1.7 copy-start.7
  625.2 1.7 copy-start.8
  (3 other events, 2.3 us)
Sparse Core Ops, SparseCore 0:
  159.0 59.0 reduce-scatter.4
  415.8 25.6 reduce-scatter.8
  443.9 45.7 reduce-scatter.6
  537.7 60.2 reduce-scatter.10

commit v7 on v6

--- a/solution.py
+++ b/solution.py
@@ -174,10 +174,28 @@
     )
     holders = fsdp_size()
     rows = width // holders
+    at = 4 * heads_width
+    small = packed[:, at:]
+    high = lax.reduce_precision(small, exponent_bits=8, mantissa_bits=7)
+    wire = jnp.concatenate(
+        [
+            packed[:, :at].astype(jnp.bfloat16),
+            high.astype(jnp.bfloat16),
+            (small - high).astype(jnp.bfloat16),
+        ],
+        axis=1,
+    )
     moved = lax.all_to_all(
-        packed.reshape(holders, rows, packed.shape[1]), FSDP, split_axis=0, concat_axis=0, tiled=True
-    )
-    part = jnp.sum(moved, axis=0)
+        wire.reshape(holders, rows, wire.shape[1]), FSDP, split_axis=0, concat_axis=0, tiled=True
+    ).astype(jnp.float32)
+    count = small.shape[1]
+    part = jnp.concatenate(
+        [
+            jnp.sum(moved[..., :at], axis=0),
+            jnp.sum(moved[..., at : at + count] + moved[..., at + count :], axis=0),
+        ],
+        axis=1,
+    )
     at = 3 * heads_width
     qkv_grad = jnp.transpose(part[:, :at].reshape(rows, 3, heads_width), (1, 0, 2))
     proj_grad = part[:, at : at + heads_width].T

time: 741 us -> 692 us (0.934)
  the two profiles are of different devices: /device:TPU:18 before, /device:TPU:1 now
where the time goes in v7:
time: 692 us; the launch traced here: 679 us
  waiting for transfers between devices  187 us (27%)
  local copies, waits for them, and re-layouts  173 us (25%)
  matrix products  97.8 us (14%)
  starting transfers between devices  88.6 us (13%)
  blocking collectives  75.9 us (11%)
  other arithmetic  41.5 us (6%)
  between operations  14.9 us (2%)
    reduce_scatter x4, waiting for transfers between devices, owned_rows(): return lax.psum_scatter(value, 'tp', scatter_dimension=0, tiled=True)  86.2 us
    all_gather x4, blocking collectives, group_rows(): return lax.all_gather(value, 'tp', axis=0, tiled=True)  70.6 us
    all_to_all x1, waiting for transfers between devices, gather_dense(): full = lax.all_to_all(spread, FSDP, split_axis=0, concat_axis=0, tiled=True)  42.3 us
    all_to_all x1, waiting for transfers between devices, reduce_dense(): lax.all_to_all(wire.reshape(holders, rows, wire.shape[1]), FSDP, split_ax...  32.8 us
    dot_general x1, matrix products, per_device(): owner_hgrad = jnp.dot(owner_g, own_out, preferred_element_type=f32)  20 us
    all_to_all x1, starting transfers between devices, reduce_dense(): lax.all_to_all(wire.reshape(holders, rows, wire.shape[1]), FSDP, split_ax...  18.9 us
    all_to_all x2, starting transfers between devices, weight_home(): lax.all_to_all(partial.astype(jnp.bfloat16).reshape(devices, rows, units)...  18.2 us
    all_to_all x2, waiting for transfers between devices, weight_home(): lax.all_to_all(partial.astype(jnp.bfloat16).reshape(devices, rows, units)...  15 us
  transfers between devices with their start and end apart: 14, of which 8 were waited for; matrix products, arithmetic and copies ran while one was open for 36% of the time, Pallas kernels for 0%

profile of v7, /device:TPU:1, one launch (start us, length us, event | category | flops | bytes accessed | tf_op | source)
XLA Modules:
  0.0 678.6 jit_solution(13231019430560085218)
XLA Ops:
  13.8 10.6 %all-to-all-start = ((bf16[64,12,1556]{2,1,0:T(8,128)(2,1)}), bf16[64,12,1556]{2,1,0:T(8,128)(2,1)}, u32[]{:S(2)}, u32[]{:S(2)}) async-start(bf16[64,12,1556]{2,1,0:T(8,128)(2,1)} %broadcast_in_dim.54), calls=%async_computation | async-start | bytes 6815744 | tf_op jit(solution)/shard_map/all_to_all | solution.py:149
  25.3 42.3 %all-to-all-done = bf16[64,12,1556]{2,1,0:T(8,128)(2,1)} async-done(((bf16[64,12,1556]{2,1,0:T(8,128)(2,1)}), bf16[64,12,1556]{2,1,0:T(8,128)(2,1)}, u32[]{:S(2)}, u32[]{:S(2)}) %all-to-all-start) | async-done | bytes 2390048 | tf_op jit(solution)/shard_map/all_to_all | solution.py:149
  69.6 7.3 %all-to-all-start.2 = ((bf16[12,64,1536]{2,0,1:T(8,128)(2,1)}), bf16[12,64,1536]{2,0,1:T(8,128)(2,1)}, u32[]{:S(2)}, u32[]{:S(2)}) async-start(bf16[12,64,1536]{2,0,1:T(8,128)(2,1)} %bitcast.115), calls=%async_computation.3 | async-start | bytes 6291456 | tf_op jit(solution)/shard_map/all_to_all | solution.py:232
  77.0 4.2 reshape.289
  83.4 39.9 %all_gather.12 = bf16[400,768]{1,0:T(8,128)(2,1)} all-gather(bf16[200,768]{1,0:T(8,128)(2,1)S(1)} %add_convert_fusion.2), channel_id=1, replica_groups=mesh['fa'=16,'fb'=4,'tp'=2] {'tp'}, dimensions={0}, use_global_device_ids=true | all-gather | bytes 921600 | tf_op jit(solution)/shard_map/all_gather | solution.py:210
  150.2 4.4 fusion.48
  167.0 6.8 all-to-all-start.3
  173.8 5.3 scatter_custom_fusion.1
  179.1 5.3 scatter_custom_fusion
  184.5 34.6 %reduce-scatter.5.cloned.1.call-done = f32[200,768]{1,0:T(8,128)} async-done(((f32[400,768]{1,0:T(8,128)}), f32[200,768]{1,0:T(8,128)}) %reduce-scatter.5.cloned.1.call-update) | async-done | bytes 614416 | tf_op jit(solution)/shard_map/reduce_scatter | solution.py:214
  220.8 10.7 %all_gather.13 = bf16[400,768]{1,0:T(8,128)(2,1)S(1)} all-gather(bf16[200,768]{1,0:T(8,128)(2,1)S(1)} %add_convert_fusion.1), channel_id=1, replica_groups=mesh['fa'=16,'fb'=4,'tp'=2] {'tp'}, dimensions={0}, use_global_device_ids=true | all-gather | bytes 921600 | tf_op jit(solution)/shard_map/all_gather | solution.py:210
  231.5 5.2 gather_fusion
  239.8 6.7 all-to-all-start.1
  246.5 9.2 %all_gather.14 = bf16[400,768]{1,0:T(8,128)(2,1)S(1)} all-gather(bf16[200,768]{1,0:T(8,128)(2,1)S(1)} %convert_element_type.179), channel_id=1, replica_groups=mesh['fa'=16,'fb'=4,'tp'=2] {'tp'}, dimensions={0}, use_global_device_ids=true | all-gather | bytes 921600 | tf_op jit(solution)/shard_map/all_gather | solution.py:210
  255.8 5.3 gather_fusion.2
  266.6 5.3 scatter_custom_fusion.2
  275.4 6.3 all-to-all-start.5
  281.7 4.9 reshape.296
  286.6 4.9 reshape.298
  294.0 7.3 %fusion.112 = f32[1008,1536]{1,0:T(8,128)} fusion(bf16[1008,768]{1,0:T(8,128)(2,1)} %reshape.294, bf16[768,1536]{1,0:T(8,128)(2,1)} %reshape.296), kind=kOutput, calls=%fused_computation.179 | convolution fusion | flops 2378170368 | bytes 10100736 | tf_op jit(solution)/shard_map/dot_general | solution.py:308
  303.8 20.0 %add_convert_fusion = (bf16[1008,1536]{1,0:T(8,128)(2,1)}, f32[1008,1536]{1,0:T(8,128)S(1)}) fusion(f32[1008,1536]{1,0:T(8,128)} %fusion.112, bf16[1008,768]{1,0:T(8,128)(2,1)} %reshape.304, bf16[768,1536]{1,0:T(8,128)(2,1)} %reshape.298), kind=kOutput, calls=%fused_computation.14 | convolution fusion | flops 2489647104 | bytes 19390464 | tf_op jit(solution)/shard_map/dot_general | solution.py:326
  327.1 5.4 convolution_convert_fusion.4
  335.1 6.7 all-to-all-start.4
  341.7 6.3 convolution_convert_fusion.3
  350.6 10.3 %all-to-all-done.4 = bf16[16,63,768]{2,1,0:T(8,128)(2,1)} async-done(((bf16[16,63,768]{2,1,0:T(8,128)(2,1)}), bf16[16,63,768]{2,1,0:T(8,128)(2,1)}, u32[]{:S(2)}, u32[]{:S(2)}) %all-to-all-start.4) | async-done | bytes 1548320 | tf_op jit(solution)/shard_map/all_to_all | solution.py:225
  360.9 6.7 all-to-all-start.6
  370.9 6.6 gather_fusion.1
  377.5 4.1 reshape.302
  381.6 8.1 %multiply_reduce_fusion.1 = (f32[400,2]{1,0:T(8,128)S(1)}, f32[400,768]{1,0:T(8,128)}) fusion(f32[400,2,768]{2,1,0:T(2,128)} %reshape.302, f32[400,768]{1,0:T(8,128)S(1)} %convert_element_type.180, f32[400,2]{1,0:T(8,128)S(1)} %copy.266), kind=kLoop, calls=%fused_computation.38 | loop fusion | flops 2149600 | bytes 4921600 | tf_op jit(solution)/shard_map/reduce_sum | solution.py:324
  393.6 6.6 gather_fusion.3
  404.3 4.6 reduce_sum.246
  415.6 6.4 convolution_convert_fusion
  422.0 4.9 reshape.312
  426.9 10.7 %all-to-all-start.9 = ((bf16[64,12,1536]{2,1,0:T(8,128)(2,1)}), bf16[64,12,1536]{2,1,0:T(8,128)(2,1)}, u32[]{:S(2)}, u32[]{:S(2)}) async-start(bf16[64,12,1536]{2,1,0:T(8,128)(2,1)} %reshape.312), calls=%async_computation.13 | async-start | bytes 6291456 | tf_op jit(solution)/shard_map/all_to_all | solution.py:242
  442.1 48.9 %reduce-scatter.7.cloned.1.call-done = f32[200,768]{1,0:T(8,128)} async-done(((f32[400,768]{1,0:T(8,128)}), f32[200,768]{1,0:T(8,128)}) %reduce-scatter.7.cloned.1.call-update) | async-done | bytes 614416 | tf_op jit(solution)/shard_map/reduce_scatter | solution.py:214
  493.5 10.8 %all_gather.15 = bf16[400,768]{1,0:T(8,128)(2,1)S(1)} all-gather(bf16[200,768]{1,0:T(8,128)(2,1)S(1)} %get-tuple-element.73), channel_id=1, replica_groups=mesh['fa'=16,'fb'=4,'tp'=2] {'tp'}, dimensions={0}, use_global_device_ids=true | all-gather | bytes 921600 | tf_op jit(solution)/shard_map/all_gather | solution.py:210
  509.2 4.4 fusion.49
  519.4 5.4 fusion.50
  527.5 5.4 fusion.53
  541.2 6.4 convolution_convert_fusion.1
  547.5 4.8 reshape.311
  552.4 7.5 %all-to-all-start.8 = ((bf16[64,12,1536]{2,1,0:T(8,128)(2,1)}), bf16[64,12,1536]{2,1,0:T(8,128)(2,1)}, u32[]{:S(2)}, u32[]{:S(2)}) async-start(bf16[64,12,1536]{2,1,0:T(8,128)(2,1)} %reshape.311), calls=%async_computation.12 | async-start | bytes 6291456 | tf_op jit(solution)/shard_map/all_to_all | solution.py:242
  569.2 4.9 concatenate.30
  578.9 5.9 concatenate.37
  584.8 15.0 %all-to-all-done.8 = bf16[64,12,1536]{2,1,0:T(8,128)(2,1)} async-done(((bf16[64,12,1536]{2,1,0:T(8,128)(2,1)}), bf16[64,12,1536]{2,1,0:T(8,128)(2,1)}, u32[]{:S(2)}, u32[]{:S(2)}) %all-to-all-start.8) | async-done | bytes 2359328 | tf_op jit(solution)/shard_map/all_to_all | solution.py:242
  599.7 18.9 %all-to-all-start.7 = ((bf16[64,12,1576]{2,1,0:T(8,128)(2,1)}), bf16[64,12,1576]{2,1,0:T(8,128)(2,1)}, u32[]{:S(2)}, u32[]{:S(2)}) async-start(bf16[64,12,1576]{2,1,0:T(8,128)(2,1)} %concatenate.37), calls=%async_computation.11 | async-start | bytes 6815744 | tf_op jit(solution)/shard_map/all_to_all | solution.py:188
  628.8 32.8 %all-to-all-done.7 = bf16[64,12,1576]{2,1,0:T(8,128)(2,1)} async-done(((bf16[64,12,1576]{2,1,0:T(8,128)(2,1)}), bf16[64,12,1576]{2,1,0:T(8,128)(2,1)}, u32[]{:S(2)}, u32[]{:S(2)}) %all-to-all-start.7) | async-done | bytes 2420768 | tf_op jit(solution)/shard_map/all_to_all | solution.py:188
  665.9 5.3 psum.7
  (245 shorter events, 153.5 us)
Async XLA Ops:
  13.8 10.7 %copy-start.14 = (bf16[12,16,1536]{2,1,0:T(8,128)(2,1)S(1)}, bf16[12,16,1536]{2,1,0:T(8,128)(2,1)}, u32[]{:S(2)}) copy-start(bf16[12,16,1536]{2,1,0:T(8,128)(2,1)} %param.21) | copy-start | bytes 1769476
  13.8 11.0 %copy-start = (f32[200,768]{1,0:T(8,128)S(1)}, f32[200,768]{1,0:T(8,128)}, u32[]{:S(2)}) copy-start(f32[200,768]{1,0:T(8,128)} %param.12) | copy-start | bytes 1843204
  13.8 53.7 %all-to-all-start = ((bf16[64,12,1556]{2,1,0:T(8,128)(2,1)}), bf16[64,12,1556]{2,1,0:T(8,128)(2,1)}, u32[]{:S(2)}, u32[]{:S(2)}) async-start(bf16[64,12,1556]{2,1,0:T(8,128)(2,1)} %broadcast_in_dim.54), calls=%async_computation | async-start | bytes 6815744 | tf_op jit(solution)/shard_map/all_to_all | solution.py:149
  25.0 125.2 %copy-start.43 = (pred[200]{0:T(512)(128)(4,1)}, pred[200]{0:T(512)(128)(4,1)S(1)}, u32[]{:S(2)}) copy-start(pred[200]{0:T(512)(128)(4,1)S(1)} %iota_compare_fusion.3) | copy-start | bytes 604
  25.0 58.2 %copy-start.26 = (f32[200]{0:T(256)}, f32[200]{0:T(256)S(1)}, u32[]{:S(2)}) copy-start(f32[200]{0:T(256)S(1)} %broadcast_multiply_fusion.6) | copy-start | bytes 2404
  25.2 57.9 %copy-start.34 = (f32[200]{0:T(256)}, f32[200]{0:T(256)S(1)}, u32[]{:S(2)}) copy-start(f32[200]{0:T(256)S(1)} %add_rsqrt_fusion.1) | copy-start | bytes 2404
  69.6 95.3 %all-to-all-start.2 = ((bf16[12,64,1536]{2,0,1:T(8,128)(2,1)}), bf16[12,64,1536]{2,0,1:T(8,128)(2,1)}, u32[]{:S(2)}, u32[]{:S(2)}) async-start(bf16[12,64,1536]{2,0,1:T(8,128)(2,1)} %bitcast.115), calls=%async_computation.3 | async-start | bytes 6291456 | tf_op jit(solution)/shard_map/all_to_all | solution.py:232
  77.0 142.1 %reduce-scatter.5.cloned.1.call-start = ((), (), s32[]{:S(2)}) async-start(), calls=%async_computation.14 | async-start | bytes 1843200 | tf_op jit(solution)/shard_map/reduce_scatter | solution.py:214
  81.2 77.6 %copy-start.1 = (bf16[768,1556]{1,0:T(8,128)(2,1)}, bf16[768,1556]{1,0:T(8,128)(2,1)S(1)}, u32[]{:S(2)}) copy-start(bf16[768,1556]{1,0:T(8,128)(2,1)S(1)} %reshape.289) | copy-start | bytes 7170052
  154.6 6.8 %copy-start.23 = (s32[400,2]{0,1:T(2,128)S(1)}, s32[400,2]{0,1:T(2,128)}, u32[]{:S(2)}) copy-start(s32[400,2]{0,1:T(2,128)} %param.13) | copy-start | bytes 9604
  161.4 3.0 copy-start.15
  167.0 72.8 %all-to-all-start.3 = ((bf16[12,64,1536]{2,0,1:T(8,128)(2,1)}), bf16[12,64,1536]{2,0,1:T(8,128)(2,1)}, u32[]{:S(2)}, u32[]{:S(2)}) async-start(bf16[12,64,1536]{2,0,1:T(8,128)(2,1)} %bitcast.116), calls=%async_computation.4 | async-start | bytes 6291456 | tf_op jit(solution)/shard_map/all_to_all | solution.py:232
  220.4 16.4 %copy-start.29 = (f32[200]{0:T(256)}, f32[200]{0:T(256)S(1)}, u32[]{:S(2)}) copy-start(f32[200]{0:T(256)S(1)} %broadcast_multiply_fusion.5) | copy-start | bytes 2404
  220.6 16.2 %copy-start.37 = (f32[200]{0:T(256)}, f32[200]{0:T(256)S(1)}, u32[]{:S(2)}) copy-start(f32[200]{0:T(256)S(1)} %add_rsqrt_fusion) | copy-start | bytes 2404
  239.8 6.7 copy-start.4
  239.8 35.6 %all-to-all-start.1 = ((bf16[16,63,768]{2,1,0:T(8,128)(2,1)}), bf16[16,63,768]{2,1,0:T(8,128)(2,1)}, u32[]{:S(2)}, u32[]{:S(2)}) async-start(bf16[16,63,768]{2,1,0:T(8,128)(2,1)} %broadcast_select_fusion), calls=%async_computation.2 | async-start | bytes 3145728 | tf_op jit(solution)/shard_map/all_to_all | solution.py:218
  275.4 25.9 %all-to-all-start.5 = ((bf16[16,63,768]{2,1,0:T(8,128)(2,1)}), bf16[16,63,768]{2,1,0:T(8,128)(2,1)}, u32[]{:S(2)}, u32[]{:S(2)}) async-start(bf16[16,63,768]{2,1,0:T(8,128)(2,1)} %select_convert_fusion), calls=%async_computation.7 | async-start | bytes 3145728 | tf_op jit(solution)/shard_map/all_to_all | solution.py:218
  303.8 20.0 %copy-start.2 = (f32[1008,1536]{1,0:T(8,128)S(1)}, f32[1008,1536]{1,0:T(8,128)}, u32[]{:S(2)}) copy-start(f32[1008,1536]{1,0:T(8,128)} %fusion.112) | copy-start | bytes 18579460
  335.1 25.8 %all-to-all-start.4 = ((bf16[16,63,768]{2,1,0:T(8,128)(2,1)}), bf16[16,63,768]{2,1,0:T(8,128)(2,1)}, u32[]{:S(2)}, u32[]{:S(2)}) async-start(bf16[16,63,768]{2,1,0:T(8,128)(2,1)} %reshape.299), calls=%async_computation.5 | async-start | bytes 3145728 | tf_op jit(solution)/shard_map/all_to_all | solution.py:225
  360.9 29.7 %all-to-all-start.6 = ((bf16[16,63,768]{2,1,0:T(8,128)(2,1)}), bf16[16,63,768]{2,1,0:T(8,128)(2,1)}, u32[]{:S(2)}, u32[]{:S(2)}) async-start(bf16[16,63,768]{2,1,0:T(8,128)(2,1)} %reshape.305), calls=%async_computation.8 | async-start | bytes 3145728 | tf_op jit(solution)/shard_map/all_to_all | solution.py:225
  367.6 72.5 %reduce-scatter.9.cloned.1.call-start = ((), (), s32[]{:S(2)}) async-start(), calls=%async_computation.16 | async-start | bytes 1843200 | tf_op jit(solution)/shard_map/reduce_scatter | solution.py:214
  367.8 9.6 %copy-start.24 = (s32[1024]{0:T(1024)}, s32[1024]{0:T(1024)S(1)}, u32[]{:S(2)}) copy-start(s32[1024]{0:T(1024)S(1)} %pad_clamp_fusion) | copy-start | bytes 12292
  389.6 4.0 copy-start.25
  408.9 3.6 copy-start.8
  408.9 3.6 copy-start.44
  411.7 79.3 %reduce-scatter.7.cloned.1.call-start = ((), (), s32[]{:S(2)}) async-start(), calls=%async_computation.15 | async-start | bytes 1843200 | tf_op jit(solution)/shard_map/reduce_scatter | solution.py:214
  426.9 13.2 %copy-start.30 = (f32[200]{0:T(256)S(1)}, f32[200]{0:T(256)}, u32[]{:S(2)}) copy-start(f32[200]{0:T(256)} %copy-done.29) | copy-start | bytes 2404
  426.9 13.2 %copy-start.38 = (f32[200]{0:T(256)S(1)}, f32[200]{0:T(256)}, u32[]{:S(2)}) copy-start(f32[200]{0:T(256)} %copy-done.37) | copy-start | bytes 2404
  426.9 64.1 %copy-start.5 = (f32[200,768]{1,0:T(8,128)S(1)}, f32[200,768]{1,0:T(8,128)}, u32[]{:S(2)}) copy-start(f32[200,768]{1,0:T(8,128)} %param.23) | copy-start | bytes 1843204
  426.9 125.5 %all-to-all-start.9 = ((bf16[64,12,1536]{2,1,0:T(8,128)(2,1)}), bf16[64,12,1536]{2,1,0:T(8,128)(2,1)}, u32[]{:S(2)}, u32[]{:S(2)}) async-start(bf16[64,12,1536]{2,1,0:T(8,128)(2,1)} %reshape.312), calls=%async_computation.13 | async-start | bytes 6291456 | tf_op jit(solution)/shard_map/all_to_all | solution.py:242
  437.6 136.7 %reduce-scatter.11.cloned.1.call-start = ((), (), s32[]{:S(2)}) async-start(), calls=%async_computation.17 | async-start | bytes 1843200 | tf_op jit(solution)/shard_map/reduce_scatter | solution.py:214
  532.8 3.7 copy-start.12
  532.8 3.8 copy-start.11
  552.3 8.7 %copy-start.40 = (f32[768]{0:T(1024)S(1)}, f32[768]{0:T(1024)}, u32[]{:S(2)}) copy-start(f32[768]{0:T(1024)} %get-tuple-element.61) | copy-start | bytes 9220
  552.4 9.5 %copy-start.39 = (f32[768]{0:T(1024)S(1)}, f32[768]{0:T(1024)}, u32[]{:S(2)}) copy-start(f32[768]{0:T(1024)} %get-tuple-element.67) | copy-start | bytes 9220
  552.4 47.4 %all-to-all-start.8 = ((bf16[64,12,1536]{2,1,0:T(8,128)(2,1)}), bf16[64,12,1536]{2,1,0:T(8,128)(2,1)}, u32[]{:S(2)}, u32[]{:S(2)}) async-start(bf16[64,12,1536]{2,1,0:T(8,128)(2,1)} %reshape.311), calls=%async_computation.12 | async-start | bytes 6291456 | tf_op jit(solution)/shard_map/all_to_all | solution.py:242
  560.2 2.9 copy-start.10
  562.9 2.1 copy-start.13
  563.1 1.9 copy-start.19
  569.2 5.2 copy-start.21
  569.2 5.2 copy-start.27
  569.2 5.2 copy-start.35
  569.2 7.5 %copy-start.31 = (f32[64,12,1]{0,2,1:T(1,128)S(1)}, f32[64,12,1]{0,2,1:T(1,128)}, u32[]{:S(2)}) copy-start(f32[64,12,1]{0,2,1:T(1,128)} %copy.297) | copy-start | bytes 9220
  569.2 7.5 %copy-start.32 = (f32[64,12,1]{0,2,1:T(1,128)S(1)}, f32[64,12,1]{0,2,1:T(1,128)}, u32[]{:S(2)}) copy-start(f32[64,12,1]{0,2,1:T(1,128)} %copy.298) | copy-start | bytes 9220
  599.7 61.8 %all-to-all-start.7 = ((bf16[64,12,1576]{2,1,0:T(8,128)(2,1)}), bf16[64,12,1576]{2,1,0:T(8,128)(2,1)}, u32[]{:S(2)}, u32[]{:S(2)}) async-start(bf16[64,12,1576]{2,1,0:T(8,128)(2,1)} %concatenate.37), calls=%async_computation.11 | async-start | bytes 6815744 | tf_op jit(solution)/shard_map/all_to_all | solution.py:188
  625.9 1.8 copy-start.42
  625.9 1.8 copy-start.41
  625.9 1.8 copy-start.6
  (11 other events, 14.4 us)
Sparse Core Ops, SparseCore 0:
  161.6 57.5 reduce-scatter.4
  411.9 28.1 reduce-scatter.8
  442.4 48.5 reduce-scatter.6
  541.3 32.9 reduce-scatter.10

commit v8 on v7

--- a/solution.py
+++ b/solution.py
@@ -207,11 +207,18 @@
 
 
 def group_rows(value):
-    return lax.all_gather(value, "tp", axis=0, tiled=True)
+    halves = lax.axis_size("tp")
+    spread = jnp.broadcast_to(value[None], (halves,) + value.shape)
+    moved = lax.all_to_all(spread, "tp", split_axis=0, concat_axis=0, tiled=True)
+    return moved.reshape(-1, value.shape[1])
 
 
 def owned_rows(value):
-    return lax.psum_scatter(value, "tp", scatter_dimension=0, tiled=True)
+    halves = lax.axis_size("tp")
+    moved = lax.all_to_all(
+        value.reshape(halves, -1, value.shape[1]), "tp", split_axis=0, concat_axis=0, tiled=True
+    )
+    return jnp.sum(moved, axis=0)
 
 
 def to_owners(slots):

time: 692 us -> 656 us (0.948)
  blocking collectives: 75.9 us -> 20.8 us
  starting transfers between devices: 88.6 us -> 108 us
  between operations: 14.9 us -> 1.81 us
  waiting for transfers between devices: 187 us -> 199 us
    reduce_scatter x4 -> x0, waiting for transfers between devices: 86.2 us -> none  [owned_rows(): return lax.psum_scatter(value, 'tp', scatter_dimension=0, tiled=True)]
    all_gather x4 -> x0, blocking collectives: 70.6 us -> none  [group_rows(): return lax.all_gather(value, 'tp', axis=0, tiled=True)]
    all_to_all x2, waiting for transfers between devices: 0.01 us -> 57.2 us  [expert_weights(): lax.all_to_all(spread.reshape(rows, experts * holders, units), FSDP, spli...]
    all_to_all x0 -> x7, waiting for transfers between devices: none -> 44 us  [the longest x3 33.4 us: owned_rows(): lax.all_to_all(value.reshape(halves, -1, value.shape[1]), 'tp', split_axi...]
    all_to_all x0 -> x7, starting transfers between devices: none -> 30.2 us  [the longest x4 16.5 us: group_rows(): lax.all_to_all(spread, 'tp', split_axis=0, concat_axis=0, tiled=True)]
    all_to_all x0 -> x1, blocking collectives: none -> 15.5 us  [owned_rows(): lax.all_to_all(value.reshape(halves, -1, value.shape[1]), 'tp', split_axi...]
    all_to_all x1, starting transfers between devices: 18.9 us -> 7.21 us  [reduce_dense(): lax.all_to_all(wire.reshape(holders, rows, wire.shape[1]), FSDP, split_ax...]
    dot_general x0 -> x6, local copies, waits for them, and re-layouts: none -> 8.49 us  [the longest x4 5.85 us: per_device(): jnp.einsum('td,ith->idh', tokens_a, stacked, preferred_element_type=f32)]
  transfers between devices with their start and end apart: 14 -> 17, of which waited for: 8 -> 14; matrix products, arithmetic and copies ran while one was open for 36% -> 36% of each run, Pallas kernels for 0% -> 0%
where the time goes in v8:
time: 656 us; the launch traced here: 644 us
  waiting for transfers between devices  199 us (30%)
  local copies, waits for them, and re-layouts  176 us (27%)
  starting transfers between devices  108 us (16%)
  matrix products  98.6 us (15%)
  other arithmetic  39.5 us (6%)
  blocking collectives  20.8 us (3%)
    all_to_all x2, waiting for transfers between devices, expert_weights(): lax.all_to_all(spread.reshape(rows, experts * holders, units), FSDP, spli...  57.2 us
    all_to_all x1, waiting for transfers between devices, gather_dense(): full = lax.all_to_all(spread, FSDP, split_axis=0, concat_axis=0, tiled=True)  42.7 us
    all_to_all x3, waiting for transfers between devices, owned_rows(): lax.all_to_all(value.reshape(halves, -1, value.shape[1]), 'tp', split_axi...  33.4 us
    all_to_all x1, waiting for transfers between devices, reduce_dense(): lax.all_to_all(wire.reshape(holders, rows, wire.shape[1]), FSDP, split_ax...  33.1 us
    all_to_all x2, starting transfers between devices, weight_home(): lax.all_to_all(partial.astype(jnp.bfloat16).reshape(devices, rows, units)...  21 us
    dot_general x1, matrix products, per_device(): owner_hgrad = jnp.dot(owner_g, own_out, preferred_element_type=f32)  20 us
    all_to_all x4, starting transfers between devices, group_rows(): lax.all_to_all(spread, 'tp', split_axis=0, concat_axis=0, tiled=True)  16.5 us
    all_to_all x2, starting transfers between devices, expert_weights(): lax.all_to_all(spread.reshape(rows, experts * holders, units), FSDP, spli...  15.8 us
  transfers between devices with their start and end apart: 17, of which 14 were waited for; matrix products, arithmetic and copies ran while one was open for 36% of the time, Pallas kernels for 0%

profile of v8, /device:TPU:1, one launch (start us, length us, event | category | flops | bytes accessed | tf_op | source)
XLA Modules:
  0.0 643.7 jit_solution(5332075376050426592)
XLA Ops:
  7.3 10.6 %all-to-all-start = ((bf16[64,12,1556]{2,1,0:T(8,128)(2,1)}), bf16[64,12,1556]{2,1,0:T(8,128)(2,1)}, u32[]{:S(2)}, u32[]{:S(2)}) async-start(bf16[64,12,1556]{2,1,0:T(8,128)(2,1)} %broadcast_in_dim.62), calls=%async_computation | async-start | bytes 6815744 | tf_op jit(solution)/shard_map/all_to_all | solution.py:149
  18.3 42.7 %all-to-all-done = bf16[64,12,1556]{2,1,0:T(8,128)(2,1)} async-done(((bf16[64,12,1556]{2,1,0:T(8,128)(2,1)}), bf16[64,12,1556]{2,1,0:T(8,128)(2,1)}, u32[]{:S(2)}, u32[]{:S(2)}) %all-to-all-start) | async-done | bytes 2390048 | tf_op jit(solution)/shard_map/all_to_all | solution.py:149
  67.6 4.6 all-to-all-start.1
  107.2 4.4 convolution_convert_fusion.7
  114.3 4.4 all-to-all-start.2
  118.9 15.2 %all-to-all-done.2 = f32[2,200,768]{2,1,0:T(8,128)S(1)} async-done(((f32[2,200,768]{2,1,0:T(8,128)}), f32[2,200,768]{2,1,0:T(8,128)S(1)}, u32[]{:S(2)}, u32[]{:S(2)}) %all-to-all-start.2) | async-done | bytes 1228832 | tf_op jit(solution)/shard_map/all_to_all | solution.py:218
  136.2 8.6 %all-to-all-start.5 = ((bf16[12,64,1536]{2,0,1:T(8,128)(2,1)}), bf16[12,64,1536]{2,0,1:T(8,128)(2,1)}, u32[]{:S(2)}, u32[]{:S(2)}) async-start(bf16[12,64,1536]{2,0,1:T(8,128)(2,1)} %bitcast.133), calls=%async_computation.5 | async-start | bytes 6291456 | tf_op jit(solution)/shard_map/all_to_all | solution.py:239
  145.6 39.3 %all-to-all-done.5 = bf16[12,64,1536]{2,0,1:T(8,128)(2,1)} async-done(((bf16[12,64,1536]{2,0,1:T(8,128)(2,1)}), bf16[12,64,1536]{2,0,1:T(8,128)(2,1)}, u32[]{:S(2)}, u32[]{:S(2)}) %all-to-all-start.5) | async-done | bytes 2359328 | tf_op jit(solution)/shard_map/all_to_all | solution.py:239
  189.8 10.3 %all-to-all-done.3 = bf16[2,200,768]{2,1,0:T(8,128)(2,1)S(1)} async-done(((bf16[2,200,768]{2,1,0:T(8,128)(2,1)}), bf16[2,200,768]{2,1,0:T(8,128)(2,1)S(1)}, u32[]{:S(2)}, u32[]{:S(2)}) %all-to-all-start.3) | async-done | bytes 614432 | tf_op jit(solution)/shard_map/all_to_all | solution.py:212
  202.2 7.1 %all-to-all-start.6 = ((bf16[12,64,1536]{2,0,1:T(8,128)(2,1)}), bf16[12,64,1536]{2,0,1:T(8,128)(2,1)}, u32[]{:S(2)}, u32[]{:S(2)}) async-start(bf16[12,64,1536]{2,0,1:T(8,128)(2,1)} %bitcast.132), calls=%async_computation.6 | async-start | bytes 6291456 | tf_op jit(solution)/shard_map/all_to_all | solution.py:239
  212.5 5.3 scatter_custom_fusion.1
  217.8 5.3 scatter_custom_fusion
  223.2 5.2 gather_fusion
  231.5 17.9 %all-to-all-done.6 = bf16[12,64,1536]{2,0,1:T(8,128)(2,1)} async-done(((bf16[12,64,1536]{2,0,1:T(8,128)(2,1)}), bf16[12,64,1536]{2,0,1:T(8,128)(2,1)}, u32[]{:S(2)}, u32[]{:S(2)}) %all-to-all-start.6) | async-done | bytes 2359328 | tf_op jit(solution)/shard_map/all_to_all | solution.py:239
  249.4 5.5 all-to-all-start.4
  256.1 5.2 gather_fusion.2
  266.2 5.3 scatter_custom_fusion.2
  275.5 6.6 %all-to-all-start.10 = ((bf16[16,63,768]{2,1,0:T(8,128)(2,1)}), bf16[16,63,768]{2,1,0:T(8,128)(2,1)}, u32[]{:S(2)}, u32[]{:S(2)}) async-start(bf16[16,63,768]{2,1,0:T(8,128)(2,1)} %select_convert_fusion), calls=%async_computation.10 | async-start | bytes 3145728 | tf_op jit(solution)/shard_map/all_to_all | solution.py:225
  282.1 4.9 reshape.330
  287.0 4.9 reshape.332
  294.5 7.3 %fusion.111 = f32[1008,1536]{1,0:T(8,128)} fusion(bf16[1008,768]{1,0:T(8,128)(2,1)} %reshape.328, bf16[768,1536]{1,0:T(8,128)(2,1)} %reshape.330), kind=kOutput, calls=%fused_computation.180 | convolution fusion | flops 2378170368 | bytes 10100736 | tf_op jit(solution)/shard_map/dot_general | solution.py:315
  304.8 20.0 %add_convert_fusion = (bf16[1008,1536]{1,0:T(8,128)(2,1)}, f32[1008,1536]{1,0:T(8,128)S(1)}) fusion(f32[1008,1536]{1,0:T(8,128)} %fusion.111, bf16[1008,768]{1,0:T(8,128)(2,1)} %reshape.339, bf16[768,1536]{1,0:T(8,128)(2,1)} %reshape.332), kind=kOutput, calls=%fused_computation.14 | convolution fusion | flops 2489647104 | bytes 19390464 | tf_op jit(solution)/shard_map/dot_general | solution.py:333
  328.1 5.4 convolution_convert_fusion.4
  336.1 6.2 all-to-all-start.7
  342.3 6.3 convolution_convert_fusion.3
  351.2 11.1 %all-to-all-done.7 = bf16[16,63,768]{2,1,0:T(8,128)(2,1)} async-done(((bf16[16,63,768]{2,1,0:T(8,128)(2,1)}), bf16[16,63,768]{2,1,0:T(8,128)(2,1)}, u32[]{:S(2)}, u32[]{:S(2)}) %all-to-all-start.7) | async-done | bytes 1548320 | tf_op jit(solution)/shard_map/all_to_all | solution.py:232
  362.3 4.8 all-to-all-start.11
  370.1 6.6 %gather_fusion.1 = f32[800,768]{1,0:T(8,128)} fusion(f32[1008,768]{1,0:T(8,128)} %reshape.358, s32[1024]{0:T(1024)S(1)} %pad_clamp_fusion), kind=kCustom, calls=%fused_computation.1 | custom fusion | bytes 4918400 | tf_op jit(solution)/shard_map/gather | solution.py:319
  380.8 8.2 %multiply_reduce_fusion.1 = (f32[400,2]{1,0:T(8,128)S(1)}, f32[400,768]{1,0:T(8,128)}) fusion(f32[400,2,768]{2,1,0:T(2,128)} %reshape.336, f32[400,768]{1,0:T(8,128)S(1)} %convert.24, f32[400,2]{1,0:T(8,128)S(1)} %copy.279), kind=kLoop, calls=%fused_computation.39 | loop fusion | flops 2149600 | bytes 4921600 | tf_op jit(solution)/shard_map/reduce_sum | solution.py:331
  392.2 6.6 %gather_fusion.3 = f32[800,768]{1,0:T(8,128)} fusion(f32[1008,768]{1,0:T(8,128)} %reshape.361, s32[1024]{0:T(1024)S(1)} %pad_clamp_fusion), kind=kCustom, calls=%fused_computation.3 | custom fusion | bytes 4918400 | tf_op jit(solution)/shard_map/gather | solution.py:344
  402.9 4.6 reduce_sum.284
  409.2 15.5 %all_to_all.110 = f32[2,200,768]{2,1,0:T(8,128)S(1)} all-to-all(f32[2,200,768]{2,1,0:T(8,128)S(1)} %bitcast.138), channel_id=1, replica_groups=mesh['fa'=16,'fb'=4,'tp'=2] {'tp'}, dimensions={0} | all-to-all | bytes 2457600 | tf_op jit(solution)/shard_map/all_to_all | solution.py:218
  424.6 4.5 all-to-all-start.8
  429.7 11.6 %all-to-all-done.8 = f32[2,200,768]{2,1,0:T(8,128)} async-done(((f32[2,200,768]{2,1,0:T(8,128)}), f32[2,200,768]{2,1,0:T(8,128)}, u32[]{:S(2)}, u32[]{:S(2)}) %all-to-all-start.8) | async-done | bytes 1228832 | tf_op jit(solution)/shard_map/all_to_all | solution.py:218
  448.7 6.4 convolution_convert_fusion
  455.2 4.8 reshape.351
  460.0 13.5 %all-to-all-start.17 = ((bf16[64,12,1536]{2,1,0:T(8,128)(2,1)}), bf16[64,12,1536]{2,1,0:T(8,128)(2,1)}, u32[]{:S(2)}, u32[]{:S(2)}) async-start(bf16[64,12,1536]{2,1,0:T(8,128)(2,1)} %reshape.351), calls=%async_computation.17 | async-start | bytes 6291456 | tf_op jit(solution)/shard_map/all_to_all | solution.py:249
  494.2 5.4 fusion.49
  507.5 6.0 all-to-all-done.17
  513.5 4.8 all-to-all-start.14
  518.3 5.8 convolution_convert_fusion.1
  524.1 4.8 reshape.350
  528.9 6.6 %all-to-all-done.14 = f32[2,200,768]{2,1,0:T(8,128)S(1)} async-done(((f32[2,200,768]{2,1,0:T(8,128)}), f32[2,200,768]{2,1,0:T(8,128)S(1)}, u32[]{:S(2)}, u32[]{:S(2)}) %all-to-all-start.14) | async-done | bytes 1228832 | tf_op jit(solution)/shard_map/all_to_all | solution.py:218
  535.5 7.6 %all-to-all-start.16 = ((bf16[64,12,1536]{2,1,0:T(8,128)(2,1)}), bf16[64,12,1536]{2,1,0:T(8,128)(2,1)}, u32[]{:S(2)}, u32[]{:S(2)}) async-start(bf16[64,12,1536]{2,1,0:T(8,128)(2,1)} %reshape.350), calls=%async_computation.16 | async-start | bytes 6291456 | tf_op jit(solution)/shard_map/all_to_all | solution.py:249
  562.9 4.6 convolution_convert_fusion.2
  582.9 7.2 %all-to-all-start.15 = ((bf16[64,12,1576]{2,1,0:T(8,128)(2,1)}), bf16[64,12,1576]{2,1,0:T(8,128)(2,1)}, u32[]{:S(2)}, u32[]{:S(2)}) async-start(bf16[64,12,1576]{2,1,0:T(8,128)(2,1)} %copy.317), calls=%async_computation.15 | async-start | bytes 6815744 | tf_op jit(solution)/shard_map/all_to_all | solution.py:188
  600.1 33.1 %all-to-all-done.15 = bf16[64,12,1576]{2,1,0:T(8,128)(2,1)} async-done(((bf16[64,12,1576]{2,1,0:T(8,128)(2,1)}), bf16[64,12,1576]{2,1,0:T(8,128)(2,1)}, u32[]{:S(2)}, u32[]{:S(2)}) %all-to-all-start.15) | async-done | bytes 2420768 | tf_op jit(solution)/shard_map/all_to_all | solution.py:188
  637.5 5.3 psum.7
  (236 shorter events, 194.1 us)
Async XLA Ops:
  7.3 10.7 %copy-start = (f32[200,768]{1,0:T(8,128)S(1)}, f32[200,768]{1,0:T(8,128)}, u32[]{:S(2)}) copy-start(f32[200,768]{1,0:T(8,128)} %param.12) | copy-start | bytes 1843204
  7.3 53.7 %all-to-all-start = ((bf16[64,12,1556]{2,1,0:T(8,128)(2,1)}), bf16[64,12,1556]{2,1,0:T(8,128)(2,1)}, u32[]{:S(2)}, u32[]{:S(2)}) async-start(bf16[64,12,1556]{2,1,0:T(8,128)(2,1)} %broadcast_in_dim.62), calls=%async_computation | async-start | bytes 6815744 | tf_op jit(solution)/shard_map/all_to_all | solution.py:149
  18.1 47.6 %copy-start.31 = (f32[200]{0:T(256)}, f32[200]{0:T(256)S(1)}, u32[]{:S(2)}) copy-start(f32[200]{0:T(256)S(1)} %broadcast_multiply_fusion.6) | copy-start | bytes 2404
  18.3 47.4 %copy-start.33 = (f32[200]{0:T(256)}, f32[200]{0:T(256)S(1)}, u32[]{:S(2)}) copy-start(f32[200]{0:T(256)S(1)} %add_rsqrt_fusion.1) | copy-start | bytes 2404
  65.2 46.5 %copy-start.2 = (bf16[768,1556]{1,0:T(8,128)(2,1)}, bf16[768,1556]{1,0:T(8,128)(2,1)S(1)}, u32[]{:S(2)}) copy-start(bf16[768,1556]{1,0:T(8,128)(2,1)S(1)} %reshape.322) | copy-start | bytes 7170052
  67.6 15.1 %all-to-all-start.1 = ((bf16[2,200,768]{2,1,0:T(8,128)(2,1)}), bf16[2,200,768]{2,1,0:T(8,128)(2,1)}, u32[]{:S(2)}, u32[]{:S(2)}) async-start(bf16[2,200,768]{2,1,0:T(8,128)(2,1)} %broadcast_in_dim.63), calls=%async_computation.1 | async-start | bytes 1228800 | tf_op jit(solution)/shard_map/all_to_all | solution.py:212
  73.3 33.8 %copy-start.35 = (pred[200]{0:T(512)(128)(4,1)}, pred[200]{0:T(512)(128)(4,1)S(1)}, u32[]{:S(2)}) copy-start(pred[200]{0:T(512)(128)(4,1)S(1)} %iota_compare_fusion.3) | copy-start | bytes 604
  83.6 30.7 %all-to-all-start.9 = ((bf16[2,200,768]{2,1,0:T(8,128)(2,1)}), bf16[2,200,768]{2,1,0:T(8,128)(2,1)}, u32[]{:S(2)}, u32[]{:S(2)}) async-start(bf16[2,200,768]{2,1,0:T(8,128)(2,1)} %broadcast_in_dim.79), calls=%async_computation.9 | async-start | bytes 1228800 | tf_op jit(solution)/shard_map/all_to_all | solution.py:212
  114.2 4.4 copy-start.23
  114.3 19.8 %all-to-all-start.2 = ((f32[2,200,768]{2,1,0:T(8,128)}), f32[2,200,768]{2,1,0:T(8,128)S(1)}, u32[]{:S(2)}, u32[]{:S(2)}) async-start(f32[2,200,768]{2,1,0:T(8,128)} %fusion.58), calls=%async_computation.2 | async-start | bytes 2457600 | tf_op jit(solution)/shard_map/all_to_all | solution.py:218
  136.2 48.7 %all-to-all-start.5 = ((bf16[12,64,1536]{2,0,1:T(8,128)(2,1)}), bf16[12,64,1536]{2,0,1:T(8,128)(2,1)}, u32[]{:S(2)}, u32[]{:S(2)}) async-start(bf16[12,64,1536]{2,0,1:T(8,128)(2,1)} %bitcast.133), calls=%async_computation.5 | async-start | bytes 6291456 | tf_op jit(solution)/shard_map/all_to_all | solution.py:239
  145.0 44.5 %copy-start.24 = (bf16[12,16,1536]{2,1,0:T(8,128)(2,1)S(1)}, bf16[12,16,1536]{2,1,0:T(8,128)(2,1)}, u32[]{:S(2)}) copy-start(bf16[12,16,1536]{2,1,0:T(8,128)(2,1)} %param.22) | copy-start | bytes 1769476
  185.7 14.4 %all-to-all-start.3 = ((bf16[2,200,768]{2,1,0:T(8,128)(2,1)}), bf16[2,200,768]{2,1,0:T(8,128)(2,1)S(1)}, u32[]{:S(2)}, u32[]{:S(2)}) async-start(bf16[2,200,768]{2,1,0:T(8,128)(2,1)} %broadcast_in_dim.66), calls=%async_computation.3 | async-start | bytes 1228800 | tf_op jit(solution)/shard_map/all_to_all | solution.py:212
  202.2 7.2 %copy-start.30 = (s32[400,2]{0,1:T(2,128)S(1)}, s32[400,2]{0,1:T(2,128)}, u32[]{:S(2)}) copy-start(s32[400,2]{0,1:T(2,128)} %param.13) | copy-start | bytes 9604
  202.2 47.2 %all-to-all-start.6 = ((bf16[12,64,1536]{2,0,1:T(8,128)(2,1)}), bf16[12,64,1536]{2,0,1:T(8,128)(2,1)}, u32[]{:S(2)}, u32[]{:S(2)}) async-start(bf16[12,64,1536]{2,0,1:T(8,128)(2,1)} %bitcast.132), calls=%async_computation.6 | async-start | bytes 6291456 | tf_op jit(solution)/shard_map/all_to_all | solution.py:239
  249.4 26.1 %all-to-all-start.4 = ((bf16[16,63,768]{2,1,0:T(8,128)(2,1)}), bf16[16,63,768]{2,1,0:T(8,128)(2,1)}, u32[]{:S(2)}, u32[]{:S(2)}) async-start(bf16[16,63,768]{2,1,0:T(8,128)(2,1)} %broadcast_select_fusion), calls=%async_computation.4 | async-start | bytes 3145728 | tf_op jit(solution)/shard_map/all_to_all | solution.py:225
  275.5 26.8 %all-to-all-start.10 = ((bf16[16,63,768]{2,1,0:T(8,128)(2,1)}), bf16[16,63,768]{2,1,0:T(8,128)(2,1)}, u32[]{:S(2)}, u32[]{:S(2)}) async-start(bf16[16,63,768]{2,1,0:T(8,128)(2,1)} %select_convert_fusion), calls=%async_computation.10 | async-start | bytes 3145728 | tf_op jit(solution)/shard_map/all_to_all | solution.py:225
  304.8 20.0 %copy-start.3 = (f32[1008,1536]{1,0:T(8,128)S(1)}, f32[1008,1536]{1,0:T(8,128)}, u32[]{:S(2)}) copy-start(f32[1008,1536]{1,0:T(8,128)} %fusion.111) | copy-start | bytes 18579460
  336.1 26.2 %all-to-all-start.7 = ((bf16[16,63,768]{2,1,0:T(8,128)(2,1)}), bf16[16,63,768]{2,1,0:T(8,128)(2,1)}, u32[]{:S(2)}, u32[]{:S(2)}) async-start(bf16[16,63,768]{2,1,0:T(8,128)(2,1)} %reshape.333), calls=%async_computation.7 | async-start | bytes 3145728 | tf_op jit(solution)/shard_map/all_to_all | solution.py:232
  362.3 26.9 %all-to-all-start.11 = ((bf16[16,63,768]{2,1,0:T(8,128)(2,1)}), bf16[16,63,768]{2,1,0:T(8,128)(2,1)}, u32[]{:S(2)}, u32[]{:S(2)}) async-start(bf16[16,63,768]{2,1,0:T(8,128)(2,1)} %reshape.340), calls=%async_computation.11 | async-start | bytes 3145728 | tf_op jit(solution)/shard_map/all_to_all | solution.py:232
  389.1 18.4 %copy-start.25 = (f32[400,16]{0,1:T(8,128)}, f32[400,16]{0,1:T(8,128)S(1)}, u32[]{:S(2)}) copy-start(f32[400,16]{0,1:T(8,128)S(1)} %multiply_reduce_fusion.11) | copy-start | bytes 76804
  424.6 16.7 %all-to-all-start.8 = ((f32[2,200,768]{2,1,0:T(8,128)}), f32[2,200,768]{2,1,0:T(8,128)}, u32[]{:S(2)}, u32[]{:S(2)}) async-start(f32[2,200,768]{2,1,0:T(8,128)} %bitcast.137), calls=%async_computation.8 | async-start | bytes 2457600 | tf_op jit(solution)/shard_map/all_to_all | solution.py:218
  429.3 13.4 %copy-start.8 = (f32[200,768]{1,0:T(8,128)S(1)}, f32[200,768]{1,0:T(8,128)}, u32[]{:S(2)}) copy-start(f32[200,768]{1,0:T(8,128)} %param.23) | copy-start | bytes 1843204
  444.8 15.1 %all-to-all-start.13 = ((bf16[2,200,768]{2,1,0:T(8,128)(2,1)}), bf16[2,200,768]{2,1,0:T(8,128)(2,1)S(1)}, u32[]{:S(2)}, u32[]{:S(2)}) async-start(bf16[2,200,768]{2,1,0:T(8,128)(2,1)} %broadcast_in_dim.81), calls=%async_computation.13 | async-start | bytes 1228800 | tf_op jit(solution)/shard_map/all_to_all | solution.py:212
  459.9 13.5 %copy-start.15 = (bf16[2,200,6,64]{1,3,2,0:T(8,128)(2,1)S(1)}, bf16[2,200,6,64]{1,3,2,0:T(8,128)(2,1)}, u32[]{:S(2)}) copy-start(bf16[2,200,6,64]{1,3,2,0:T(8,128)(2,1)} %copy.275) | copy-start | bytes 921604
  459.9 13.5 %copy-start.16 = (bf16[2,200,6,64]{1,3,2,0:T(8,128)(2,1)S(1)}, bf16[2,200,6,64]{1,3,2,0:T(8,128)(2,1)}, u32[]{:S(2)}) copy-start(bf16[2,200,6,64]{1,3,2,0:T(8,128)(2,1)} %copy.274) | copy-start | bytes 921604
  459.9 13.5 %copy-start.36 = (pred[200]{0:T(512)(128)(4,1)S(1)}, pred[200]{0:T(512)(128)(4,1)}, u32[]{:S(2)}) copy-start(pred[200]{0:T(512)(128)(4,1)} %copy-done.35) | copy-start | bytes 604
  460.0 16.4 %copy-start.10 = (bf16[2,200,768]{2,1,0:T(8,128)(2,1)}, bf16[2,200,768]{2,1,0:T(8,128)(2,1)S(1)}, u32[]{:S(2)}) copy-start(bf16[2,200,768]{2,1,0:T(8,128)(2,1)S(1)} %all-to-all-done.13) | copy-start | bytes 1843204
  460.0 53.5 %all-to-all-start.17 = ((bf16[64,12,1536]{2,1,0:T(8,128)(2,1)}), bf16[64,12,1536]{2,1,0:T(8,128)(2,1)}, u32[]{:S(2)}, u32[]{:S(2)}) async-start(bf16[64,12,1536]{2,1,0:T(8,128)(2,1)} %reshape.351), calls=%async_computation.17 | async-start | bytes 6291456 | tf_op jit(solution)/shard_map/all_to_all | solution.py:249
  478.8 4.2 copy-start.19
  499.6 4.8 copy-start.22
  499.6 5.8 copy-start.12
  507.5 10.8 %copy-start.21 = (bf16[1008,768]{1,0:T(8,128)(2,1)S(1)}, bf16[1008,768]{1,0:T(8,128)(2,1)}, u32[]{:S(2)}) copy-start(bf16[1008,768]{1,0:T(8,128)(2,1)} %reshape.328) | copy-start | bytes 4644868
  513.5 22.0 %all-to-all-start.14 = ((f32[2,200,768]{2,1,0:T(8,128)}), f32[2,200,768]{2,1,0:T(8,128)S(1)}, u32[]{:S(2)}, u32[]{:S(2)}) async-start(f32[2,200,768]{2,1,0:T(8,128)} %bitcast.144), calls=%async_computation.14 | async-start | bytes 2457600 | tf_op jit(solution)/shard_map/all_to_all | solution.py:218
  528.9 14.2 %copy-start.20 = (bf16[2,6,64,200]{3,2,1,0:T(8,128)(2,1)S(1)}, bf16[2,6,64,200]{3,2,1,0:T(8,128)(2,1)}, u32[]{:S(2)}) copy-start(bf16[2,6,64,200]{3,2,1,0:T(8,128)(2,1)} %convolution_convert_fusion.7) | copy-start | bytes 921604
  535.5 47.5 %all-to-all-start.16 = ((bf16[64,12,1536]{2,1,0:T(8,128)(2,1)}), bf16[64,12,1536]{2,1,0:T(8,128)(2,1)}, u32[]{:S(2)}, u32[]{:S(2)}) async-start(bf16[64,12,1536]{2,1,0:T(8,128)(2,1)} %reshape.350), calls=%async_computation.16 | async-start | bytes 6291456 | tf_op jit(solution)/shard_map/all_to_all | solution.py:249
  547.0 8.4 %copy-start.11 = (bf16[2,200,768]{2,1,0:T(8,128)(2,1)S(1)}, bf16[2,200,768]{2,1,0:T(8,128)(2,1)}, u32[]{:S(2)}) copy-start(bf16[2,200,768]{2,1,0:T(8,128)(2,1)} %copy-done.10) | copy-start | bytes 1843204
  557.0 3.3 copy-start.26
  562.9 5.6 copy-start.1
  562.9 5.6 copy-start.29
  562.9 5.6 copy-start.32
  562.9 5.6 copy-start.34
  567.5 2.8 copy-start.14
  567.5 2.8 copy-start.17
  567.5 2.8 copy-start.18
  582.9 50.3 %all-to-all-start.15 = ((bf16[64,12,1576]{2,1,0:T(8,128)(2,1)}), bf16[64,12,1576]{2,1,0:T(8,128)(2,1)}, u32[]{:S(2)}, u32[]{:S(2)}) async-start(bf16[64,12,1576]{2,1,0:T(8,128)(2,1)} %copy.317), calls=%async_computation.15 | async-start | bytes 6815744 | tf_op jit(solution)/shard_map/all_to_all | solution.py:188
  597.3 1.7 copy-start.5
  597.3 1.7 copy-start.9
  (6 other events, 6.5 us)

commit v9 on v8

--- a/solution.py
+++ b/solution.py
@@ -309,8 +309,10 @@
         experts, CAP, width
     )
     holders = lax.axis_size("fb")
-    own_in = expert_weights(expert_in, holders)
-    own_out = expert_weights(expert_out, holders)
+    units_half = expert_in.shape[2]
+    own_both = expert_weights(jnp.concatenate([expert_in, expert_out], axis=2), holders)
+    own_in = own_both[:, :units_half]
+    own_out = own_both[:, units_half:]
     owner_x = to_owners(slotted)
     owner_pre = jnp.dot(owner_x, own_in, preferred_element_type=f32)
     owner_hidden = gelu_exact(owner_pre).astype(bf16)
@@ -336,8 +338,9 @@
     slot_in_grad = to_groups(owner_back, experts, CAP)
     in_local = jnp.einsum("cd,cf->df", owner_x, owner_pgrad, preferred_element_type=f32)
     out_local = jnp.einsum("cd,cf->df", owner_g, owner_hidden, preferred_element_type=f32)
-    in_grad = weight_home(in_local, experts, holders)
-    out_grad = weight_home(out_local, experts, holders)
+    both_grad = weight_home(jnp.concatenate([in_local, out_local], axis=1), experts, holders)
+    in_grad = both_grad[:, :, :units_half]
+    out_grad = both_grad[:, :, units_half:]
     choice_grad = jnp.sum(picked.astype(f32) * gate_grad[:, :, None], axis=1)
     logit_grad = probs * (choice_grad - jnp.sum(probs * choice_grad, axis=-1, keepdims=True))
     router_part = jnp.einsum("td,te->de", tokens_m.astype(f32), logit_grad, precision=TOP)

time: 656 us -> 676 us (1.030)
  waiting for transfers between devices: 199 us -> 214 us
    all_to_all x2 -> x1, waiting for transfers between devices: 10.3 us -> 44.1 us  [weight_home(): lax.all_to_all(partial.astype(jnp.bfloat16).reshape(devices, rows, units)...]
    all_to_all x3, waiting for transfers between devices: 33.4 us -> 16 us  [owned_rows(): lax.all_to_all(value.reshape(halves, -1, value.shape[1]), 'tp', split_axi...]
    dot_general x1, matrix products: 7.3 us -> 19.4 us  [per_device(): owner_pre = jnp.dot(owner_x, own_in, preferred_element_type=f32)]
    dot_general x1, matrix products: 20 us -> 9.61 us  [per_device(): owner_hgrad = jnp.dot(owner_g, own_out, preferred_element_type=f32)]
    dot_general x0 -> x4, local copies, waits for them, and re-layouts: none -> 9.82 us  [the longest x2 6.43 us: per_device(): jnp.einsum('cd,cf->df', owner_g, owner_hidden, preferred_element_type=f32)]
    reshape x2 -> x0, local copies, waits for them, and re-layouts: 9.53 us -> none  [weight_home(): partial.astype(jnp.bfloat16).reshape(devices, rows, units)]
    concatenate x0 -> x2, local copies, waits for them, and re-layouts: none -> 7.15 us  [the longest x1 5.31 us: per_device(): jnp.concatenate([in_local, out_local], axis=1)]
    all_to_all x2 -> x1, starting transfers between devices: 21 us -> 15.8 us  [weight_home(): lax.all_to_all(partial.astype(jnp.bfloat16).reshape(devices, rows, units)...]
  transfers between devices with their start and end apart: 17 -> 15, of which waited for: 14 -> 9; matrix products, arithmetic and copies ran while one was open for 36% -> 29% of each run, Pallas kernels for 0% -> 0%
where the time goes in v9:
time: 676 us; the launch traced here: 664 us
  waiting for transfers between devices  214 us (32%)
  local copies, waits for them, and re-layouts  179 us (26%)
  starting transfers between devices  107 us (16%)
  matrix products  101 us (15%)
  other arithmetic  41.3 us (6%)
  blocking collectives  20.7 us (3%)
    all_to_all x1, waiting for transfers between devices, expert_weights(): lax.all_to_all(spread.reshape(rows, experts * holders, units), FSDP, spli...  53.4 us
    all_to_all x1, waiting for transfers between devices, weight_home(): lax.all_to_all(partial.astype(jnp.bfloat16).reshape(devices, rows, units)...  44.1 us
    all_to_all x1, waiting for transfers between devices, gather_dense(): full = lax.all_to_all(spread, FSDP, split_axis=0, concat_axis=0, tiled=True)  42.7 us
    all_to_all x1, waiting for transfers between devices, reduce_dense(): lax.all_to_all(wire.reshape(holders, rows, wire.shape[1]), FSDP, split_ax...  33.9 us
    dot_general x1, matrix products, per_device(): owner_pre = jnp.dot(owner_x, own_in, preferred_element_type=f32)  19.4 us
    all_to_all x2, starting transfers between devices, to_owners(): moved = lax.all_to_all(slots, 'fa', split_axis=0, concat_axis=0, tiled=True)  16.8 us
    all_to_all x3, waiting for transfers between devices, owned_rows(): lax.all_to_all(value.reshape(halves, -1, value.shape[1]), 'tp', split_axi...  16 us
    all_to_all x1, starting transfers between devices, weight_home(): lax.all_to_all(partial.astype(jnp.bfloat16).reshape(devices, rows, units)...  15.8 us
  transfers between devices with their start and end apart: 15, of which 9 were waited for; matrix products, arithmetic and copies ran while one was open for 29% of the time, Pallas kernels for 0%

profile of v9, /device:TPU:1, one launch (start us, length us, event | category | flops | bytes accessed | tf_op | source)
XLA Modules:
  0.0 664.1 jit_solution(1511770723207876742)
XLA Ops:
  7.3 10.6 %all-to-all-start = ((bf16[64,12,1556]{2,1,0:T(8,128)(2,1)}), bf16[64,12,1556]{2,1,0:T(8,128)(2,1)}, u32[]{:S(2)}, u32[]{:S(2)}) async-start(bf16[64,12,1556]{2,1,0:T(8,128)(2,1)} %broadcast_in_dim.60), calls=%async_computation | async-start | bytes 6815744 | tf_op jit(solution)/shard_map/all_to_all | solution.py:149
  18.3 42.7 %all-to-all-done = bf16[64,12,1556]{2,1,0:T(8,128)(2,1)} async-done(((bf16[64,12,1556]{2,1,0:T(8,128)(2,1)}), bf16[64,12,1556]{2,1,0:T(8,128)(2,1)}, u32[]{:S(2)}, u32[]{:S(2)}) %all-to-all-start) | async-done | bytes 2390048 | tf_op jit(solution)/shard_map/all_to_all | solution.py:149
  61.0 4.2 reshape.310
  67.6 4.6 all-to-all-start.1
  102.0 4.4 convolution_convert_fusion.5
  112.8 16.0 %all-to-all-done.2 = f32[2,200,768]{2,1,0:T(8,128)S(1)} async-done(((f32[2,200,768]{2,1,0:T(8,128)}), f32[2,200,768]{2,1,0:T(8,128)S(1)}, u32[]{:S(2)}, u32[]{:S(2)}) %all-to-all-start.2) | async-done | bytes 1228832 | tf_op jit(solution)/shard_map/all_to_all | solution.py:218
  135.9 5.8 all-to-all-done.8
  148.1 5.4 all-to-all-done.3
  153.5 4.9 broadcast_in_dim.74
  158.4 12.1 %all-to-all-start.5 = ((bf16[12,64,3072]{2,0,1:T(8,128)(2,1)}), bf16[12,64,3072]{2,0,1:T(8,128)(2,1)}, u32[]{:S(2)}, u32[]{:S(2)}) async-start(bf16[12,64,3072]{2,0,1:T(8,128)(2,1)} %bitcast.122), calls=%async_computation.5 | async-start | bytes 12582912 | tf_op jit(solution)/shard_map/all_to_all | solution.py:239
  173.7 5.3 scatter_custom_fusion.1
  178.9 5.3 scatter_custom_fusion
  184.4 5.2 gather_fusion
  195.0 53.4 %all-to-all-done.5 = bf16[12,64,3072]{2,0,1:T(8,128)(2,1)} async-done(((bf16[12,64,3072]{2,0,1:T(8,128)(2,1)}), bf16[12,64,3072]{2,0,1:T(8,128)(2,1)}, u32[]{:S(2)}, u32[]{:S(2)}) %all-to-all-start.5) | async-done | bytes 4718624 | tf_op jit(solution)/shard_map/all_to_all | solution.py:239
  248.4 9.6 %all-to-all-start.4 = ((bf16[16,63,768]{2,1,0:T(8,128)(2,1)}), bf16[16,63,768]{2,1,0:T(8,128)(2,1)}, u32[]{:S(2)}, u32[]{:S(2)}) async-start(bf16[16,63,768]{2,1,0:T(8,128)(2,1)} %broadcast_select_fusion), calls=%async_computation.4 | async-start | bytes 3145728 | tf_op jit(solution)/shard_map/all_to_all | solution.py:225
  258.1 5.2 gather_fusion.2
  268.2 5.3 scatter_custom_fusion.2
  277.0 7.5 %reshape.318 = bf16[768,3072]{1,0:T(8,128)(2,1)} reshape(bf16[64,12,1,3072]{3,1,0,2:T(8,128)(2,1)} %bitcast.18) | data formatting | bytes 9437184 | tf_op jit(solution)/shard_map/reshape | solution.py:242
  284.5 7.2 %all-to-all-start.9 = ((bf16[16,63,768]{2,1,0:T(8,128)(2,1)}), bf16[16,63,768]{2,1,0:T(8,128)(2,1)}, u32[]{:S(2)}, u32[]{:S(2)}) async-start(bf16[16,63,768]{2,1,0:T(8,128)(2,1)} %select_convert_fusion), calls=%async_computation.9 | async-start | bytes 3145728 | tf_op jit(solution)/shard_map/all_to_all | solution.py:225
  294.3 19.4 %multiply_convert_fusion = (bf16[1008,1536]{1,0:T(8,128)(2,1)}, f32[1008,1536]{1,0:T(8,128)}, f32[1008,1536]{1,0:T(8,128)}) fusion(bf16[1008,768]{1,0:T(8,128)(2,1)} %reshape.316, bf16[768,3072]{1,0:T(8,128)(2,1)} %reshape.318), kind=kOutput, calls=%fused_computation.14 | convolution fusion | flops 2478809088 | bytes 19390464 | tf_op jit(solution)/shard_map/dot_general | solution.py:317
  316.2 9.6 %add_convert_fusion = bf16[1008,1536]{1,0:T(8,128)(2,1)S(1)} fusion(f32[1008,1536]{1,0:T(8,128)} %get-tuple-element.67, f32[1008,1536]{1,0:T(8,128)} %get-tuple-element.78, bf16[1008,768]{1,0:T(8,128)(2,1)} %reshape.325, bf16[768,3072]{1,0:T(8,128)(2,1)} %reshape.318), kind=kOutput, calls=%fused_computation.13 | convolution fusion | flops 2399846400 | bytes 19390464 | tf_op jit(solution)/shard_map/dot_general | solution.py:335
  327.5 5.5 fusion.40
  335.5 6.8 %all-to-all-start.10 = ((bf16[16,63,768]{2,1,0:T(8,128)(2,1)}), bf16[16,63,768]{2,1,0:T(8,128)(2,1)}, u32[]{:S(2)}, u32[]{:S(2)}) async-start(bf16[16,63,768]{2,1,0:T(8,128)(2,1)} %reshape.326), calls=%async_computation.10 | async-start | bytes 3145728 | tf_op jit(solution)/shard_map/all_to_all | solution.py:232
  342.3 6.4 fusion.43
  351.3 11.4 %all-to-all-done.10 = bf16[16,63,768]{2,1,0:T(8,128)(2,1)} async-done(((bf16[16,63,768]{2,1,0:T(8,128)(2,1)}), bf16[16,63,768]{2,1,0:T(8,128)(2,1)}, u32[]{:S(2)}, u32[]{:S(2)}) %all-to-all-start.10) | async-done | bytes 1548320 | tf_op jit(solution)/shard_map/all_to_all | solution.py:232
  362.7 4.8 all-to-all-start.6
  370.6 6.6 gather_fusion.3
  377.2 4.1 reshape.329
  381.3 5.7 reduce_sum.275
  390.0 6.6 gather_fusion.1
  400.7 8.1 %multiply_reduce_fusion.1 = (f32[400,2]{1,0:T(8,128)S(1)}, f32[400,768]{1,0:T(8,128)}) fusion(f32[400,2,768]{2,1,0:T(2,128)} %reshape.322, f32[400,768]{1,0:T(8,128)S(1)} %convert.31, f32[400,2]{1,0:T(8,128)S(1)} %copy.352), kind=kLoop, calls=%fused_computation.41 | loop fusion | flops 2149600 | bytes 4921600 | tf_op jit(solution)/shard_map/reduce_sum | solution.py:333
  411.1 15.3 %all_to_all.90 = f32[2,200,768]{2,1,0:T(8,128)} all-to-all(f32[2,200,768]{2,1,0:T(8,128)S(1)} %bitcast.127), channel_id=1, replica_groups=mesh['fa'=16,'fb'=4,'tp'=2] {'tp'}, dimensions={0} | all-to-all | bytes 2457600 | tf_op jit(solution)/shard_map/all_to_all | solution.py:218
  426.4 4.7 all-to-all-start.7
  446.0 4.2 all-to-all-start.12
  450.2 6.8 %convolution_convert_fusion = bf16[64,12,1536]{2,0,1:T(8,128)(2,1)} fusion(bf16[1008,1536]{1,0:T(8,128)(2,1)} %get-tuple-element.66, bf16[64,12,1008]{2,1,0:T(8,128)(2,1)} %dot_general.122), kind=kOutput, calls=%fused_computation.29 | convolution fusion | flops 2379350016 | bytes 7004160 | tf_op jit(solution)/shard_map/cd,cf->df/dot_general | solution.py:340
  465.4 4.3 fusion.69
  469.6 4.1 fusion.66
  473.8 4.5 fusion.65
  489.3 4.6 all-to-all-start.13
  493.9 5.5 convolution_convert_fusion.1
  500.1 5.3 copy.395
  505.4 15.8 %all-to-all-start.15 = ((bf16[64,12,3072]{2,1,0:T(8,128)(2,1)}), bf16[64,12,3072]{2,1,0:T(8,128)(2,1)}, u32[]{:S(2)}, u32[]{:S(2)}) async-start(bf16[64,12,3072]{2,1,0:T(8,128)(2,1)} %copy.395), calls=%async_computation.15 | async-start | bytes 12582912 | tf_op jit(solution)/shard_map/all_to_all | solution.py:249
  539.7 4.6 convolution_convert_fusion.2
  555.4 44.1 %all-to-all-done.15 = bf16[64,12,3072]{2,1,0:T(8,128)(2,1)} async-done(((bf16[64,12,3072]{2,1,0:T(8,128)(2,1)}), bf16[64,12,3072]{2,1,0:T(8,128)(2,1)}, u32[]{:S(2)}, u32[]{:S(2)}) %all-to-all-start.15) | async-done | bytes 4718624 | tf_op jit(solution)/shard_map/all_to_all | solution.py:249
  599.5 10.9 %all-to-all-start.14 = ((bf16[64,12,1576]{2,1,0:T(8,128)(2,1)}), bf16[64,12,1576]{2,1,0:T(8,128)(2,1)}, u32[]{:S(2)}, u32[]{:S(2)}) async-start(bf16[64,12,1576]{2,1,0:T(8,128)(2,1)} %copy.389), calls=%async_computation.14 | async-start | bytes 6815744 | tf_op jit(solution)/shard_map/all_to_all | solution.py:188
  611.5 4.4 convert_reduce_fusion
  619.5 33.9 %all-to-all-done.14 = bf16[64,12,1576]{2,1,0:T(8,128)(2,1)} async-done(((bf16[64,12,1576]{2,1,0:T(8,128)(2,1)}), bf16[64,12,1576]{2,1,0:T(8,128)(2,1)}, u32[]{:S(2)}, u32[]{:S(2)}) %all-to-all-start.14) | async-done | bytes 2420768 | tf_op jit(solution)/shard_map/all_to_all | solution.py:188
  657.0 5.5 psum.7
  (233 shorter events, 174.2 us)
Async XLA Ops:
  7.3 10.7 %copy-start = (f32[200,768]{1,0:T(8,128)S(1)}, f32[200,768]{1,0:T(8,128)}, u32[]{:S(2)}) copy-start(f32[200,768]{1,0:T(8,128)} %param.12) | copy-start | bytes 1843204
  7.3 53.7 %all-to-all-start = ((bf16[64,12,1556]{2,1,0:T(8,128)(2,1)}), bf16[64,12,1556]{2,1,0:T(8,128)(2,1)}, u32[]{:S(2)}, u32[]{:S(2)}) async-start(bf16[64,12,1556]{2,1,0:T(8,128)(2,1)} %broadcast_in_dim.60), calls=%async_computation | async-start | bytes 6815744 | tf_op jit(solution)/shard_map/all_to_all | solution.py:149
  18.1 47.6 %copy-start.30 = (f32[200]{0:T(256)}, f32[200]{0:T(256)S(1)}, u32[]{:S(2)}) copy-start(f32[200]{0:T(256)S(1)} %broadcast_multiply_fusion.6) | copy-start | bytes 2404
  18.3 47.4 %copy-start.32 = (f32[200]{0:T(256)}, f32[200]{0:T(256)S(1)}, u32[]{:S(2)}) copy-start(f32[200]{0:T(256)S(1)} %add_rsqrt_fusion.1) | copy-start | bytes 2404
  65.2 41.3 %copy-start.2 = (bf16[768,1556]{1,0:T(8,128)(2,1)}, bf16[768,1556]{1,0:T(8,128)(2,1)S(1)}, u32[]{:S(2)}) copy-start(bf16[768,1556]{1,0:T(8,128)(2,1)S(1)} %reshape.310) | copy-start | bytes 7170052
  67.6 15.1 %all-to-all-start.1 = ((bf16[2,200,768]{2,1,0:T(8,128)(2,1)}), bf16[2,200,768]{2,1,0:T(8,128)(2,1)}, u32[]{:S(2)}, u32[]{:S(2)}) async-start(bf16[2,200,768]{2,1,0:T(8,128)(2,1)} %broadcast_in_dim.61), calls=%async_computation.1 | async-start | bytes 1228800 | tf_op jit(solution)/shard_map/all_to_all | solution.py:212
  72.2 358.8 %copy-start.34 = (pred[200]{0:T(512)(128)(4,1)}, pred[200]{0:T(512)(128)(4,1)S(1)}, u32[]{:S(2)}) copy-start(pred[200]{0:T(512)(128)(4,1)S(1)} %iota_compare_fusion.3) | copy-start | bytes 604
  109.0 3.8 copy-start.5
  109.0 19.8 %all-to-all-start.2 = ((f32[2,200,768]{2,1,0:T(8,128)}), f32[2,200,768]{2,1,0:T(8,128)S(1)}, u32[]{:S(2)}, u32[]{:S(2)}) async-start(f32[2,200,768]{2,1,0:T(8,128)} %fusion.78), calls=%async_computation.2 | async-start | bytes 2457600 | tf_op jit(solution)/shard_map/all_to_all | solution.py:218
  129.7 12.1 %all-to-all-start.8 = ((bf16[2,200,768]{2,1,0:T(8,128)(2,1)}), bf16[2,200,768]{2,1,0:T(8,128)(2,1)S(1)}, u32[]{:S(2)}, u32[]{:S(2)}) async-start(bf16[2,200,768]{2,1,0:T(8,128)(2,1)} %broadcast_in_dim.76), calls=%async_computation.8 | async-start | bytes 1228800 | tf_op jit(solution)/shard_map/all_to_all | solution.py:212
  134.2 12.0 %copy-start.19 = (bf16[12,16,1536]{2,1,0:T(8,128)(2,1)S(1)}, bf16[12,16,1536]{2,1,0:T(8,128)(2,1)}, u32[]{:S(2)}) copy-start(bf16[12,16,1536]{2,1,0:T(8,128)(2,1)} %param.22) | copy-start | bytes 1769476
  134.2 12.0 %copy-start.20 = (bf16[12,16,1536]{2,1,0:T(8,128)(2,1)S(1)}, bf16[12,16,1536]{2,1,0:T(8,128)(2,1)}, u32[]{:S(2)}) copy-start(bf16[12,16,1536]{2,1,0:T(8,128)(2,1)} %param.21) | copy-start | bytes 1769476
  142.6 10.9 %all-to-all-start.3 = ((bf16[2,200,768]{2,1,0:T(8,128)(2,1)}), bf16[2,200,768]{2,1,0:T(8,128)(2,1)S(1)}, u32[]{:S(2)}, u32[]{:S(2)}) async-start(bf16[2,200,768]{2,1,0:T(8,128)(2,1)} %broadcast_in_dim.64), calls=%async_computation.3 | async-start | bytes 1228800 | tf_op jit(solution)/shard_map/all_to_all | solution.py:212
  158.4 12.1 %copy-start.29 = (s32[400,2]{0,1:T(2,128)S(1)}, s32[400,2]{0,1:T(2,128)}, u32[]{:S(2)}) copy-start(s32[400,2]{0,1:T(2,128)} %param.13) | copy-start | bytes 9604
  158.4 90.0 %all-to-all-start.5 = ((bf16[12,64,3072]{2,0,1:T(8,128)(2,1)}), bf16[12,64,3072]{2,0,1:T(8,128)(2,1)}, u32[]{:S(2)}, u32[]{:S(2)}) async-start(bf16[12,64,3072]{2,0,1:T(8,128)(2,1)} %bitcast.122), calls=%async_computation.5 | async-start | bytes 12582912 | tf_op jit(solution)/shard_map/all_to_all | solution.py:239
  248.4 36.1 %all-to-all-start.4 = ((bf16[16,63,768]{2,1,0:T(8,128)(2,1)}), bf16[16,63,768]{2,1,0:T(8,128)(2,1)}, u32[]{:S(2)}, u32[]{:S(2)}) async-start(bf16[16,63,768]{2,1,0:T(8,128)(2,1)} %broadcast_select_fusion), calls=%async_computation.4 | async-start | bytes 3145728 | tf_op jit(solution)/shard_map/all_to_all | solution.py:225
  284.5 29.2 %all-to-all-start.9 = ((bf16[16,63,768]{2,1,0:T(8,128)(2,1)}), bf16[16,63,768]{2,1,0:T(8,128)(2,1)}, u32[]{:S(2)}, u32[]{:S(2)}) async-start(bf16[16,63,768]{2,1,0:T(8,128)(2,1)} %select_convert_fusion), calls=%async_computation.9 | async-start | bytes 3145728 | tf_op jit(solution)/shard_map/all_to_all | solution.py:225
  325.8 1.6 copy-start.36
  335.5 27.2 %all-to-all-start.10 = ((bf16[16,63,768]{2,1,0:T(8,128)(2,1)}), bf16[16,63,768]{2,1,0:T(8,128)(2,1)}, u32[]{:S(2)}, u32[]{:S(2)}) async-start(bf16[16,63,768]{2,1,0:T(8,128)(2,1)} %reshape.326), calls=%async_computation.10 | async-start | bytes 3145728 | tf_op jit(solution)/shard_map/all_to_all | solution.py:232
  362.7 24.2 %all-to-all-start.6 = ((bf16[16,63,768]{2,1,0:T(8,128)(2,1)}), bf16[16,63,768]{2,1,0:T(8,128)(2,1)}, u32[]{:S(2)}, u32[]{:S(2)}) async-start(bf16[16,63,768]{2,1,0:T(8,128)(2,1)} %reshape.319), calls=%async_computation.6 | async-start | bytes 3145728 | tf_op jit(solution)/shard_map/all_to_all | solution.py:232
  408.9 17.5 %copy-start.21 = (f32[400,16]{0,1:T(8,128)}, f32[400,16]{0,1:T(8,128)S(1)}, u32[]{:S(2)}) copy-start(f32[400,16]{0,1:T(8,128)S(1)} %multiply_reduce_fusion.11) | copy-start | bytes 76804
  411.1 20.0 %copy-start.13 = (bf16[2,200,6,64]{1,3,2,0:T(8,128)(2,1)S(1)}, bf16[2,200,6,64]{1,3,2,0:T(8,128)(2,1)}, u32[]{:S(2)}) copy-start(bf16[2,200,6,64]{1,3,2,0:T(8,128)(2,1)} %copy.347) | copy-start | bytes 921604
  411.1 20.0 %copy-start.15 = (bf16[2,200,6,64]{1,3,2,0:T(8,128)(2,1)S(1)}, bf16[2,200,6,64]{1,3,2,0:T(8,128)(2,1)}, u32[]{:S(2)}) copy-start(bf16[2,200,6,64]{1,3,2,0:T(8,128)(2,1)} %copy.348) | copy-start | bytes 921604
  426.4 16.0 %all-to-all-start.7 = ((f32[2,200,768]{2,1,0:T(8,128)}), f32[2,200,768]{2,1,0:T(8,128)}, u32[]{:S(2)}, u32[]{:S(2)}) async-start(f32[2,200,768]{2,1,0:T(8,128)} %bitcast.19), calls=%async_computation.7 | async-start | bytes 2457600 | tf_op jit(solution)/shard_map/all_to_all | solution.py:218
  440.4 3.4 copy-start.6
  446.0 14.4 %all-to-all-start.12 = ((bf16[2,200,768]{2,1,0:T(8,128)(2,1)}), bf16[2,200,768]{2,1,0:T(8,128)(2,1)S(1)}, u32[]{:S(2)}, u32[]{:S(2)}) async-start(bf16[2,200,768]{2,1,0:T(8,128)(2,1)} %broadcast_in_dim.78), calls=%async_computation.12 | async-start | bytes 1228800 | tf_op jit(solution)/shard_map/all_to_all | solution.py:212
  460.4 3.4 copy-start.12
  460.4 2.3 copy-start.8
  465.3 4.3 copy-start.14
  465.3 8.4 %copy-start.35 = (pred[200]{0:T(512)(128)(4,1)S(1)}, pred[200]{0:T(512)(128)(4,1)}, u32[]{:S(2)}) copy-start(pred[200]{0:T(512)(128)(4,1)} %copy-done.34) | copy-start | bytes 604
  473.8 4.5 copy-start.25
  478.3 1.7 copy-start.24
  480.4 5.7 copy-start.11
  489.3 16.1 %all-to-all-start.13 = ((f32[2,200,768]{2,1,0:T(8,128)}), f32[2,200,768]{2,1,0:T(8,128)S(1)}, u32[]{:S(2)}, u32[]{:S(2)}) async-start(f32[2,200,768]{2,1,0:T(8,128)} %bitcast.134), calls=%async_computation.13 | async-start | bytes 2457600 | tf_op jit(solution)/shard_map/all_to_all | solution.py:218
  493.9 5.5 copy-start.10
  505.4 94.1 %all-to-all-start.15 = ((bf16[64,12,3072]{2,1,0:T(8,128)(2,1)}), bf16[64,12,3072]{2,1,0:T(8,128)(2,1)}, u32[]{:S(2)}, u32[]{:S(2)}) async-start(bf16[64,12,3072]{2,1,0:T(8,128)(2,1)} %copy.395), calls=%async_computation.15 | async-start | bytes 12582912 | tf_op jit(solution)/shard_map/all_to_all | solution.py:249
  521.2 2.6 copy-start.18
  523.9 4.1 copy-start.22
  530.9 4.7 copy-start.9
  539.7 5.6 copy-start.1
  539.7 5.6 copy-start.28
  539.7 5.6 copy-start.31
  539.7 5.6 copy-start.33
  544.3 2.7 copy-start.16
  544.3 2.8 copy-start.17
  555.4 55.0 %copy-start.4 = (f32[200,768]{1,0:T(8,128)S(1)}, f32[200,768]{1,0:T(8,128)}, u32[]{:S(2)}) copy-start(f32[200,768]{1,0:T(8,128)} %copy-done.3) | copy-start | bytes 1843204
  555.4 55.0 %copy-start.7 = (f32[200,768]{1,0:T(8,128)S(1)}, f32[200,768]{1,0:T(8,128)}, u32[]{:S(2)}) copy-start(f32[200,768]{1,0:T(8,128)} %get-tuple-element.65) | copy-start | bytes 1843204
  599.5 53.9 %all-to-all-start.14 = ((bf16[64,12,1576]{2,1,0:T(8,128)(2,1)}), bf16[64,12,1576]{2,1,0:T(8,128)(2,1)}, u32[]{:S(2)}, u32[]{:S(2)}) async-start(bf16[64,12,1576]{2,1,0:T(8,128)(2,1)} %copy.389), calls=%async_computation.14 | async-start | bytes 6815744 | tf_op jit(solution)/shard_map/all_to_all | solution.py:188
  (4 other events, 4.6 us)

commit v10 on v8

--- a/solution.py
+++ b/solution.py
@@ -159,51 +159,23 @@
     return (qkv_full, proj_full, router_full, norms[:, 0], norms[:, 1], norms[:, 2], norms[:, 3])
 
 
-def reduce_dense(qkv_part, proj_part, router_part, norm_parts):
-    width = qkv_part.shape[1]
-    heads_width = qkv_part.shape[2]
-    experts = router_part.shape[1]
-    packed = jnp.concatenate(
-        [
-            jnp.transpose(qkv_part, (1, 0, 2)).reshape(width, -1),
-            proj_part.T,
-            router_part,
-            jnp.stack(norm_parts, axis=1),
-        ],
-        axis=1,
-    )
+def reduce_pack(big, small):
+    width = big.shape[0]
     holders = fsdp_size()
     rows = width // holders
-    at = 4 * heads_width
-    small = packed[:, at:]
     high = lax.reduce_precision(small, exponent_bits=8, mantissa_bits=7)
     wire = jnp.concatenate(
-        [
-            packed[:, :at].astype(jnp.bfloat16),
-            high.astype(jnp.bfloat16),
-            (small - high).astype(jnp.bfloat16),
-        ],
+        [big.astype(jnp.bfloat16), high.astype(jnp.bfloat16), (small - high).astype(jnp.bfloat16)],
         axis=1,
     )
     moved = lax.all_to_all(
         wire.reshape(holders, rows, wire.shape[1]), FSDP, split_axis=0, concat_axis=0, tiled=True
     ).astype(jnp.float32)
+    at = big.shape[1]
     count = small.shape[1]
-    part = jnp.concatenate(
-        [
-            jnp.sum(moved[..., :at], axis=0),
-            jnp.sum(moved[..., at : at + count] + moved[..., at + count :], axis=0),
-        ],
-        axis=1,
-    )
-    at = 3 * heads_width
-    qkv_grad = jnp.transpose(part[:, :at].reshape(rows, 3, heads_width), (1, 0, 2))
-    proj_grad = part[:, at : at + heads_width].T
-    at += heads_width
-    shared = lax.psum(part[:, at:], "tp")
-    router_grad = shared[:, :experts]
-    norm_grads = [shared[:, experts + i] for i in range(len(norm_parts))]
-    return qkv_grad, proj_grad, router_grad, norm_grads
+    big_sum = jnp.sum(moved[..., :at], axis=0)
+    small_sum = jnp.sum(moved[..., at : at + count] + moved[..., at + count :], axis=0)
+    return big_sum, small_sum
 
 
 def group_rows(value):
@@ -354,6 +326,12 @@
     middle_grad = cotangent + expert_norm_backward
     mid_rows = group_rows(middle_grad.astype(bf16))
     proj_part = jnp.einsum("th,td->hd", context, mid_rows, preferred_element_type=f32)
+    early = reduce_pack(
+        proj_part.T,
+        jnp.concatenate(
+            [router_part, jnp.stack([expert_gain_partial, expert_shift_partial], axis=1)], axis=1
+        ),
+    )
     context_grad = jnp.einsum("td,hd->th", mid_rows, proj_back, preferred_element_type=f32).astype(
         bf16
     )
@@ -372,22 +350,26 @@
         attention_gain_gradient,
     )
     input_grad = middle_grad + attention_norm_backward
-    qkv_grad, proj_grad, router_grad, norm_grads = reduce_dense(
-        qkv_part,
-        proj_part,
-        router_part,
-        [attention_gain_partial, attention_shift_partial, expert_gain_partial, expert_shift_partial],
-    )
+    late = reduce_pack(
+        jnp.transpose(qkv_part, (1, 0, 2)).reshape(qkv_part.shape[1], -1),
+        jnp.stack([attention_gain_partial, attention_shift_partial], axis=1),
+    )
+    rows = late[0].shape[0]
+    heads_w = qkv_part.shape[2]
+    experts_w = router_part.shape[1]
+    qkv_grad = jnp.transpose(late[0].reshape(rows, 3, heads_w), (1, 0, 2))
+    proj_grad = early[0].T
+    shared = lax.psum(jnp.concatenate([early[1], late[1]], axis=1), "tp")
     return (
         outputs,
         input_grad,
-        norm_grads[0],
-        norm_grads[1],
+        shared[:, experts_w + 2],
+        shared[:, experts_w + 3],
         qkv_grad,
         proj_grad,
-        norm_grads[2],
-        norm_grads[3],
-        router_grad,
+        shared[:, experts_w],
+        shared[:, experts_w + 1],
+        shared[:, :experts_w],
         in_grad,
         out_grad,
     )

time: 656 us -> 663 us (1.011)
  waiting for transfers between devices: 199 us -> 224 us
  local copies, waits for them, and re-layouts: 176 us -> 159 us
    all_to_all x2, waiting for transfers between devices: 10.3 us -> 39.7 us  [weight_home(): lax.all_to_all(partial.astype(jnp.bfloat16).reshape(devices, rows, units)...]
    concatenate x11 -> x2, local copies, waits for them, and re-layouts: 11.7 us -> 2.69 us  [reduce_pack(): jnp.concatenate([big.astype(jnp.bfloat16), high.astype(jnp.bfloat16), (sm...]
    all_to_all x1 -> x2, waiting for transfers between devices: 33.1 us -> 29.4 us  [reduce_pack(): lax.all_to_all(wire.reshape(holders, rows, wire.shape[1]), FSDP, split_ax...]
    unnamed x83 -> x78, local copies, waits for them, and re-layouts: 12.1 us -> 13.3 us
  transfers between devices with their start and end apart: 17 -> 18, of which waited for: 14 -> 16; matrix products, arithmetic and copies ran while one was open for 36% -> 33% of each run, Pallas kernels for 0% -> 0%
where the time goes in v10:
time: 663 us; the launch traced here: 652 us
  waiting for transfers between devices  224 us (34%)
  local copies, waits for them, and re-layouts  159 us (24%)
  starting transfers between devices  112 us (17%)
  matrix products  93.4 us (14%)
  other arithmetic  40.3 us (6%)
  blocking collectives  20.8 us (3%)
    all_to_all x2, waiting for transfers between devices, expert_weights(): lax.all_to_all(spread.reshape(rows, experts * holders, units), FSDP, spli...  57.2 us
    all_to_all x1, waiting for transfers between devices, gather_dense(): full = lax.all_to_all(spread, FSDP, split_axis=0, concat_axis=0, tiled=True)  42.7 us
    all_to_all x2, waiting for transfers between devices, weight_home(): lax.all_to_all(partial.astype(jnp.bfloat16).reshape(devices, rows, units)...  39.7 us
    all_to_all x2, waiting for transfers between devices, reduce_pack(): lax.all_to_all(wire.reshape(holders, rows, wire.shape[1]), FSDP, split_ax...  29.4 us
    all_to_all x3, waiting for transfers between devices, owned_rows(): lax.all_to_all(value.reshape(halves, -1, value.shape[1]), 'tp', split_axi...  28.9 us
    all_to_all x2, starting transfers between devices, weight_home(): lax.all_to_all(partial.astype(jnp.bfloat16).reshape(devices, rows, units)...  20.7 us
    dot_general x1, matrix products, per_device(): owner_hgrad = jnp.dot(owner_g, own_out, preferred_element_type=f32)  20 us
    all_to_all x4, starting transfers between devices, group_rows(): lax.all_to_all(spread, 'tp', split_axis=0, concat_axis=0, tiled=True)  16.8 us
  transfers between devices with their start and end apart: 18, of which 16 were waited for; matrix products, arithmetic and copies ran while one was open for 33% of the time, Pallas kernels for 0%

profile of v10, /device:TPU:1, one launch (start us, length us, event | category | flops | bytes accessed | tf_op | source)
XLA Modules:
  0.0 651.6 jit_solution(17369185017885764337)
XLA Ops:
  7.3 10.6 %all-to-all-start = ((bf16[64,12,1556]{2,1,0:T(8,128)(2,1)}), bf16[64,12,1556]{2,1,0:T(8,128)(2,1)}, u32[]{:S(2)}, u32[]{:S(2)}) async-start(bf16[64,12,1556]{2,1,0:T(8,128)(2,1)} %broadcast_in_dim.62), calls=%async_computation | async-start | bytes 6815744 | tf_op jit(solution)/shard_map/all_to_all | solution.py:149
  18.3 42.7 %all-to-all-done = bf16[64,12,1556]{2,1,0:T(8,128)(2,1)} async-done(((bf16[64,12,1556]{2,1,0:T(8,128)(2,1)}), bf16[64,12,1556]{2,1,0:T(8,128)(2,1)}, u32[]{:S(2)}, u32[]{:S(2)}) %all-to-all-start) | async-done | bytes 2390048 | tf_op jit(solution)/shard_map/all_to_all | solution.py:149
  67.6 4.6 all-to-all-start.1
  83.6 4.3 all-to-all-start.9
  107.1 4.4 convolution_convert_fusion.7
  114.2 4.3 all-to-all-start.2
  118.8 15.2 %all-to-all-done.2 = f32[2,200,768]{2,1,0:T(8,128)S(1)} async-done(((f32[2,200,768]{2,1,0:T(8,128)}), f32[2,200,768]{2,1,0:T(8,128)S(1)}, u32[]{:S(2)}, u32[]{:S(2)}) %all-to-all-start.2) | async-done | bytes 1228832 | tf_op jit(solution)/shard_map/all_to_all | solution.py:190
  136.1 8.7 %all-to-all-start.5 = ((bf16[12,64,1536]{2,0,1:T(8,128)(2,1)}), bf16[12,64,1536]{2,0,1:T(8,128)(2,1)}, u32[]{:S(2)}, u32[]{:S(2)}) async-start(bf16[12,64,1536]{2,0,1:T(8,128)(2,1)} %bitcast.124), calls=%async_computation.5 | async-start | bytes 6291456 | tf_op jit(solution)/shard_map/all_to_all | solution.py:211
  145.5 39.3 %all-to-all-done.5 = bf16[12,64,1536]{2,0,1:T(8,128)(2,1)} async-done(((bf16[12,64,1536]{2,0,1:T(8,128)(2,1)}), bf16[12,64,1536]{2,0,1:T(8,128)(2,1)}, u32[]{:S(2)}, u32[]{:S(2)}) %all-to-all-start.5) | async-done | bytes 2359328 | tf_op jit(solution)/shard_map/all_to_all | solution.py:211
  189.7 10.3 %all-to-all-done.3 = bf16[2,200,768]{2,1,0:T(8,128)(2,1)S(1)} async-done(((bf16[2,200,768]{2,1,0:T(8,128)(2,1)}), bf16[2,200,768]{2,1,0:T(8,128)(2,1)S(1)}, u32[]{:S(2)}, u32[]{:S(2)}) %all-to-all-start.3) | async-done | bytes 614432 | tf_op jit(solution)/shard_map/all_to_all | solution.py:184
  202.2 7.1 %all-to-all-start.6 = ((bf16[12,64,1536]{2,0,1:T(8,128)(2,1)}), bf16[12,64,1536]{2,0,1:T(8,128)(2,1)}, u32[]{:S(2)}, u32[]{:S(2)}) async-start(bf16[12,64,1536]{2,0,1:T(8,128)(2,1)} %bitcast.123), calls=%async_computation.6 | async-start | bytes 6291456 | tf_op jit(solution)/shard_map/all_to_all | solution.py:211
  212.4 5.3 scatter_custom_fusion.1
  217.7 5.3 scatter_custom_fusion
  223.1 5.2 gather_fusion
  231.4 17.9 %all-to-all-done.6 = bf16[12,64,1536]{2,0,1:T(8,128)(2,1)} async-done(((bf16[12,64,1536]{2,0,1:T(8,128)(2,1)}), bf16[12,64,1536]{2,0,1:T(8,128)(2,1)}, u32[]{:S(2)}, u32[]{:S(2)}) %all-to-all-start.6) | async-done | bytes 2359328 | tf_op jit(solution)/shard_map/all_to_all | solution.py:211
  249.3 5.5 all-to-all-start.4
  256.0 5.2 gather_fusion.2
  266.1 5.3 scatter_custom_fusion.2
  275.4 6.4 all-to-all-start.10
  281.8 4.9 reshape.309
  286.7 4.9 reshape.311
  294.2 7.3 %fusion.109 = f32[1008,1536]{1,0:T(8,128)} fusion(bf16[1008,768]{1,0:T(8,128)(2,1)} %reshape.307, bf16[768,1536]{1,0:T(8,128)(2,1)} %reshape.309), kind=kOutput, calls=%fused_computation.184 | convolution fusion | flops 2378170368 | bytes 10100736 | tf_op jit(solution)/shard_map/dot_general | solution.py:287
  304.6 20.0 %add_convert_fusion = (bf16[1008,1536]{1,0:T(8,128)(2,1)}, f32[1008,1536]{1,0:T(8,128)S(1)}) fusion(f32[1008,1536]{1,0:T(8,128)} %fusion.109, bf16[1008,768]{1,0:T(8,128)(2,1)} %reshape.318, bf16[768,1536]{1,0:T(8,128)(2,1)} %reshape.311), kind=kOutput, calls=%fused_computation.13 | convolution fusion | flops 2489647104 | bytes 19390464 | tf_op jit(solution)/shard_map/dot_general | solution.py:305
  327.9 5.4 convolution_convert_fusion.4
  335.8 6.3 all-to-all-start.7
  342.1 6.3 convolution_convert_fusion.3
  351.0 11.1 %all-to-all-done.7 = bf16[16,63,768]{2,1,0:T(8,128)(2,1)} async-done(((bf16[16,63,768]{2,1,0:T(8,128)(2,1)}), bf16[16,63,768]{2,1,0:T(8,128)(2,1)}, u32[]{:S(2)}, u32[]{:S(2)}) %all-to-all-start.7) | async-done | bytes 1548320 | tf_op jit(solution)/shard_map/all_to_all | solution.py:204
  362.0 5.1 all-to-all-start.11
  370.1 6.6 %gather_fusion.1 = f32[800,768]{1,0:T(8,128)} fusion(f32[1008,768]{1,0:T(8,128)} %reshape.339, s32[1024]{0:T(1024)S(1)} %pad_clamp_fusion), kind=kCustom, calls=%fused_computation.1 | custom fusion | bytes 4918400 | tf_op jit(solution)/shard_map/gather | solution.py:291
  380.8 8.1 %multiply_reduce_fusion.1 = (f32[400,2]{1,0:T(8,128)S(1)}, f32[400,768]{1,0:T(8,128)}) fusion(f32[400,2,768]{2,1,0:T(2,128)} %reshape.315, f32[400,768]{1,0:T(8,128)S(1)} %convert.16, f32[400,2]{1,0:T(8,128)S(1)} %copy.240), kind=kLoop, calls=%fused_computation.39 | loop fusion | flops 2149600 | bytes 4921600 | tf_op jit(solution)/shard_map/reduce_sum | solution.py:303
  392.2 6.6 %gather_fusion.3 = f32[800,768]{1,0:T(8,128)} fusion(f32[1008,768]{1,0:T(8,128)} %reshape.342, s32[1024]{0:T(1024)S(1)} %pad_clamp_fusion), kind=kCustom, calls=%fused_computation.3 | custom fusion | bytes 4918400 | tf_op jit(solution)/shard_map/gather | solution.py:316
  402.8 4.6 reduce_sum.302
  409.1 15.5 %all_to_all.115 = f32[2,200,768]{2,1,0:T(8,128)S(1)} all-to-all(f32[2,200,768]{2,1,0:T(8,128)S(1)} %bitcast.129), channel_id=1, replica_groups=mesh['fa'=16,'fb'=4,'tp'=2] {'tp'}, dimensions={0} | all-to-all | bytes 2457600 | tf_op jit(solution)/shard_map/all_to_all | solution.py:190
  424.6 4.7 all-to-all-start.8
  429.3 6.4 convolution_convert_fusion
  435.7 4.8 reshape.332
  441.5 13.3 %all-to-all-start.18 = ((bf16[64,12,1536]{2,1,0:T(8,128)(2,1)}), bf16[64,12,1536]{2,1,0:T(8,128)(2,1)}, u32[]{:S(2)}, u32[]{:S(2)}) async-start(bf16[64,12,1536]{2,1,0:T(8,128)(2,1)} %reshape.332), calls=%async_computation.18 | async-start | bytes 6291456 | tf_op jit(solution)/shard_map/all_to_all | solution.py:221
  459.4 35.4 %all-to-all-done.18 = bf16[64,12,1536]{2,1,0:T(8,128)(2,1)} async-done(((bf16[64,12,1536]{2,1,0:T(8,128)(2,1)}), bf16[64,12,1536]{2,1,0:T(8,128)(2,1)}, u32[]{:S(2)}, u32[]{:S(2)}) %all-to-all-start.18) | async-done | bytes 2359328 | tf_op jit(solution)/shard_map/all_to_all | solution.py:221
  499.9 5.0 convolution_convert_fusion.1
  510.7 7.4 %all-to-all-start.17 = ((bf16[64,12,1536]{2,1,0:T(8,128)(2,1)}), bf16[64,12,1536]{2,1,0:T(8,128)(2,1)}, u32[]{:S(2)}, u32[]{:S(2)}) async-start(bf16[64,12,1536]{2,1,0:T(8,128)(2,1)} %reshape.331), calls=%async_computation.17 | async-start | bytes 6291456 | tf_op jit(solution)/shard_map/all_to_all | solution.py:221
  540.5 5.4 fusion.49
  553.7 4.4 all-to-all-done.17
  566.2 12.7 %all-to-all-done.14 = f32[2,200,768]{2,1,0:T(8,128)S(1)} async-done(((f32[2,200,768]{2,1,0:T(8,128)}), f32[2,200,768]{2,1,0:T(8,128)S(1)}, u32[]{:S(2)}, u32[]{:S(2)}) %all-to-all-start.14) | async-done | bytes 1228832 | tf_op jit(solution)/shard_map/all_to_all | solution.py:190
  578.9 7.5 %all-to-all-start.15 = ((bf16[64,12,420]{2,1,0:T(8,128)(2,1)}), bf16[64,12,420]{2,1,0:T(8,128)(2,1)}, u32[]{:S(2)}, u32[]{:S(2)}) async-start(bf16[64,12,420]{2,1,0:T(8,128)(2,1)} %reshape.328), calls=%async_computation.15 | async-start | bytes 2097152 | tf_op jit(solution)/shard_map/all_to_all | solution.py:171
  596.8 7.3 %all-to-all-done.15 = bf16[64,12,420]{2,1,0:T(8,128)(2,1)} async-done(((bf16[64,12,420]{2,1,0:T(8,128)(2,1)}), bf16[64,12,420]{2,1,0:T(8,128)(2,1)}, u32[]{:S(2)}, u32[]{:S(2)}) %all-to-all-start.15) | async-done | bytes 645152 | tf_op jit(solution)/shard_map/all_to_all | solution.py:171
  604.1 4.5 all-to-all-start.16
  621.0 22.1 %all-to-all-done.16 = bf16[64,12,1156]{2,1,0:T(8,128)(2,1)S(1)} async-done(((bf16[64,12,1156]{2,1,0:T(8,128)(2,1)}), bf16[64,12,1156]{2,1,0:T(8,128)(2,1)S(1)}, u32[]{:S(2)}, u32[]{:S(2)}) %all-to-all-start.16) | async-done | bytes 1775648 | tf_op jit(solution)/shard_map/all_to_all | solution.py:171
  644.4 5.3 psum.7
  (228 shorter events, 183.1 us)
Async XLA Ops:
  7.3 10.7 %copy-start = (f32[200,768]{1,0:T(8,128)S(1)}, f32[200,768]{1,0:T(8,128)}, u32[]{:S(2)}) copy-start(f32[200,768]{1,0:T(8,128)} %param.12) | copy-start | bytes 1843204
  7.3 53.7 %all-to-all-start = ((bf16[64,12,1556]{2,1,0:T(8,128)(2,1)}), bf16[64,12,1556]{2,1,0:T(8,128)(2,1)}, u32[]{:S(2)}, u32[]{:S(2)}) async-start(bf16[64,12,1556]{2,1,0:T(8,128)(2,1)} %broadcast_in_dim.62), calls=%async_computation | async-start | bytes 6815744 | tf_op jit(solution)/shard_map/all_to_all | solution.py:149
  18.1 47.6 %copy-start.28 = (f32[200]{0:T(256)}, f32[200]{0:T(256)S(1)}, u32[]{:S(2)}) copy-start(f32[200]{0:T(256)S(1)} %broadcast_multiply_fusion.6) | copy-start | bytes 2404
  18.3 47.4 %copy-start.30 = (f32[200]{0:T(256)}, f32[200]{0:T(256)S(1)}, u32[]{:S(2)}) copy-start(f32[200]{0:T(256)S(1)} %add_rsqrt_fusion.1) | copy-start | bytes 2404
  65.2 46.4 %copy-start.2 = (bf16[768,1556]{1,0:T(8,128)(2,1)}, bf16[768,1556]{1,0:T(8,128)(2,1)S(1)}, u32[]{:S(2)}) copy-start(bf16[768,1556]{1,0:T(8,128)(2,1)S(1)} %reshape.301) | copy-start | bytes 7170052
  67.6 15.1 %all-to-all-start.1 = ((bf16[2,200,768]{2,1,0:T(8,128)(2,1)}), bf16[2,200,768]{2,1,0:T(8,128)(2,1)}, u32[]{:S(2)}, u32[]{:S(2)}) async-start(bf16[2,200,768]{2,1,0:T(8,128)(2,1)} %broadcast_in_dim.63), calls=%async_computation.1 | async-start | bytes 1228800 | tf_op jit(solution)/shard_map/all_to_all | solution.py:184
  73.3 33.7 %copy-start.32 = (pred[200]{0:T(512)(128)(4,1)}, pred[200]{0:T(512)(128)(4,1)S(1)}, u32[]{:S(2)}) copy-start(pred[200]{0:T(512)(128)(4,1)S(1)} %iota_compare_fusion.3) | copy-start | bytes 604
  83.6 30.6 %all-to-all-start.9 = ((bf16[2,200,768]{2,1,0:T(8,128)(2,1)}), bf16[2,200,768]{2,1,0:T(8,128)(2,1)}, u32[]{:S(2)}, u32[]{:S(2)}) async-start(bf16[2,200,768]{2,1,0:T(8,128)(2,1)} %broadcast_in_dim.79), calls=%async_computation.9 | async-start | bytes 1228800 | tf_op jit(solution)/shard_map/all_to_all | solution.py:184
  114.2 4.4 copy-start.19
  114.2 19.8 %all-to-all-start.2 = ((f32[2,200,768]{2,1,0:T(8,128)}), f32[2,200,768]{2,1,0:T(8,128)S(1)}, u32[]{:S(2)}, u32[]{:S(2)}) async-start(f32[2,200,768]{2,1,0:T(8,128)} %fusion.54), calls=%async_computation.2 | async-start | bytes 2457600 | tf_op jit(solution)/shard_map/all_to_all | solution.py:190
  136.1 48.7 %all-to-all-start.5 = ((bf16[12,64,1536]{2,0,1:T(8,128)(2,1)}), bf16[12,64,1536]{2,0,1:T(8,128)(2,1)}, u32[]{:S(2)}, u32[]{:S(2)}) async-start(bf16[12,64,1536]{2,0,1:T(8,128)(2,1)} %bitcast.124), calls=%async_computation.5 | async-start | bytes 6291456 | tf_op jit(solution)/shard_map/all_to_all | solution.py:211
  144.9 44.4 %copy-start.20 = (bf16[12,16,1536]{2,1,0:T(8,128)(2,1)S(1)}, bf16[12,16,1536]{2,1,0:T(8,128)(2,1)}, u32[]{:S(2)}) copy-start(bf16[12,16,1536]{2,1,0:T(8,128)(2,1)} %param.22) | copy-start | bytes 1769476
  185.7 14.4 %all-to-all-start.3 = ((bf16[2,200,768]{2,1,0:T(8,128)(2,1)}), bf16[2,200,768]{2,1,0:T(8,128)(2,1)S(1)}, u32[]{:S(2)}, u32[]{:S(2)}) async-start(bf16[2,200,768]{2,1,0:T(8,128)(2,1)} %broadcast_in_dim.66), calls=%async_computation.3 | async-start | bytes 1228800 | tf_op jit(solution)/shard_map/all_to_all | solution.py:184
  202.1 7.2 %copy-start.27 = (s32[400,2]{0,1:T(2,128)S(1)}, s32[400,2]{0,1:T(2,128)}, u32[]{:S(2)}) copy-start(s32[400,2]{0,1:T(2,128)} %param.13) | copy-start | bytes 9604
  202.2 47.2 %all-to-all-start.6 = ((bf16[12,64,1536]{2,0,1:T(8,128)(2,1)}), bf16[12,64,1536]{2,0,1:T(8,128)(2,1)}, u32[]{:S(2)}, u32[]{:S(2)}) async-start(bf16[12,64,1536]{2,0,1:T(8,128)(2,1)} %bitcast.123), calls=%async_computation.6 | async-start | bytes 6291456 | tf_op jit(solution)/shard_map/all_to_all | solution.py:211
  249.3 26.1 %all-to-all-start.4 = ((bf16[16,63,768]{2,1,0:T(8,128)(2,1)}), bf16[16,63,768]{2,1,0:T(8,128)(2,1)}, u32[]{:S(2)}, u32[]{:S(2)}) async-start(bf16[16,63,768]{2,1,0:T(8,128)(2,1)} %broadcast_select_fusion), calls=%async_computation.4 | async-start | bytes 3145728 | tf_op jit(solution)/shard_map/all_to_all | solution.py:197
  275.4 26.6 %all-to-all-start.10 = ((bf16[16,63,768]{2,1,0:T(8,128)(2,1)}), bf16[16,63,768]{2,1,0:T(8,128)(2,1)}, u32[]{:S(2)}, u32[]{:S(2)}) async-start(bf16[16,63,768]{2,1,0:T(8,128)(2,1)} %select_convert_fusion), calls=%async_computation.10 | async-start | bytes 3145728 | tf_op jit(solution)/shard_map/all_to_all | solution.py:197
  304.6 20.0 %copy-start.3 = (f32[1008,1536]{1,0:T(8,128)S(1)}, f32[1008,1536]{1,0:T(8,128)}, u32[]{:S(2)}) copy-start(f32[1008,1536]{1,0:T(8,128)} %fusion.109) | copy-start | bytes 18579460
  326.2 1.6 copy-start.6
  335.8 26.2 %all-to-all-start.7 = ((bf16[16,63,768]{2,1,0:T(8,128)(2,1)}), bf16[16,63,768]{2,1,0:T(8,128)(2,1)}, u32[]{:S(2)}, u32[]{:S(2)}) async-start(bf16[16,63,768]{2,1,0:T(8,128)(2,1)} %reshape.312), calls=%async_computation.7 | async-start | bytes 3145728 | tf_op jit(solution)/shard_map/all_to_all | solution.py:204
  362.0 27.1 %all-to-all-start.11 = ((bf16[16,63,768]{2,1,0:T(8,128)(2,1)}), bf16[16,63,768]{2,1,0:T(8,128)(2,1)}, u32[]{:S(2)}, u32[]{:S(2)}) async-start(bf16[16,63,768]{2,1,0:T(8,128)(2,1)} %reshape.319), calls=%async_computation.11 | async-start | bytes 3145728 | tf_op jit(solution)/shard_map/all_to_all | solution.py:204
  389.1 18.4 %copy-start.21 = (f32[400,16]{0,1:T(8,128)}, f32[400,16]{0,1:T(8,128)S(1)}, u32[]{:S(2)}) copy-start(f32[400,16]{0,1:T(8,128)S(1)} %multiply_reduce_fusion.11) | copy-start | bytes 76804
  424.6 16.8 %all-to-all-start.8 = ((f32[2,200,768]{2,1,0:T(8,128)}), f32[2,200,768]{2,1,0:T(8,128)}, u32[]{:S(2)}, u32[]{:S(2)}) async-start(f32[2,200,768]{2,1,0:T(8,128)} %bitcast.128), calls=%async_computation.8 | async-start | bytes 2457600 | tf_op jit(solution)/shard_map/all_to_all | solution.py:190
  441.5 53.3 %all-to-all-start.18 = ((bf16[64,12,1536]{2,1,0:T(8,128)(2,1)}), bf16[64,12,1536]{2,1,0:T(8,128)(2,1)}, u32[]{:S(2)}, u32[]{:S(2)}) async-start(bf16[64,12,1536]{2,1,0:T(8,128)(2,1)} %reshape.332), calls=%async_computation.18 | async-start | bytes 6291456 | tf_op jit(solution)/shard_map/all_to_all | solution.py:221
  454.8 2.9 copy-start.8
  495.7 15.1 %all-to-all-start.13 = ((bf16[2,200,768]{2,1,0:T(8,128)(2,1)}), bf16[2,200,768]{2,1,0:T(8,128)(2,1)}, u32[]{:S(2)}, u32[]{:S(2)}) async-start(bf16[2,200,768]{2,1,0:T(8,128)(2,1)} %broadcast_in_dim.81), calls=%async_computation.13 | async-start | bytes 1228800 | tf_op jit(solution)/shard_map/all_to_all | solution.py:184
  507.3 10.8 %copy-start.17 = (bf16[2,6,64,200]{3,2,1,0:T(8,128)(2,1)S(1)}, bf16[2,6,64,200]{3,2,1,0:T(8,128)(2,1)}, u32[]{:S(2)}) copy-start(bf16[2,6,64,200]{3,2,1,0:T(8,128)(2,1)} %convolution_convert_fusion.7) | copy-start | bytes 921604
  507.3 12.3 %copy-start.14 = (bf16[2,200,6,64]{1,3,2,0:T(8,128)(2,1)S(1)}, bf16[2,200,6,64]{1,3,2,0:T(8,128)(2,1)}, u32[]{:S(2)}) copy-start(bf16[2,200,6,64]{1,3,2,0:T(8,128)(2,1)} %copy.236) | copy-start | bytes 921604
  507.3 12.3 %copy-start.15 = (bf16[2,200,6,64]{1,3,2,0:T(8,128)(2,1)S(1)}, bf16[2,200,6,64]{1,3,2,0:T(8,128)(2,1)}, u32[]{:S(2)}) copy-start(bf16[2,200,6,64]{1,3,2,0:T(8,128)(2,1)} %copy.235) | copy-start | bytes 921604
  507.3 12.3 %copy-start.33 = (pred[200]{0:T(512)(128)(4,1)S(1)}, pred[200]{0:T(512)(128)(4,1)}, u32[]{:S(2)}) copy-start(pred[200]{0:T(512)(128)(4,1)} %copy-done.32) | copy-start | bytes 604
  510.7 47.3 %all-to-all-start.17 = ((bf16[64,12,1536]{2,1,0:T(8,128)(2,1)}), bf16[64,12,1536]{2,1,0:T(8,128)(2,1)}, u32[]{:S(2)}, u32[]{:S(2)}) async-start(bf16[64,12,1536]{2,1,0:T(8,128)(2,1)} %reshape.331), calls=%async_computation.17 | async-start | bytes 6291456 | tf_op jit(solution)/shard_map/all_to_all | solution.py:221
  525.0 4.2 copy-start.16
  532.1 1.5 copy-start.7
  545.8 4.8 copy-start.18
  545.8 5.8 copy-start.11
  553.7 8.0 %copy-start.22 = (f32[400,16]{0,1:T(8,128)S(1)}, f32[400,16]{0,1:T(8,128)}, u32[]{:S(2)}) copy-start(f32[400,16]{0,1:T(8,128)} %copy-done.21) | copy-start | bytes 76804
  553.7 8.4 %copy-start.23 = (bf16[400,384]{0,1:T(8,128)(2,1)S(1)}, bf16[400,384]{0,1:T(8,128)(2,1)}, u32[]{:S(2)}) copy-start(bf16[400,384]{0,1:T(8,128)(2,1)} %reshape.327) | copy-start | bytes 921604
  558.0 20.9 %all-to-all-start.14 = ((f32[2,200,768]{2,1,0:T(8,128)}), f32[2,200,768]{2,1,0:T(8,128)S(1)}, u32[]{:S(2)}, u32[]{:S(2)}) async-start(f32[2,200,768]{2,1,0:T(8,128)} %bitcast.133), calls=%async_computation.14 | async-start | bytes 2457600 | tf_op jit(solution)/shard_map/all_to_all | solution.py:190
  564.0 1.2 copy-start.13
  578.9 25.2 %all-to-all-start.15 = ((bf16[64,12,420]{2,1,0:T(8,128)(2,1)}), bf16[64,12,420]{2,1,0:T(8,128)(2,1)}, u32[]{:S(2)}, u32[]{:S(2)}) async-start(bf16[64,12,420]{2,1,0:T(8,128)(2,1)} %reshape.328), calls=%async_computation.15 | async-start | bytes 2097152 | tf_op jit(solution)/shard_map/all_to_all | solution.py:171
  586.4 4.9 copy-start.1
  586.5 4.9 copy-start.26
  586.5 4.9 copy-start.29
  586.5 4.9 copy-start.31
  604.1 39.1 %all-to-all-start.16 = ((bf16[64,12,1156]{2,1,0:T(8,128)(2,1)}), bf16[64,12,1156]{2,1,0:T(8,128)(2,1)S(1)}, u32[]{:S(2)}, u32[]{:S(2)}) async-start(bf16[64,12,1156]{2,1,0:T(8,128)(2,1)} %reshape.329), calls=%async_computation.16 | async-start | bytes 5242880 | tf_op jit(solution)/shard_map/all_to_all | solution.py:171
  615.8 1.7 copy-start.5
  615.8 1.7 copy-start.9
  649.7 1.4 copy-start.24
  (4 other events, 3.7 us)

commit v11 on v9

--- a/solution.py
+++ b/solution.py
@@ -338,9 +338,8 @@
     slot_in_grad = to_groups(owner_back, experts, CAP)
     in_local = jnp.einsum("cd,cf->df", owner_x, owner_pgrad, preferred_element_type=f32)
     out_local = jnp.einsum("cd,cf->df", owner_g, owner_hidden, preferred_element_type=f32)
-    both_grad = weight_home(jnp.concatenate([in_local, out_local], axis=1), experts, holders)
-    in_grad = both_grad[:, :, :units_half]
-    out_grad = both_grad[:, :, units_half:]
+    in_grad = weight_home(in_local, experts, holders)
+    out_grad = weight_home(out_local, experts, holders)
     choice_grad = jnp.sum(picked.astype(f32) * gate_grad[:, :, None], axis=1)
     logit_grad = probs * (choice_grad - jnp.sum(probs * choice_grad, axis=-1, keepdims=True))
     router_part = jnp.einsum("td,te->de", tokens_m.astype(f32), logit_grad, precision=TOP)

time: 676 us -> 647 us (0.957)
  waiting for transfers between devices: 214 us -> 193 us
    all_to_all x1 -> x2, waiting for transfers between devices: 44.1 us -> 10.3 us  [weight_home(): lax.all_to_all(partial.astype(jnp.bfloat16).reshape(devices, rows, units)...]
    all_to_all x3, waiting for transfers between devices: 16 us -> 35.7 us  [owned_rows(): lax.all_to_all(value.reshape(halves, -1, value.shape[1]), 'tp', split_axi...]
    all_to_all x2, waiting for transfers between devices: 11.4 us -> 0.01 us  [to_groups(): lax.all_to_all(pieces, 'fa', split_axis=0, concat_axis=0, tiled=True)]
    dot_general x4 -> x0, local copies, waits for them, and re-layouts: 9.82 us -> none  [the longest x2 6.43 us: per_device(): jnp.einsum('cd,cf->df', owner_g, owner_hidden, preferred_element_type=f32)]
    reshape x0 -> x2, local copies, waits for them, and re-layouts: none -> 9.53 us  [weight_home(): partial.astype(jnp.bfloat16).reshape(devices, rows, units)]
    all_to_all x1 -> x2, starting transfers between devices: 15.8 us -> 19.4 us  [weight_home(): lax.all_to_all(partial.astype(jnp.bfloat16).reshape(devices, rows, units)...]
  transfers between devices with their start and end apart: 15 -> 16, of which waited for: 9 -> 11; matrix products, arithmetic and copies ran while one was open for 29% -> 36% of each run, Pallas kernels for 0% -> 0%
where the time goes in v11:
time: 647 us; the launch traced here: 635 us
  waiting for transfers between devices  193 us (30%)
  local copies, waits for them, and re-layouts  174 us (27%)
  starting transfers between devices  108 us (17%)
  matrix products  99.1 us (15%)
  other arithmetic  35.7 us (6%)
  blocking collectives  22.3 us (3%)
    all_to_all x1, waiting for transfers between devices, expert_weights(): lax.all_to_all(spread.reshape(rows, experts * holders, units), FSDP, spli...  55.8 us
    all_to_all x1, waiting for transfers between devices, gather_dense(): full = lax.all_to_all(spread, FSDP, split_axis=0, concat_axis=0, tiled=True)  42.7 us
    all_to_all x3, waiting for transfers between devices, owned_rows(): lax.all_to_all(value.reshape(halves, -1, value.shape[1]), 'tp', split_axi...  35.7 us
    all_to_all x1, waiting for transfers between devices, reduce_dense(): lax.all_to_all(wire.reshape(holders, rows, wire.shape[1]), FSDP, split_ax...  33.1 us
    all_to_all x2, starting transfers between devices, weight_home(): lax.all_to_all(partial.astype(jnp.bfloat16).reshape(devices, rows, units)...  19.4 us
    dot_general x1, matrix products, per_device(): owner_pre = jnp.dot(owner_x, own_in, preferred_element_type=f32)  19.2 us
    all_to_all x1, blocking collectives, owned_rows(): lax.all_to_all(value.reshape(halves, -1, value.shape[1]), 'tp', split_axi...  17 us
    all_to_all x2, starting transfers between devices, to_owners(): moved = lax.all_to_all(slots, 'fa', split_axis=0, concat_axis=0, tiled=True)  16.7 us
  transfers between devices with their start and end apart: 16, of which 11 were waited for; matrix products, arithmetic and copies ran while one was open for 36% of the time, Pallas kernels for 0%

profile of v11, /device:TPU:1, one launch (start us, length us, event | category | flops | bytes accessed | tf_op | source)
XLA Modules:
  0.0 634.7 jit_solution(7905701077344230268)
XLA Ops:
  7.3 10.6 %all-to-all-start = ((bf16[64,12,1556]{2,1,0:T(8,128)(2,1)}), bf16[64,12,1556]{2,1,0:T(8,128)(2,1)}, u32[]{:S(2)}, u32[]{:S(2)}) async-start(bf16[64,12,1556]{2,1,0:T(8,128)(2,1)} %broadcast_in_dim.60), calls=%async_computation | async-start | bytes 6815744 | tf_op jit(solution)/shard_map/all_to_all | solution.py:149
  18.4 42.7 %all-to-all-done = bf16[64,12,1556]{2,1,0:T(8,128)(2,1)} async-done(((bf16[64,12,1556]{2,1,0:T(8,128)(2,1)}), bf16[64,12,1556]{2,1,0:T(8,128)(2,1)}, u32[]{:S(2)}, u32[]{:S(2)}) %all-to-all-start) | async-done | bytes 2390048 | tf_op jit(solution)/shard_map/all_to_all | solution.py:149
  61.0 4.2 reshape.314
  67.7 4.6 all-to-all-start.1
  102.0 4.4 convolution_convert_fusion.5
  112.8 16.0 %all-to-all-done.2 = f32[2,200,768]{2,1,0:T(8,128)S(1)} async-done(((f32[2,200,768]{2,1,0:T(8,128)}), f32[2,200,768]{2,1,0:T(8,128)S(1)}, u32[]{:S(2)}, u32[]{:S(2)}) %all-to-all-start.2) | async-done | bytes 1228832 | tf_op jit(solution)/shard_map/all_to_all | solution.py:218
  133.9 7.8 %all-to-all-done.8 = bf16[2,200,768]{2,1,0:T(8,128)(2,1)S(1)} async-done(((bf16[2,200,768]{2,1,0:T(8,128)(2,1)}), bf16[2,200,768]{2,1,0:T(8,128)(2,1)S(1)}, u32[]{:S(2)}, u32[]{:S(2)}) %all-to-all-start.8) | async-done | bytes 614432 | tf_op jit(solution)/shard_map/all_to_all | solution.py:212
  146.9 6.6 %all-to-all-done.3 = bf16[2,200,768]{2,1,0:T(8,128)(2,1)S(1)} async-done(((bf16[2,200,768]{2,1,0:T(8,128)(2,1)}), bf16[2,200,768]{2,1,0:T(8,128)(2,1)S(1)}, u32[]{:S(2)}, u32[]{:S(2)}) %all-to-all-start.3) | async-done | bytes 614432 | tf_op jit(solution)/shard_map/all_to_all | solution.py:212
  157.0 12.2 %all-to-all-start.5 = ((bf16[12,64,3072]{2,0,1:T(8,128)(2,1)}), bf16[12,64,3072]{2,0,1:T(8,128)(2,1)}, u32[]{:S(2)}, u32[]{:S(2)}) async-start(bf16[12,64,3072]{2,0,1:T(8,128)(2,1)} %bitcast.122), calls=%async_computation.5 | async-start | bytes 12582912 | tf_op jit(solution)/shard_map/all_to_all | solution.py:239
  172.2 5.3 scatter_custom_fusion.1
  177.5 5.3 scatter_custom_fusion
  182.9 5.2 gather_fusion
  191.2 55.8 %all-to-all-done.5 = bf16[12,64,3072]{2,0,1:T(8,128)(2,1)} async-done(((bf16[12,64,3072]{2,0,1:T(8,128)(2,1)}), bf16[12,64,3072]{2,0,1:T(8,128)(2,1)}, u32[]{:S(2)}, u32[]{:S(2)}) %all-to-all-start.5) | async-done | bytes 4718624 | tf_op jit(solution)/shard_map/all_to_all | solution.py:239
  247.0 9.6 %all-to-all-start.4 = ((bf16[16,63,768]{2,1,0:T(8,128)(2,1)}), bf16[16,63,768]{2,1,0:T(8,128)(2,1)}, u32[]{:S(2)}, u32[]{:S(2)}) async-start(bf16[16,63,768]{2,1,0:T(8,128)(2,1)} %broadcast_select_fusion), calls=%async_computation.4 | async-start | bytes 3145728 | tf_op jit(solution)/shard_map/all_to_all | solution.py:225
  256.7 5.2 gather_fusion.2
  266.8 5.3 scatter_custom_fusion.2
  275.6 7.5 %reshape.322 = bf16[768,3072]{1,0:T(8,128)(2,1)} reshape(bf16[64,12,1,3072]{3,1,0,2:T(8,128)(2,1)} %bitcast.18) | data formatting | bytes 9437184 | tf_op jit(solution)/shard_map/reshape | solution.py:242
  283.1 7.1 %all-to-all-start.9 = ((bf16[16,63,768]{2,1,0:T(8,128)(2,1)}), bf16[16,63,768]{2,1,0:T(8,128)(2,1)}, u32[]{:S(2)}, u32[]{:S(2)}) async-start(bf16[16,63,768]{2,1,0:T(8,128)(2,1)} %select_convert_fusion), calls=%async_computation.9 | async-start | bytes 3145728 | tf_op jit(solution)/shard_map/all_to_all | solution.py:225
  292.8 19.2 %multiply_convert_fusion = (bf16[1008,1536]{1,0:T(8,128)(2,1)S(1)}, f32[1008,1536]{1,0:T(8,128)}, f32[1008,1536]{1,0:T(8,128)}) fusion(bf16[1008,768]{1,0:T(8,128)(2,1)} %reshape.320, bf16[768,3072]{1,0:T(8,128)(2,1)} %reshape.322), kind=kOutput, calls=%fused_computation.15 | convolution fusion | flops 2478809088 | bytes 19390464 | tf_op jit(solution)/shard_map/dot_general | solution.py:317
  313.6 5.4 fusion.41
  321.6 6.8 %all-to-all-start.6 = ((bf16[16,63,768]{2,1,0:T(8,128)(2,1)}), bf16[16,63,768]{2,1,0:T(8,128)(2,1)}, u32[]{:S(2)}, u32[]{:S(2)}) async-start(bf16[16,63,768]{2,1,0:T(8,128)(2,1)} %reshape.323), calls=%async_computation.6 | async-start | bytes 3145728 | tf_op jit(solution)/shard_map/all_to_all | solution.py:232
  331.0 9.6 %add_convert_fusion = bf16[1008,1536]{1,0:T(8,128)(2,1)S(1)} fusion(f32[1008,1536]{1,0:T(8,128)} %get-tuple-element.67, f32[1008,1536]{1,0:T(8,128)} %get-tuple-element.76, bf16[1008,768]{1,0:T(8,128)(2,1)} %reshape.329, bf16[768,3072]{1,0:T(8,128)(2,1)} %reshape.322), kind=kOutput, calls=%fused_computation.14 | convolution fusion | flops 2399846400 | bytes 19390464 | tf_op jit(solution)/shard_map/dot_general | solution.py:335
  342.3 5.4 fusion.38
  350.3 6.9 %all-to-all-start.10 = ((bf16[16,63,768]{2,1,0:T(8,128)(2,1)}), bf16[16,63,768]{2,1,0:T(8,128)(2,1)}, u32[]{:S(2)}, u32[]{:S(2)}) async-start(bf16[16,63,768]{2,1,0:T(8,128)(2,1)} %reshape.330), calls=%async_computation.10 | async-start | bytes 3145728 | tf_op jit(solution)/shard_map/all_to_all | solution.py:232
  360.1 6.6 %gather_fusion.1 = f32[800,768]{1,0:T(8,128)} fusion(f32[1008,768]{1,0:T(8,128)} %reshape.348, s32[1024]{0:T(1024)S(1)} %pad_clamp_fusion), kind=kCustom, calls=%fused_computation.1 | custom fusion | bytes 4918400 | tf_op jit(solution)/shard_map/gather | solution.py:321
  366.8 4.1 reshape.326
  370.9 8.1 %multiply_reduce_fusion.1 = (f32[400,2]{1,0:T(8,128)S(1)}, f32[400,768]{1,0:T(8,128)}) fusion(f32[400,2,768]{2,1,0:T(2,128)} %reshape.326, f32[400,768]{1,0:T(8,128)S(1)} %convert.24, f32[400,2]{1,0:T(8,128)S(1)} %copy.275), kind=kLoop, calls=%fused_computation.39 | loop fusion | flops 2149600 | bytes 4921600 | tf_op jit(solution)/shard_map/reduce_sum | solution.py:333
  382.1 6.6 %gather_fusion.3 = f32[800,768]{1,0:T(8,128)} fusion(f32[1008,768]{1,0:T(8,128)} %reshape.351, s32[1024]{0:T(1024)S(1)} %pad_clamp_fusion), kind=kCustom, calls=%fused_computation.3 | custom fusion | bytes 4918400 | tf_op jit(solution)/shard_map/gather | solution.py:346
  392.8 4.6 reduce_sum.284
  399.1 17.0 %all_to_all.95 = f32[2,200,768]{2,1,0:T(8,128)S(1)} all-to-all(f32[2,200,768]{2,1,0:T(8,128)S(1)} %bitcast.127), channel_id=1, replica_groups=mesh['fa'=16,'fb'=4,'tp'=2] {'tp'}, dimensions={0} | all-to-all | bytes 2457600 | tf_op jit(solution)/shard_map/all_to_all | solution.py:218
  416.1 4.5 all-to-all-start.7
  421.1 13.2 %all-to-all-done.7 = f32[2,200,768]{2,1,0:T(8,128)} async-done(((f32[2,200,768]{2,1,0:T(8,128)}), f32[2,200,768]{2,1,0:T(8,128)}, u32[]{:S(2)}, u32[]{:S(2)}) %all-to-all-start.7) | async-done | bytes 1228832 | tf_op jit(solution)/shard_map/all_to_all | solution.py:218
  441.7 6.4 %convolution_convert_fusion = bf16[768,1536]{1,0:T(8,128)(2,1)} fusion(bf16[1008,768]{1,0:T(8,128)(2,1)} %reshape.329, bf16[1008,1536]{1,0:T(8,128)(2,1)} %copy-done.37), kind=kOutput, calls=%fused_computation.29 | convolution fusion | flops 2379350016 | bytes 7004160 | tf_op jit(solution)/shard_map/cd,cf->df/dot_general | solution.py:340
  448.1 4.8 reshape.341
  452.9 11.9 %all-to-all-start.16 = ((bf16[64,12,1536]{2,1,0:T(8,128)(2,1)}), bf16[64,12,1536]{2,1,0:T(8,128)(2,1)}, u32[]{:S(2)}, u32[]{:S(2)}) async-start(bf16[64,12,1536]{2,1,0:T(8,128)(2,1)} %reshape.341), calls=%async_computation.16 | async-start | bytes 6291456 | tf_op jit(solution)/shard_map/all_to_all | solution.py:249
  478.6 4.3 fusion.62
  485.5 5.4 fusion.65
  498.8 6.0 all-to-all-done.16
  504.8 4.5 all-to-all-start.13
  509.3 5.8 convolution_convert_fusion.1
  515.1 4.8 reshape.340
  519.8 6.6 %all-to-all-done.13 = f32[2,200,768]{2,1,0:T(8,128)S(1)} async-done(((f32[2,200,768]{2,1,0:T(8,128)}), f32[2,200,768]{2,1,0:T(8,128)S(1)}, u32[]{:S(2)}, u32[]{:S(2)}) %all-to-all-start.13) | async-done | bytes 1228832 | tf_op jit(solution)/shard_map/all_to_all | solution.py:218
  526.4 7.6 %all-to-all-start.15 = ((bf16[64,12,1536]{2,1,0:T(8,128)(2,1)}), bf16[64,12,1536]{2,1,0:T(8,128)(2,1)}, u32[]{:S(2)}, u32[]{:S(2)}) async-start(bf16[64,12,1536]{2,1,0:T(8,128)(2,1)} %reshape.340), calls=%async_computation.15 | async-start | bytes 6291456 | tf_op jit(solution)/shard_map/all_to_all | solution.py:249
  553.9 4.6 convolution_convert_fusion.2
  569.6 4.3 all-to-all-done.15
  573.9 7.2 %all-to-all-start.14 = ((bf16[64,12,1576]{2,1,0:T(8,128)(2,1)}), bf16[64,12,1576]{2,1,0:T(8,128)(2,1)}, u32[]{:S(2)}, u32[]{:S(2)}) async-start(bf16[64,12,1576]{2,1,0:T(8,128)(2,1)} %copy.312), calls=%async_computation.14 | async-start | bytes 6815744 | tf_op jit(solution)/shard_map/all_to_all | solution.py:188
  591.1 33.1 %all-to-all-done.14 = bf16[64,12,1576]{2,1,0:T(8,128)(2,1)} async-done(((bf16[64,12,1576]{2,1,0:T(8,128)(2,1)}), bf16[64,12,1576]{2,1,0:T(8,128)(2,1)}, u32[]{:S(2)}, u32[]{:S(2)}) %all-to-all-start.14) | async-done | bytes 2420768 | tf_op jit(solution)/shard_map/all_to_all | solution.py:188
  628.4 5.3 psum.7
  (233 shorter events, 177.4 us)
Async XLA Ops:
  7.3 10.7 %copy-start = (f32[200,768]{1,0:T(8,128)S(1)}, f32[200,768]{1,0:T(8,128)}, u32[]{:S(2)}) copy-start(f32[200,768]{1,0:T(8,128)} %param.12) | copy-start | bytes 1843204
  7.3 53.7 %all-to-all-start = ((bf16[64,12,1556]{2,1,0:T(8,128)(2,1)}), bf16[64,12,1556]{2,1,0:T(8,128)(2,1)}, u32[]{:S(2)}, u32[]{:S(2)}) async-start(bf16[64,12,1556]{2,1,0:T(8,128)(2,1)} %broadcast_in_dim.60), calls=%async_computation | async-start | bytes 6815744 | tf_op jit(solution)/shard_map/all_to_all | solution.py:149
  18.1 47.6 %copy-start.30 = (f32[200]{0:T(256)}, f32[200]{0:T(256)S(1)}, u32[]{:S(2)}) copy-start(f32[200]{0:T(256)S(1)} %broadcast_multiply_fusion.6) | copy-start | bytes 2404
  18.3 47.4 %copy-start.32 = (f32[200]{0:T(256)}, f32[200]{0:T(256)S(1)}, u32[]{:S(2)}) copy-start(f32[200]{0:T(256)S(1)} %add_rsqrt_fusion.1) | copy-start | bytes 2404
  65.2 41.2 %copy-start.2 = (bf16[768,1556]{1,0:T(8,128)(2,1)}, bf16[768,1556]{1,0:T(8,128)(2,1)S(1)}, u32[]{:S(2)}) copy-start(bf16[768,1556]{1,0:T(8,128)(2,1)S(1)} %reshape.314) | copy-start | bytes 7170052
  67.7 15.1 %all-to-all-start.1 = ((bf16[2,200,768]{2,1,0:T(8,128)(2,1)}), bf16[2,200,768]{2,1,0:T(8,128)(2,1)}, u32[]{:S(2)}, u32[]{:S(2)}) async-start(bf16[2,200,768]{2,1,0:T(8,128)(2,1)} %broadcast_in_dim.61), calls=%async_computation.1 | async-start | bytes 1228800 | tf_op jit(solution)/shard_map/all_to_all | solution.py:212
  72.2 29.8 %copy-start.34 = (pred[200]{0:T(512)(128)(4,1)}, pred[200]{0:T(512)(128)(4,1)S(1)}, u32[]{:S(2)}) copy-start(pred[200]{0:T(512)(128)(4,1)S(1)} %iota_compare_fusion.3) | copy-start | bytes 604
  109.0 3.8 copy-start.6
  109.0 19.8 %all-to-all-start.2 = ((f32[2,200,768]{2,1,0:T(8,128)}), f32[2,200,768]{2,1,0:T(8,128)S(1)}, u32[]{:S(2)}, u32[]{:S(2)}) async-start(f32[2,200,768]{2,1,0:T(8,128)} %fusion.74), calls=%async_computation.2 | async-start | bytes 2457600 | tf_op jit(solution)/shard_map/all_to_all | solution.py:218
  129.7 12.0 %all-to-all-start.8 = ((bf16[2,200,768]{2,1,0:T(8,128)(2,1)}), bf16[2,200,768]{2,1,0:T(8,128)(2,1)S(1)}, u32[]{:S(2)}, u32[]{:S(2)}) async-start(bf16[2,200,768]{2,1,0:T(8,128)(2,1)} %broadcast_in_dim.76), calls=%async_computation.8 | async-start | bytes 1228800 | tf_op jit(solution)/shard_map/all_to_all | solution.py:212
  133.3 12.8 %copy-start.22 = (bf16[12,16,1536]{2,1,0:T(8,128)(2,1)S(1)}, bf16[12,16,1536]{2,1,0:T(8,128)(2,1)}, u32[]{:S(2)}) copy-start(bf16[12,16,1536]{2,1,0:T(8,128)(2,1)} %param.22) | copy-start | bytes 1769476
  133.5 12.6 %copy-start.23 = (bf16[12,16,1536]{2,1,0:T(8,128)(2,1)S(1)}, bf16[12,16,1536]{2,1,0:T(8,128)(2,1)}, u32[]{:S(2)}) copy-start(bf16[12,16,1536]{2,1,0:T(8,128)(2,1)} %param.21) | copy-start | bytes 1769476
  142.6 10.9 %all-to-all-start.3 = ((bf16[2,200,768]{2,1,0:T(8,128)(2,1)}), bf16[2,200,768]{2,1,0:T(8,128)(2,1)S(1)}, u32[]{:S(2)}, u32[]{:S(2)}) async-start(bf16[2,200,768]{2,1,0:T(8,128)(2,1)} %broadcast_in_dim.64), calls=%async_computation.3 | async-start | bytes 1228800 | tf_op jit(solution)/shard_map/all_to_all | solution.py:212
  157.0 12.2 %copy-start.29 = (s32[400,2]{0,1:T(2,128)S(1)}, s32[400,2]{0,1:T(2,128)}, u32[]{:S(2)}) copy-start(s32[400,2]{0,1:T(2,128)} %param.13) | copy-start | bytes 9604
  157.0 90.0 %all-to-all-start.5 = ((bf16[12,64,3072]{2,0,1:T(8,128)(2,1)}), bf16[12,64,3072]{2,0,1:T(8,128)(2,1)}, u32[]{:S(2)}, u32[]{:S(2)}) async-start(bf16[12,64,3072]{2,0,1:T(8,128)(2,1)} %bitcast.122), calls=%async_computation.5 | async-start | bytes 12582912 | tf_op jit(solution)/shard_map/all_to_all | solution.py:239
  247.0 36.1 %all-to-all-start.4 = ((bf16[16,63,768]{2,1,0:T(8,128)(2,1)}), bf16[16,63,768]{2,1,0:T(8,128)(2,1)}, u32[]{:S(2)}, u32[]{:S(2)}) async-start(bf16[16,63,768]{2,1,0:T(8,128)(2,1)} %broadcast_select_fusion), calls=%async_computation.4 | async-start | bytes 3145728 | tf_op jit(solution)/shard_map/all_to_all | solution.py:225
  283.1 38.5 %all-to-all-start.9 = ((bf16[16,63,768]{2,1,0:T(8,128)(2,1)}), bf16[16,63,768]{2,1,0:T(8,128)(2,1)}, u32[]{:S(2)}, u32[]{:S(2)}) async-start(bf16[16,63,768]{2,1,0:T(8,128)(2,1)} %select_convert_fusion), calls=%async_computation.9 | async-start | bytes 3145728 | tf_op jit(solution)/shard_map/all_to_all | solution.py:225
  321.6 28.6 %all-to-all-start.6 = ((bf16[16,63,768]{2,1,0:T(8,128)(2,1)}), bf16[16,63,768]{2,1,0:T(8,128)(2,1)}, u32[]{:S(2)}, u32[]{:S(2)}) async-start(bf16[16,63,768]{2,1,0:T(8,128)(2,1)} %reshape.323), calls=%async_computation.6 | async-start | bytes 3145728 | tf_op jit(solution)/shard_map/all_to_all | solution.py:232
  340.6 1.7 copy-start.36
  350.3 28.8 %all-to-all-start.10 = ((bf16[16,63,768]{2,1,0:T(8,128)(2,1)}), bf16[16,63,768]{2,1,0:T(8,128)(2,1)}, u32[]{:S(2)}, u32[]{:S(2)}) async-start(bf16[16,63,768]{2,1,0:T(8,128)(2,1)} %reshape.330), calls=%async_computation.10 | async-start | bytes 3145728 | tf_op jit(solution)/shard_map/all_to_all | solution.py:232
  379.1 18.4 %copy-start.24 = (f32[400,16]{0,1:T(8,128)}, f32[400,16]{0,1:T(8,128)S(1)}, u32[]{:S(2)}) copy-start(f32[400,16]{0,1:T(8,128)S(1)} %multiply_reduce_fusion.11) | copy-start | bytes 76804
  416.1 18.2 %all-to-all-start.7 = ((f32[2,200,768]{2,1,0:T(8,128)}), f32[2,200,768]{2,1,0:T(8,128)}, u32[]{:S(2)}, u32[]{:S(2)}) async-start(f32[2,200,768]{2,1,0:T(8,128)} %bitcast.126), calls=%async_computation.7 | async-start | bytes 2457600 | tf_op jit(solution)/shard_map/all_to_all | solution.py:218
  420.7 15.0 %copy-start.7 = (f32[200,768]{1,0:T(8,128)S(1)}, f32[200,768]{1,0:T(8,128)}, u32[]{:S(2)}) copy-start(f32[200,768]{1,0:T(8,128)} %param.23) | copy-start | bytes 1843204
  437.8 15.1 %all-to-all-start.12 = ((bf16[2,200,768]{2,1,0:T(8,128)(2,1)}), bf16[2,200,768]{2,1,0:T(8,128)(2,1)S(1)}, u32[]{:S(2)}, u32[]{:S(2)}) async-start(bf16[2,200,768]{2,1,0:T(8,128)(2,1)} %broadcast_in_dim.78), calls=%async_computation.12 | async-start | bytes 1228800 | tf_op jit(solution)/shard_map/all_to_all | solution.py:212
  452.9 11.9 %copy-start.14 = (bf16[2,200,6,64]{1,3,2,0:T(8,128)(2,1)S(1)}, bf16[2,200,6,64]{1,3,2,0:T(8,128)(2,1)}, u32[]{:S(2)}) copy-start(bf16[2,200,6,64]{1,3,2,0:T(8,128)(2,1)} %copy.271) | copy-start | bytes 921604
  452.9 11.9 %copy-start.15 = (bf16[2,200,6,64]{1,3,2,0:T(8,128)(2,1)S(1)}, bf16[2,200,6,64]{1,3,2,0:T(8,128)(2,1)}, u32[]{:S(2)}) copy-start(bf16[2,200,6,64]{1,3,2,0:T(8,128)(2,1)} %copy.270) | copy-start | bytes 921604
  452.9 11.9 %copy-start.35 = (pred[200]{0:T(512)(128)(4,1)S(1)}, pred[200]{0:T(512)(128)(4,1)}, u32[]{:S(2)}) copy-start(pred[200]{0:T(512)(128)(4,1)} %copy-done.34) | copy-start | bytes 604
  452.9 14.7 %copy-start.9 = (bf16[2,200,768]{2,1,0:T(8,128)(2,1)}, bf16[2,200,768]{2,1,0:T(8,128)(2,1)S(1)}, u32[]{:S(2)}) copy-start(bf16[2,200,768]{2,1,0:T(8,128)(2,1)S(1)} %all-to-all-done.12) | copy-start | bytes 1843204
  452.9 51.9 %all-to-all-start.16 = ((bf16[64,12,1536]{2,1,0:T(8,128)(2,1)}), bf16[64,12,1536]{2,1,0:T(8,128)(2,1)}, u32[]{:S(2)}, u32[]{:S(2)}) async-start(bf16[64,12,1536]{2,1,0:T(8,128)(2,1)} %reshape.341), calls=%async_computation.16 | async-start | bytes 6291456 | tf_op jit(solution)/shard_map/all_to_all | solution.py:249
  470.1 4.2 copy-start.18
  490.9 4.8 copy-start.21
  490.9 5.8 copy-start.11
  498.8 10.5 %copy-start.20 = (bf16[1008,768]{1,0:T(8,128)(2,1)S(1)}, bf16[1008,768]{1,0:T(8,128)(2,1)}, u32[]{:S(2)}) copy-start(bf16[1008,768]{1,0:T(8,128)(2,1)} %reshape.320) | copy-start | bytes 4644868
  504.8 21.6 %all-to-all-start.13 = ((f32[2,200,768]{2,1,0:T(8,128)}), f32[2,200,768]{2,1,0:T(8,128)S(1)}, u32[]{:S(2)}, u32[]{:S(2)}) async-start(f32[2,200,768]{2,1,0:T(8,128)} %bitcast.134), calls=%async_computation.13 | async-start | bytes 2457600 | tf_op jit(solution)/shard_map/all_to_all | solution.py:218
  519.8 14.2 %copy-start.19 = (bf16[2,6,64,200]{3,2,1,0:T(8,128)(2,1)S(1)}, bf16[2,6,64,200]{3,2,1,0:T(8,128)(2,1)}, u32[]{:S(2)}) copy-start(bf16[2,6,64,200]{3,2,1,0:T(8,128)(2,1)} %convolution_convert_fusion.5) | copy-start | bytes 921604
  526.4 47.5 %all-to-all-start.15 = ((bf16[64,12,1536]{2,1,0:T(8,128)(2,1)}), bf16[64,12,1536]{2,1,0:T(8,128)(2,1)}, u32[]{:S(2)}, u32[]{:S(2)}) async-start(bf16[64,12,1536]{2,1,0:T(8,128)(2,1)} %reshape.340), calls=%async_computation.15 | async-start | bytes 6291456 | tf_op jit(solution)/shard_map/all_to_all | solution.py:249
  538.0 8.5 %copy-start.10 = (bf16[2,200,768]{2,1,0:T(8,128)(2,1)S(1)}, bf16[2,200,768]{2,1,0:T(8,128)(2,1)}, u32[]{:S(2)}) copy-start(bf16[2,200,768]{2,1,0:T(8,128)(2,1)} %copy-done.9) | copy-start | bytes 1843204
  548.0 3.3 copy-start.25
  553.9 5.6 copy-start.1
  553.9 5.6 copy-start.28
  553.9 5.6 copy-start.31
  553.9 5.6 copy-start.33
  558.5 2.8 copy-start.13
  558.5 2.8 copy-start.16
  558.5 2.8 copy-start.17
  573.9 50.3 %all-to-all-start.14 = ((bf16[64,12,1576]{2,1,0:T(8,128)(2,1)}), bf16[64,12,1576]{2,1,0:T(8,128)(2,1)}, u32[]{:S(2)}, u32[]{:S(2)}) async-start(bf16[64,12,1576]{2,1,0:T(8,128)(2,1)} %copy.312), calls=%async_computation.14 | async-start | bytes 6815744 | tf_op jit(solution)/shard_map/all_to_all | solution.py:188
  588.3 1.7 copy-start.4
  588.3 1.7 copy-start.8
  (6 other events, 6.6 us)

commit v12 on v11

--- a/solution.py
+++ b/solution.py
@@ -216,9 +216,13 @@
 def owned_rows(value):
     halves = lax.axis_size("tp")
     moved = lax.all_to_all(
-        value.reshape(halves, -1, value.shape[1]), "tp", split_axis=0, concat_axis=0, tiled=True
-    )
-    return jnp.sum(moved, axis=0)
+        value.astype(jnp.bfloat16).reshape(halves, -1, value.shape[1]),
+        "tp",
+        split_axis=0,
+        concat_axis=0,
+        tiled=True,
+    )
+    return jnp.sum(moved.astype(jnp.float32), axis=0)
 
 
 def to_owners(slots):

time: 647 us -> 626 us (0.968)
  waiting for transfers between devices: 193 us -> 177 us
    all_to_all x3, waiting for transfers between devices: 35.7 us -> 14 us  [owned_rows(): lax.all_to_all(value.astype(jnp.bfloat16).reshape(halves, -1, value.shape...]
    unnamed x83 -> x79, local copies, waits for them, and re-layouts: 13.1 us -> 14 us
  transfers between devices with their start and end apart: 16 -> 16, of which waited for: 11 -> 10; matrix products, arithmetic and copies ran while one was open for 36% -> 37% of each run, Pallas kernels for 0% -> 0%
where the time goes in v12:
time: 626 us; the launch traced here: 614 us
  waiting for transfers between devices  177 us (28%)
  local copies, waits for them, and re-layouts  175 us (28%)
  starting transfers between devices  108 us (17%)
  matrix products  97.8 us (16%)
  other arithmetic  36.5 us (6%)
  blocking collectives  17 us (3%)
    all_to_all x1, waiting for transfers between devices, expert_weights(): lax.all_to_all(spread.reshape(rows, experts * holders, units), FSDP, spli...  55.8 us
    all_to_all x1, waiting for transfers between devices, gather_dense(): full = lax.all_to_all(spread, FSDP, split_axis=0, concat_axis=0, tiled=True)  42.7 us
    all_to_all x1, waiting for transfers between devices, reduce_dense(): lax.all_to_all(wire.reshape(holders, rows, wire.shape[1]), FSDP, split_ax...  32.9 us
    all_to_all x2, starting transfers between devices, weight_home(): lax.all_to_all(partial.astype(jnp.bfloat16).reshape(devices, rows, units)...  20.5 us
    dot_general x1, matrix products, per_device(): owner_pre = jnp.dot(owner_x, own_in, preferred_element_type=f32)  19.2 us
    all_to_all x2, starting transfers between devices, to_owners(): moved = lax.all_to_all(slots, 'fa', split_axis=0, concat_axis=0, tiled=True)  16.7 us
    all_to_all x2, waiting for transfers between devices, weight_home(): lax.all_to_all(partial.astype(jnp.bfloat16).reshape(devices, rows, units)...  16.2 us
    all_to_all x4, waiting for transfers between devices, group_rows(): lax.all_to_all(spread, 'tp', split_axis=0, concat_axis=0, tiled=True)  15.9 us
  transfers between devices with their start and end apart: 16, of which 10 were waited for; matrix products, arithmetic and copies ran while one was open for 37% of the time, Pallas kernels for 0%

profile of v12, /device:TPU:1, one launch (start us, length us, event | category | flops | bytes accessed | tf_op | source)
XLA Modules:
  0.0 613.8 jit_solution(11681496372680157774)
XLA Ops:
  7.3 10.6 %all-to-all-start = ((bf16[64,12,1556]{2,1,0:T(8,128)(2,1)}), bf16[64,12,1556]{2,1,0:T(8,128)(2,1)}, u32[]{:S(2)}, u32[]{:S(2)}) async-start(bf16[64,12,1556]{2,1,0:T(8,128)(2,1)} %broadcast_in_dim.60), calls=%async_computation | async-start | bytes 6815744 | tf_op jit(solution)/shard_map/all_to_all | solution.py:149
  18.4 42.7 %all-to-all-done = bf16[64,12,1556]{2,1,0:T(8,128)(2,1)} async-done(((bf16[64,12,1556]{2,1,0:T(8,128)(2,1)}), bf16[64,12,1556]{2,1,0:T(8,128)(2,1)}, u32[]{:S(2)}, u32[]{:S(2)}) %all-to-all-start) | async-done | bytes 2390048 | tf_op jit(solution)/shard_map/all_to_all | solution.py:149
  61.0 4.2 reshape.314
  67.7 4.6 all-to-all-start.1
  73.6 3.8 copy.260
  102.0 4.4 fusion.68
  117.5 8.3 %all-to-all-done.2 = bf16[2,200,768]{2,1,0:T(8,128)(2,1)S(1)} async-done(((bf16[2,200,768]{2,1,0:T(8,128)(2,1)}), bf16[2,200,768]{2,1,0:T(8,128)(2,1)S(1)}, u32[]{:S(2)}, u32[]{:S(2)}) %all-to-all-start.2) | async-done | bytes 614432 | tf_op jit(solution)/shard_map/all_to_all | solution.py:218
  130.9 7.8 %all-to-all-done.8 = bf16[2,200,768]{2,1,0:T(8,128)(2,1)S(1)} async-done(((bf16[2,200,768]{2,1,0:T(8,128)(2,1)}), bf16[2,200,768]{2,1,0:T(8,128)(2,1)S(1)}, u32[]{:S(2)}, u32[]{:S(2)}) %all-to-all-start.8) | async-done | bytes 614432 | tf_op jit(solution)/shard_map/all_to_all | solution.py:212
  144.0 6.6 %all-to-all-done.3 = bf16[2,200,768]{2,1,0:T(8,128)(2,1)S(1)} async-done(((bf16[2,200,768]{2,1,0:T(8,128)(2,1)}), bf16[2,200,768]{2,1,0:T(8,128)(2,1)S(1)}, u32[]{:S(2)}, u32[]{:S(2)}) %all-to-all-start.3) | async-done | bytes 614432 | tf_op jit(solution)/shard_map/all_to_all | solution.py:212
  154.0 12.4 %all-to-all-start.5 = ((bf16[12,64,3072]{2,0,1:T(8,128)(2,1)}), bf16[12,64,3072]{2,0,1:T(8,128)(2,1)}, u32[]{:S(2)}, u32[]{:S(2)}) async-start(bf16[12,64,3072]{2,0,1:T(8,128)(2,1)} %bitcast.127), calls=%async_computation.5 | async-start | bytes 12582912 | tf_op jit(solution)/shard_map/all_to_all | solution.py:243
  169.5 5.3 scatter_custom_fusion.1
  174.8 5.3 scatter_custom_fusion
  180.2 5.2 gather_fusion
  188.5 55.8 %all-to-all-done.5 = bf16[12,64,3072]{2,0,1:T(8,128)(2,1)} async-done(((bf16[12,64,3072]{2,0,1:T(8,128)(2,1)}), bf16[12,64,3072]{2,0,1:T(8,128)(2,1)}, u32[]{:S(2)}, u32[]{:S(2)}) %all-to-all-start.5) | async-done | bytes 4718624 | tf_op jit(solution)/shard_map/all_to_all | solution.py:243
  244.3 9.6 %all-to-all-start.4 = ((bf16[16,63,768]{2,1,0:T(8,128)(2,1)}), bf16[16,63,768]{2,1,0:T(8,128)(2,1)}, u32[]{:S(2)}, u32[]{:S(2)}) async-start(bf16[16,63,768]{2,1,0:T(8,128)(2,1)} %broadcast_select_fusion), calls=%async_computation.4 | async-start | bytes 3145728 | tf_op jit(solution)/shard_map/all_to_all | solution.py:229
  254.0 5.2 gather_fusion.2
  264.1 5.3 scatter_custom_fusion.2
  272.9 7.5 %reshape.324 = bf16[768,3072]{1,0:T(8,128)(2,1)} reshape(bf16[64,12,1,3072]{3,1,0,2:T(8,128)(2,1)} %bitcast.17) | data formatting | bytes 9437184 | tf_op jit(solution)/shard_map/reshape | solution.py:246
  280.4 7.1 %all-to-all-start.9 = ((bf16[16,63,768]{2,1,0:T(8,128)(2,1)}), bf16[16,63,768]{2,1,0:T(8,128)(2,1)}, u32[]{:S(2)}, u32[]{:S(2)}) async-start(bf16[16,63,768]{2,1,0:T(8,128)(2,1)} %select_convert_fusion), calls=%async_computation.9 | async-start | bytes 3145728 | tf_op jit(solution)/shard_map/all_to_all | solution.py:229
  290.0 19.2 %multiply_convert_fusion = (bf16[1008,1536]{1,0:T(8,128)(2,1)S(1)}, f32[1008,1536]{1,0:T(8,128)}, f32[1008,1536]{1,0:T(8,128)}) fusion(bf16[1008,768]{1,0:T(8,128)(2,1)} %reshape.322, bf16[768,3072]{1,0:T(8,128)(2,1)} %reshape.324), kind=kOutput, calls=%fused_computation.15 | convolution fusion | flops 2478809088 | bytes 19390464 | tf_op jit(solution)/shard_map/dot_general | solution.py:321
  310.9 5.4 fusion.41
  318.9 6.8 %all-to-all-start.6 = ((bf16[16,63,768]{2,1,0:T(8,128)(2,1)}), bf16[16,63,768]{2,1,0:T(8,128)(2,1)}, u32[]{:S(2)}, u32[]{:S(2)}) async-start(bf16[16,63,768]{2,1,0:T(8,128)(2,1)} %reshape.325), calls=%async_computation.6 | async-start | bytes 3145728 | tf_op jit(solution)/shard_map/all_to_all | solution.py:236
  328.3 9.6 %add_convert_fusion = bf16[1008,1536]{1,0:T(8,128)(2,1)S(1)} fusion(f32[1008,1536]{1,0:T(8,128)} %get-tuple-element.67, f32[1008,1536]{1,0:T(8,128)} %get-tuple-element.76, bf16[1008,768]{1,0:T(8,128)(2,1)} %reshape.330, bf16[768,3072]{1,0:T(8,128)(2,1)} %reshape.324), kind=kOutput, calls=%fused_computation.14 | convolution fusion | flops 2399846400 | bytes 19390464 | tf_op jit(solution)/shard_map/dot_general | solution.py:339
  339.5 5.4 fusion.38
  347.6 6.9 %all-to-all-start.10 = ((bf16[16,63,768]{2,1,0:T(8,128)(2,1)}), bf16[16,63,768]{2,1,0:T(8,128)(2,1)}, u32[]{:S(2)}, u32[]{:S(2)}) async-start(bf16[16,63,768]{2,1,0:T(8,128)(2,1)} %reshape.331), calls=%async_computation.10 | async-start | bytes 3145728 | tf_op jit(solution)/shard_map/all_to_all | solution.py:236
  357.4 6.6 %gather_fusion.1 = f32[800,768]{1,0:T(8,128)} fusion(f32[1008,768]{1,0:T(8,128)} %reshape.348, s32[1024]{0:T(1024)S(1)} %pad_clamp_fusion), kind=kCustom, calls=%fused_computation.1 | custom fusion | bytes 4918400 | tf_op jit(solution)/shard_map/gather | solution.py:325
  364.0 4.1 reshape.328
  368.1 7.9 %multiply_reduce_fusion.1 = (f32[400,2]{1,0:T(8,128)S(1)}, bf16[400,768]{1,0:T(8,128)(2,1)}) fusion(f32[400,2,768]{2,1,0:T(2,128)} %reshape.328, f32[400,768]{1,0:T(8,128)S(1)} %convert.24, f32[400,2]{1,0:T(8,128)S(1)} %copy.270), kind=kLoop, calls=%fused_computation.39 | loop fusion | flops 2149600 | bytes 4307200 | tf_op jit(solution)/shard_map/reduce_sum | solution.py:337
  379.2 6.6 %gather_fusion.3 = f32[800,768]{1,0:T(8,128)} fusion(f32[1008,768]{1,0:T(8,128)} %reshape.351, s32[1024]{0:T(1024)S(1)} %pad_clamp_fusion), kind=kCustom, calls=%fused_computation.3 | custom fusion | bytes 4918400 | tf_op jit(solution)/shard_map/gather | solution.py:350
  385.8 4.1 reshape.334
  389.9 4.6 reduce_sum.284
  396.2 11.0 %all_to_all.95 = bf16[2,200,768]{2,1,0:T(8,128)(2,1)} all-to-all(bf16[2,200,768]{2,1,0:T(8,128)(2,1)S(1)} %bitcast.133), channel_id=1, replica_groups=mesh['fa'=16,'fb'=4,'tp'=2] {'tp'}, dimensions={0} | all-to-all | bytes 1228800 | tf_op jit(solution)/shard_map/all_to_all | solution.py:218
  412.6 5.7 all-to-all-done.7
  424.0 6.4 %convolution_convert_fusion = bf16[768,1536]{1,0:T(8,128)(2,1)} fusion(bf16[1008,768]{1,0:T(8,128)(2,1)} %reshape.330, bf16[1008,1536]{1,0:T(8,128)(2,1)} %copy-done.35), kind=kOutput, calls=%fused_computation.29 | convolution fusion | flops 2379350016 | bytes 7004160 | tf_op jit(solution)/shard_map/cd,cf->df/dot_general | solution.py:344
  430.4 4.8 reshape.341
  435.2 13.0 %all-to-all-start.16 = ((bf16[64,12,1536]{2,1,0:T(8,128)(2,1)}), bf16[64,12,1536]{2,1,0:T(8,128)(2,1)}, u32[]{:S(2)}, u32[]{:S(2)}) async-start(bf16[64,12,1536]{2,1,0:T(8,128)(2,1)} %reshape.341), calls=%async_computation.16 | async-start | bytes 6291456 | tf_op jit(solution)/shard_map/all_to_all | solution.py:253
  462.0 4.3 fusion.70
  468.9 5.4 fusion.73
  482.0 6.1 all-to-all-done.16
  488.1 4.5 all-to-all-start.13
  492.6 6.4 %convolution_convert_fusion.1 = bf16[768,1536]{1,0:T(8,128)(2,1)} fusion(bf16[1008,768]{1,0:T(8,128)(2,1)} %reshape.322, bf16[1008,1536]{1,0:T(8,128)(2,1)} %copy-done.34), kind=kOutput, calls=%fused_computation.30 | convolution fusion | flops 2379350016 | bytes 7004160 | tf_op jit(solution)/shard_map/cd,cf->df/dot_general | solution.py:343
  499.0 4.8 reshape.340
  504.6 7.5 %all-to-all-start.15 = ((bf16[64,12,1536]{2,1,0:T(8,128)(2,1)}), bf16[64,12,1536]{2,1,0:T(8,128)(2,1)}, u32[]{:S(2)}, u32[]{:S(2)}) async-start(bf16[64,12,1536]{2,1,0:T(8,128)(2,1)} %reshape.340), calls=%async_computation.15 | async-start | bytes 6291456 | tf_op jit(solution)/shard_map/all_to_all | solution.py:253
  526.3 4.6 convolution_convert_fusion.2
  542.1 10.0 %all-to-all-done.15 = bf16[64,12,1536]{2,1,0:T(8,128)(2,1)} async-done(((bf16[64,12,1536]{2,1,0:T(8,128)(2,1)}), bf16[64,12,1536]{2,1,0:T(8,128)(2,1)}, u32[]{:S(2)}, u32[]{:S(2)}) %all-to-all-start.15) | async-done | bytes 2359328 | tf_op jit(solution)/shard_map/all_to_all | solution.py:253
  552.1 7.6 %all-to-all-start.14 = ((bf16[64,12,1576]{2,1,0:T(8,128)(2,1)}), bf16[64,12,1576]{2,1,0:T(8,128)(2,1)}, u32[]{:S(2)}, u32[]{:S(2)}) async-start(bf16[64,12,1576]{2,1,0:T(8,128)(2,1)} %copy.306), calls=%async_computation.14 | async-start | bytes 6815744 | tf_op jit(solution)/shard_map/all_to_all | solution.py:188
  569.7 32.9 %all-to-all-done.14 = bf16[64,12,1576]{2,1,0:T(8,128)(2,1)} async-done(((bf16[64,12,1576]{2,1,0:T(8,128)(2,1)}), bf16[64,12,1576]{2,1,0:T(8,128)(2,1)}, u32[]{:S(2)}, u32[]{:S(2)}) %all-to-all-start.14) | async-done | bytes 2420768 | tf_op jit(solution)/shard_map/all_to_all | solution.py:188
  606.9 6.0 psum.7
  (229 shorter events, 172.1 us)
Async XLA Ops:
  7.3 10.7 %copy-start = (f32[200,768]{1,0:T(8,128)S(1)}, f32[200,768]{1,0:T(8,128)}, u32[]{:S(2)}) copy-start(f32[200,768]{1,0:T(8,128)} %param.12) | copy-start | bytes 1843204
  7.3 53.7 %all-to-all-start = ((bf16[64,12,1556]{2,1,0:T(8,128)(2,1)}), bf16[64,12,1556]{2,1,0:T(8,128)(2,1)}, u32[]{:S(2)}, u32[]{:S(2)}) async-start(bf16[64,12,1556]{2,1,0:T(8,128)(2,1)} %broadcast_in_dim.60), calls=%async_computation | async-start | bytes 6815744 | tf_op jit(solution)/shard_map/all_to_all | solution.py:149
  18.1 47.6 %copy-start.28 = (f32[200]{0:T(256)}, f32[200]{0:T(256)S(1)}, u32[]{:S(2)}) copy-start(f32[200]{0:T(256)S(1)} %broadcast_multiply_fusion.6) | copy-start | bytes 2404
  18.3 47.4 %copy-start.30 = (f32[200]{0:T(256)}, f32[200]{0:T(256)S(1)}, u32[]{:S(2)}) copy-start(f32[200]{0:T(256)S(1)} %add_rsqrt_fusion.1) | copy-start | bytes 2404
  65.2 45.4 %copy-start.2 = (bf16[768,1556]{1,0:T(8,128)(2,1)}, bf16[768,1556]{1,0:T(8,128)(2,1)S(1)}, u32[]{:S(2)}) copy-start(bf16[768,1556]{1,0:T(8,128)(2,1)S(1)} %reshape.314) | copy-start | bytes 7170052
  67.7 15.1 %all-to-all-start.1 = ((bf16[2,200,768]{2,1,0:T(8,128)(2,1)}), bf16[2,200,768]{2,1,0:T(8,128)(2,1)}, u32[]{:S(2)}, u32[]{:S(2)}) async-start(bf16[2,200,768]{2,1,0:T(8,128)(2,1)} %broadcast_in_dim.61), calls=%async_computation.1 | async-start | bytes 1228800 | tf_op jit(solution)/shard_map/all_to_all | solution.py:212
  72.2 29.8 %copy-start.32 = (pred[200]{0:T(512)(128)(4,1)}, pred[200]{0:T(512)(128)(4,1)S(1)}, u32[]{:S(2)}) copy-start(pred[200]{0:T(512)(128)(4,1)S(1)} %iota_compare_fusion.3) | copy-start | bytes 604
  112.9 13.0 %all-to-all-start.2 = ((bf16[2,200,768]{2,1,0:T(8,128)(2,1)}), bf16[2,200,768]{2,1,0:T(8,128)(2,1)S(1)}, u32[]{:S(2)}, u32[]{:S(2)}) async-start(bf16[2,200,768]{2,1,0:T(8,128)(2,1)} %bitcast.132), calls=%async_computation.2 | async-start | bytes 1228800 | tf_op jit(solution)/shard_map/all_to_all | solution.py:218
  126.7 12.0 %all-to-all-start.8 = ((bf16[2,200,768]{2,1,0:T(8,128)(2,1)}), bf16[2,200,768]{2,1,0:T(8,128)(2,1)S(1)}, u32[]{:S(2)}, u32[]{:S(2)}) async-start(bf16[2,200,768]{2,1,0:T(8,128)(2,1)} %broadcast_in_dim.76), calls=%async_computation.8 | async-start | bytes 1228800 | tf_op jit(solution)/shard_map/all_to_all | solution.py:212
  130.3 12.8 %copy-start.20 = (bf16[12,16,1536]{2,1,0:T(8,128)(2,1)S(1)}, bf16[12,16,1536]{2,1,0:T(8,128)(2,1)}, u32[]{:S(2)}) copy-start(bf16[12,16,1536]{2,1,0:T(8,128)(2,1)} %param.22) | copy-start | bytes 1769476
  130.5 12.7 %copy-start.21 = (bf16[12,16,1536]{2,1,0:T(8,128)(2,1)S(1)}, bf16[12,16,1536]{2,1,0:T(8,128)(2,1)}, u32[]{:S(2)}) copy-start(bf16[12,16,1536]{2,1,0:T(8,128)(2,1)} %param.21) | copy-start | bytes 1769476
  139.6 10.9 %all-to-all-start.3 = ((bf16[2,200,768]{2,1,0:T(8,128)(2,1)}), bf16[2,200,768]{2,1,0:T(8,128)(2,1)S(1)}, u32[]{:S(2)}, u32[]{:S(2)}) async-start(bf16[2,200,768]{2,1,0:T(8,128)(2,1)} %broadcast_in_dim.64), calls=%async_computation.3 | async-start | bytes 1228800 | tf_op jit(solution)/shard_map/all_to_all | solution.py:212
  154.0 12.4 %copy-start.27 = (s32[400,2]{0,1:T(2,128)S(1)}, s32[400,2]{0,1:T(2,128)}, u32[]{:S(2)}) copy-start(s32[400,2]{0,1:T(2,128)} %param.13) | copy-start | bytes 9604
  154.0 90.2 %all-to-all-start.5 = ((bf16[12,64,3072]{2,0,1:T(8,128)(2,1)}), bf16[12,64,3072]{2,0,1:T(8,128)(2,1)}, u32[]{:S(2)}, u32[]{:S(2)}) async-start(bf16[12,64,3072]{2,0,1:T(8,128)(2,1)} %bitcast.127), calls=%async_computation.5 | async-start | bytes 12582912 | tf_op jit(solution)/shard_map/all_to_all | solution.py:243
  244.3 36.1 %all-to-all-start.4 = ((bf16[16,63,768]{2,1,0:T(8,128)(2,1)}), bf16[16,63,768]{2,1,0:T(8,128)(2,1)}, u32[]{:S(2)}, u32[]{:S(2)}) async-start(bf16[16,63,768]{2,1,0:T(8,128)(2,1)} %broadcast_select_fusion), calls=%async_computation.4 | async-start | bytes 3145728 | tf_op jit(solution)/shard_map/all_to_all | solution.py:229
  280.4 38.5 %all-to-all-start.9 = ((bf16[16,63,768]{2,1,0:T(8,128)(2,1)}), bf16[16,63,768]{2,1,0:T(8,128)(2,1)}, u32[]{:S(2)}, u32[]{:S(2)}) async-start(bf16[16,63,768]{2,1,0:T(8,128)(2,1)} %select_convert_fusion), calls=%async_computation.9 | async-start | bytes 3145728 | tf_op jit(solution)/shard_map/all_to_all | solution.py:229
  309.3 1.6 copy-start.35
  318.9 28.6 %all-to-all-start.6 = ((bf16[16,63,768]{2,1,0:T(8,128)(2,1)}), bf16[16,63,768]{2,1,0:T(8,128)(2,1)}, u32[]{:S(2)}, u32[]{:S(2)}) async-start(bf16[16,63,768]{2,1,0:T(8,128)(2,1)} %reshape.325), calls=%async_computation.6 | async-start | bytes 3145728 | tf_op jit(solution)/shard_map/all_to_all | solution.py:236
  337.9 1.7 copy-start.34
  347.6 28.7 %all-to-all-start.10 = ((bf16[16,63,768]{2,1,0:T(8,128)(2,1)}), bf16[16,63,768]{2,1,0:T(8,128)(2,1)}, u32[]{:S(2)}, u32[]{:S(2)}) async-start(bf16[16,63,768]{2,1,0:T(8,128)(2,1)} %reshape.331), calls=%async_computation.10 | async-start | bytes 3145728 | tf_op jit(solution)/shard_map/all_to_all | solution.py:236
  376.2 18.4 %copy-start.22 = (f32[400,16]{0,1:T(8,128)}, f32[400,16]{0,1:T(8,128)S(1)}, u32[]{:S(2)}) copy-start(f32[400,16]{0,1:T(8,128)S(1)} %multiply_reduce_fusion.11) | copy-start | bytes 76804
  407.2 11.1 %copy-start.6 = (f32[200,768]{1,0:T(8,128)S(1)}, f32[200,768]{1,0:T(8,128)}, u32[]{:S(2)}) copy-start(f32[200,768]{1,0:T(8,128)} %param.23) | copy-start | bytes 1843204
  407.2 11.0 %all-to-all-start.7 = ((bf16[2,200,768]{2,1,0:T(8,128)(2,1)}), bf16[2,200,768]{2,1,0:T(8,128)(2,1)S(1)}, u32[]{:S(2)}, u32[]{:S(2)}) async-start(bf16[2,200,768]{2,1,0:T(8,128)(2,1)} %bitcast.18), calls=%async_computation.7 | async-start | bytes 1228800 | tf_op jit(solution)/shard_map/all_to_all | solution.py:218
  420.5 14.7 %all-to-all-start.12 = ((bf16[2,200,768]{2,1,0:T(8,128)(2,1)}), bf16[2,200,768]{2,1,0:T(8,128)(2,1)S(1)}, u32[]{:S(2)}, u32[]{:S(2)}) async-start(bf16[2,200,768]{2,1,0:T(8,128)(2,1)} %broadcast_in_dim.78), calls=%async_computation.12 | async-start | bytes 1228800 | tf_op jit(solution)/shard_map/all_to_all | solution.py:212
  435.2 13.1 %copy-start.14 = (bf16[2,200,6,64]{1,3,2,0:T(8,128)(2,1)S(1)}, bf16[2,200,6,64]{1,3,2,0:T(8,128)(2,1)}, u32[]{:S(2)}) copy-start(bf16[2,200,6,64]{1,3,2,0:T(8,128)(2,1)} %copy.266) | copy-start | bytes 921604
  435.2 13.1 %copy-start.15 = (bf16[2,200,6,64]{1,3,2,0:T(8,128)(2,1)S(1)}, bf16[2,200,6,64]{1,3,2,0:T(8,128)(2,1)}, u32[]{:S(2)}) copy-start(bf16[2,200,6,64]{1,3,2,0:T(8,128)(2,1)} %copy.265) | copy-start | bytes 921604
  435.2 13.1 %copy-start.33 = (pred[200]{0:T(512)(128)(4,1)S(1)}, pred[200]{0:T(512)(128)(4,1)}, u32[]{:S(2)}) copy-start(pred[200]{0:T(512)(128)(4,1)} %copy-done.32) | copy-start | bytes 604
  435.2 15.9 %copy-start.8 = (bf16[2,200,768]{2,1,0:T(8,128)(2,1)}, bf16[2,200,768]{2,1,0:T(8,128)(2,1)S(1)}, u32[]{:S(2)}) copy-start(bf16[2,200,768]{2,1,0:T(8,128)(2,1)S(1)} %all-to-all-done.12) | copy-start | bytes 1843204
  435.2 52.9 %all-to-all-start.16 = ((bf16[64,12,1536]{2,1,0:T(8,128)(2,1)}), bf16[64,12,1536]{2,1,0:T(8,128)(2,1)}, u32[]{:S(2)}, u32[]{:S(2)}) async-start(bf16[64,12,1536]{2,1,0:T(8,128)(2,1)} %reshape.341), calls=%async_computation.16 | async-start | bytes 6291456 | tf_op jit(solution)/shard_map/all_to_all | solution.py:253
  453.5 4.2 copy-start.17
  460.6 1.5 copy-start.5
  474.3 4.8 copy-start.19
  474.3 5.8 copy-start.12
  479.2 1.0 copy-start.13
  488.1 15.7 %all-to-all-start.13 = ((bf16[2,200,768]{2,1,0:T(8,128)(2,1)}), bf16[2,200,768]{2,1,0:T(8,128)(2,1)S(1)}, u32[]{:S(2)}, u32[]{:S(2)}) async-start(bf16[2,200,768]{2,1,0:T(8,128)(2,1)} %bitcast.137), calls=%async_computation.13 | async-start | bytes 1228800 | tf_op jit(solution)/shard_map/all_to_all | solution.py:218
  504.6 47.5 %all-to-all-start.15 = ((bf16[64,12,1536]{2,1,0:T(8,128)(2,1)}), bf16[64,12,1536]{2,1,0:T(8,128)(2,1)}, u32[]{:S(2)}, u32[]{:S(2)}) async-start(bf16[64,12,1536]{2,1,0:T(8,128)(2,1)} %reshape.340), calls=%async_computation.15 | async-start | bytes 6291456 | tf_op jit(solution)/shard_map/all_to_all | solution.py:253
  513.5 1.8 copy-start.23
  514.7 4.1 copy-start.9
  520.4 3.3 copy-start.18
  526.3 4.6 copy-start.11
  526.3 5.7 copy-start.1
  526.3 5.7 copy-start.26
  526.3 5.7 copy-start.29
  526.3 5.7 copy-start.31
  530.9 2.9 copy-start.16
  552.1 50.5 %all-to-all-start.14 = ((bf16[64,12,1576]{2,1,0:T(8,128)(2,1)}), bf16[64,12,1576]{2,1,0:T(8,128)(2,1)}, u32[]{:S(2)}, u32[]{:S(2)}) async-start(bf16[64,12,1576]{2,1,0:T(8,128)(2,1)} %copy.306), calls=%async_computation.14 | async-start | bytes 6815744 | tf_op jit(solution)/shard_map/all_to_all | solution.py:188
  566.9 1.7 copy-start.4
  567.0 1.7 copy-start.7
  (4 other events, 3.3 us)

commit v13 on v12

--- a/solution.py
+++ b/solution.py
@@ -200,7 +200,14 @@
     qkv_grad = jnp.transpose(part[:, :at].reshape(rows, 3, heads_width), (1, 0, 2))
     proj_grad = part[:, at : at + heads_width].T
     at += heads_width
-    shared = lax.psum(part[:, at:], "tp")
+    small = part[:, at:]
+    halves = lax.axis_size("tp")
+    shared = jnp.sum(
+        lax.all_to_all(
+            jnp.broadcast_to(small[None], (halves,) + small.shape), "tp", 0, 0, tiled=True
+        ),
+        axis=0,
+    )
     router_grad = shared[:, :experts]
     norm_grads = [shared[:, experts + i] for i in range(len(norm_parts))]
     return qkv_grad, proj_grad, router_grad, norm_grads

time: 626 us -> 629 us (level)
    unnamed x79 -> x81, local copies, waits for them, and re-layouts: 14 us -> 13.9 us
  transfers between devices with their start and end apart: 16 -> 17, of which waited for: 10 -> 11; matrix products, arithmetic and copies ran while one was open for 37% -> 37% of each run, Pallas kernels for 0% -> 0%
where the time goes in v13:
time: 629 us; the launch traced here: 616 us
  waiting for transfers between devices  181 us (29%)
  local copies, waits for them, and re-layouts  175 us (28%)
  starting transfers between devices  113 us (18%)
  matrix products  97.5 us (16%)
  other arithmetic  37.1 us (6%)
  blocking collectives  11 us (2%)
    all_to_all x1, waiting for transfers between devices, expert_weights(): lax.all_to_all(spread.reshape(rows, experts * holders, units), FSDP, spli...  55.8 us
    all_to_all x1, waiting for transfers between devices, gather_dense(): full = lax.all_to_all(spread, FSDP, split_axis=0, concat_axis=0, tiled=True)  42.7 us
    all_to_all x1, waiting for transfers between devices, reduce_dense(): lax.all_to_all(wire.reshape(holders, rows, wire.shape[1]), FSDP, split_ax...  32.9 us
    all_to_all x2, starting transfers between devices, weight_home(): lax.all_to_all(partial.astype(jnp.bfloat16).reshape(devices, rows, units)...  20.5 us
    dot_general x1, matrix products, per_device(): owner_pre = jnp.dot(owner_x, own_in, preferred_element_type=f32)  19.2 us
    all_to_all x2, waiting for transfers between devices, weight_home(): lax.all_to_all(partial.astype(jnp.bfloat16).reshape(devices, rows, units)...  17 us
    all_to_all x2, starting transfers between devices, to_owners(): moved = lax.all_to_all(slots, 'fa', split_axis=0, concat_axis=0, tiled=True)  16.7 us
    all_to_all x4, waiting for transfers between devices, group_rows(): lax.all_to_all(spread, 'tp', split_axis=0, concat_axis=0, tiled=True)  15.9 us
  transfers between devices with their start and end apart: 17, of which 11 were waited for; matrix products, arithmetic and copies ran while one was open for 37% of the time, Pallas kernels for 0%

profile of v13, /device:TPU:1, one launch (start us, length us, event | category | flops | bytes accessed | tf_op | source)
XLA Modules:
  0.0 616.4 jit_solution(5835870972824332575)
XLA Ops:
  7.3 10.6 %all-to-all-start = ((bf16[64,12,1556]{2,1,0:T(8,128)(2,1)}), bf16[64,12,1556]{2,1,0:T(8,128)(2,1)}, u32[]{:S(2)}, u32[]{:S(2)}) async-start(bf16[64,12,1556]{2,1,0:T(8,128)(2,1)} %broadcast_in_dim.62), calls=%async_computation | async-start | bytes 6815744 | tf_op jit(solution)/shard_map/all_to_all | solution.py:149
  18.4 42.7 %all-to-all-done = bf16[64,12,1556]{2,1,0:T(8,128)(2,1)} async-done(((bf16[64,12,1556]{2,1,0:T(8,128)(2,1)}), bf16[64,12,1556]{2,1,0:T(8,128)(2,1)}, u32[]{:S(2)}, u32[]{:S(2)}) %all-to-all-start) | async-done | bytes 2390048 | tf_op jit(solution)/shard_map/all_to_all | solution.py:149
  61.0 4.2 reshape.315
  67.7 4.6 all-to-all-start.1
  73.6 3.8 copy.260
  102.0 4.4 fusion.68
  117.5 8.3 %all-to-all-done.2 = bf16[2,200,768]{2,1,0:T(8,128)(2,1)S(1)} async-done(((bf16[2,200,768]{2,1,0:T(8,128)(2,1)}), bf16[2,200,768]{2,1,0:T(8,128)(2,1)S(1)}, u32[]{:S(2)}, u32[]{:S(2)}) %all-to-all-start.2) | async-done | bytes 614432 | tf_op jit(solution)/shard_map/all_to_all | solution.py:225
  130.9 7.8 %all-to-all-done.8 = bf16[2,200,768]{2,1,0:T(8,128)(2,1)S(1)} async-done(((bf16[2,200,768]{2,1,0:T(8,128)(2,1)}), bf16[2,200,768]{2,1,0:T(8,128)(2,1)S(1)}, u32[]{:S(2)}, u32[]{:S(2)}) %all-to-all-start.8) | async-done | bytes 614432 | tf_op jit(solution)/shard_map/all_to_all | solution.py:219
  143.9 6.6 %all-to-all-done.3 = bf16[2,200,768]{2,1,0:T(8,128)(2,1)S(1)} async-done(((bf16[2,200,768]{2,1,0:T(8,128)(2,1)}), bf16[2,200,768]{2,1,0:T(8,128)(2,1)S(1)}, u32[]{:S(2)}, u32[]{:S(2)}) %all-to-all-start.3) | async-done | bytes 614432 | tf_op jit(solution)/shard_map/all_to_all | solution.py:219
  154.0 12.4 %all-to-all-start.5 = ((bf16[12,64,3072]{2,0,1:T(8,128)(2,1)}), bf16[12,64,3072]{2,0,1:T(8,128)(2,1)}, u32[]{:S(2)}, u32[]{:S(2)}) async-start(bf16[12,64,3072]{2,0,1:T(8,128)(2,1)} %bitcast.127), calls=%async_computation.5 | async-start | bytes 12582912 | tf_op jit(solution)/shard_map/all_to_all | solution.py:250
  169.5 5.3 scatter_custom_fusion.1
  174.8 5.3 scatter_custom_fusion
  180.2 5.2 gather_fusion
  188.4 55.8 %all-to-all-done.5 = bf16[12,64,3072]{2,0,1:T(8,128)(2,1)} async-done(((bf16[12,64,3072]{2,0,1:T(8,128)(2,1)}), bf16[12,64,3072]{2,0,1:T(8,128)(2,1)}, u32[]{:S(2)}, u32[]{:S(2)}) %all-to-all-start.5) | async-done | bytes 4718624 | tf_op jit(solution)/shard_map/all_to_all | solution.py:250
  244.2 9.6 %all-to-all-start.4 = ((bf16[16,63,768]{2,1,0:T(8,128)(2,1)}), bf16[16,63,768]{2,1,0:T(8,128)(2,1)}, u32[]{:S(2)}, u32[]{:S(2)}) async-start(bf16[16,63,768]{2,1,0:T(8,128)(2,1)} %broadcast_select_fusion), calls=%async_computation.4 | async-start | bytes 3145728 | tf_op jit(solution)/shard_map/all_to_all | solution.py:236
  253.9 5.2 gather_fusion.2
  264.1 5.3 scatter_custom_fusion.2
  272.9 7.5 %reshape.325 = bf16[768,3072]{1,0:T(8,128)(2,1)} reshape(bf16[64,12,1,3072]{3,1,0,2:T(8,128)(2,1)} %bitcast.17) | data formatting | bytes 9437184 | tf_op jit(solution)/shard_map/reshape | solution.py:253
  280.4 7.1 %all-to-all-start.9 = ((bf16[16,63,768]{2,1,0:T(8,128)(2,1)}), bf16[16,63,768]{2,1,0:T(8,128)(2,1)}, u32[]{:S(2)}, u32[]{:S(2)}) async-start(bf16[16,63,768]{2,1,0:T(8,128)(2,1)} %select_convert_fusion), calls=%async_computation.9 | async-start | bytes 3145728 | tf_op jit(solution)/shard_map/all_to_all | solution.py:236
  290.0 19.2 %multiply_convert_fusion = (bf16[1008,1536]{1,0:T(8,128)(2,1)S(1)}, f32[1008,1536]{1,0:T(8,128)}, f32[1008,1536]{1,0:T(8,128)}) fusion(bf16[1008,768]{1,0:T(8,128)(2,1)} %reshape.323, bf16[768,3072]{1,0:T(8,128)(2,1)} %reshape.325), kind=kOutput, calls=%fused_computation.15 | convolution fusion | flops 2478809088 | bytes 19390464 | tf_op jit(solution)/shard_map/dot_general | solution.py:328
  310.9 5.4 fusion.41
  318.9 6.8 %all-to-all-start.6 = ((bf16[16,63,768]{2,1,0:T(8,128)(2,1)}), bf16[16,63,768]{2,1,0:T(8,128)(2,1)}, u32[]{:S(2)}, u32[]{:S(2)}) async-start(bf16[16,63,768]{2,1,0:T(8,128)(2,1)} %reshape.326), calls=%async_computation.6 | async-start | bytes 3145728 | tf_op jit(solution)/shard_map/all_to_all | solution.py:243
  328.2 9.6 %add_convert_fusion = bf16[1008,1536]{1,0:T(8,128)(2,1)S(1)} fusion(f32[1008,1536]{1,0:T(8,128)} %get-tuple-element.67, f32[1008,1536]{1,0:T(8,128)} %get-tuple-element.76, bf16[1008,768]{1,0:T(8,128)(2,1)} %reshape.331, bf16[768,3072]{1,0:T(8,128)(2,1)} %reshape.325), kind=kOutput, calls=%fused_computation.14 | convolution fusion | flops 2399846400 | bytes 19390464 | tf_op jit(solution)/shard_map/dot_general | solution.py:346
  339.5 5.4 fusion.38
  347.5 6.9 %all-to-all-start.10 = ((bf16[16,63,768]{2,1,0:T(8,128)(2,1)}), bf16[16,63,768]{2,1,0:T(8,128)(2,1)}, u32[]{:S(2)}, u32[]{:S(2)}) async-start(bf16[16,63,768]{2,1,0:T(8,128)(2,1)} %reshape.332), calls=%async_computation.10 | async-start | bytes 3145728 | tf_op jit(solution)/shard_map/all_to_all | solution.py:243
  357.4 6.6 %gather_fusion.1 = f32[800,768]{1,0:T(8,128)} fusion(f32[1008,768]{1,0:T(8,128)} %reshape.349, s32[1024]{0:T(1024)S(1)} %pad_clamp_fusion), kind=kCustom, calls=%fused_computation.1 | custom fusion | bytes 4918400 | tf_op jit(solution)/shard_map/gather | solution.py:332
  364.0 4.1 reshape.329
  368.1 7.9 %multiply_reduce_fusion.1 = (f32[400,2]{1,0:T(8,128)S(1)}, bf16[400,768]{1,0:T(8,128)(2,1)}) fusion(f32[400,2,768]{2,1,0:T(2,128)} %reshape.329, f32[400,768]{1,0:T(8,128)S(1)} %convert.24, f32[400,2]{1,0:T(8,128)S(1)} %copy.270), kind=kLoop, calls=%fused_computation.39 | loop fusion | flops 2149600 | bytes 4307200 | tf_op jit(solution)/shard_map/reduce_sum | solution.py:344
  379.2 6.6 %gather_fusion.3 = f32[800,768]{1,0:T(8,128)} fusion(f32[1008,768]{1,0:T(8,128)} %reshape.352, s32[1024]{0:T(1024)S(1)} %pad_clamp_fusion), kind=kCustom, calls=%fused_computation.3 | custom fusion | bytes 4918400 | tf_op jit(solution)/shard_map/gather | solution.py:357
  385.8 4.1 reshape.335
  389.9 4.6 reduce_sum.293
  396.2 11.0 %all_to_all.100 = bf16[2,200,768]{2,1,0:T(8,128)(2,1)} all-to-all(bf16[2,200,768]{2,1,0:T(8,128)(2,1)S(1)} %bitcast.133), channel_id=1, replica_groups=mesh['fa'=16,'fb'=4,'tp'=2] {'tp'}, dimensions={0} | all-to-all | bytes 1228800 | tf_op jit(solution)/shard_map/all_to_all | solution.py:225
  412.6 5.7 all-to-all-done.7
  424.0 6.4 %convolution_convert_fusion = bf16[768,1536]{1,0:T(8,128)(2,1)} fusion(bf16[1008,768]{1,0:T(8,128)(2,1)} %reshape.331, bf16[1008,1536]{1,0:T(8,128)(2,1)} %copy-done.35), kind=kOutput, calls=%fused_computation.29 | convolution fusion | flops 2379350016 | bytes 7004160 | tf_op jit(solution)/shard_map/cd,cf->df/dot_general | solution.py:351
  430.4 4.8 reshape.342
  435.2 13.0 %all-to-all-start.17 = ((bf16[64,12,1536]{2,1,0:T(8,128)(2,1)}), bf16[64,12,1536]{2,1,0:T(8,128)(2,1)}, u32[]{:S(2)}, u32[]{:S(2)}) async-start(bf16[64,12,1536]{2,1,0:T(8,128)(2,1)} %reshape.342), calls=%async_computation.17 | async-start | bytes 6291456 | tf_op jit(solution)/shard_map/all_to_all | solution.py:260
  462.0 4.2 fusion.70
  468.9 5.4 fusion.73
  481.9 6.2 all-to-all-done.17
  488.1 4.5 all-to-all-start.13
  492.6 6.4 %convolution_convert_fusion.1 = bf16[768,1536]{1,0:T(8,128)(2,1)} fusion(bf16[1008,768]{1,0:T(8,128)(2,1)} %reshape.323, bf16[1008,1536]{1,0:T(8,128)(2,1)} %copy-done.34), kind=kOutput, calls=%fused_computation.30 | convolution fusion | flops 2379350016 | bytes 7004160 | tf_op jit(solution)/shard_map/cd,cf->df/dot_general | solution.py:350
  499.0 4.8 reshape.341
  503.8 7.5 %all-to-all-start.16 = ((bf16[64,12,1536]{2,1,0:T(8,128)(2,1)}), bf16[64,12,1536]{2,1,0:T(8,128)(2,1)}, u32[]{:S(2)}, u32[]{:S(2)}) async-start(bf16[64,12,1536]{2,1,0:T(8,128)(2,1)} %reshape.341), calls=%async_computation.16 | async-start | bytes 6291456 | tf_op jit(solution)/shard_map/all_to_all | solution.py:260
  525.1 4.3 convolution_convert_fusion.2
  540.4 10.9 %all-to-all-done.16 = bf16[64,12,1536]{2,1,0:T(8,128)(2,1)} async-done(((bf16[64,12,1536]{2,1,0:T(8,128)(2,1)}), bf16[64,12,1536]{2,1,0:T(8,128)(2,1)}, u32[]{:S(2)}, u32[]{:S(2)}) %all-to-all-start.16) | async-done | bytes 2359328 | tf_op jit(solution)/shard_map/all_to_all | solution.py:260
  551.3 7.6 %all-to-all-start.14 = ((bf16[64,12,1576]{2,1,0:T(8,128)(2,1)}), bf16[64,12,1576]{2,1,0:T(8,128)(2,1)}, u32[]{:S(2)}, u32[]{:S(2)}) async-start(bf16[64,12,1576]{2,1,0:T(8,128)(2,1)} %copy.306), calls=%async_computation.14 | async-start | bytes 6815744 | tf_op jit(solution)/shard_map/all_to_all | solution.py:188
  568.8 32.9 %all-to-all-done.14 = bf16[64,12,1576]{2,1,0:T(8,128)(2,1)} async-done(((bf16[64,12,1576]{2,1,0:T(8,128)(2,1)}), bf16[64,12,1576]{2,1,0:T(8,128)(2,1)}, u32[]{:S(2)}, u32[]{:S(2)}) %all-to-all-start.14) | async-done | bytes 2420768 | tf_op jit(solution)/shard_map/all_to_all | solution.py:188
  605.4 4.5 all-to-all-start.15
  (236 shorter events, 175.5 us)
Async XLA Ops:
  7.3 10.7 %copy-start = (f32[200,768]{1,0:T(8,128)S(1)}, f32[200,768]{1,0:T(8,128)}, u32[]{:S(2)}) copy-start(f32[200,768]{1,0:T(8,128)} %param.12) | copy-start | bytes 1843204
  7.3 53.7 %all-to-all-start = ((bf16[64,12,1556]{2,1,0:T(8,128)(2,1)}), bf16[64,12,1556]{2,1,0:T(8,128)(2,1)}, u32[]{:S(2)}, u32[]{:S(2)}) async-start(bf16[64,12,1556]{2,1,0:T(8,128)(2,1)} %broadcast_in_dim.62), calls=%async_computation | async-start | bytes 6815744 | tf_op jit(solution)/shard_map/all_to_all | solution.py:149
  18.1 47.6 %copy-start.28 = (f32[200]{0:T(256)}, f32[200]{0:T(256)S(1)}, u32[]{:S(2)}) copy-start(f32[200]{0:T(256)S(1)} %broadcast_multiply_fusion.6) | copy-start | bytes 2404
  18.3 47.4 %copy-start.30 = (f32[200]{0:T(256)}, f32[200]{0:T(256)S(1)}, u32[]{:S(2)}) copy-start(f32[200]{0:T(256)S(1)} %add_rsqrt_fusion.1) | copy-start | bytes 2404
  65.2 45.4 %copy-start.2 = (bf16[768,1556]{1,0:T(8,128)(2,1)}, bf16[768,1556]{1,0:T(8,128)(2,1)S(1)}, u32[]{:S(2)}) copy-start(bf16[768,1556]{1,0:T(8,128)(2,1)S(1)} %reshape.315) | copy-start | bytes 7170052
  67.7 15.1 %all-to-all-start.1 = ((bf16[2,200,768]{2,1,0:T(8,128)(2,1)}), bf16[2,200,768]{2,1,0:T(8,128)(2,1)}, u32[]{:S(2)}, u32[]{:S(2)}) async-start(bf16[2,200,768]{2,1,0:T(8,128)(2,1)} %broadcast_in_dim.63), calls=%async_computation.1 | async-start | bytes 1228800 | tf_op jit(solution)/shard_map/all_to_all | solution.py:219
  72.2 29.8 %copy-start.32 = (pred[200]{0:T(512)(128)(4,1)}, pred[200]{0:T(512)(128)(4,1)S(1)}, u32[]{:S(2)}) copy-start(pred[200]{0:T(512)(128)(4,1)S(1)} %iota_compare_fusion.3) | copy-start | bytes 604
  112.9 13.0 %all-to-all-start.2 = ((bf16[2,200,768]{2,1,0:T(8,128)(2,1)}), bf16[2,200,768]{2,1,0:T(8,128)(2,1)S(1)}, u32[]{:S(2)}, u32[]{:S(2)}) async-start(bf16[2,200,768]{2,1,0:T(8,128)(2,1)} %bitcast.132), calls=%async_computation.2 | async-start | bytes 1228800 | tf_op jit(solution)/shard_map/all_to_all | solution.py:225
  126.7 12.0 %all-to-all-start.8 = ((bf16[2,200,768]{2,1,0:T(8,128)(2,1)}), bf16[2,200,768]{2,1,0:T(8,128)(2,1)S(1)}, u32[]{:S(2)}, u32[]{:S(2)}) async-start(bf16[2,200,768]{2,1,0:T(8,128)(2,1)} %broadcast_in_dim.78), calls=%async_computation.8 | async-start | bytes 1228800 | tf_op jit(solution)/shard_map/all_to_all | solution.py:219
  130.3 12.8 %copy-start.20 = (bf16[12,16,1536]{2,1,0:T(8,128)(2,1)S(1)}, bf16[12,16,1536]{2,1,0:T(8,128)(2,1)}, u32[]{:S(2)}) copy-start(bf16[12,16,1536]{2,1,0:T(8,128)(2,1)} %param.22) | copy-start | bytes 1769476
  130.5 12.6 %copy-start.21 = (bf16[12,16,1536]{2,1,0:T(8,128)(2,1)S(1)}, bf16[12,16,1536]{2,1,0:T(8,128)(2,1)}, u32[]{:S(2)}) copy-start(bf16[12,16,1536]{2,1,0:T(8,128)(2,1)} %param.21) | copy-start | bytes 1769476
  139.6 10.9 %all-to-all-start.3 = ((bf16[2,200,768]{2,1,0:T(8,128)(2,1)}), bf16[2,200,768]{2,1,0:T(8,128)(2,1)S(1)}, u32[]{:S(2)}, u32[]{:S(2)}) async-start(bf16[2,200,768]{2,1,0:T(8,128)(2,1)} %broadcast_in_dim.70), calls=%async_computation.3 | async-start | bytes 1228800 | tf_op jit(solution)/shard_map/all_to_all | solution.py:219
  154.0 12.4 %copy-start.27 = (s32[400,2]{0,1:T(2,128)S(1)}, s32[400,2]{0,1:T(2,128)}, u32[]{:S(2)}) copy-start(s32[400,2]{0,1:T(2,128)} %param.13) | copy-start | bytes 9604
  154.0 90.3 %all-to-all-start.5 = ((bf16[12,64,3072]{2,0,1:T(8,128)(2,1)}), bf16[12,64,3072]{2,0,1:T(8,128)(2,1)}, u32[]{:S(2)}, u32[]{:S(2)}) async-start(bf16[12,64,3072]{2,0,1:T(8,128)(2,1)} %bitcast.127), calls=%async_computation.5 | async-start | bytes 12582912 | tf_op jit(solution)/shard_map/all_to_all | solution.py:250
  244.2 36.1 %all-to-all-start.4 = ((bf16[16,63,768]{2,1,0:T(8,128)(2,1)}), bf16[16,63,768]{2,1,0:T(8,128)(2,1)}, u32[]{:S(2)}, u32[]{:S(2)}) async-start(bf16[16,63,768]{2,1,0:T(8,128)(2,1)} %broadcast_select_fusion), calls=%async_computation.4 | async-start | bytes 3145728 | tf_op jit(solution)/shard_map/all_to_all | solution.py:236
  280.4 38.5 %all-to-all-start.9 = ((bf16[16,63,768]{2,1,0:T(8,128)(2,1)}), bf16[16,63,768]{2,1,0:T(8,128)(2,1)}, u32[]{:S(2)}, u32[]{:S(2)}) async-start(bf16[16,63,768]{2,1,0:T(8,128)(2,1)} %select_convert_fusion), calls=%async_computation.9 | async-start | bytes 3145728 | tf_op jit(solution)/shard_map/all_to_all | solution.py:236
  309.2 1.6 copy-start.35
  318.9 28.6 %all-to-all-start.6 = ((bf16[16,63,768]{2,1,0:T(8,128)(2,1)}), bf16[16,63,768]{2,1,0:T(8,128)(2,1)}, u32[]{:S(2)}, u32[]{:S(2)}) async-start(bf16[16,63,768]{2,1,0:T(8,128)(2,1)} %reshape.326), calls=%async_computation.6 | async-start | bytes 3145728 | tf_op jit(solution)/shard_map/all_to_all | solution.py:243
  337.8 1.7 copy-start.34
  347.5 28.7 %all-to-all-start.10 = ((bf16[16,63,768]{2,1,0:T(8,128)(2,1)}), bf16[16,63,768]{2,1,0:T(8,128)(2,1)}, u32[]{:S(2)}, u32[]{:S(2)}) async-start(bf16[16,63,768]{2,1,0:T(8,128)(2,1)} %reshape.332), calls=%async_computation.10 | async-start | bytes 3145728 | tf_op jit(solution)/shard_map/all_to_all | solution.py:243
  376.2 18.4 %copy-start.22 = (f32[400,16]{0,1:T(8,128)}, f32[400,16]{0,1:T(8,128)S(1)}, u32[]{:S(2)}) copy-start(f32[400,16]{0,1:T(8,128)S(1)} %multiply_reduce_fusion.11) | copy-start | bytes 76804
  407.2 11.1 %copy-start.6 = (f32[200,768]{1,0:T(8,128)S(1)}, f32[200,768]{1,0:T(8,128)}, u32[]{:S(2)}) copy-start(f32[200,768]{1,0:T(8,128)} %param.23) | copy-start | bytes 1843204
  407.2 11.0 %all-to-all-start.7 = ((bf16[2,200,768]{2,1,0:T(8,128)(2,1)}), bf16[2,200,768]{2,1,0:T(8,128)(2,1)S(1)}, u32[]{:S(2)}, u32[]{:S(2)}) async-start(bf16[2,200,768]{2,1,0:T(8,128)(2,1)} %bitcast.18), calls=%async_computation.7 | async-start | bytes 1228800 | tf_op jit(solution)/shard_map/all_to_all | solution.py:225
  420.5 14.7 %all-to-all-start.12 = ((bf16[2,200,768]{2,1,0:T(8,128)(2,1)}), bf16[2,200,768]{2,1,0:T(8,128)(2,1)S(1)}, u32[]{:S(2)}, u32[]{:S(2)}) async-start(bf16[2,200,768]{2,1,0:T(8,128)(2,1)} %broadcast_in_dim.80), calls=%async_computation.12 | async-start | bytes 1228800 | tf_op jit(solution)/shard_map/all_to_all | solution.py:219
  435.1 13.1 %copy-start.13 = (bf16[2,200,6,64]{1,3,2,0:T(8,128)(2,1)S(1)}, bf16[2,200,6,64]{1,3,2,0:T(8,128)(2,1)}, u32[]{:S(2)}) copy-start(bf16[2,200,6,64]{1,3,2,0:T(8,128)(2,1)} %copy.266) | copy-start | bytes 921604
  435.1 13.1 %copy-start.14 = (bf16[2,200,6,64]{1,3,2,0:T(8,128)(2,1)S(1)}, bf16[2,200,6,64]{1,3,2,0:T(8,128)(2,1)}, u32[]{:S(2)}) copy-start(bf16[2,200,6,64]{1,3,2,0:T(8,128)(2,1)} %copy.265) | copy-start | bytes 921604
  435.1 13.1 %copy-start.33 = (pred[200]{0:T(512)(128)(4,1)S(1)}, pred[200]{0:T(512)(128)(4,1)}, u32[]{:S(2)}) copy-start(pred[200]{0:T(512)(128)(4,1)} %copy-done.32) | copy-start | bytes 604
  435.2 15.9 %copy-start.8 = (bf16[2,200,768]{2,1,0:T(8,128)(2,1)}, bf16[2,200,768]{2,1,0:T(8,128)(2,1)S(1)}, u32[]{:S(2)}) copy-start(bf16[2,200,768]{2,1,0:T(8,128)(2,1)S(1)} %all-to-all-done.12) | copy-start | bytes 1843204
  435.2 52.9 %all-to-all-start.17 = ((bf16[64,12,1536]{2,1,0:T(8,128)(2,1)}), bf16[64,12,1536]{2,1,0:T(8,128)(2,1)}, u32[]{:S(2)}, u32[]{:S(2)}) async-start(bf16[64,12,1536]{2,1,0:T(8,128)(2,1)} %reshape.342), calls=%async_computation.17 | async-start | bytes 6291456 | tf_op jit(solution)/shard_map/all_to_all | solution.py:260
  453.5 4.2 copy-start.17
  460.5 1.5 copy-start.5
  474.3 4.8 copy-start.18
  474.3 5.8 copy-start.10
  488.1 15.7 %all-to-all-start.13 = ((bf16[2,200,768]{2,1,0:T(8,128)(2,1)}), bf16[2,200,768]{2,1,0:T(8,128)(2,1)S(1)}, u32[]{:S(2)}, u32[]{:S(2)}) async-start(bf16[2,200,768]{2,1,0:T(8,128)(2,1)} %bitcast.27), calls=%async_computation.13 | async-start | bytes 1228800 | tf_op jit(solution)/shard_map/all_to_all | solution.py:225
  503.8 47.5 %all-to-all-start.16 = ((bf16[64,12,1536]{2,1,0:T(8,128)(2,1)}), bf16[64,12,1536]{2,1,0:T(8,128)(2,1)}, u32[]{:S(2)}, u32[]{:S(2)}) async-start(bf16[64,12,1536]{2,1,0:T(8,128)(2,1)} %reshape.341), calls=%async_computation.16 | async-start | bytes 6291456 | tf_op jit(solution)/shard_map/all_to_all | solution.py:260
  512.6 1.8 copy-start.23
  513.9 4.9 copy-start.9
  520.7 4.3 copy-start.19
  525.0 5.4 copy-start.1
  525.0 5.4 copy-start.26
  525.0 5.4 copy-start.29
  525.0 5.4 copy-start.31
  529.3 2.8 copy-start.15
  529.3 2.8 copy-start.16
  551.3 50.5 %all-to-all-start.14 = ((bf16[64,12,1576]{2,1,0:T(8,128)(2,1)}), bf16[64,12,1576]{2,1,0:T(8,128)(2,1)}, u32[]{:S(2)}, u32[]{:S(2)}) async-start(bf16[64,12,1576]{2,1,0:T(8,128)(2,1)} %copy.306), calls=%async_computation.14 | async-start | bytes 6815744 | tf_op jit(solution)/shard_map/all_to_all | solution.py:188
  566.0 1.7 copy-start.4
  566.1 1.7 copy-start.7
  605.4 8.7 %all-to-all-start.15 = ((f32[2,1,240]{2,1,0:T(1,128)}), f32[2,1,240]{2,1,0:T(1,128)S(1)}, u32[]{:S(2)}, u32[]{:S(2)}) async-start(f32[2,1,240]{2,1,0:T(1,128)} %reshape.442), calls=%async_computation.15 | async-start | bytes 4096 | tf_op jit(solution)/shard_map/all_to_all | solution.py:206
  (5 other events, 4.7 us)
